TPU v7x, 32 devices: a whole 2x2x4 slice. The times are simulated.
32 devices in a mesh: ctx: 2 (over core), fsdp: 16 (over z, y, x).
Axes of the slice: x: 2, y: 2, z: 4, core: 2. Of those that a mesh axis runs over, the one named last changes fastest.
Arguments:
- tokens: bfloat16 [16, 1024, 2048], P('fsdp', 'ctx'), may hold values from -6 to 6
- route_ids: int32 [16, 1024, 2], P('fsdp', 'ctx'), may hold values from 0 to 3, all different within a row
- gate_values: float32 [16, 1024, 2], P('fsdp', 'ctx'), may hold values from 0.25 to 0.75
- deal: int32 [16, 4], P('fsdp'), may hold values from 0 to 3, each once within a row
- norm1_gain: float32 [2048], replicated, may hold values from 0.1 to 1.9
- w_query: bfloat16 [2048, 2048], P('fsdp'), may hold values from -0.125 to 0.125
- w_key: bfloat16 [2048, 2048], P('fsdp'), may hold values from -0.125 to 0.125
- w_value: bfloat16 [2048, 2048], P('fsdp'), may hold values from -0.125 to 0.125
- w_out: bfloat16 [2048, 2048], P('fsdp'), may hold values from -1.5 to 1.5
- norm2_gain: float32 [2048], replicated, may hold values from 0.1 to 1.9
- w_gate: bfloat16 [22528, 2048], P('fsdp'), may hold values from -0.125 to 0.125
- w_up: bfloat16 [22528, 2048], P('fsdp'), may hold values from -0.125 to 0.125
- w_down: bfloat16 [22528, 2048], P('fsdp'), may hold values from -0.078125 to 0.078125
- cotangent: bfloat16 [16, 1024, 2048], P('fsdp', 'ctx'), may hold values from -6 to 6
Outputs:
- mixed: bfloat16 [16, 1024, 2048], P('fsdp', 'ctx')
- tokens_grad: bfloat16 [16, 1024, 2048], P('fsdp', 'ctx')
- norm1_grad: float32 [2048], P(('ctx', 'fsdp'))
- query_grad: float32 [2048, 2048], P(('ctx', 'fsdp'))
- key_grad: float32 [2048, 2048], P(('ctx', 'fsdp'))
- value_grad: float32 [2048, 2048], P(('ctx', 'fsdp'))
- out_grad: float32 [2048, 2048], P(('ctx', 'fsdp'))
- norm2_grad: float32 [2048], P(('ctx', 'fsdp'))
- gate_grad: float32 [22528, 2048], P('fsdp', 'ctx')
- up_grad: float32 [22528, 2048], P('fsdp', 'ctx')
- down_grad: float32 [22528, 2048], P('fsdp', 'ctx')
Inputs may be any that keep to these rules, and one draw needn't show every extreme that they name: Each row of deal names every block of the group once. `route_ids`: a token's two experts differ.
All inputs are finite; a program needn't handle non-finite values.
Results may differ from a plain program's by a relative error of at most 0.015.
Values may be sent and summed in bfloat16 or wider, within the bound.
No kernel may reach another device: no remote copies, remote signals or barrier semaphores. Data moves between devices by JAX's collectives and lax.ppermute only.
A program may use at most 448 MiB of HBM per device.

v0:
```python
import math

import jax
import jax.numpy as jnp
from jax import lax
from jax.sharding import PartitionSpec as P

D = 2048
HEADS = 16
HD = 128
EXPERTS = 4
TOPK = 2
PROMPT = 512
CONT = 256


norm_eps = 1e-05
highest = lax.Precision.HIGHEST


def rotate(vector, position, orient):
    half_size = vector.shape[-1] // 2
    frequency = jnp.exp(-math.log(10000.0) * jnp.arange(half_size, dtype=jnp.float32) / half_size)
    angles = position.astype(jnp.float32)[:, None] * frequency[None, :]
    cosine = jnp.cos(angles)[:, None, :]
    sine_part = orient * jnp.sin(angles)[:, None, :]
    first_half = vector[..., :half_size]
    second = vector[..., half_size:]
    return jnp.concatenate(
        [first_half * cosine - second * sine_part, second * cosine + first_half * sine_part],
        axis=-1,
    )


def layout(deal_row, group_len):
    block_size = group_len // deal_row.shape[0]
    token_index = jnp.arange(group_len, dtype=jnp.int32)
    anchor = deal_row[token_index // block_size] * block_size + token_index % block_size
    after_prompt = anchor - PROMPT
    in_prompt = anchor < PROMPT
    segment = jnp.where(in_prompt, 0, after_prompt // CONT + 1)
    position = jnp.where(in_prompt, anchor, PROMPT + after_prompt % CONT)
    return (position, segment)


def visibility(query_pos, query_seg, key_pos, key_seg):
    earlier = key_pos[None, :] <= query_pos[:, None]
    shared = (key_seg[None, :] == 0) | (key_seg[None, :] == query_seg[:, None])
    return earlier & shared


def route_slots(expert_ids, capacity):
    flat_ids = expert_ids.reshape(-1)
    onehot = (flat_ids[:, None] == jnp.arange(EXPERTS, dtype=jnp.int32)[None, :]).astype(jnp.int32)
    earlier = jnp.cumsum(onehot, axis=0) - onehot
    slot_index = jnp.sum(earlier * onehot, axis=1)
    kept_pair = slot_index < capacity
    place = flat_ids * capacity + jnp.minimum(slot_index, capacity - 1)
    target = jnp.arange(EXPERTS * capacity, dtype=jnp.int32)[None, :]
    return (place[:, None] == target) & kept_pair[:, None]


def normalize_parts(values, gain):
    inverse = lax.rsqrt(jnp.mean(values * values, axis=-1, keepdims=True) + norm_eps)
    unit_rows = values * inverse
    return (unit_rows * gain, unit_rows, inverse)


def norm_backward(grad_outer, unit_rows, inverse, gain):
    grad_unit = grad_outer * gain
    grad_inner = inverse * (
        grad_unit - unit_rows * jnp.mean(grad_unit * unit_rows, axis=-1, keepdims=True)
    )
    return (grad_inner, jnp.sum(grad_outer * unit_rows, axis=0))


def split_heads(matrix):
    return matrix.reshape(matrix.shape[0], HEADS, HD).transpose(1, 0, 2)


def join_heads(stacked):
    return stacked.transpose(1, 0, 2).reshape(stacked.shape[1], HEADS * HD)


def spread_experts(per_expert, repeats):
    capacity = per_expert.shape[1]
    widened = jnp.broadcast_to(
        per_expert[:, None], (EXPERTS, repeats, capacity, per_expert.shape[2])
    )
    return widened.reshape(EXPERTS * repeats, capacity, per_expert.shape[2])


def shards(
    tokens,
    route_ids,
    gate_values,
    deal,
    norm1_gain,
    w_query,
    w_key,
    w_value,
    w_out,
    norm2_gain,
    w_gate,
    w_up,
    w_down,
    cotangent,
):
    row_count = tokens.shape[1]
    ctx_count = lax.axis_size("ctx")
    fsdp_count = lax.axis_size("fsdp")
    group_len = row_count * ctx_count
    capacity = 5 * row_count * TOPK // (4 * EXPERTS)
    repeats = fsdp_count // EXPERTS
    score_scale = 1.0 / math.sqrt(HD)
    inputs = tokens[0].astype(jnp.float32)
    gates = gate_values[0]
    position_all, segment_all = layout(deal[0], group_len)
    offset = lax.axis_index("ctx") * row_count
    position = lax.dynamic_slice_in_dim(position_all, offset, row_count)
    segment = lax.dynamic_slice_in_dim(segment_all, offset, row_count)
    visible = visibility(position, segment, position_all, segment_all)
    full_q, full_k, full_v, full_o = (
        lax.all_gather(w_query, "fsdp", axis=0, tiled=True),
        lax.all_gather(w_key, "fsdp", axis=0, tiled=True),
        lax.all_gather(w_value, "fsdp", axis=0, tiled=True),
        lax.all_gather(w_out, "fsdp", axis=0, tiled=True),
    )
    normed_f, unit_one, inverse_one = normalize_parts(inputs, norm1_gain)
    normed = normed_f.astype(jnp.bfloat16)
    query_pre = jnp.dot(normed, full_q, preferred_element_type=jnp.float32)
    key_pre = jnp.dot(normed, full_k, preferred_element_type=jnp.float32)
    query = rotate(query_pre.reshape(row_count, HEADS, HD), position, 1.0).astype(jnp.bfloat16)
    keys = rotate(key_pre.reshape(row_count, HEADS, HD), position, 1.0).astype(jnp.bfloat16)
    values = jnp.dot(normed, full_v, preferred_element_type=jnp.float32).astype(jnp.bfloat16)
    all_keys, all_values = (
        lax.all_gather(keys.reshape(row_count, D), "ctx", axis=0, tiled=True),
        lax.all_gather(values, "ctx", axis=0, tiled=True),
    )
    query_heads = query.transpose(1, 0, 2)
    key_heads = split_heads(all_keys)
    value_heads = split_heads(all_values)

    def head_forward(head_item):
        query_one, keys_one, values_one = head_item
        scores = jnp.dot(query_one, keys_one.T, preferred_element_type=jnp.float32) * score_scale
        scores = jnp.where(visible, scores, -1e30)
        row_max = jnp.max(scores, axis=1, keepdims=True)
        expo = jnp.exp(scores - row_max)
        row_total = jnp.sum(expo, axis=1, keepdims=True)
        weights_low = (expo / row_total).astype(jnp.bfloat16)
        context_one = jnp.dot(weights_low, values_one, preferred_element_type=jnp.float32)
        return (context_one, row_max + jnp.log(row_total))

    context_heads, log_total = lax.map(head_forward, (query_heads, key_heads, value_heads))
    context = join_heads(context_heads).astype(jnp.bfloat16)
    attention = jnp.dot(context, full_o, preferred_element_type=jnp.float32)
    hidden_in = inputs + attention
    normed_two_f, unit_two, inverse_two = normalize_parts(hidden_in, norm2_gain)
    normed_two = normed_two_f.astype(jnp.bfloat16)
    select = route_slots(route_ids[0], capacity)
    select_low = select.astype(jnp.bfloat16)
    select_full = select.astype(jnp.float32)
    pairs = jnp.repeat(normed_two, TOPK, axis=0)
    dispatched = jnp.dot(select_low.T, pairs, preferred_element_type=jnp.float32).astype(
        jnp.bfloat16
    )
    outgoing = spread_experts(dispatched.reshape(EXPERTS, capacity, D), repeats)
    arrived = lax.all_to_all(outgoing, "fsdp", split_axis=0, concat_axis=0, tiled=True).reshape(
        fsdp_count * capacity, D
    )
    gate_act = jnp.dot(arrived, w_gate.T, preferred_element_type=jnp.float32)
    up_act = jnp.dot(arrived, w_up.T, preferred_element_type=jnp.float32)
    sigmoid_gate = jax.nn.sigmoid(gate_act)
    silu_gate = gate_act * sigmoid_gate
    hidden = (silu_gate * up_act).astype(jnp.bfloat16)
    partial_out = jnp.dot(hidden, w_down, preferred_element_type=jnp.float32).reshape(
        fsdp_count, capacity, D
    )
    returned = lax.all_to_all(
        partial_out.astype(jnp.bfloat16), "fsdp", split_axis=0, concat_axis=0, tiled=True
    ).astype(partial_out.dtype)
    slot_out = jnp.sum(returned.reshape(EXPERTS, repeats, capacity, D), axis=1).reshape(
        EXPERTS * capacity, D
    )
    pair_out = jnp.dot(select_full, slot_out, precision=highest).reshape(row_count, TOPK, D)
    mixed = hidden_in + jnp.sum(pair_out * gates[:, :, None], axis=1)
    grad_outer = cotangent[0].astype(jnp.float32)
    grad_pairs = (grad_outer[:, None, :] * gates[:, :, None]).reshape(row_count * TOPK, D)
    grad_slots = jnp.dot(select_full.T, grad_pairs, precision=highest).astype(jnp.bfloat16)
    grad_outgoing = spread_experts(grad_slots.reshape(EXPERTS, capacity, D), repeats)
    grad_arrived = lax.all_to_all(
        grad_outgoing, "fsdp", split_axis=0, concat_axis=0, tiled=True
    ).reshape(fsdp_count * capacity, D)
    grad_hidden = jnp.dot(grad_arrived, w_down.T, preferred_element_type=jnp.float32)
    down_grad = jnp.dot(hidden.T, grad_arrived, preferred_element_type=jnp.float32)
    grad_gate = (
        grad_hidden * up_act * sigmoid_gate * (1.0 + gate_act * (1.0 - sigmoid_gate))
    ).astype(jnp.bfloat16)
    grad_up = (grad_hidden * silu_gate).astype(jnp.bfloat16)
    gate_grad = jnp.dot(grad_gate.T, arrived, preferred_element_type=jnp.float32)
    up_grad = jnp.dot(grad_up.T, arrived, preferred_element_type=jnp.float32)
    grad_inputs = jnp.dot(grad_gate, w_gate, preferred_element_type=jnp.float32) + jnp.dot(
        grad_up, w_up, preferred_element_type=jnp.float32
    )
    grad_returned = lax.all_to_all(
        grad_inputs.reshape(fsdp_count, capacity, D).astype(jnp.bfloat16),
        "fsdp",
        split_axis=0,
        concat_axis=0,
        tiled=True,
    ).astype(jnp.float32)
    grad_slot_in = jnp.sum(grad_returned.reshape(EXPERTS, repeats, capacity, D), axis=1).reshape(
        EXPERTS * capacity, D
    )
    grad_normed_two = jnp.sum(
        jnp.dot(select_full, grad_slot_in, precision=highest).reshape(row_count, TOPK, D), axis=1
    )
    grad_norm_two, norm2_grad = norm_backward(grad_normed_two, unit_two, inverse_two, norm2_gain)
    grad_hidden_in = grad_outer + grad_norm_two
    grad_attention = grad_hidden_in.astype(jnp.bfloat16)
    back_q, back_k, back_v, back_o = (
        lax.all_gather(w_query, "fsdp", axis=0, tiled=True),
        lax.all_gather(w_key, "fsdp", axis=0, tiled=True),
        lax.all_gather(w_value, "fsdp", axis=0, tiled=True),
        lax.all_gather(w_out, "fsdp", axis=0, tiled=True),
    )
    out_grad = jnp.dot(context.T, grad_attention, preferred_element_type=jnp.float32)
    grad_context = jnp.dot(grad_attention, back_o.T, preferred_element_type=jnp.float32).astype(
        jnp.bfloat16
    )
    grad_context_heads = split_heads(grad_context)

    def head_backward(head_item):
        query_one, keys_one, values_one, grad_one, log_one = head_item
        scores = jnp.dot(query_one, keys_one.T, preferred_element_type=jnp.float32) * score_scale
        soft = jnp.where(visible, jnp.exp(scores - log_one), 0.0)
        values_back = jnp.dot(
            soft.astype(jnp.bfloat16).T, grad_one, preferred_element_type=jnp.float32
        )
        grad_prob = jnp.dot(grad_one, values_one.T, preferred_element_type=jnp.float32)
        delta_rows = jnp.sum(grad_prob * soft, axis=1, keepdims=True)
        grad_scores = (soft * (grad_prob - delta_rows)).astype(jnp.bfloat16)
        query_back = (
            jnp.dot(grad_scores, keys_one, preferred_element_type=jnp.float32) * score_scale
        )
        keys_back = (
            jnp.dot(grad_scores.T, query_one, preferred_element_type=jnp.float32) * score_scale
        )
        return (query_back, keys_back, values_back)

    query_back_heads, keys_back_heads, values_back_heads = lax.map(
        head_backward, (query_heads, key_heads, value_heads, grad_context_heads, log_total)
    )
    keys_back_all = join_heads(keys_back_heads)
    values_back_all = join_heads(values_back_heads)
    keys_back_own, values_back_own = (
        lax.psum_scatter(
            keys_back_all.astype(jnp.bfloat16), "ctx", scatter_dimension=0, tiled=True
        ).astype(jnp.float32),
        lax.psum_scatter(
            values_back_all.astype(jnp.bfloat16), "ctx", scatter_dimension=0, tiled=True
        ).astype(jnp.float32),
    )
    grad_query = (
        rotate(query_back_heads.transpose(1, 0, 2), position, -1.0)
        .reshape(row_count, D)
        .astype(jnp.bfloat16)
    )
    grad_key = (
        rotate(keys_back_own.reshape(row_count, HEADS, HD), position, -1.0)
        .reshape(row_count, D)
        .astype(jnp.bfloat16)
    )
    grad_value = values_back_own.astype(jnp.bfloat16)
    query_grad = jnp.dot(normed.T, grad_query, preferred_element_type=jnp.float32)
    key_grad = jnp.dot(normed.T, grad_key, preferred_element_type=jnp.float32)
    value_grad = jnp.dot(normed.T, grad_value, preferred_element_type=jnp.float32)
    grad_normed = jnp.dot(grad_query, back_q.T, preferred_element_type=jnp.float32)
    grad_normed = grad_normed + jnp.dot(grad_key, back_k.T, preferred_element_type=jnp.float32)
    grad_normed = grad_normed + jnp.dot(grad_value, back_v.T, preferred_element_type=jnp.float32)
    grad_norm_one, norm1_grad = norm_backward(grad_normed, unit_one, inverse_one, norm1_gain)
    tokens_grad = (grad_hidden_in + grad_norm_one).astype(jnp.bfloat16)
    summed = (
        lax.psum_scatter(norm1_grad, ("ctx", "fsdp"), scatter_dimension=0, tiled=True),
        lax.psum_scatter(query_grad, ("ctx", "fsdp"), scatter_dimension=0, tiled=True),
        lax.psum_scatter(key_grad, ("ctx", "fsdp"), scatter_dimension=0, tiled=True),
        lax.psum_scatter(value_grad, ("ctx", "fsdp"), scatter_dimension=0, tiled=True),
        lax.psum_scatter(out_grad, ("ctx", "fsdp"), scatter_dimension=0, tiled=True),
        lax.psum_scatter(norm2_grad, ("ctx", "fsdp"), scatter_dimension=0, tiled=True),
    )
    gate_sum, up_sum, down_sum = (
        lax.psum_scatter(
            gate_grad.astype(jnp.bfloat16), "ctx", scatter_dimension=1, tiled=True
        ).astype(jnp.float32),
        lax.psum_scatter(
            up_grad.astype(jnp.bfloat16), "ctx", scatter_dimension=1, tiled=True
        ).astype(jnp.float32),
        lax.psum_scatter(
            down_grad.astype(jnp.bfloat16), "ctx", scatter_dimension=1, tiled=True
        ).astype(jnp.float32),
    )
    return (
        mixed.astype(jnp.bfloat16)[None],
        tokens_grad[None],
        summed[0],
        summed[1],
        summed[2],
        summed[3],
        summed[4],
        summed[5],
        gate_sum,
        up_sum,
        down_sum,
    )


def solution(mesh):
    in_specs = (
        P("fsdp", "ctx", None),
        P("fsdp", "ctx", None),
        P("fsdp", "ctx", None),
        P("fsdp", None),
        P(),
        P("fsdp", None),
        P("fsdp", None),
        P("fsdp", None),
        P("fsdp", None),
        P(),
        P("fsdp", None),
        P("fsdp", None),
        P("fsdp", None),
        P("fsdp", "ctx", None),
    )
    out_specs = (
        P("fsdp", "ctx", None),
        P("fsdp", "ctx", None),
        P(("ctx", "fsdp")),
        P(("ctx", "fsdp"), None),
        P(("ctx", "fsdp"), None),
        P(("ctx", "fsdp"), None),
        P(("ctx", "fsdp"), None),
        P(("ctx", "fsdp")),
        P("fsdp", "ctx"),
        P("fsdp", "ctx"),
        P("fsdp", "ctx"),
    )
    return jax.shard_map(shards, mesh=mesh, in_specs=in_specs, out_specs=out_specs, check_vma=False)
```

profile of v0, /device:TPU:0, one launch (start us, length us, event | category | flops | bytes accessed | tf_op | source)
XLA Modules:
  0.0 4445.2 jit_solution(11487067371904511674)
XLA Ops:
  16.9 109.5 %all-gather.9.cloned.1.call-done = bf16[2048,2048]{1,0:T(8,128)(2,1)} async-done(((bf16[128,2048]{1,0:T(8,128)(2,1)}), bf16[2048,2048]{1,0:T(8,128)(2,1)}) %all-gather.9.cloned.1.call-update) | async-done | bytes 8388624 | tf_op jit(solution)/shard_map/all_gather | solution.py:125
  126.3 12.3 copy.51
  138.7 101.5 %all-gather.7.cloned.1.call-done = bf16[2048,2048]{1,0:T(8,128)(2,1)} async-done(((bf16[128,2048]{1,0:T(8,128)(2,1)}), bf16[2048,2048]{1,0:T(8,128)(2,1)}) %all-gather.7.cloned.1.call-update) | async-done | bytes 8388624 | tf_op jit(solution)/shard_map/all_gather | solution.py:124
  240.2 12.5 copy.50
  268.7 85.3 %all-gather.13.cloned.1.call-done = bf16[2048,2048]{1,0:T(8,128)(2,1)} async-done(((bf16[128,2048]{1,0:T(8,128)(2,1)}), bf16[2048,2048]{1,0:T(8,128)(2,1)}) %all-gather.13.cloned.1.call-update) | async-done | bytes 8388624 | tf_op jit(solution)/shard_map/all_gather | solution.py:126
  354.0 9.2 convolution_convert_fusion.6
  390.0 84.9 %while.30 = (s32[]{:T(128)}, bf16[16,512,128]{1,2,0:T(8,128)(2,1)}, f32[16,512,1]{1,2,0:T(1,128)}, bf16[16,512,128]{2,1,0:T(8,128)(2,1)}, bf16[16,1024,128]{2,1,...) while((s32[]{:T(128)}, bf16[16,512,128]{1,2,0:T(8,128)(2,1)}, ...), condition=%wide.region_4.5_spmd.clone.clone, body=%wide.region_1.4_spmd.clone.sunk.clone | while | flops 274726400 | bytes 7245421 | solution.py:155
  474.9 26.5 all-gather.17.cloned.1.call-done
  501.4 7.8 multiply_reduce_fusion.4
  522.7 8.3 convolution_convert_fusion.1
  531.0 7.4 broadcast_in_dim.45
  550.6 10.9 mul.405
  561.8 22.8 fusion.42
  584.7 352.8 %all-to-all-done = bf16[16,320,2048]{2,1,0:T(8,128)(2,1)} async-done(((bf16[16,320,2048]{2,1,0:T(8,128)(2,1)}), bf16[16,320,2048]{2,1,0:T(8,128)(2,1)}, u32[]{:S(2)}, u32[]{:S(2)}) %all-to-all-start) | async-done | bytes 20971552 | tf_op jit(solution)/shard_map/all_to_all | solution.py:169
  937.5 9.1 broadcast_in_dim.50
  946.6 91.0 %all-to-all-start.2 = ((bf16[16,320,2048]{2,1,0:T(8,128)(2,1)}), bf16[16,320,2048]{2,1,0:T(8,128)(2,1)}, u32[]{:S(2)}, u32[]{:S(2)}) async-start(bf16[16,320,2048]{2,1,0:T(8,128)(2,1)} %bitcast.294), calls=%async_computation.2 | async-start | bytes 41943040 | tf_op jit(solution)/shard_map/all_to_all | solution.py:192
  1037.6 40.0 fusion.122
  1077.6 38.1 fusion.123
  1115.8 313.1 %all-to-all-done.2 = bf16[16,320,2048]{2,1,0:T(8,128)(2,1)} async-done(((bf16[16,320,2048]{2,1,0:T(8,128)(2,1)}), bf16[16,320,2048]{2,1,0:T(8,128)(2,1)}, u32[]{:S(2)}, u32[]{:S(2)}) %all-to-all-start.2) | async-done | bytes 20971552 | tf_op jit(solution)/shard_map/all_to_all | solution.py:192
  1428.9 52.5 %multiply_convert_fusion.1 = (bf16[5120,1408]{1,0:T(8,128)(2,1)}, bf16[5120,1408]{1,0:T(8,128)(2,1)}, bf16[5120,1408]{1,0:T(8,128)(2,1)}) fusion(f32[5120,1408]{1,0:T(8,128)} %fusion.122, f32[5120,1408]{1,0:T(8,128)} %fusion.123, bf16[5120,2048]{1,0:T(8,128)(2,1)} %bitcast.35, bf16[1408,2048]{1,0:T(8,128)(2,1)} %param.30), kind=kOutput, calls=%fused_computation.55 | convolution fusion | flops 29636034560 | bytes 127664128 | tf_op jit(solution)/shard_map/dot_general | solution.py:195
  1481.4 40.0 fusion.124
  1521.5 42.7 add_convert_fusion
  1564.2 89.6 %all-to-all-start.3 = ((bf16[16,320,2048]{2,1,0:T(8,128)(2,1)}), bf16[16,320,2048]{2,1,0:T(8,128)(2,1)}, u32[]{:S(2)}, u32[]{:S(2)}) async-start(bf16[16,320,2048]{2,1,0:T(8,128)(2,1)} %bitcast.296), calls=%async_computation.3 | async-start | bytes 41943040 | tf_op jit(solution)/shard_map/all_to_all | solution.py:206
  1653.8 38.7 convolution_convert_fusion
  1692.5 350.2 %all-to-all-done.3 = bf16[16,320,2048]{2,1,0:T(8,128)(2,1)} async-done(((bf16[16,320,2048]{2,1,0:T(8,128)(2,1)}), bf16[16,320,2048]{2,1,0:T(8,128)(2,1)}, u32[]{:S(2)}, u32[]{:S(2)}) %all-to-all-start.3) | async-done | bytes 20971552 | tf_op jit(solution)/shard_map/all_to_all | solution.py:206
  2042.7 88.9 %all-to-all-start.1 = ((bf16[16,320,2048]{2,1,0:T(8,128)(2,1)}), bf16[16,320,2048]{2,1,0:T(8,128)(2,1)}, u32[]{:S(2)}, u32[]{:S(2)}) async-start(bf16[16,320,2048]{2,1,0:T(8,128)(2,1)} %bitcast.295), calls=%async_computation.1 | async-start | bytes 41943040 | tf_op jit(solution)/shard_map/all_to_all | solution.py:180
  2132.5 16.2 convert_reduce_fusion
  2148.7 20.0 fusion.72
  2170.7 348.9 %all-to-all-done.1 = bf16[16,320,2048]{2,1,0:T(8,128)(2,1)} async-done(((bf16[16,320,2048]{2,1,0:T(8,128)(2,1)}), bf16[16,320,2048]{2,1,0:T(8,128)(2,1)}, u32[]{:S(2)}, u32[]{:S(2)}) %all-to-all-start.1) | async-done | bytes 20971552 | tf_op jit(solution)/shard_map/all_to_all | solution.py:180
  2519.6 15.9 convert_reduce_fusion.1
  2535.5 20.4 multiply_reduce_fusion.1
  2558.5 9.7 fusion.95
  2570.2 201.9 %while.31 = (s32[]{:T(128)}, f32[16,512,128]{1,2,0:T(8,128)}, bf16[16,1024,128]{1,2,0:T(8,128)(2,1)}, bf16[16,1024,128]{1,2,0:T(8,128)(2,1)}, bf16[16,512,128]{2...) while((s32[]{:T(128)}, f32[16,512,128]{1,2,0:T(8,128)}, ...), condition=%wide.region_16.17_spmd.clone.clone, body=%wide.region_14.16_spmd.clone.sunk.clone | while | flops 678231552 | bytes 20213896 | solution.py:252
  2772.8 38.5 convolution_convert_fusion.4
  2811.4 38.9 convolution_convert_fusion.3
  2850.4 38.6 convolution_convert_fusion.2
  2889.2 14.9 fusion.96
  2912.3 8.4 fusion.93
  2920.7 10.2 fusion.91
  2931.2 10.6 fusion.99
  2952.9 33.7 reduce-scatter.26.cloned.1.call-done
  2991.9 9.9 fusion.126
  3007.9 10.0 fusion.67
  3017.9 91.1 %all-reduce.2 = (f32[2048]{0:T(1024)S(1)}, f32[2048]{0:T(1024)S(1)}) all-reduce(f32[2048]{0:T(1024)S(1)} %get-tuple-element.249, f32[2048]{0:T(1024)S(1)} %copy-done.22), channel_id=4, replica_groups=mesh['ctx'=2,'fsdp'=16] {'ctx','fsdp'}, use_global_device_ids=true, to_apply=%region_21.22.clone | all-reduce | flops 4096 | bytes 32768
  3116.1 233.4 %reduce-scatter.20.cloned.1.call-done = f32[64,2048]{1,0:T(8,128)} async-done(((f32[2048,2048]{1,0:T(8,128)}), f32[64,2048]{1,0:T(8,128)}) %reduce-scatter.20.cloned.1.call-update) | async-done | bytes 524304 | tf_op jit(solution)/shard_map/reduce_scatter | solution.py:289
  3349.5 363.0 %reduce-scatter.14.cloned.1.call-done = f32[64,2048]{1,0:T(8,128)} async-done(((f32[2048,2048]{1,0:T(8,128)}), f32[64,2048]{1,0:T(8,128)}) %reduce-scatter.14.cloned.1.call-update) | async-done | bytes 524304 | tf_op jit(solution)/shard_map/reduce_scatter | solution.py:286
  3712.5 362.9 %reduce-scatter.16.cloned.1.call-done = f32[64,2048]{1,0:T(8,128)} async-done(((f32[2048,2048]{1,0:T(8,128)}), f32[64,2048]{1,0:T(8,128)}) %reduce-scatter.16.cloned.1.call-update) | async-done | bytes 524304 | tf_op jit(solution)/shard_map/reduce_scatter | solution.py:287
  4075.4 362.9 %reduce-scatter.18.cloned.1.call-done = f32[64,2048]{1,0:T(8,128)} async-done(((f32[2048,2048]{1,0:T(8,128)}), f32[64,2048]{1,0:T(8,128)}) %reduce-scatter.18.cloned.1.call-update) | async-done | bytes 524304 | tf_op jit(solution)/shard_map/reduce_scatter | solution.py:288
  (460 shorter events, 410.6 us)
Async XLA Ops:
  7.2 119.2 %all-gather.9.cloned.1.call-start = ((), (), s32[]{:S(2)}) async-start(), calls=%async_computation.14 | async-start | bytes 8912896 | tf_op jit(solution)/shard_map/all_gather | solution.py:125
  7.9 232.3 %all-gather.7.cloned.1.call-start = ((), (), s32[]{:S(2)}) async-start(), calls=%async_computation.13 | async-start | bytes 8912896 | tf_op jit(solution)/shard_map/all_gather | solution.py:124
  8.7 345.3 %all-gather.13.cloned.1.call-start = ((), (), s32[]{:S(2)}) async-start(), calls=%async_computation.16 | async-start | bytes 8912896 | tf_op jit(solution)/shard_map/all_gather | solution.py:126
  9.4 365.5 %all-gather.11.cloned.1.call-start = ((), (), s32[]{:S(2)}) async-start(), calls=%async_computation.15 | async-start | bytes 6291456 | tf_op jit(solution)/shard_map/all_gather | solution.py:137
  15.6 338.4 %copy-start.32 = (f32[512]{0:T(512)}, f32[512]{0:T(512)S(1)}, u32[]{:S(2)}) copy-start(f32[512]{0:T(512)S(1)} %add_rsqrt_fusion.1) | copy-start | bytes 6148
  16.9 247.8 %copy-start.17 = (f32[512,64]{0,1:T(8,128)}, f32[512,64]{0,1:T(8,128)S(1)}, u32[]{:S(2)}) copy-start(f32[512,64]{0,1:T(8,128)S(1)} %get-tuple-element.332) | copy-start | bytes 393220
  240.2 12.5 copy-start.6
  240.2 12.5 copy-start.30
  268.6 116.1 %all-gather.15.cloned.1.call-start = ((), (), s32[]{:S(2)}) async-start(), calls=%async_computation.17 | async-start | bytes 6291456 | tf_op jit(solution)/shard_map/all_gather | solution.py:138
  363.2 138.2 %all-gather.17.cloned.1.call-start = ((), (), s32[]{:S(2)}) async-start(), calls=%async_computation.18 | async-start | bytes 8912896 | tf_op jit(solution)/shard_map/all_gather | solution.py:127
  368.1 193.7 %copy-start.37 = (pred[1024]{0:T(1024)(128)(4,1)}, pred[1024]{0:T(1024)(128)(4,1)S(1)}, u32[]{:S(2)}) copy-start(pred[1024]{0:T(1024)(128)(4,1)S(1)} %broadcast_compare_fusion.1) | copy-start | bytes 3076
  474.9 34.3 copy-start.26
  474.9 34.3 copy-start.28
  474.9 34.3 copy-start.39
  474.9 34.3 copy-start.41
  474.9 34.3 copy-start.43
  501.4 9.9 copy-start.20
  538.4 399.1 %all-to-all-start = ((bf16[16,320,2048]{2,1,0:T(8,128)(2,1)}), bf16[16,320,2048]{2,1,0:T(8,128)(2,1)}, u32[]{:S(2)}, u32[]{:S(2)}) async-start(bf16[16,320,2048]{2,1,0:T(8,128)(2,1)} %bitcast.293), calls=%async_computation | async-start | bytes 41943040 | tf_op jit(solution)/shard_map/all_to_all | solution.py:169
  550.6 10.9 copy-start.35
  946.6 131.0 %slice-start.4 = ((s8[5767168]{0:T(1024)(128)(4,1)}), s8[1572864]{0:T(1024)(128)(4,1)S(1)}, s32[]{:S(2)}) async-start(s8[5767168]{0:T(1024)(128)(4,1)} %bitcast.326), calls=%async_computation.32 | async-start | bytes 3145728
  946.6 482.3 %all-to-all-start.2 = ((bf16[16,320,2048]{2,1,0:T(8,128)(2,1)}), bf16[16,320,2048]{2,1,0:T(8,128)(2,1)}, u32[]{:S(2)}, u32[]{:S(2)}) async-start(bf16[16,320,2048]{2,1,0:T(8,128)(2,1)} %bitcast.294), calls=%async_computation.2 | async-start | bytes 41943040 | tf_op jit(solution)/shard_map/all_to_all | solution.py:192
  1037.6 40.0 slice-start.5
  1564.2 478.5 %all-to-all-start.3 = ((bf16[16,320,2048]{2,1,0:T(8,128)(2,1)}), bf16[16,320,2048]{2,1,0:T(8,128)(2,1)}, u32[]{:S(2)}, u32[]{:S(2)}) async-start(bf16[16,320,2048]{2,1,0:T(8,128)(2,1)} %bitcast.296), calls=%async_computation.3 | async-start | bytes 41943040 | tf_op jit(solution)/shard_map/all_to_all | solution.py:206
  2042.7 89.0 %copy-start.38 = (pred[1024]{0:T(1024)(128)(4,1)S(1)}, pred[1024]{0:T(1024)(128)(4,1)}, u32[]{:S(2)}) copy-start(pred[1024]{0:T(1024)(128)(4,1)} %copy-done.37) | copy-start | bytes 3076
  2042.7 89.3 %copy-start.25 = (s32[1024]{0:T(1024)S(1)}, s32[1024]{0:T(1024)}, u32[]{:S(2)}) copy-start(s32[1024]{0:T(1024)} %get-tuple-element.328) | copy-start | bytes 12292
  2042.7 89.5 %copy-start.13 = (s32[1,512,2]{2,1,0:T(8,128)S(1)}, s32[1,512,2]{2,1,0:T(8,128)}, u32[]{:S(2)}) copy-start(s32[1,512,2]{2,1,0:T(8,128)} %copy-done.12) | copy-start | bytes 12292
  2042.7 476.9 %all-to-all-start.1 = ((bf16[16,320,2048]{2,1,0:T(8,128)(2,1)}), bf16[16,320,2048]{2,1,0:T(8,128)(2,1)}, u32[]{:S(2)}, u32[]{:S(2)}) async-start(bf16[16,320,2048]{2,1,0:T(8,128)(2,1)} %bitcast.295), calls=%async_computation.1 | async-start | bytes 41943040 | tf_op jit(solution)/shard_map/all_to_all | solution.py:180
  2131.6 772.6 %reduce-scatter.10.cloned.1.call-start = ((), (), s32[]{:S(2)}) async-start(), calls=%async_computation.19 | async-start | bytes 6291456 | tf_op jit(solution)/shard_map/reduce_scatter | solution.py:258
  2148.7 20.0 copy-start.1
  2148.7 20.0 copy-start.21
  2148.7 20.0 copy-start.24
  2170.7 364.8 %copy-start.36 = (f32[1,512,2]{1,2,0:T(2,128)S(1)}, f32[1,512,2]{1,2,0:T(2,128)}, u32[]{:S(2)}) copy-start(f32[1,512,2]{1,2,0:T(2,128)} %param.20) | copy-start | bytes 12292
  2535.5 20.4 copy-start.2
  2535.5 20.4 copy-start.5
  2535.5 20.5 copy-start.10
  2772.1 159.1 %reduce-scatter.12.cloned.1.call-start = ((), (), s32[]{:S(2)}) async-start(), calls=%async_computation.20 | async-start | bytes 6291456 | tf_op jit(solution)/shard_map/reduce_scatter | solution.py:261
  2772.8 169.0 %reduce-scatter.22.cloned.1.call-start = ((), (), s32[]{:S(2)}) async-start(), calls=%async_computation.25 | async-start | bytes 8650752 | tf_op jit(solution)/shard_map/reduce_scatter | solution.py:293
  2811.3 136.5 %reduce-scatter.24.cloned.1.call-start = ((), (), s32[]{:S(2)}) async-start(), calls=%async_computation.26 | async-start | bytes 8650752 | tf_op jit(solution)/shard_map/reduce_scatter | solution.py:296
  2850.3 136.4 %reduce-scatter.26.cloned.1.call-start = ((), (), s32[]{:S(2)}) async-start(), calls=%async_computation.27 | async-start | bytes 8650752 | tf_op jit(solution)/shard_map/reduce_scatter | solution.py:299
  2888.9 460.6 %reduce-scatter.20.cloned.1.call-start = ((), (), s32[]{:S(2)}) async-start(), calls=%async_computation.24 | async-start | bytes 17301504 | tf_op jit(solution)/shard_map/reduce_scatter | solution.py:289
  2904.2 808.4 %reduce-scatter.14.cloned.1.call-start = ((), (), s32[]{:S(2)}) async-start(), calls=%async_computation.21 | async-start | bytes 17301504 | tf_op jit(solution)/shard_map/reduce_scatter | solution.py:286
  2920.6 1154.8 %reduce-scatter.16.cloned.1.call-start = ((), (), s32[]{:S(2)}) async-start(), calls=%async_computation.22 | async-start | bytes 17301504 | tf_op jit(solution)/shard_map/reduce_scatter | solution.py:287
  2930.9 1507.3 %reduce-scatter.18.cloned.1.call-start = ((), (), s32[]{:S(2)}) async-start(), calls=%async_computation.23 | async-start | bytes 17301504 | tf_op jit(solution)/shard_map/reduce_scatter | solution.py:288
  2986.7 15.1 slice-start
  2991.9 9.9 slice-start.1
  2991.9 9.9 copy-start.15
  2991.9 16.0 slice-start.2
  3007.9 10.0 copy-start.22
  (22 other events, 81.2 us)
Sparse Core Ops, SparseCore 0:
  10.8 115.5 all-gather.8
  129.1 111.0 all-gather.6
  242.9 111.0 all-gather.12
  356.0 11.8 all-gather.10
  369.8 14.8 all-gather.14
  387.4 113.9 all-gather.16
  2772.2 94.1 reduce-scatter.9
  2868.7 13.3 reduce-scatter.11
  2885.0 23.0 reduce-scatter.21
  2910.9 36.7 reduce-scatter.23
  2950.0 36.5 reduce-scatter.25
  2989.5 359.9 reduce-scatter.19
  3352.5 360.0 reduce-scatter.13
  3715.3 359.9 reduce-scatter.15
  4078.2 359.9 reduce-scatter.17
where the time goes:
time: 4460 us; the launch traced here: 4450 us
  waiting for transfers between devices  3050 us (68%)
  matrix products  759 us (17%)
  starting transfers between devices  277 us (6%)
  local copies, waits for them, and re-layouts  158 us (4%)
  other arithmetic  94.3 us (2%)
  blocking collectives  91.1 us (2%)
    reduce_scatter x1, waiting for transfers between devices, shards(): lax.psum_scatter(query_grad, ('ctx', 'fsdp'), scatter_dimension=0, tiled=...  363 us
    reduce_scatter x1, waiting for transfers between devices, shards(): lax.psum_scatter(key_grad, ('ctx', 'fsdp'), scatter_dimension=0, tiled=True)  363 us
    reduce_scatter x1, waiting for transfers between devices, shards(): lax.psum_scatter(value_grad, ('ctx', 'fsdp'), scatter_dimension=0, tiled=...  363 us
    all_to_all x1, waiting for transfers between devices, shards(): lax.all_to_all(outgoing, 'fsdp', split_axis=0, concat_axis=0, tiled=True)  353 us
    all_to_all x1, waiting for transfers between devices, shards(): lax.all_to_all(grad_inputs.reshape(fsdp_count, capacity, D).astype(jnp.bf...  350 us
    all_to_all x1, waiting for transfers between devices, shards(): lax.all_to_all(partial_out.astype(jnp.bfloat16), 'fsdp', split_axis=0, co...  349 us
    all_to_all x1, waiting for transfers between devices, shards(): lax.all_to_all(grad_outgoing, 'fsdp', split_axis=0, concat_axis=0, tiled=...  313 us
    reduce_scatter x1, waiting for transfers between devices, shards(): lax.psum_scatter(out_grad, ('ctx', 'fsdp'), scatter_dimension=0, tiled=True)  233 us
  transfers between devices with their start and end apart: 19, of which 14 were waited for; matrix products, arithmetic and copies ran while one was open for 13% of the time, Pallas kernels for 0%

commit v1 on v0

v1 whole, which is shorter than its diff:
```python
import functools
import math

import jax
import jax.numpy as jnp
from jax import lax
from jax.experimental import pallas as pl
from jax.experimental.pallas import tpu as pltpu
from jax.sharding import PartitionSpec as P

D = 2048
HEADS = 16
HD = 128
EXPERTS = 4
TOPK = 2
PROMPT = 512
CONT = 256
TILE = 256

norm_eps = 1e-05
scale = 1.0 / math.sqrt(HD)
bf16 = jnp.bfloat16
f32 = jnp.float32


def dot(a, b, ca, cb, out=f32):
    r = lax.dot_general(a, b, (((ca,), (cb,)), ((), ())), preferred_element_type=f32)
    return r.astype(out)


def tile_keys(t):
    prompt_tiles = PROMPT // TILE
    if t < prompt_tiles:
        return list(range(t + 1))
    per = CONT // TILE
    first = prompt_tiles + ((t - prompt_tiles) // per) * per
    return list(range(prompt_tiles)) + list(range(first, t + 1))


def load_tile(ref, perm, t, block, cols):
    per = TILE // block
    parts = [
        ref[pl.ds(pl.multiple_of(perm[t * per + i] * block, block), block), cols]
        for i in range(per)
    ]
    return parts[0] if per == 1 else jnp.concatenate(parts, axis=0)


def store_tile(ref, perm, t, block, cols, value):
    per = TILE // block
    for i in range(per):
        ref[pl.ds(pl.multiple_of(perm[t * per + i] * block, block), block), cols] = value[
            i * block : (i + 1) * block
        ]


def spread_keys(ref, tiles):
    runs, start = [], tiles[0]
    for a, b in zip(tiles, tiles[1:] + [None]):
        if b != a + 1:
            runs.append((start, a + 1))
            start = b
    parts = [ref[lo * TILE : hi * TILE, :] for lo, hi in runs]
    return parts[0] if len(parts) == 1 else jnp.concatenate(parts, axis=0)


def causal_fill(scores, value):
    width = scores.shape[1] - TILE
    row = lax.broadcasted_iota(jnp.int32, (TILE, TILE), 0)
    col = lax.broadcasted_iota(jnp.int32, (TILE, TILE), 1)
    last = jnp.where(col <= row, scores[:, width:], value)
    return last if width == 0 else jnp.concatenate([scores[:, :width], last], axis=1)


def forward_kernel(block, perm, pre_ref, cos_ref, sin_ref, ctx_ref, q_ref, k_ref, v_ref, log_ref):
    tiles = pre_ref.shape[0] // TILE
    for t in range(tiles):
        rows = slice(t * TILE, (t + 1) * TILE)
        cos, sin = cos_ref[rows, :], sin_ref[rows, :]
        q = load_tile(pre_ref, perm, t, block, slice(0, HD))
        q_ref[rows, :] = (q * cos + pltpu.roll(q, HD // 2, 1) * sin).astype(bf16)
        k = load_tile(pre_ref, perm, t, block, slice(HD, 2 * HD))
        k_ref[rows, :] = (k * cos + pltpu.roll(k, HD // 2, 1) * sin).astype(bf16)
        v_ref[rows, :] = load_tile(pre_ref, perm, t, block, slice(2 * HD, 3 * HD)).astype(bf16)
    for t in range(tiles):
        rows = slice(t * TILE, (t + 1) * TILE)
        seen = tile_keys(t)
        keys, values = spread_keys(k_ref, seen), spread_keys(v_ref, seen)
        scores = dot(q_ref[rows, :], keys, 1, 1) * scale
        scores = causal_fill(scores, -1e30)
        top = jnp.max(scores, axis=1, keepdims=True)
        expo = jnp.exp(scores - top)
        total = jnp.sum(expo, axis=1, keepdims=True)
        probs = (expo * (1.0 / total)).astype(bf16)
        context = dot(probs, values, 1, 0).astype(bf16)
        store_tile(ctx_ref, perm, t, block, slice(None), context)
        log_ref[rows, :] = jnp.broadcast_to(top + jnp.log(total), (TILE, HD))


def backward_kernel(
    block, perm, q_ref, k_ref, v_ref, log_ref, do_ref, cos_ref, sin_ref, out_ref, dk_ref, dv_ref
):
    tiles = q_ref.shape[0] // TILE
    dk_ref[...] = jnp.zeros_like(dk_ref)
    dv_ref[...] = jnp.zeros_like(dv_ref)
    for t in range(tiles):
        rows = slice(t * TILE, (t + 1) * TILE)
        seen = tile_keys(t)
        keys, values = spread_keys(k_ref, seen), spread_keys(v_ref, seen)
        query = q_ref[rows, :]
        grad = load_tile(do_ref, perm, t, block, slice(None))
        scores = dot(query, keys, 1, 1) * scale
        soft = causal_fill(jnp.exp(scores - log_ref[rows, 0:1]), 0.0)
        grad_prob = dot(grad, values, 1, 1)
        delta = jnp.sum(grad_prob * soft, axis=1, keepdims=True)
        grad_scores = (soft * (grad_prob - delta)).astype(bf16)
        values_back = dot(soft.astype(bf16), grad, 0, 0)
        keys_back = dot(grad_scores, query, 0, 0)
        for i, s in enumerate(seen):
            part, own = slice(i * TILE, (i + 1) * TILE), slice(s * TILE, (s + 1) * TILE)
            dv_ref[own, :] += values_back[part]
            dk_ref[own, :] += keys_back[part]
        back = dot(grad_scores, keys, 1, 0) * scale
        cos, sin = cos_ref[rows, :], sin_ref[rows, :]
        back = back * cos - pltpu.roll(back, HD // 2, 1) * sin
        store_tile(out_ref, perm, t, block, slice(0, HD), back.astype(bf16))
    for t in range(tiles):
        rows = slice(t * TILE, (t + 1) * TILE)
        cos, sin = cos_ref[rows, :], sin_ref[rows, :]
        back = dk_ref[rows, :] * scale
        back = back * cos - pltpu.roll(back, HD // 2, 1) * sin
        store_tile(out_ref, perm, t, block, slice(HD, 2 * HD), back.astype(bf16))
        store_tile(out_ref, perm, t, block, slice(2 * HD, 3 * HD), dv_ref[rows, :].astype(bf16))


def attention_forward(perm, block, pre, cos, sin):
    rows, heads = pre.shape[0], pre.shape[1] // (3 * HD)
    per_head = pl.BlockSpec((rows, HD), lambda h, p: (0, h))
    table = pl.BlockSpec((rows, HD), lambda h, p: (0, 0))
    head_array = jax.ShapeDtypeStruct((rows, heads * HD), bf16)
    return pl.pallas_call(
        functools.partial(forward_kernel, block),
        grid_spec=pltpu.PrefetchScalarGridSpec(
            num_scalar_prefetch=1,
            grid=(heads,),
            in_specs=[pl.BlockSpec((rows, 3 * HD), lambda h, p: (0, h)), table, table],
            out_specs=[per_head] * 5,
        ),
        out_shape=[head_array] * 4 + [jax.ShapeDtypeStruct((rows, heads * HD), f32)],
        name="attention_forward",
    )(perm, pre, cos, sin)


def attention_backward(perm, block, q, k, v, log_total, grad, cos, sin):
    rows, heads = q.shape[0], q.shape[1] // HD
    per_head = pl.BlockSpec((rows, HD), lambda h, p: (0, h))
    table = pl.BlockSpec((rows, HD), lambda h, p: (0, 0))
    return pl.pallas_call(
        functools.partial(backward_kernel, block),
        grid_spec=pltpu.PrefetchScalarGridSpec(
            num_scalar_prefetch=1,
            grid=(heads,),
            in_specs=[per_head] * 5 + [table, table],
            out_specs=pl.BlockSpec((rows, 3 * HD), lambda h, p: (0, h)),
            scratch_shapes=[pltpu.VMEM((rows, HD), f32), pltpu.VMEM((rows, HD), f32)],
        ),
        out_shape=jax.ShapeDtypeStruct((rows, heads * 3 * HD), bf16),
        name="attention_backward",
    )(perm, q, k, v, log_total, grad, cos, sin)


def rope_tables(group_len):
    index = jnp.arange(group_len, dtype=jnp.int32)
    position = jnp.where(index < PROMPT, index, PROMPT + (index - PROMPT) % CONT).astype(f32)
    half = HD // 2
    frequency = jnp.exp(-math.log(10000.0) * jnp.arange(half, dtype=f32) / half)
    angles = position[:, None] * frequency[None, :]
    cosine, sine = jnp.cos(angles), jnp.sin(angles)
    return (
        jnp.concatenate([cosine, cosine], axis=1),
        jnp.concatenate([-sine, sine], axis=1),
    )


def normalize_parts(values, gain):
    inverse = lax.rsqrt(jnp.mean(values * values, axis=-1, keepdims=True) + norm_eps)
    unit_rows = values * inverse
    return (unit_rows * gain, unit_rows, inverse)


def norm_backward(grad_outer, unit_rows, inverse, gain):
    grad_unit = grad_outer * gain
    grad_inner = inverse * (
        grad_unit - unit_rows * jnp.mean(grad_unit * unit_rows, axis=-1, keepdims=True)
    )
    return (grad_inner, jnp.sum(grad_outer * unit_rows, axis=0))


def shards(
    tokens,
    route_ids,
    gate_values,
    deal,
    norm1_gain,
    w_query,
    w_key,
    w_value,
    w_out,
    norm2_gain,
    w_gate,
    w_up,
    w_down,
    cotangent,
):
    rows = tokens.shape[1]
    ctx_count = lax.axis_size("ctx")
    fsdp_count = lax.axis_size("fsdp")
    group_len = rows * ctx_count
    capacity = 5 * rows * TOPK // (4 * EXPERTS)
    repeats = fsdp_count // EXPERTS
    pair = 2
    columns = repeats // pair
    core = lax.axis_index("ctx")
    expert = lax.axis_index("fsdp") // repeats
    width = D // ctx_count
    heads = HEADS // ctx_count

    def core_shift(a, s):
        return lax.ppermute(a, "ctx", [(i, (i + s) % ctx_count) for i in range(ctx_count)])

    def fsdp_shift(a, move):
        return lax.ppermute(a, "fsdp", [(i, move(i)) for i in range(fsdp_count)])

    def expert_shift(a, k):
        return fsdp_shift(a, lambda i: (i + k * repeats) % fsdp_count)

    def column_shift(a, j):
        def move(i):
            e, r = divmod(i, repeats)
            t, w = divmod(r, pair)
            return e * repeats + ((t + j) % columns) * pair + w

        return fsdp_shift(a, move)

    def pair_swap(a):
        return fsdp_shift(a, lambda i: i ^ 1)

    def core_gather(a):
        return jnp.concatenate([a] + [core_shift(a, s) for s in range(1, ctx_count)], axis=0)

    block_count = deal.shape[1]
    block = group_len // block_count
    local_blocks = block_count // ctx_count
    dealt = jnp.argsort(deal[0]).astype(jnp.int32)
    perm = ((core - dealt // local_blocks) % ctx_count) * local_blocks + dealt % local_blocks
    cos, sin = rope_tables(group_len)

    def own_columns(w):
        return lax.dynamic_slice_in_dim(w, core * width, width, axis=1)

    stack = jnp.stack(
        [own_columns(w).reshape(-1, heads, HD) for w in (w_query, w_key, w_value)], axis=2
    ).reshape(-1, 3 * width)
    packed = jnp.concatenate([stack, own_columns(w_out)], axis=1)
    gathered = lax.all_gather(packed, "fsdp", axis=0, tiled=True)
    w_qkv = gathered[:, : 3 * width]
    out_columns = gathered[:, 3 * width :]

    def out_rows(c):
        return lax.dynamic_slice_in_dim(out_columns, (c % ctx_count) * width, width, axis=0)

    if ctx_count == 2:
        mine, other = out_rows(core), core_shift(out_rows(core + 1), 1)
        w_o = jnp.concatenate(
            [jnp.where(core == 0, mine, other), jnp.where(core == 0, other, mine)], axis=1
        )
    else:
        w_o = lax.all_to_all(
            out_columns.reshape(ctx_count, width, width), "ctx", 0, 0, tiled=False
        )
        w_o = w_o.transpose(1, 0, 2).reshape(width, D)

    def pair_weights(w):
        count = w.shape[0] // ctx_count
        part = pair_swap(lax.dynamic_slice_in_dim(w, core * count, count, axis=0))
        if ctx_count == 2:
            again = core_shift(part, 1)
            first, second = jnp.where(core == 0, part, again), jnp.where(core == 0, again, part)
            return jnp.concatenate([w, first, second], axis=0)
        return jnp.concatenate([w, lax.all_gather(part, "ctx", axis=0, tiled=True)], axis=0)

    wg, wu, wd = pair_weights(w_gate), pair_weights(w_up), pair_weights(w_down)

    ids = route_ids[0]
    flat = ids.reshape(-1)
    onehot = (flat[:, None] == jnp.arange(EXPERTS, dtype=jnp.int32)[None, :]).astype(jnp.int32)
    earlier = jnp.cumsum(onehot, axis=0) - onehot
    slot = jnp.sum(earlier * onehot, axis=1)
    relative = (flat - expert) % EXPERTS
    place = jnp.where(slot < capacity, relative * capacity + slot, -1).reshape(rows, TOPK)
    targets = jnp.arange(EXPERTS * capacity, dtype=jnp.int32)
    select = [(place[:, k : k + 1] == targets[None, :]).astype(bf16) for k in range(TOPK)]
    spread = [(targets[:, None] == place[None, :, k]).astype(bf16) for k in range(TOPK)]
    gates = gate_values[0]

    def send_slots(blocks):
        parts = []
        for k in range(EXPERTS):
            arrived = blocks[k] if k == 0 else expert_shift(blocks[k], k)
            parts.append(arrived)
            parts.extend(column_shift(arrived, j) for j in range(1, columns))
        return jnp.concatenate(parts, axis=0)

    def return_slots(partial):
        parts = partial.reshape(EXPERTS, columns, capacity, D)
        home = []
        for k in range(EXPERTS):
            total = parts[k, 0].astype(f32)
            for j in range(1, columns):
                total = total + column_shift(parts[k, j], -j).astype(f32)
            total = total.astype(bf16)
            home.append(total if k == 0 else expert_shift(total, -k))
        return jnp.concatenate(home, axis=0)

    dy = cotangent[0].astype(f32)
    grad_pairs = jnp.concatenate([(dy * gates[:, k : k + 1]).astype(bf16) for k in range(TOPK)])
    spread_both = jnp.concatenate(spread, axis=1)
    grad_arrived = send_slots(
        [
            dot(spread_both[k * capacity : (k + 1) * capacity], grad_pairs, 1, 0, bf16)
            for k in range(EXPERTS)
        ]
    )

    inputs = tokens[0].astype(f32)
    normed_f, _, _ = normalize_parts(inputs, norm1_gain)
    normed = core_gather(normed_f.astype(bf16))
    pre = dot(normed, w_qkv, 1, 0)
    context, q, k, v, log_total = attention_forward(perm, block, pre, cos, sin)
    attention = dot(context[:rows], w_o, 1, 0)
    for s in range(1, ctx_count):
        away = dot(context[s * rows : (s + 1) * rows], w_o, 1, 0, bf16)
        attention = attention + core_shift(away, -s).astype(f32)
    hidden_in = inputs + attention
    normed_two_f, unit_two, inverse_two = normalize_parts(hidden_in, norm2_gain)
    normed_two = normed_two_f.astype(bf16)

    spread_any = spread[0] + spread[1]
    arrived = send_slots(
        [
            dot(spread_any[k * capacity : (k + 1) * capacity], normed_two, 1, 0, bf16)
            for k in range(EXPERTS)
        ]
    )
    grad_hidden = dot(grad_arrived, wd, 1, 1, bf16)
    gate_act = dot(arrived, wg, 1, 1)
    up_act = dot(arrived, wu, 1, 1)
    sigmoid_gate = jax.nn.sigmoid(gate_act)
    silu_gate = gate_act * sigmoid_gate
    hidden = (silu_gate * up_act).astype(bf16)
    gh = grad_hidden.astype(f32)
    grad_gate = (gh * up_act * sigmoid_gate * (1.0 + gate_act * (1.0 - sigmoid_gate))).astype(bf16)
    grad_up = (gh * silu_gate).astype(bf16)
    grad_in = (dot(grad_gate, wg, 1, 0) + dot(grad_up, wu, 1, 0)).astype(bf16)
    grad_slot_in = return_slots(grad_in)
    slot_out = return_slots(dot(hidden, wd, 1, 0, bf16))

    grad_normed_two = dot(select[0] + select[1], grad_slot_in, 1, 0)
    grad_norm_two, norm2_part = norm_backward(grad_normed_two, unit_two, inverse_two, norm2_gain)
    grad_hidden_in = dy + grad_norm_two
    grad_attention = core_gather(grad_hidden_in.astype(bf16))
    grad_context = dot(grad_attention, w_o, 1, 1, bf16)
    out_part = dot(context, grad_attention, 0, 0, bf16)
    out_grad = lax.psum_scatter(out_part, "fsdp", scatter_dimension=0, tiled=True).astype(f32)

    grad_qkv = attention_backward(perm, block, q, k, v, log_total, grad_context, cos, sin)
    per = D // (ctx_count * fsdp_count)
    normed_mixed = (
        normed.reshape(group_len, ctx_count, fsdp_count, per)
        .transpose(0, 2, 1, 3)
        .reshape(group_len, D)
    )
    qkv_part = dot(normed_mixed, grad_qkv, 0, 0, bf16)
    qkv_sum = lax.psum_scatter(qkv_part, "fsdp", scatter_dimension=0, tiled=True)
    qkv_sum = qkv_sum.reshape(ctx_count, per, heads, 3, HD)
    if ctx_count == 2:
        mine = lax.dynamic_index_in_dim(qkv_sum, core, 0, keepdims=False)
        other = core_shift(lax.dynamic_index_in_dim(qkv_sum, 1 - core, 0, keepdims=False), 1)
        qkv_own = jnp.where(
            core == 0,
            jnp.concatenate([mine, other], axis=1),
            jnp.concatenate([other, mine], axis=1),
        )
    else:
        qkv_own = lax.all_to_all(qkv_sum, "ctx", 0, 0, tiled=False)
        qkv_own = qkv_own.transpose(1, 0, 2, 3, 4).reshape(per, HEADS, 3, HD)
    qkv_own = qkv_own.astype(f32)
    query_grad, key_grad, value_grad = (qkv_own[:, :, i].reshape(per, D) for i in range(3))

    grad_normed = dot(grad_qkv[:rows], w_qkv, 1, 1)
    for s in range(1, ctx_count):
        away = dot(grad_qkv[s * rows : (s + 1) * rows], w_qkv, 1, 1, bf16)
        grad_normed = grad_normed + core_shift(away, -s).astype(f32)
    _, unit_one, inverse_one = normalize_parts(inputs, norm1_gain)
    grad_norm_one, norm1_part = norm_backward(grad_normed, unit_one, inverse_one, norm1_gain)
    tokens_grad = (grad_hidden_in + grad_norm_one).astype(bf16)

    gains = jnp.stack([norm1_part, norm2_part])
    step = 1
    while step < ctx_count:
        gains = gains + lax.ppermute(gains, "ctx", [(i, i ^ step) for i in range(ctx_count)])
        step *= 2
    step = 1
    while step < fsdp_count:
        gains = gains + fsdp_shift(gains, lambda i, step=step: i ^ step)
        step *= 2
    place_own = (core * fsdp_count + lax.axis_index("fsdp")) * per
    gains_own = lax.dynamic_slice_in_dim(gains, place_own, per, axis=1)

    def expert_grad(left, right):
        part = dot(left, right, 0, 0, bf16)
        total = lax.dynamic_slice_in_dim(part, core * width, width, axis=1).astype(f32)
        for s in range(1, ctx_count):
            start = ((core + s) % ctx_count) * width
            total = total + core_shift(
                lax.dynamic_slice_in_dim(part, start, width, axis=1), s
            ).astype(f32)
        count = total.shape[0] // pair
        return total[:count] + pair_swap(total[count:].astype(bf16)).astype(f32)

    down_grad = expert_grad(hidden, grad_arrived)
    gate_grad = expert_grad(grad_gate, arrived)
    up_grad = expert_grad(grad_up, arrived)

    mixed = hidden_in
    for k in range(TOPK):
        mixed = mixed + dot(select[k], slot_out, 1, 0) * gates[:, k : k + 1]

    return (
        mixed.astype(bf16)[None],
        tokens_grad[None],
        gains_own[0],
        query_grad,
        key_grad,
        value_grad,
        out_grad,
        gains_own[1],
        gate_grad,
        up_grad,
        down_grad,
    )


def solution(mesh):
    in_specs = (
        P("fsdp", "ctx", None),
        P("fsdp", "ctx", None),
        P("fsdp", "ctx", None),
        P("fsdp", None),
        P(),
        P("fsdp", None),
        P("fsdp", None),
        P("fsdp", None),
        P("fsdp", None),
        P(),
        P("fsdp", None),
        P("fsdp", None),
        P("fsdp", None),
        P("fsdp", "ctx", None),
    )
    out_specs = (
        P("fsdp", "ctx", None),
        P("fsdp", "ctx", None),
        P(("ctx", "fsdp")),
        P(("ctx", "fsdp"), None),
        P(("ctx", "fsdp"), None),
        P(("ctx", "fsdp"), None),
        P(("ctx", "fsdp"), None),
        P(("ctx", "fsdp")),
        P("fsdp", "ctx"),
        P("fsdp", "ctx"),
        P("fsdp", "ctx"),
    )
    return jax.shard_map(shards, mesh=mesh, in_specs=in_specs, out_specs=out_specs, check_vma=False)
```

time: 4460 us -> 1860 us (0.42)
  waiting for transfers between devices: 3050 us -> 905 us
  matrix products: 759 us -> 489 us
  starting transfers between devices: 277 us -> 151 us
  blocking collectives: 91.1 us -> 0 us
  local copies, waits for them, and re-layouts: 158 us -> 107 us
  Pallas kernels: 0 us -> 49.2 us
    all_to_all x4 -> x0, waiting for transfers between devices: 1370 us -> none  [the longest x1 353 us: shards(): lax.all_to_all(outgoing, 'fsdp', split_axis=0, concat_axis=0, tiled=True)]
    reduce_scatter x9 -> x2, waiting for transfers between devices: 1360 us -> 0.01 us  [the longest x1 0.01 us: shards(): lax.psum_scatter(qkv_part, 'fsdp', scatter_dimension=0, tiled=True)]
    ppermute x0 -> x51, waiting for transfers between devices: none -> 664 us  [the longest x38 664 us: fsdp_shift(): return lax.ppermute(a, 'fsdp', [(i, move(i)) for i in range(fsdp_count)])]
    all_to_all x4 -> x0, starting transfers between devices: 275 us -> none  [the longest x1 91 us: shards(): lax.all_to_all(grad_outgoing, 'fsdp', split_axis=0, concat_axis=0, tiled=...]
    dot_general x137 -> x28, matrix products: 759 us -> 489 us  [dot(): lax.dot_general(a, b, (((ca,), (cb,)), ((), ())), preferred_element_type=...]
    ppermute x0 -> x51, starting transfers between devices: none -> 151 us  [the longest x38 150 us: fsdp_shift(): return lax.ppermute(a, 'fsdp', [(i, move(i)) for i in range(fsdp_count)])]
    unnamed x1 -> x0, blocking collectives: 91.1 us -> none
    all_gather x6 -> x1, waiting for transfers between devices: 326 us -> 241 us  [shards(): gathered = lax.all_gather(packed, 'fsdp', axis=0, tiled=True)]
  transfers between devices with their start and end apart: 19 -> 54, of which waited for: 14 -> 21; matrix products, arithmetic and copies ran while one was open for 13% -> 27% of each run, Pallas kernels for 0% -> 3%
where the time goes in v1:
time: 1860 us; the launch traced here: 1830 us
  waiting for transfers between devices  905 us (49%)
  matrix products  489 us (26%)
  starting transfers between devices  151 us (8%)
  other arithmetic  114 us (6%)
  local copies, waits for them, and re-layouts  107 us (6%)
  Pallas kernels  49.2 us (3%)
    ppermute x38, waiting for transfers between devices, fsdp_shift(): return lax.ppermute(a, 'fsdp', [(i, move(i)) for i in range(fsdp_count)])  664 us
    dot_general x28, matrix products, dot(): lax.dot_general(a, b, (((ca,), (cb,)), ((), ())), preferred_element_type=...  489 us
    all_gather x1, waiting for transfers between devices, shards(): gathered = lax.all_gather(packed, 'fsdp', axis=0, tiled=True)  241 us
    ppermute x38, starting transfers between devices, fsdp_shift(): return lax.ppermute(a, 'fsdp', [(i, move(i)) for i in range(fsdp_count)])  150 us
  transfers between devices with their start and end apart: 54, of which 21 were waited for; matrix products, arithmetic and copies ran while one was open for 27% of the time, Pallas kernels for 3%

profile of v1, /device:TPU:0, one launch (start us, length us, event | category | flops | bytes accessed | tf_op | source)
XLA Modules:
  0.0 1830.4 jit_solution(4586121778161461643)
XLA Ops:
  40.2 241.5 %all-gather.2.cloned.1.call-done = bf16[2048,4096]{0,1:T(8,128)(2,1)} async-done(((bf16[128,4096]{0,1:T(8,128)(2,1)}), bf16[2048,4096]{0,1:T(8,128)(2,1)}) %all-gather.2.cloned.1.call-update) | async-done | bytes 16777232 | tf_op jit(solution)/shard_map/all_gather | solution.py:265
  307.4 73.8 %collective-permute-done.26 = bf16[320,2048]{1,0:T(8,128)(2,1)} collective-permute-done((bf16[320,2048]{1,0:T(8,128)(2,1)}, bf16[320,2048]{1,0:T(8,128)(2,1)}, u32[]{:S(2)}, u32[]{:S(2)}) %collective-permute-start.26) | collective-permute-done | bytes 1310752 | tf_op jit(solution)/shard_map/ppermute | solution.py:232
  385.3 19.2 %fusion.9.pre_ref = f32[1024,3072]{1,0:T(8,128)} fusion(bf16[2048,4096]{0,1:T(8,128)(2,1)} %all-gather.2.cloned.1.call-done, bf16[512,2048]{1,0:T(8,128)(2,1)} %collective-permute-done, bf16[512,2048]{1,0:T(8,128)(2,1)} %fusion.26), kind=kOutput, calls=%fused_computation.26 | convolution fusion | flops 12893290496 | bytes 29360128 | tf_op jit(solution)/shard_map/dot_general | solution.py:27
  404.5 21.9 %attention_forward.1 = (bf16[1024,1024]{1,0:T(8,128)(2,1)}, bf16[1024,1024]{1,0:T(8,128)(2,1)}, bf16[1024,1024]{1,0:T(8,128)(2,1)}, bf16[1024,1024]{1,0:T(8,128)(2,1)}, f32[1024,1024]{1,0:T(8,128)}) custom-call(s32[4]{0:T(128)} %fusion.100.perm, f32[1024,3072]{1,0:T(8,128)} %fusion.9.pre_ref, f32[1024,128]{1,0:T(8,128)} %get-tuple-element.82.cos_ref, ...), custom_call_target="tpu_custom_call" | custom-call | tf_op jit(solution)/shard_map/attention_forward/pallas_call | solution.py:141
  433.9 9.5 collective-permute-done.25
  454.8 14.9 collective-permute-done.29
  470.9 36.8 %collective-permute-done.10 = bf16[704,2048]{1,0:T(8,128)(2,1)} collective-permute-done((bf16[704,2048]{1,0:T(8,128)(2,1)}, bf16[704,2048]{1,0:T(8,128)(2,1)}, u32[]{:S(2)}, u32[]{:S(2)}) %collective-permute-start.10) | collective-permute-done | bytes 2883616 | tf_op jit(solution)/shard_map/ppermute | solution.py:232
  520.8 42.0 %convolution_convert_fusion = bf16[2560,2816]{1,0:T(8,128)(2,1)} fusion(bf16[2560,2048]{1,0:T(8,128)(2,1)} %constant_dynamic-update-slice_fusion.8, bf16[704,2048]{1,0:T(8,128)(2,1)} %get-tuple-element.51, bf16[704,2048]{1,0:T(8,128)(2,1)S(1)} %copy-done.13, bf16[1408,2048]{1,0:T(8,128)(2,1)} %param.26), kind=kOutput, calls=%fused_computation.10 | convolution fusion | flops 29569712128 | bytes 36438016 | tf_op jit(solution)/shard_map/dot_general | solution.py:27
  578.2 47.9 %collective-permute-done.6 = bf16[320,2048]{1,0:T(8,128)(2,1)S(1)} collective-permute-done((bf16[320,2048]{1,0:T(8,128)(2,1)S(1)}, bf16[320,2048]{1,0:T(8,128)(2,1)S(1)}, u32[]{:S(2)}, u32[]{:S(2)}) %collective-permute-start.6) | collective-permute-done | bytes 1310752 | tf_op jit(solution)/shard_map/ppermute | solution.py:232
  637.8 21.5 %collective-permute-done.7 = bf16[320,2048]{1,0:T(8,128)(2,1)S(1)} collective-permute-done((bf16[320,2048]{1,0:T(8,128)(2,1)S(1)}, bf16[320,2048]{1,0:T(8,128)(2,1)S(1)}, u32[]{:S(2)}, u32[]{:S(2)}) %collective-permute-start.7) | collective-permute-done | bytes 1310752 | tf_op jit(solution)/shard_map/ppermute | solution.py:232
  661.9 24.6 %collective-permute-done.9 = bf16[320,2048]{1,0:T(8,128)(2,1)S(1)} collective-permute-done((bf16[320,2048]{1,0:T(8,128)(2,1)S(1)}, bf16[320,2048]{1,0:T(8,128)(2,1)S(1)}, u32[]{:S(2)}, u32[]{:S(2)}) %collective-permute-start.9) | collective-permute-done | bytes 1310752 | tf_op jit(solution)/shard_map/ppermute | solution.py:232
  687.7 36.5 %fusion.25 = f32[2560,2816]{1,0:T(8,128)} fusion(bf16[2560,2048]{1,0:T(8,128)(2,1)} %constant_dynamic-update-slice_fusion, bf16[704,2048]{1,0:T(8,128)(2,1)S(1)} %get-tuple-element.53, bf16[704,2048]{1,0:T(8,128)(2,1)S(1)} %get-tuple-element.52, bf16[1408,2048]{1,0:T(8,128)(2,1)S(1)} %bitcast.182), kind=kOutput, calls=%fused_computation.55 | convolution fusion | flops 29562503168 | bytes 50855936 | tf_op jit(solution)/shard_map/dot_general | solution.py:27
  724.2 60.2 %fusion.2 = (bf16[2560,2816]{1,0:T(8,128)(2,1)}, bf16[2560,2816]{1,0:T(8,128)(2,1)}, bf16[2560,2816]{1,0:T(8,128)(2,1)}) fusion(bf16[2560,2816]{1,0:T(8,128)(2,1)} %convolution_convert_fusion, f32[2560,2816]{1,0:T(8,128)} %fusion.25, bf16[2560,2048]{1,0:T(8,128)(2,1)} %constant_dynamic-update-slice_fusion, bf16[704,2048]{1,0:T(8,128)(2,1)} %get-tuple-element.55, ...), kind=kOutput, calls=%fused_computation.4 | convolution fusion | flops 29677846528 | bytes 108527616 | tf_op jit(solution)/shard_map/dot_general | solution.py:27
  784.5 37.4 %fusion.23 = f32[2560,2048]{1,0:T(8,128)} fusion(bf16[2560,2816]{1,0:T(8,128)(2,1)} %get-tuple-element.31, bf16[704,2048]{1,0:T(8,128)(2,1)} %get-tuple-element.55, bf16[704,2048]{1,0:T(8,128)(2,1)S(1)} %get-tuple-element.54, bf16[1408,2048]{1,0:T(8,128)(2,1)} %param.25), kind=kOutput, calls=%fused_computation.53 | convolution fusion | flops 29562503168 | bytes 46923776 | tf_op jit(solution)/shard_map/dot_general | solution.py:27
  821.9 40.3 %add_convert_fusion = bf16[2560,2048]{1,0:T(8,128)(2,1)} fusion(f32[2560,2048]{1,0:T(8,128)} %fusion.23, bf16[2560,2816]{1,0:T(8,128)(2,1)} %get-tuple-element.29, bf16[704,2048]{1,0:T(8,128)(2,1)} %copy-done.15, bf16[704,2048]{1,0:T(8,128)(2,1)} %copy-done.14, bf16[1408,2048]{1,0:T(8,128)(2,1)} %param.24), kind=kOutput, calls=%fused_computation.9 | convolution fusion | flops 29572988928 | bytes 57409536 | tf_op jit(solution)/shard_map/dot_general | solution.py:27
  869.4 27.7 %collective-permute-done.30 = bf16[320,2048]{1,0:T(8,128)(2,1)S(1)} collective-permute-done((bf16[320,2048]{1,0:T(8,128)(2,1)S(1)}, bf16[320,2048]{1,0:T(8,128)(2,1)S(1)}, u32[]{:S(2)}, u32[]{:S(2)}) %collective-permute-start.30) | collective-permute-done | bytes 1310752 | tf_op jit(solution)/shard_map/ppermute | solution.py:232
  897.1 28.1 %collective-permute-done.35 = bf16[320,2048]{1,0:T(8,128)(2,1)S(1)} collective-permute-done((bf16[320,2048]{1,0:T(8,128)(2,1)S(1)}, bf16[320,2048]{1,0:T(8,128)(2,1)S(1)}, u32[]{:S(2)}, u32[]{:S(2)}) %collective-permute-start.35) | collective-permute-done | bytes 1310752 | tf_op jit(solution)/shard_map/ppermute | solution.py:232
  925.2 28.1 %collective-permute-done.33 = bf16[320,2048]{1,0:T(8,128)(2,1)S(1)} collective-permute-done((bf16[320,2048]{1,0:T(8,128)(2,1)S(1)}, bf16[320,2048]{1,0:T(8,128)(2,1)S(1)}, u32[]{:S(2)}, u32[]{:S(2)}) %collective-permute-start.33) | collective-permute-done | bytes 1310752 | tf_op jit(solution)/shard_map/ppermute | solution.py:232
  953.3 26.2 %collective-permute-done.31 = bf16[320,2048]{1,0:T(8,128)(2,1)S(1)} collective-permute-done((bf16[320,2048]{1,0:T(8,128)(2,1)S(1)}, bf16[320,2048]{1,0:T(8,128)(2,1)S(1)}, u32[]{:S(2)}, u32[]{:S(2)}) %collective-permute-start.31) | collective-permute-done | bytes 1310752 | tf_op jit(solution)/shard_map/ppermute | solution.py:232
  983.6 24.8 %collective-permute-start.36 = (bf16[320,2048]{1,0:T(8,128)(2,1)}, bf16[320,2048]{1,0:T(8,128)(2,1)}, u32[]{:S(2)}, u32[]{:S(2)}) collective-permute-start(bf16[320,2048]{1,0:T(8,128)(2,1)} %get-tuple-element.33), channel_id=1, source_target_pairs={{0,4},{1,5},{2,6},{3,7},{4,8},{5,9},{6,10},{7,11},{8,12},{9,13},{1... | collective-permute-start | bytes 3932168 | tf_op jit(solution)/shard_map/ppermute | solution.py:232
  1016.6 6.4 copy.43
  1028.0 13.2 collective-permute-done.36
  1041.3 53.7 %collective-permute-done.34 = bf16[320,2048]{1,0:T(8,128)(2,1)} collective-permute-done((bf16[320,2048]{1,0:T(8,128)(2,1)}, bf16[320,2048]{1,0:T(8,128)(2,1)}, u32[]{:S(2)}, u32[]{:S(2)}) %collective-permute-start.34) | collective-permute-done | bytes 1310752 | tf_op jit(solution)/shard_map/ppermute | solution.py:232
  1095.1 6.2 multiply_reduce_fusion
  1103.2 37.7 %convolution_convert_fusion.4 = bf16[2560,2048]{1,0:T(8,128)(2,1)S(1)} fusion(bf16[2560,2816]{1,0:T(8,128)(2,1)} %get-tuple-element.30, bf16[704,2048]{1,0:T(8,128)(2,1)} %get-tuple-element.51, bf16[704,2048]{1,0:T(8,128)(2,1)} %get-tuple-element.50, bf16[1408,2048]{1,0:T(8,128)(2,1)} %param.26), kind=kOutput, calls=%fused_computation.20 | convolution fusion | flops 29567746048 | bytes 36438016 | tf_op jit(solution)/shard_map/dot_general | solution.py:27
  1151.6 7.5 fusion.63.do_ref
  1159.0 27.3 %attention_backward.1 = bf16[1024,3072]{1,0:T(8,128)(2,1)} custom-call(s32[4]{0:T(128)} %fusion.100.perm, bf16[1024,1024]{1,0:T(8,128)(2,1)} %get-tuple-element.19.q_ref, bf16[1024,1024]{1,0:T(8,128)(2,1)} %get-tuple-element.20.k_ref, bf16[1024,1024]{1,0:T(8,128)(2,1)} %get-tuple-element.21.v_ref, f32[1024,1024]{1,0:T(8,128)} %get-tuple-element.22.log_ref, ...), custom_call_target="tpu_custom_call" | custom-call | tf_op jit(solution)/shard_map/attention_backward/pallas_call | solution.py:158
  1186.3 19.3 %convolution_convert_fusion.5 = bf16[2048,3072]{1,0:T(8,128)(2,1)} fusion(bf16[1024,2048]{0,1:T(8,128)(2,1)} %bitcast.175, bf16[1024,3072]{1,0:T(8,128)(2,1)} %attention_backward.1), kind=kOutput, calls=%fused_computation.21 | convolution fusion | flops 12891193344 | bytes 23068672 | tf_op jit(solution)/shard_map/dot_general | solution.py:27
  1205.7 38.8 %convolution_convert_fusion.1 = bf16[2816,2048]{1,0:T(8,128)(2,1)} fusion(bf16[2560,2816]{1,0:T(8,128)(2,1)} %get-tuple-element.30, bf16[2560,2048]{1,0:T(8,128)(2,1)} %constant_dynamic-update-slice_fusion.8), kind=kOutput, calls=%fused_computation.17 | convolution fusion | flops 29533667328 | bytes 36438016 | tf_op jit(solution)/shard_map/dot_general | solution.py:27
  1244.5 38.5 %convolution_convert_fusion.3 = bf16[2816,2048]{1,0:T(8,128)(2,1)} fusion(bf16[2560,2816]{1,0:T(8,128)(2,1)} %get-tuple-element.29, bf16[2560,2048]{1,0:T(8,128)(2,1)} %constant_dynamic-update-slice_fusion), kind=kOutput, calls=%fused_computation.19 | convolution fusion | flops 29533667328 | bytes 36438016 | tf_op jit(solution)/shard_map/dot_general | solution.py:27
  1283.0 35.9 %convolution_convert_fusion.2 = bf16[2816,2048]{1,0:T(8,128)(2,1)S(1)} fusion(bf16[2560,2816]{1,0:T(8,128)(2,1)} %get-tuple-element.31, bf16[2560,2048]{1,0:T(8,128)(2,1)} %constant_dynamic-update-slice_fusion), kind=kOutput, calls=%fused_computation.18 | convolution fusion | flops 29533667328 | bytes 36438016 | tf_op jit(solution)/shard_map/dot_general | solution.py:27
  1319.0 10.8 fusion.56
  1329.8 28.6 %collective-permute-start.22 = (bf16[320,2048]{1,0:T(8,128)(2,1)S(1)}, bf16[320,2048]{1,0:T(8,128)(2,1)S(1)}, u32[]{:S(2)}, u32[]{:S(2)}) collective-permute-start(bf16[320,2048]{1,0:T(8,128)(2,1)S(1)} %get-tuple-element.41), channel_id=1, source_target_pairs={{0,4},{1,5},{2,6},{3,7},{4,8},{5,9},{6,10},{7,11},{8,12},{9,13},{1... | collective-permute-start | bytes 3932168 | tf_op jit(solution)/shard_map/ppermute | solution.py:232
  1360.8 6.1 constant_dynamic-slice_fusion.1
  1376.5 28.0 %collective-permute-done.22 = bf16[320,2048]{1,0:T(8,128)(2,1)S(1)} collective-permute-done((bf16[320,2048]{1,0:T(8,128)(2,1)S(1)}, bf16[320,2048]{1,0:T(8,128)(2,1)S(1)}, u32[]{:S(2)}, u32[]{:S(2)}) %collective-permute-start.22) | collective-permute-done | bytes 1310752 | tf_op jit(solution)/shard_map/ppermute | solution.py:232
  1404.5 70.3 %collective-permute-done.20 = bf16[320,2048]{1,0:T(8,128)(2,1)S(1)} collective-permute-done((bf16[320,2048]{1,0:T(8,128)(2,1)S(1)}, bf16[320,2048]{1,0:T(8,128)(2,1)S(1)}, u32[]{:S(2)}, u32[]{:S(2)}) %collective-permute-start.20) | collective-permute-done | bytes 1310752 | tf_op jit(solution)/shard_map/ppermute | solution.py:232
  1481.4 10.9 fusion.42
  1492.4 6.2 fusion.47
  1498.6 7.8 convolution_convert_fusion.6
  1508.0 13.4 fusion.32
  1521.9 11.4 convert_add_fusion
  1540.1 11.4 convert_add_fusion.2
  1556.6 100.7 %collective-permute-done.40 = f32[2,2048]{1,0:T(2,128)S(1)} collective-permute-done((f32[2,2048]{1,0:T(2,128)S(1)}, f32[2,2048]{1,0:T(2,128)S(1)}, u32[]{:S(2)}, u32[]{:S(2)}) %collective-permute-start.40) | collective-permute-done | bytes 16416 | tf_op jit(solution)/shard_map/ppermute | solution.py:232
  1661.7 11.5 convert_add_fusion.1
  1678.1 47.8 %collective-permute-start.42 = (f32[2,2048]{1,0:T(2,128)S(1)}, f32[2,2048]{1,0:T(2,128)S(1)}, u32[]{:S(2)}, u32[]{:S(2)}) collective-permute-start(f32[2,2048]{1,0:T(2,128)S(1)} %add.263), channel_id=1, source_target_pairs={{0,4},{1,5},{2,6},{3,7},{4,0},{5,1},{6,2},{7,3},{8,12},{9,13},{10,... | collective-permute-start | bytes 49160 | tf_op jit(solution)/shard_map/ppermute | solution.py:232
  1732.5 6.7 fusion.62
  1759.1 51.9 %collective-permute-done.48 = bf16[1408,1024]{1,0:T(8,128)(2,1)} collective-permute-done((bf16[1408,1024]{1,0:T(8,128)(2,1)}, bf16[1408,1024]{1,0:T(8,128)(2,1)}, u32[]{:S(2)}, u32[]{:S(2)}) %collective-permute-start.48) | collective-permute-done | bytes 2883616 | tf_op jit(solution)/shard_map/ppermute | solution.py:232
  1811.0 7.5 slice_add_fusion.1
  (338 shorter events, 237.1 us)
Async XLA Ops:
  7.2 274.5 %all-gather.2.cloned.1.call-start = ((), (), s32[]{:S(2)}) async-start(), calls=%async_computation.2 | async-start | bytes 17825792 | tf_op jit(solution)/shard_map/all_gather | solution.py:265
  11.5 1744.4 %reduce-scatter.3.cloned.1.call-start = ((), (), s32[]{:S(2)}) async-start(), calls=%async_computation.3 | async-start | bytes 13369344 | tf_op jit(solution)/shard_map/reduce_scatter | solution.py:384
  13.9 369.3 %collective-permute-start = (bf16[512,2048]{1,0:T(8,128)(2,1)}, bf16[512,2048]{1,0:T(8,128)(2,1)}, u32[]{:S(2)}, u32[]{:S(2)}) collective-permute-start(bf16[512,2048]{1,0:T(8,128)(2,1)} %fusion.26), channel_id=1, source_target_pairs={{0,16},{16,0},{1,17},{17,1},{2,18},{18,2},{3,19},{19,3},{4,20},{20... | collective-permute-start | bytes 6291464 | tf_op jit(solution)/shard_map/ppermute | solution.py:229
  18.1 366.6 %collective-permute-start.14 = (bf16[704,2048]{1,0:T(8,128)(2,1)}, bf16[704,2048]{1,0:T(8,128)(2,1)}, u32[]{:S(2)}, u32[]{:S(2)}) collective-permute-start(bf16[704,2048]{1,0:T(8,128)(2,1)} %constant_dynamic-slice_fusion.7), channel_id=1, source_target_pairs={{0,1},{1,0},{2,3},{3,2},{4,5},{5,4},{6,7},{7,6},{8,9},{9,8},{10,11... | collective-permute-start | bytes 8650760 | tf_op jit(solution)/shard_map/ppermute | solution.py:232
  28.0 266.3 %collective-permute-start.28 = (bf16[320,2048]{1,0:T(8,128)(2,1)}, bf16[320,2048]{1,0:T(8,128)(2,1)S(1)}, u32[]{:S(2)}, u32[]{:S(2)}) collective-permute-start(bf16[320,2048]{1,0:T(8,128)(2,1)} %convolution_convert_fusion.8), channel_id=1, source_target_pairs={{0,12},{1,13},{2,14},{3,15},{4,0},{5,1},{6,2},{7,3},{8,4},{9,5},{1... | collective-permute-start | bytes 3932168 | tf_op jit(solution)/shard_map/ppermute | solution.py:232
  34.9 260.9 %collective-permute-start.23 = (bf16[320,2048]{1,0:T(8,128)(2,1)}, bf16[320,2048]{1,0:T(8,128)(2,1)}, u32[]{:S(2)}, u32[]{:S(2)}) collective-permute-start(bf16[320,2048]{1,0:T(8,128)(2,1)} %get-tuple-element.75), channel_id=1, source_target_pairs={{0,2},{1,3},{2,0},{3,1},{4,6},{5,7},{6,4},{7,5},{8,10},{9,11},{10,... | collective-permute-start | bytes 3932168 | tf_op jit(solution)/shard_map/ppermute | solution.py:232
  285.8 99.4 %collective-permute-start.1 = (bf16[1024,1024]{0,1:T(8,128)(2,1)}, bf16[1024,1024]{0,1:T(8,128)(2,1)}, u32[]{:S(2)}, u32[]{:S(2)}) collective-permute-start(bf16[1024,1024]{0,1:T(8,128)(2,1)} %constant_dynamic-slice_fusion.10), channel_id=1, source_target_pairs={{0,16},{16,0},{1,17},{17,1},{2,18},{18,2},{3,19},{19,3},{4,20},{20... | collective-permute-start | bytes 6291464 | tf_op jit(solution)/shard_map/ppermute | solution.py:229
  294.3 86.9 %collective-permute-start.26 = (bf16[320,2048]{1,0:T(8,128)(2,1)}, bf16[320,2048]{1,0:T(8,128)(2,1)}, u32[]{:S(2)}, u32[]{:S(2)}) collective-permute-start(bf16[320,2048]{1,0:T(8,128)(2,1)} %convolution_convert_fusion.9), channel_id=1, source_target_pairs={{0,8},{1,9},{2,10},{3,11},{4,12},{5,13},{6,14},{7,15},{8,0},{9,1},... | collective-permute-start | bytes 3932168 | tf_op jit(solution)/shard_map/ppermute | solution.py:232
  295.8 85.9 %collective-permute-start.24 = (bf16[320,2048]{1,0:T(8,128)(2,1)}, bf16[320,2048]{1,0:T(8,128)(2,1)}, u32[]{:S(2)}, u32[]{:S(2)}) collective-permute-start(bf16[320,2048]{1,0:T(8,128)(2,1)} %convolution_convert_fusion.10), channel_id=1, source_target_pairs={{0,4},{1,5},{2,6},{3,7},{4,8},{5,9},{6,10},{7,11},{8,12},{9,13},{1... | collective-permute-start | bytes 3932168 | tf_op jit(solution)/shard_map/ppermute | solution.py:232
  381.2 89.7 %collective-permute-start.12 = (bf16[704,2048]{1,0:T(8,128)(2,1)}, bf16[704,2048]{1,0:T(8,128)(2,1)}, u32[]{:S(2)}, u32[]{:S(2)}) collective-permute-start(bf16[704,2048]{1,0:T(8,128)(2,1)} %constant_dynamic-slice_fusion.8), channel_id=1, source_target_pairs={{0,1},{1,0},{2,3},{3,2},{4,5},{5,4},{6,7},{7,6},{8,9},{9,8},{10,11... | collective-permute-start | bytes 8650760 | tf_op jit(solution)/shard_map/ppermute | solution.py:232
  381.7 126.0 %collective-permute-start.10 = (bf16[704,2048]{1,0:T(8,128)(2,1)}, bf16[704,2048]{1,0:T(8,128)(2,1)}, u32[]{:S(2)}, u32[]{:S(2)}) collective-permute-start(bf16[704,2048]{1,0:T(8,128)(2,1)} %constant_dynamic-slice_fusion.9), channel_id=1, source_target_pairs={{0,1},{1,0},{2,3},{3,2},{4,5},{5,4},{6,7},{7,6},{8,9},{9,8},{10,11... | collective-permute-start | bytes 8650760 | tf_op jit(solution)/shard_map/ppermute | solution.py:232
  383.2 46.7 %collective-permute-start.27 = (bf16[320,2048]{1,0:T(8,128)(2,1)}, bf16[320,2048]{1,0:T(8,128)(2,1)}, u32[]{:S(2)}, u32[]{:S(2)}) collective-permute-start(bf16[320,2048]{1,0:T(8,128)(2,1)} %collective-permute-done.26), channel_id=1, source_target_pairs={{0,2},{1,3},{2,0},{3,1},{4,6},{5,7},{6,4},{7,5},{8,10},{9,11},{10,... | collective-permute-start | bytes 3932168 | tf_op jit(solution)/shard_map/ppermute | solution.py:232
  384.7 58.6 %collective-permute-start.25 = (bf16[320,2048]{1,0:T(8,128)(2,1)}, bf16[320,2048]{1,0:T(8,128)(2,1)}, u32[]{:S(2)}, u32[]{:S(2)}) collective-permute-start(bf16[320,2048]{1,0:T(8,128)(2,1)} %collective-permute-done.24), channel_id=1, source_target_pairs={{0,2},{1,3},{2,0},{3,1},{4,6},{5,7},{6,4},{7,5},{8,10},{9,11},{10,... | collective-permute-start | bytes 3932168 | tf_op jit(solution)/shard_map/ppermute | solution.py:232
  385.3 122.5 %collective-permute-start.15 = (bf16[704,2048]{1,0:T(8,128)(2,1)}, bf16[704,2048]{1,0:T(8,128)(2,1)}, u32[]{:S(2)}, u32[]{:S(2)}) collective-permute-start(bf16[704,2048]{1,0:T(8,128)(2,1)} %collective-permute-done.14), channel_id=1, source_target_pairs={{0,16},{16,0},{1,17},{17,1},{2,18},{18,2},{3,19},{19,3},{4,20},{20... | collective-permute-start | bytes 8650760 | tf_op jit(solution)/shard_map/ppermute | solution.py:229
  429.9 39.8 %collective-permute-start.29 = (bf16[320,2048]{1,0:T(8,128)(2,1)S(1)}, bf16[320,2048]{1,0:T(8,128)(2,1)S(1)}, u32[]{:S(2)}, u32[]{:S(2)}) collective-permute-start(bf16[320,2048]{1,0:T(8,128)(2,1)S(1)} %collective-permute-done.28), channel_id=1, source_target_pairs={{0,2},{1,3},{2,0},{3,1},{4,6},{5,7},{6,4},{7,5},{8,10},{9,11},{10,... | collective-permute-start | bytes 3932168 | tf_op jit(solution)/shard_map/ppermute | solution.py:232
  443.3 70.1 %collective-permute-start.2 = (bf16[512,2048]{1,0:T(8,128)(2,1)S(1)}, bf16[512,2048]{1,0:T(8,128)(2,1)S(1)}, u32[]{:S(2)}, u32[]{:S(2)}) collective-permute-start(bf16[512,2048]{1,0:T(8,128)(2,1)S(1)} %convolution_convert_fusion.7), channel_id=1, source_target_pairs={{0,16},{16,0},{1,17},{17,1},{2,18},{18,2},{3,19},{19,3},{4,20},{20... | collective-permute-start | bytes 6291464 | tf_op jit(solution)/shard_map/ppermute | solution.py:229
  470.9 100.6 %collective-permute-start.13 = (bf16[704,2048]{1,0:T(8,128)(2,1)}, bf16[704,2048]{1,0:T(8,128)(2,1)}, u32[]{:S(2)}, u32[]{:S(2)}) collective-permute-start(bf16[704,2048]{1,0:T(8,128)(2,1)} %collective-permute-done.12), channel_id=1, source_target_pairs={{0,16},{16,0},{1,17},{17,1},{2,18},{18,2},{3,19},{19,3},{4,20},{20... | collective-permute-start | bytes 8650760 | tf_op jit(solution)/shard_map/ppermute | solution.py:229
  507.7 119.8 %collective-permute-start.11 = (bf16[704,2048]{1,0:T(8,128)(2,1)}, bf16[704,2048]{1,0:T(8,128)(2,1)}, u32[]{:S(2)}, u32[]{:S(2)}) collective-permute-start(bf16[704,2048]{1,0:T(8,128)(2,1)} %collective-permute-done.10), channel_id=1, source_target_pairs={{0,16},{16,0},{1,17},{17,1},{2,18},{18,2},{3,19},{19,3},{4,20},{20... | collective-permute-start | bytes 8650760 | tf_op jit(solution)/shard_map/ppermute | solution.py:229
  520.1 52.9 %collective-permute-start.4 = (bf16[320,2048]{1,0:T(8,128)(2,1)}, bf16[320,2048]{1,0:T(8,128)(2,1)}, u32[]{:S(2)}, u32[]{:S(2)}) collective-permute-start(bf16[320,2048]{1,0:T(8,128)(2,1)} %convolution_convert_fusion.14), channel_id=1, source_target_pairs={{0,4},{1,5},{2,6},{3,7},{4,8},{5,9},{6,10},{7,11},{8,12},{9,13},{1... | collective-permute-start | bytes 3932168 | tf_op jit(solution)/shard_map/ppermute | solution.py:232
  565.5 60.5 %collective-permute-start.6 = (bf16[320,2048]{1,0:T(8,128)(2,1)S(1)}, bf16[320,2048]{1,0:T(8,128)(2,1)S(1)}, u32[]{:S(2)}, u32[]{:S(2)}) collective-permute-start(bf16[320,2048]{1,0:T(8,128)(2,1)S(1)} %convolution_convert_fusion.13), channel_id=1, source_target_pairs={{0,8},{1,9},{2,10},{3,11},{4,12},{5,13},{6,14},{7,15},{8,0},{9,1},... | collective-permute-start | bytes 3932168 | tf_op jit(solution)/shard_map/ppermute | solution.py:232
  566.5 64.2 %collective-permute-start.8 = (bf16[320,2048]{1,0:T(8,128)(2,1)S(1)}, bf16[320,2048]{1,0:T(8,128)(2,1)S(1)}, u32[]{:S(2)}, u32[]{:S(2)}) collective-permute-start(bf16[320,2048]{1,0:T(8,128)(2,1)S(1)} %convolution_convert_fusion.12), channel_id=1, source_target_pairs={{0,12},{1,13},{2,14},{3,15},{4,0},{5,1},{6,2},{7,3},{8,4},{9,5},{1... | collective-permute-start | bytes 3932168 | tf_op jit(solution)/shard_map/ppermute | solution.py:232
  571.5 59.7 %collective-permute-start.3 = (bf16[320,2048]{1,0:T(8,128)(2,1)S(1)}, bf16[320,2048]{1,0:T(8,128)(2,1)S(1)}, u32[]{:S(2)}, u32[]{:S(2)}) collective-permute-start(bf16[320,2048]{1,0:T(8,128)(2,1)S(1)} %get-tuple-element.73), channel_id=1, source_target_pairs={{0,2},{1,3},{2,0},{3,1},{4,6},{5,7},{6,4},{7,5},{8,10},{9,11},{10,... | collective-permute-start | bytes 3932168 | tf_op jit(solution)/shard_map/ppermute | solution.py:232
  573.0 62.5 %collective-permute-start.5 = (bf16[320,2048]{1,0:T(8,128)(2,1)}, bf16[320,2048]{1,0:T(8,128)(2,1)S(1)}, u32[]{:S(2)}, u32[]{:S(2)}) collective-permute-start(bf16[320,2048]{1,0:T(8,128)(2,1)} %collective-permute-done.4), channel_id=1, source_target_pairs={{0,2},{1,3},{2,0},{3,1},{4,6},{5,7},{6,4},{7,5},{8,10},{9,11},{10,... | collective-permute-start | bytes 3932168 | tf_op jit(solution)/shard_map/ppermute | solution.py:232
  630.6 55.8 %collective-permute-start.9 = (bf16[320,2048]{1,0:T(8,128)(2,1)S(1)}, bf16[320,2048]{1,0:T(8,128)(2,1)S(1)}, u32[]{:S(2)}, u32[]{:S(2)}) collective-permute-start(bf16[320,2048]{1,0:T(8,128)(2,1)S(1)} %collective-permute-done.8), channel_id=1, source_target_pairs={{0,2},{1,3},{2,0},{3,1},{4,6},{5,7},{6,4},{7,5},{8,10},{9,11},{10,... | collective-permute-start | bytes 3932168 | tf_op jit(solution)/shard_map/ppermute | solution.py:232
  866.9 58.3 %collective-permute-start.35 = (bf16[320,2048]{1,0:T(8,128)(2,1)S(1)}, bf16[320,2048]{1,0:T(8,128)(2,1)S(1)}, u32[]{:S(2)}, u32[]{:S(2)}) collective-permute-start(bf16[320,2048]{1,0:T(8,128)(2,1)S(1)} %get-tuple-element.37), channel_id=1, source_target_pairs={{0,2},{1,3},{2,0},{3,1},{4,6},{5,7},{6,4},{7,5},{8,10},{9,11},{10,... | collective-permute-start | bytes 3932168 | tf_op jit(solution)/shard_map/ppermute | solution.py:232
  867.4 85.9 %collective-permute-start.33 = (bf16[320,2048]{1,0:T(8,128)(2,1)S(1)}, bf16[320,2048]{1,0:T(8,128)(2,1)S(1)}, u32[]{:S(2)}, u32[]{:S(2)}) collective-permute-start(bf16[320,2048]{1,0:T(8,128)(2,1)S(1)} %get-tuple-element.38), channel_id=1, source_target_pairs={{0,2},{1,3},{2,0},{3,1},{4,6},{5,7},{6,4},{7,5},{8,10},{9,11},{10,... | collective-permute-start | bytes 3932168 | tf_op jit(solution)/shard_map/ppermute | solution.py:232
  868.9 110.5 %collective-permute-start.31 = (bf16[320,2048]{1,0:T(8,128)(2,1)S(1)}, bf16[320,2048]{1,0:T(8,128)(2,1)S(1)}, u32[]{:S(2)}, u32[]{:S(2)}) collective-permute-start(bf16[320,2048]{1,0:T(8,128)(2,1)S(1)} %get-tuple-element.39), channel_id=1, source_target_pairs={{0,2},{1,3},{2,0},{3,1},{4,6},{5,7},{6,4},{7,5},{8,10},{9,11},{10,... | collective-permute-start | bytes 3932168 | tf_op jit(solution)/shard_map/ppermute | solution.py:232
  983.6 57.7 %collective-permute-start.36 = (bf16[320,2048]{1,0:T(8,128)(2,1)}, bf16[320,2048]{1,0:T(8,128)(2,1)}, u32[]{:S(2)}, u32[]{:S(2)}) collective-permute-start(bf16[320,2048]{1,0:T(8,128)(2,1)} %get-tuple-element.33), channel_id=1, source_target_pairs={{0,4},{1,5},{2,6},{3,7},{4,8},{5,9},{6,10},{7,11},{8,12},{9,13},{1... | collective-permute-start | bytes 3932168 | tf_op jit(solution)/shard_map/ppermute | solution.py:232
  1008.3 86.7 %collective-permute-start.34 = (bf16[320,2048]{1,0:T(8,128)(2,1)}, bf16[320,2048]{1,0:T(8,128)(2,1)}, u32[]{:S(2)}, u32[]{:S(2)}) collective-permute-start(bf16[320,2048]{1,0:T(8,128)(2,1)} %get-tuple-element.34), channel_id=1, source_target_pairs={{0,8},{1,9},{2,10},{3,11},{4,12},{5,13},{6,14},{7,15},{8,0},{9,1},... | collective-permute-start | bytes 3932168 | tf_op jit(solution)/shard_map/ppermute | solution.py:232
  1011.7 83.3 %collective-permute-start.32 = (bf16[320,2048]{1,0:T(8,128)(2,1)S(1)}, bf16[320,2048]{1,0:T(8,128)(2,1)}, u32[]{:S(2)}, u32[]{:S(2)}) collective-permute-start(bf16[320,2048]{1,0:T(8,128)(2,1)S(1)} %get-tuple-element.35), channel_id=1, source_target_pairs={{0,12},{1,13},{2,14},{3,15},{4,0},{5,1},{6,2},{7,3},{8,4},{9,5},{1... | collective-permute-start | bytes 3932168 | tf_op jit(solution)/shard_map/ppermute | solution.py:232
  1103.2 48.3 %collective-permute-start.37 = (bf16[512,2048]{1,0:T(8,128)(2,1)S(1)}, bf16[512,2048]{1,0:T(8,128)(2,1)}, u32[]{:S(2)}, u32[]{:S(2)}) collective-permute-start(bf16[512,2048]{1,0:T(8,128)(2,1)S(1)} %fusion.121), channel_id=1, source_target_pairs={{0,16},{16,0},{1,17},{17,1},{2,18},{18,2},{3,19},{19,3},{4,20},{20... | collective-permute-start | bytes 6291464 | tf_op jit(solution)/shard_map/ppermute | solution.py:229
  1147.5 171.4 %collective-permute-start.16 = (bf16[320,2048]{1,0:T(8,128)(2,1)}, bf16[320,2048]{1,0:T(8,128)(2,1)}, u32[]{:S(2)}, u32[]{:S(2)}) collective-permute-start(bf16[320,2048]{1,0:T(8,128)(2,1)} %get-tuple-element.44), channel_id=1, source_target_pairs={{0,2},{1,3},{2,0},{3,1},{4,6},{5,7},{6,4},{7,5},{8,10},{9,11},{10,... | collective-permute-start | bytes 3932168 | tf_op jit(solution)/shard_map/ppermute | solution.py:232
  1149.0 170.0 %collective-permute-start.21 = (bf16[320,2048]{1,0:T(8,128)(2,1)}, bf16[320,2048]{1,0:T(8,128)(2,1)}, u32[]{:S(2)}, u32[]{:S(2)}) collective-permute-start(bf16[320,2048]{1,0:T(8,128)(2,1)} %get-tuple-element.45), channel_id=1, source_target_pairs={{0,2},{1,3},{2,0},{3,1},{4,6},{5,7},{6,4},{7,5},{8,10},{9,11},{10,... | collective-permute-start | bytes 3932168 | tf_op jit(solution)/shard_map/ppermute | solution.py:232
  1149.5 169.4 %collective-permute-start.19 = (bf16[320,2048]{1,0:T(8,128)(2,1)}, bf16[320,2048]{1,0:T(8,128)(2,1)}, u32[]{:S(2)}, u32[]{:S(2)}) collective-permute-start(bf16[320,2048]{1,0:T(8,128)(2,1)} %get-tuple-element.46), channel_id=1, source_target_pairs={{0,2},{1,3},{2,0},{3,1},{4,6},{5,7},{6,4},{7,5},{8,10},{9,11},{10,... | collective-permute-start | bytes 3932168 | tf_op jit(solution)/shard_map/ppermute | solution.py:232
  1151.0 168.0 %collective-permute-start.17 = (bf16[320,2048]{1,0:T(8,128)(2,1)}, bf16[320,2048]{1,0:T(8,128)(2,1)}, u32[]{:S(2)}, u32[]{:S(2)}) collective-permute-start(bf16[320,2048]{1,0:T(8,128)(2,1)} %get-tuple-element.47), channel_id=1, source_target_pairs={{0,2},{1,3},{2,0},{3,1},{4,6},{5,7},{6,4},{7,5},{8,10},{9,11},{10,... | collective-permute-start | bytes 3932168 | tf_op jit(solution)/shard_map/ppermute | solution.py:232
  1205.7 612.9 %reduce-scatter.5.cloned.1.call-start = ((), (), s32[]{:S(2)}) async-start(), calls=%async_computation.4 | async-start | bytes 4456448 | tf_op jit(solution)/shard_map/reduce_scatter | solution.py:374
  1329.8 74.7 %collective-permute-start.22 = (bf16[320,2048]{1,0:T(8,128)(2,1)S(1)}, bf16[320,2048]{1,0:T(8,128)(2,1)S(1)}, u32[]{:S(2)}, u32[]{:S(2)}) collective-permute-start(bf16[320,2048]{1,0:T(8,128)(2,1)S(1)} %get-tuple-element.41), channel_id=1, source_target_pairs={{0,4},{1,5},{2,6},{3,7},{4,8},{5,9},{6,10},{7,11},{8,12},{9,13},{1... | collective-permute-start | bytes 3932168 | tf_op jit(solution)/shard_map/ppermute | solution.py:232
  1358.4 116.4 %collective-permute-start.20 = (bf16[320,2048]{1,0:T(8,128)(2,1)S(1)}, bf16[320,2048]{1,0:T(8,128)(2,1)S(1)}, u32[]{:S(2)}, u32[]{:S(2)}) collective-permute-start(bf16[320,2048]{1,0:T(8,128)(2,1)S(1)} %get-tuple-element.42), channel_id=1, source_target_pairs={{0,8},{1,9},{2,10},{3,11},{4,12},{5,13},{6,14},{7,15},{8,0},{9,1},... | collective-permute-start | bytes 3932168 | tf_op jit(solution)/shard_map/ppermute | solution.py:232
  1358.4 117.1 %collective-permute-start.18 = (bf16[320,2048]{1,0:T(8,128)(2,1)S(1)}, bf16[320,2048]{1,0:T(8,128)(2,1)}, u32[]{:S(2)}, u32[]{:S(2)}) collective-permute-start(bf16[320,2048]{1,0:T(8,128)(2,1)S(1)} %get-tuple-element.43), channel_id=1, source_target_pairs={{0,12},{1,13},{2,14},{3,15},{4,0},{5,1},{6,2},{7,3},{8,4},{9,5},{1... | collective-permute-start | bytes 3932168 | tf_op jit(solution)/shard_map/ppermute | solution.py:232
  1366.9 155.0 %collective-permute-start.49 = (bf16[2816,1024]{1,0:T(8,128)(2,1)}, bf16[2816,1024]{1,0:T(8,128)(2,1)}, u32[]{:S(2)}, u32[]{:S(2)}) collective-permute-start(bf16[2816,1024]{1,0:T(8,128)(2,1)} %constant_dynamic-slice_fusion.1), channel_id=1, source_target_pairs={{0,16},{16,0},{1,17},{17,1},{2,18},{18,2},{3,19},{19,3},{4,20},{20... | collective-permute-start | bytes 17301512 | tf_op jit(solution)/shard_map/ppermute | solution.py:229
  1372.9 167.2 %collective-permute-start.45 = (bf16[2816,1024]{1,0:T(8,128)(2,1)}, bf16[2816,1024]{1,0:T(8,128)(2,1)}, u32[]{:S(2)}, u32[]{:S(2)}) collective-permute-start(bf16[2816,1024]{1,0:T(8,128)(2,1)} %constant_dynamic-slice_fusion.3), channel_id=1, source_target_pairs={{0,16},{16,0},{1,17},{17,1},{2,18},{18,2},{3,19},{19,3},{4,20},{20... | collective-permute-start | bytes 17301512 | tf_op jit(solution)/shard_map/ppermute | solution.py:229
  1404.5 257.2 %collective-permute-start.47 = (bf16[2816,1024]{1,0:T(8,128)(2,1)}, bf16[2816,1024]{1,0:T(8,128)(2,1)}, u32[]{:S(2)}, u32[]{:S(2)}) collective-permute-start(bf16[2816,1024]{1,0:T(8,128)(2,1)} %constant_dynamic-slice_fusion.2), channel_id=1, source_target_pairs={{0,16},{16,0},{1,17},{17,1},{2,18},{18,2},{3,19},{19,3},{4,20},{20... | collective-permute-start | bytes 17301512 | tf_op jit(solution)/shard_map/ppermute | solution.py:229
  1538.0 201.8 %collective-permute-start.50 = (bf16[1408,1024]{1,0:T(8,128)(2,1)}, bf16[1408,1024]{1,0:T(8,128)(2,1)}, u32[]{:S(2)}, u32[]{:S(2)}) collective-permute-start(bf16[1408,1024]{1,0:T(8,128)(2,1)} %slice.336), channel_id=1, source_target_pairs={{0,1},{1,0},{2,3},{3,2},{4,5},{5,4},{6,7},{7,6},{8,9},{9,8},{10,11... | collective-permute-start | bytes 8650760 | tf_op jit(solution)/shard_map/ppermute | solution.py:232
  1538.4 118.8 %collective-permute-start.40 = (f32[2,2048]{1,0:T(2,128)S(1)}, f32[2,2048]{1,0:T(2,128)S(1)}, u32[]{:S(2)}, u32[]{:S(2)}) collective-permute-start(f32[2,2048]{1,0:T(2,128)S(1)} %fusion.120), channel_id=1, source_target_pairs={{0,1},{1,0},{2,3},{3,2},{4,5},{5,4},{6,7},{7,6},{8,9},{9,8},{10,11... | collective-permute-start | bytes 49160 | tf_op jit(solution)/shard_map/ppermute | solution.py:232
  1556.2 193.9 %collective-permute-start.46 = (bf16[1408,1024]{1,0:T(8,128)(2,1)}, bf16[1408,1024]{1,0:T(8,128)(2,1)}, u32[]{:S(2)}, u32[]{:S(2)}) collective-permute-start(bf16[1408,1024]{1,0:T(8,128)(2,1)} %slice.338), channel_id=1, source_target_pairs={{0,1},{1,0},{2,3},{3,2},{4,5},{5,4},{6,7},{7,6},{8,9},{9,8},{10,11... | collective-permute-start | bytes 8650760 | tf_op jit(solution)/shard_map/ppermute | solution.py:232
  1678.0 133.0 %collective-permute-start.48 = (bf16[1408,1024]{1,0:T(8,128)(2,1)}, bf16[1408,1024]{1,0:T(8,128)(2,1)}, u32[]{:S(2)}, u32[]{:S(2)}) collective-permute-start(bf16[1408,1024]{1,0:T(8,128)(2,1)} %slice.337), channel_id=1, source_target_pairs={{0,1},{1,0},{2,3},{3,2},{4,5},{5,4},{6,7},{7,6},{8,9},{9,8},{10,11... | collective-permute-start | bytes 8650760 | tf_op jit(solution)/shard_map/ppermute | solution.py:232
  1678.1 49.6 %collective-permute-start.42 = (f32[2,2048]{1,0:T(2,128)S(1)}, f32[2,2048]{1,0:T(2,128)S(1)}, u32[]{:S(2)}, u32[]{:S(2)}) collective-permute-start(f32[2,2048]{1,0:T(2,128)S(1)} %add.263), channel_id=1, source_target_pairs={{0,4},{1,5},{2,6},{3,7},{4,0},{5,1},{6,2},{7,3},{8,12},{9,13},{10,... | collective-permute-start | bytes 49160 | tf_op jit(solution)/shard_map/ppermute | solution.py:232
  1759.1 61.3 %collective-permute-start.44 = (bf16[64,8,3,128]{3,1,2,0:T(8,128)(2,1)S(1)}, bf16[64,8,3,128]{3,1,2,0:T(8,128)(2,1)S(1)}, u32[]{:S(2)}, u32[]{:S(2)}) collective-permute-start(bf16[64,8,3,128]{3,1,2,0:T(8,128)(2,1)S(1)} %bitcast.189), channel_id=1, source_target_pairs={{0,16},{16,0},{1,17},{17,1},{2,18},{18,2},{3,19},{19,3},{4,20},{20... | collective-permute-start | bytes 1179656 | tf_op jit(solution)/shard_map/ppermute | solution.py:229
  (77 other events, 2553.9 us)
Sparse Core Ops, SparseCore 0:
  11.6 270.0 all-gather.1
  1205.8 314.4 reduce-scatter.2
  1522.7 205.1 reduce-scatter.4

commit v2 on v1

v2 whole, which is shorter than its diff:
```python
import functools
import math

import jax
import jax.numpy as jnp
from jax import lax
from jax.experimental import pallas as pl
from jax.experimental.pallas import tpu as pltpu
from jax.sharding import PartitionSpec as P

D = 2048
HEADS = 16
HD = 128
EXPERTS = 4
TOPK = 2
PROMPT = 512
CONT = 256
TILE = 256

norm_eps = 1e-05
scale = 1.0 / math.sqrt(HD)
bf16 = jnp.bfloat16
f32 = jnp.float32


def dot(a, b, ca, cb, out=f32):
    r = lax.dot_general(a, b, (((ca,), (cb,)), ((), ())), preferred_element_type=f32)
    return r.astype(out)


def tile_keys(t):
    prompt_tiles = PROMPT // TILE
    if t < prompt_tiles:
        return list(range(t + 1))
    per = CONT // TILE
    first = prompt_tiles + ((t - prompt_tiles) // per) * per
    return list(range(prompt_tiles)) + list(range(first, t + 1))


def load_tile(ref, perm, t, block, cols):
    per = TILE // block
    parts = [
        ref[pl.ds(pl.multiple_of(perm[t * per + i] * block, block), block), cols]
        for i in range(per)
    ]
    return parts[0] if per == 1 else jnp.concatenate(parts, axis=0)


def store_tile(ref, perm, t, block, cols, value):
    per = TILE // block
    for i in range(per):
        ref[pl.ds(pl.multiple_of(perm[t * per + i] * block, block), block), cols] = value[
            i * block : (i + 1) * block
        ]


def spread_keys(ref, tiles):
    runs, start = [], tiles[0]
    for a, b in zip(tiles, tiles[1:] + [None]):
        if b != a + 1:
            runs.append((start, a + 1))
            start = b
    parts = [ref[lo * TILE : hi * TILE, :] for lo, hi in runs]
    return parts[0] if len(parts) == 1 else jnp.concatenate(parts, axis=0)


def causal_fill(scores, value):
    width = scores.shape[1] - TILE
    row = lax.broadcasted_iota(jnp.int32, (TILE, TILE), 0)
    col = lax.broadcasted_iota(jnp.int32, (TILE, TILE), 1)
    last = jnp.where(col <= row, scores[:, width:], value)
    return last if width == 0 else jnp.concatenate([scores[:, :width], last], axis=1)


def forward_kernel(
    block, perm, pre_q, pre_k, pre_v, cos_ref, sin_ref, ctx_ref, q_ref, k_ref, v_ref, log_ref
):
    tiles = pre_q.shape[0] // TILE
    for t in range(tiles):
        rows = slice(t * TILE, (t + 1) * TILE)
        cos, sin = cos_ref[rows, :], sin_ref[rows, :]
        q = load_tile(pre_q, perm, t, block, slice(None))
        q_ref[rows, :] = (q * cos + pltpu.roll(q, HD // 2, 1) * sin).astype(bf16)
        k = load_tile(pre_k, perm, t, block, slice(None))
        k_ref[rows, :] = (k * cos + pltpu.roll(k, HD // 2, 1) * sin).astype(bf16)
        v_ref[rows, :] = load_tile(pre_v, perm, t, block, slice(None)).astype(bf16)
    for t in range(tiles):
        rows = slice(t * TILE, (t + 1) * TILE)
        seen = tile_keys(t)
        keys, values = spread_keys(k_ref, seen), spread_keys(v_ref, seen)
        scores = dot(q_ref[rows, :], keys, 1, 1) * scale
        scores = causal_fill(scores, -1e30)
        top = jnp.max(scores, axis=1, keepdims=True)
        expo = jnp.exp(scores - top)
        total = jnp.sum(expo, axis=1, keepdims=True)
        probs = (expo * (1.0 / total)).astype(bf16)
        context = dot(probs, values, 1, 0).astype(bf16)
        store_tile(ctx_ref, perm, t, block, slice(None), context)
        log_ref[rows, :] = jnp.broadcast_to(top + jnp.log(total), (TILE, HD))


def backward_kernel(
    block,
    perm,
    q_ref,
    k_ref,
    v_ref,
    log_ref,
    do_ref,
    cos_ref,
    sin_ref,
    out_q,
    out_k,
    out_v,
    dk_ref,
    dv_ref,
):
    tiles = q_ref.shape[0] // TILE
    dk_ref[...] = jnp.zeros_like(dk_ref)
    dv_ref[...] = jnp.zeros_like(dv_ref)
    for t in range(tiles):
        rows = slice(t * TILE, (t + 1) * TILE)
        seen = tile_keys(t)
        keys, values = spread_keys(k_ref, seen), spread_keys(v_ref, seen)
        query = q_ref[rows, :]
        grad = load_tile(do_ref, perm, t, block, slice(None))
        scores = dot(query, keys, 1, 1) * scale
        soft = causal_fill(jnp.exp(scores - log_ref[rows, 0:1]), 0.0)
        grad_prob = dot(grad, values, 1, 1)
        delta = jnp.sum(grad_prob * soft, axis=1, keepdims=True)
        grad_scores = (soft * (grad_prob - delta)).astype(bf16)
        values_back = dot(soft.astype(bf16), grad, 0, 0)
        keys_back = dot(grad_scores, query, 0, 0)
        for i, s in enumerate(seen):
            part, own = slice(i * TILE, (i + 1) * TILE), slice(s * TILE, (s + 1) * TILE)
            dv_ref[own, :] += values_back[part]
            dk_ref[own, :] += keys_back[part]
        back = dot(grad_scores, keys, 1, 0) * scale
        cos, sin = cos_ref[rows, :], sin_ref[rows, :]
        back = back * cos - pltpu.roll(back, HD // 2, 1) * sin
        store_tile(out_q, perm, t, block, slice(None), back.astype(bf16))
    for t in range(tiles):
        rows = slice(t * TILE, (t + 1) * TILE)
        cos, sin = cos_ref[rows, :], sin_ref[rows, :]
        back = dk_ref[rows, :] * scale
        back = back * cos - pltpu.roll(back, HD // 2, 1) * sin
        store_tile(out_k, perm, t, block, slice(None), back.astype(bf16))
        store_tile(out_v, perm, t, block, slice(None), dv_ref[rows, :].astype(bf16))


def attention_forward(perm, block, pre, cos, sin):
    rows, heads = pre[0].shape[0], pre[0].shape[1] // HD
    per_head = pl.BlockSpec((rows, HD), lambda h, p: (0, h))
    table = pl.BlockSpec((rows, HD), lambda h, p: (0, 0))
    head_array = jax.ShapeDtypeStruct((rows, heads * HD), bf16)
    return pl.pallas_call(
        functools.partial(forward_kernel, block),
        grid_spec=pltpu.PrefetchScalarGridSpec(
            num_scalar_prefetch=1,
            grid=(heads,),
            in_specs=[per_head] * 3 + [table, table],
            out_specs=[per_head] * 5,
        ),
        out_shape=[head_array] * 4 + [jax.ShapeDtypeStruct((rows, heads * HD), f32)],
        name="attention_forward",
    )(perm, *pre, cos, sin)


def attention_backward(perm, block, q, k, v, log_total, grad, cos, sin):
    rows, heads = q.shape[0], q.shape[1] // HD
    per_head = pl.BlockSpec((rows, HD), lambda h, p: (0, h))
    table = pl.BlockSpec((rows, HD), lambda h, p: (0, 0))
    return pl.pallas_call(
        functools.partial(backward_kernel, block),
        grid_spec=pltpu.PrefetchScalarGridSpec(
            num_scalar_prefetch=1,
            grid=(heads,),
            in_specs=[per_head] * 5 + [table, table],
            out_specs=[per_head] * 3,
            scratch_shapes=[pltpu.VMEM((rows, HD), f32), pltpu.VMEM((rows, HD), f32)],
        ),
        out_shape=[jax.ShapeDtypeStruct((rows, heads * HD), bf16)] * 3,
        name="attention_backward",
    )(perm, q, k, v, log_total, grad, cos, sin)


def expert_kernel(kept, x_ref, g_ref, wg_ref, wu_ref, wd_ref, *refs):
    hidden_ref, gate_ref, up_ref = refs[kept:]
    count = x_ref.shape[0] // 2
    for p in range(2):
        rows = slice(p * count, (p + 1) * count)
        gate = dot(x_ref[rows, :], wg_ref[...], 1, 1)
        up = dot(x_ref[rows, :], wu_ref[...], 1, 1)
        grad = dot(g_ref[rows, :], wd_ref[...], 1, 1)
        sigmoid = jax.nn.sigmoid(gate)
        silu = gate * sigmoid
        hidden_ref[rows, :] = (silu * up).astype(bf16)
        gate_ref[rows, :] = (grad * up * sigmoid * (1.0 + gate * (1.0 - sigmoid))).astype(bf16)
        up_ref[rows, :] = (grad * silu).astype(bf16)


def expert_hidden(part, parts, slots, grads, weights, kept):
    rows, units = slots.shape[0], weights[0].shape[0]
    tile = 256 if units % 256 == 0 else 128
    whole = pl.BlockSpec((rows, D), lambda i: (0, 0))
    weight = pl.BlockSpec((tile, D), lambda i: (i, 0))
    result = pl.BlockSpec((rows, tile), lambda i: (part, i))
    return pl.pallas_call(
        functools.partial(expert_kernel, len(kept)),
        grid=(units // tile,),
        in_specs=[whole] * 2 + [weight] * 3 + [pl.BlockSpec(memory_space=pl.ANY)] * len(kept),
        out_specs=[result] * 3,
        out_shape=[jax.ShapeDtypeStruct((parts * rows, units), bf16)] * 3,
        input_output_aliases={5 + i: i for i in range(len(kept))},
        name="expert_hidden",
    )(slots, grads, *weights, *kept)


def rope_tables(group_len):
    index = jnp.arange(group_len, dtype=jnp.int32)
    position = jnp.where(index < PROMPT, index, PROMPT + (index - PROMPT) % CONT).astype(f32)
    half = HD // 2
    frequency = jnp.exp(-math.log(10000.0) * jnp.arange(half, dtype=f32) / half)
    angles = position[:, None] * frequency[None, :]
    cosine, sine = jnp.cos(angles), jnp.sin(angles)
    return (
        jnp.concatenate([cosine, cosine], axis=1),
        jnp.concatenate([-sine, sine], axis=1),
    )


def after(*arrays):
    return lax.optimization_barrier(arrays)


def normalize_parts(values, gain):
    inverse = lax.rsqrt(jnp.mean(values * values, axis=-1, keepdims=True) + norm_eps)
    unit_rows = values * inverse
    return (unit_rows * gain, unit_rows, inverse)


def norm_backward(grad_outer, unit_rows, inverse, gain):
    grad_unit = grad_outer * gain
    grad_inner = inverse * (
        grad_unit - unit_rows * jnp.mean(grad_unit * unit_rows, axis=-1, keepdims=True)
    )
    return (grad_inner, jnp.sum(grad_outer * unit_rows, axis=0))


def shards(
    tokens,
    route_ids,
    gate_values,
    deal,
    norm1_gain,
    w_query,
    w_key,
    w_value,
    w_out,
    norm2_gain,
    w_gate,
    w_up,
    w_down,
    cotangent,
):
    rows = tokens.shape[1]
    ctx_count = lax.axis_size("ctx")
    fsdp_count = lax.axis_size("fsdp")
    group_len = rows * ctx_count
    capacity = 5 * rows * TOPK // (4 * EXPERTS)
    repeats = fsdp_count // EXPERTS
    pair = 2
    columns = repeats // pair
    core = lax.axis_index("ctx")
    expert = lax.axis_index("fsdp") // repeats
    width = D // ctx_count
    heads = HEADS // ctx_count

    def core_shift(a, s):
        return lax.ppermute(a, "ctx", [(i, (i + s) % ctx_count) for i in range(ctx_count)])

    def fsdp_shift(a, move):
        return lax.ppermute(a, "fsdp", [(i, move(i)) for i in range(fsdp_count)])

    def expert_shift(a, k):
        return fsdp_shift(a, lambda i: (i + k * repeats) % fsdp_count)

    def column_shift(a, j):
        def move(i):
            e, r = divmod(i, repeats)
            t, w = divmod(r, pair)
            return e * repeats + ((t + j) % columns) * pair + w

        return fsdp_shift(a, move)

    def pair_swap(a):
        return fsdp_shift(a, lambda i: i ^ 1)

    def core_gather(a):
        return jnp.concatenate([a] + [core_shift(a, s) for s in range(1, ctx_count)], axis=0)

    block_count = deal.shape[1]
    block = group_len // block_count
    local_blocks = block_count // ctx_count
    dealt = jnp.argsort(deal[0]).astype(jnp.int32)
    perm = ((core - dealt // local_blocks) % ctx_count) * local_blocks + dealt % local_blocks
    cos, sin = rope_tables(group_len)

    def own_columns(w):
        return lax.dynamic_slice_in_dim(w, core * width, width, axis=1)

    packed = jnp.concatenate([own_columns(w) for w in (w_query, w_key, w_value, w_out)], axis=1)
    gathered = lax.all_gather(packed, "fsdp", axis=0, tiled=True)

    halves = 2
    part_slots = capacity // halves
    half = EXPERTS * part_slots
    ids = route_ids[0]
    flat = ids.reshape(-1)
    onehot = (flat[:, None] == jnp.arange(EXPERTS, dtype=jnp.int32)[None, :]).astype(jnp.int32)
    earlier = jnp.cumsum(onehot, axis=0) - onehot
    slot = jnp.sum(earlier * onehot, axis=1)
    place = (slot // part_slots) * half + flat * part_slots + slot % part_slots
    place = jnp.where(slot < capacity, place, -1).reshape(rows, TOPK)
    targets = jnp.arange(halves * half, dtype=jnp.int32)
    select = [(place[:, k : k + 1] == targets[None, :]).astype(bf16) for k in range(TOPK)]
    spread = [(targets[:, None] == place[None, :, k]).astype(bf16) for k in range(TOPK)]
    gates = gate_values[0]

    dy = cotangent[0].astype(f32)
    grad_pairs = jnp.concatenate([(dy * gates[:, k : k + 1]).astype(bf16) for k in range(TOPK)])
    spread_both = jnp.concatenate(spread, axis=1)
    grad_blocks = [
        dot(spread_both[h * half : (h + 1) * half], grad_pairs, 1, 0, bf16) for h in range(halves)
    ]

    inputs = tokens[0].astype(f32)
    normed_f, _, _ = normalize_parts(inputs, norm1_gain)
    normed = core_gather(normed_f.astype(bf16))

    per = D // (ctx_count * fsdp_count)
    mine = lax.axis_index("fsdp")
    my_column, my_side = (mine % repeats) // pair, mine % pair

    def feature_order(side_first):
        index = jnp.arange(D, dtype=jnp.int32)
        rest, j = index // per, index % per
        rest, c = rest // ctx_count, rest % ctx_count
        rest, e = rest // EXPERTS, rest % EXPERTS
        if side_first:
            w, t = rest // columns, rest % columns
        else:
            t, w = rest // pair, rest % pair
        t, w = (my_column + t) % columns, (my_side + w) % pair
        source = c * (D // ctx_count) + (e * repeats + t * pair + w) * per + j
        shuffle = (jnp.arange(D, dtype=jnp.int32)[:, None] == source[None, :]).astype(bf16)
        return dot(normed, shuffle, 1, 0, bf16)

    normed_side, normed_column = feature_order(True), feature_order(False)

    def weight_part(w):
        count = w.shape[0] // ctx_count
        return lax.dynamic_slice_in_dim(w, core * count, count, axis=0)

    weight_parts = [weight_part(w) for w in (w_gate, w_up, w_down)]
    gathered, *tied = after(gathered, normed_side, normed_column, *grad_blocks, *weight_parts)
    normed_side, normed_column = tied[:2]
    grad_blocks, weight_parts = tied[2 : 2 + halves], tied[2 + halves :]
    full_q, full_k, full_v, out_columns = (
        gathered[:, i * width : (i + 1) * width] for i in range(4)
    )

    lines = [[r + e * repeats for e in range(EXPERTS)] for r in range(repeats)]

    def swap_experts(a, width=D):
        blocks = a.reshape(EXPERTS, -1, width)
        return lax.all_to_all(blocks, "fsdp", 0, 0, axis_index_groups=lines, tiled=True)

    def to_columns(a):
        return [a] + [column_shift(a, j) for j in range(1, columns)]

    grads_first = swap_experts(grad_blocks[0]).reshape(half, D)

    sides = [[i, i ^ 1] for i in range(0, fsdp_count, 2)]
    sides = [sorted(group) for group in sides]
    swapped = [
        lax.all_gather(part, "fsdp", axis=0, tiled=True, axis_index_groups=sides)
        for part in weight_parts
    ]

    def pair_weights(part):
        if ctx_count == 2:
            again = core_shift(part, 1)
            count = part.shape[0] // pair
            rows_of = []
            for i in range(pair):
                a, b = part[i * count : (i + 1) * count], again[i * count : (i + 1) * count]
                rows_of += [jnp.where(core == 0, a, b), jnp.where(core == 0, b, a)]
            return jnp.concatenate(rows_of, axis=0)
        every = lax.all_gather(part, "ctx", axis=0, tiled=False)
        return every.reshape(ctx_count, pair, -1, D).transpose(1, 0, 2, 3).reshape(-1, D)

    pre = [dot(normed, w, 1, 0) for w in (full_q, full_k, full_v)]
    context, q, k, v, log_total = attention_forward(perm, block, pre, cos, sin)

    def out_rows(c):
        return lax.dynamic_slice_in_dim(out_columns, (c % ctx_count) * width, width, axis=0)

    if ctx_count == 2:
        own_part, other = out_rows(core), core_shift(out_rows(core + 1), 1)
        w_o = jnp.concatenate(
            [jnp.where(core == 0, own_part, other), jnp.where(core == 0, other, own_part)], axis=1
        )
    else:
        w_o = lax.all_to_all(out_columns.reshape(ctx_count, width, width), "ctx", 0, 0)
        w_o = w_o.transpose(1, 0, 2).reshape(width, D)
    away = [dot(context[s * rows : (s + 1) * rows], w_o, 1, 0, bf16) for s in range(1, ctx_count)]
    attention = dot(context[:rows], w_o, 1, 0)
    for s in range(1, ctx_count):
        attention = attention + core_shift(away[s - 1], -s).astype(f32)
    hidden_in = inputs + attention
    normed_two_f, unit_two, inverse_two = normalize_parts(hidden_in, norm2_gain)
    normed_two = normed_two_f.astype(bf16)

    spread_any = spread[0] + spread[1]
    slot_blocks = [
        dot(spread_any[h * half : (h + 1) * half], normed_two, 1, 0, bf16) for h in range(halves)
    ]
    grads_first, waiting, _ = after(grads_first, grad_blocks[1], away[0])
    grads_second = swap_experts(waiting).reshape(half, D)
    grad_parts = to_columns(grads_first)
    got = after(grads_second, *slot_blocks, *swapped[:2], *grad_parts[1:])
    grads_second, slots_a, slots_b, *swapped_two = got[:5]
    grad_parts[1:] = got[5:]
    grad_parts += to_columns(grads_second)
    first = swap_experts(slots_a).reshape(half, D)
    wg, wu = (pair_weights(w) for w in swapped_two)
    got = after(first, slots_b, swapped[2], wg, wu, *grad_parts[columns + 1 :])
    first, slots_b, swapped_down, wg, wu = got[:5]
    grad_parts[columns + 1 :] = got[5:]
    second = swap_experts(slots_b).reshape(half, D)
    wd = pair_weights(swapped_down)
    weights = (wg, wu, wd)
    parts = halves * columns

    def hidden_part(index, slots, state):
        return expert_hidden(index, parts, slots, grad_parts[index], weights, state)

    def part_rows(index):
        return slice(index * half, (index + 1) * half)

    def grad_rows(index, state):
        part = part_rows(index)
        return (dot(state[1][part], wg, 1, 0) + dot(state[2][part], wu, 1, 0)).astype(bf16)

    def columns_home(pieces):
        return [column_shift(part, -(j + 1)) for j, part in enumerate(pieces)]

    def add_parts(own, returned):
        total = own.astype(f32)
        for part in returned:
            total = total + part.astype(f32)
        return total.astype(bf16)

    slot_parts = to_columns(first)
    state, back, came = (), {}, []
    home_first = None
    for h in range(halves):
        for j in range(columns):
            index = h * columns + j
            state = hidden_part(index, slot_parts[index], state)
            if index == 0:
                second, *got = after(second, *state, *slot_parts[1:])
                state, slot_parts[1:] = got[:3], got[3:]
                slot_parts += to_columns(second)
            if h == 1 and j == 0:
                tied = after(*state, *came[0])
                home_first = add_parts(back[0], tied[3:])
                *state, home_first = after(*tied[:3], home_first)
                home_first = swap_experts(home_first)
        for j in [*range(1, columns), 0]:
            index = h * columns + j
            back[index] = grad_rows(index, state)
            back[index], *state = after(back[index], *state)
        came.append(columns_home([back[h * columns + j] for j in range(1, columns)]))
    hidden, grad_gate, grad_up = state
    all_slots = jnp.concatenate(slot_parts, axis=0)
    all_grads = jnp.concatenate(grad_parts, axis=0)

    def core_sum(part):
        total = lax.dynamic_slice_in_dim(part, core * width, width, axis=1).astype(f32)
        for s in range(1, ctx_count):
            start = ((core + s) % ctx_count) * width
            total = total + core_shift(
                lax.dynamic_slice_in_dim(part, start, width, axis=1), s
            ).astype(f32)
        return total.astype(bf16)

    def side_sum(total):
        return lax.psum_scatter(
            total, "fsdp", scatter_dimension=0, tiled=True, axis_index_groups=sides
        ).astype(f32)

    hidden_t = after(hidden, *(back[i] for i in range(parts)))[0]
    down_part = dot(hidden_t, all_grads, 0, 0, bf16)
    down_part, gate_t, home_first, *came[1] = after(down_part, grad_gate, home_first, *came[1])
    home_second = swap_experts(add_parts(back[columns], came[1]))
    gate_part = dot(gate_t, all_slots, 0, 0, bf16)
    down_total = core_sum(down_part)
    gate_part, down_total, hidden_t = after(gate_part, down_total, hidden)
    down_grad = side_sum(down_total)

    gate_total = core_sum(gate_part)
    outs, away_out = [None] * parts, []
    for j in [*range(1, columns), 0]:
        for h in range(halves):
            outs[h * columns + j] = dot(hidden_t[part_rows(h * columns + j)], wd, 1, 0, bf16)
        if j:
            *tied, hidden_t = after(*(o for o in outs if o is not None), hidden_t)
    away_out = [columns_home(outs[h * columns + 1 : (h + 1) * columns]) for h in range(halves)]
    gate_total, home_second, *outs = after(gate_total, home_second, *outs)
    gate_grad = side_sum(gate_total)
    grad_slot_in = jnp.concatenate([home_first, home_second], axis=0).reshape(halves * half, D)

    grad_normed_two = dot(select[0] + select[1], grad_slot_in, 1, 0)
    grad_norm_two, norm2_part = norm_backward(grad_normed_two, unit_two, inverse_two, norm2_gain)
    grad_hidden_in = dy + grad_norm_two
    grad_attention = core_gather(grad_hidden_in.astype(bf16))
    def reduce_blocks(blocks, shift):
        total = blocks[0].astype(f32)
        for d in range(1, len(blocks)):
            total = total + shift(blocks[d].astype(bf16), d).astype(f32)
        return total.astype(bf16)

    def cut(a, n):
        size = a.shape[0] // n
        return [a[i * size : (i + 1) * size] for i in range(n)]

    def side_shift(a, d):
        return pair_swap(a)

    def first_blocks(left, grad, n):
        size = D // n
        return [dot(left[:, i * size : (i + 1) * size], grad, 0, 0, bf16) for i in range(n)]

    def expert_sum(total):
        blocks = swap_experts(total, total.shape[1])
        return jnp.sum(blocks.reshape(EXPERTS, -1, total.shape[1]).astype(f32), axis=0)

    def row_blocks(a, n, own):
        split = a.reshape(EXPERTS, n, -1, a.shape[1])
        return [
            lax.dynamic_slice_in_dim(split, (own + d) % n, 1, axis=1).reshape(-1, a.shape[1])
            for d in range(n)
        ]

    out_part = dot(context, grad_attention, 0, 0, bf16)
    blocks_o = row_blocks(out_part, columns, my_column)
    grad_attention, *blocks_o = after(grad_attention, *blocks_o)
    sum_o = reduce_blocks(blocks_o, column_shift)
    grad_context = dot(grad_attention, w_o, 1, 1, bf16)
    grad_q, grad_k, grad_v = attention_backward(
        perm, block, q, k, v, log_total, grad_context, cos, sin
    )
    grad_q, grad_k, grad_v, *away_out[0] = after(grad_q, grad_k, grad_v, *away_out[0])
    outs_first = swap_experts(add_parts(outs[0], away_out[0]))
    blocks_q = first_blocks(normed_side, grad_q, pair)
    blocks_k = first_blocks(normed_column, grad_k, columns)
    blocks_v = first_blocks(normed_side, grad_v, pair)
    up_t, *tied = after(grad_up, grad_q, grad_k, grad_v, *blocks_q, *blocks_k, *blocks_v)
    grad_q, grad_k, grad_v = tied[:3]
    tied = tied[3:]
    blocks_q, blocks_k, blocks_v = tied[:pair], tied[pair : pair + columns], tied[pair + columns :]
    sum_q = reduce_blocks(blocks_q, side_shift)
    sum_k = reduce_blocks(blocks_k, column_shift)
    sum_v = reduce_blocks(blocks_v, side_shift)
    up_part = dot(up_t, all_slots, 0, 0, bf16)

    def back_rows(s, out):
        part = slice(s * rows, (s + 1) * rows)
        total = dot(grad_q[part], full_q, 1, 1) + dot(grad_k[part], full_k, 1, 1)
        return (total + dot(grad_v[part], full_v, 1, 1)).astype(out)

    up_part, grad_q, grad_k, grad_v = after(up_part, grad_q, grad_k, grad_v)
    up_total = core_sum(up_part)
    back_away = [back_rows(s, bf16) for s in range(1, ctx_count)]
    grad_normed = back_rows(0, f32)

    sum_q, sum_o, grad_normed, up_total, outs_first, own, *away_out[1] = after(
        sum_q, sum_o, grad_normed, up_total, outs_first, outs[columns], *away_out[1]
    )
    up_grad = side_sum(up_total)
    outs_second = swap_experts(add_parts(own, away_out[1]))
    sum_q = reduce_blocks(cut(sum_q, columns), column_shift)
    sum_o = reduce_blocks(row_blocks(sum_o, pair, my_side), side_shift)
    for s in range(1, ctx_count):
        grad_normed = grad_normed + core_shift(back_away[s - 1], -s).astype(f32)
    _, unit_one, inverse_one = normalize_parts(inputs, norm1_gain)
    grad_norm_one, norm1_part = norm_backward(grad_normed, unit_one, inverse_one, norm1_gain)
    tokens_grad = (grad_hidden_in + grad_norm_one).astype(bf16)

    sum_k, sum_v, tokens_grad = after(sum_k, sum_v, tokens_grad)
    sum_k = reduce_blocks(cut(sum_k, pair), side_shift)
    sum_v = reduce_blocks(cut(sum_v, columns), column_shift)
    out_grad = expert_sum(sum_o)
    sums = jnp.stack([expert_sum(a) for a in (sum_q, sum_k, sum_v)]).reshape(
        3, ctx_count, per, width
    )

    def core_piece(c):
        return lax.dynamic_index_in_dim(sums, c % ctx_count, 1, keepdims=False)

    if ctx_count == 2:
        own_part, other = core_piece(core), core_shift(core_piece(core + 1), 1)
        qkv_own = jnp.concatenate(
            [jnp.where(core == 0, own_part, other), jnp.where(core == 0, other, own_part)], axis=2
        )
    else:
        qkv_own = lax.all_to_all(sums.astype(bf16), "ctx", 1, 1).astype(f32)
        qkv_own = qkv_own.transpose(0, 2, 1, 3).reshape(3, per, D)
    query_grad, key_grad, value_grad = qkv_own[0], qkv_own[1], qkv_own[2]

    gains = jnp.stack([norm1_part, norm2_part])
    step = 1
    while step < ctx_count:
        gains = gains + lax.ppermute(gains, "ctx", [(i, i ^ step) for i in range(ctx_count)])
        step *= 2
    step = 1
    while step < fsdp_count:
        gains = gains + fsdp_shift(gains, lambda i, step=step: i ^ step)
        step *= 2
    place_own = (core * fsdp_count + mine) * per
    gains_own = lax.dynamic_slice_in_dim(gains, place_own, per, axis=1)

    slot_out = jnp.concatenate([outs_first, outs_second], axis=0).reshape(halves * half, D)
    mixed = hidden_in
    for i in range(TOPK):
        mixed = mixed + dot(select[i], slot_out, 1, 0) * gates[:, i : i + 1]

    return (
        mixed.astype(bf16)[None],
        tokens_grad[None],
        gains_own[0],
        query_grad,
        key_grad,
        value_grad,
        out_grad,
        gains_own[1],
        gate_grad,
        up_grad,
        down_grad,
    )


def solution(mesh):
    in_specs = (
        P("fsdp", "ctx", None),
        P("fsdp", "ctx", None),
        P("fsdp", "ctx", None),
        P("fsdp", None),
        P(),
        P("fsdp", None),
        P("fsdp", None),
        P("fsdp", None),
        P("fsdp", None),
        P(),
        P("fsdp", None),
        P("fsdp", None),
        P("fsdp", None),
        P("fsdp", "ctx", None),
    )
    out_specs = (
        P("fsdp", "ctx", None),
        P("fsdp", "ctx", None),
        P(("ctx", "fsdp")),
        P(("ctx", "fsdp"), None),
        P(("ctx", "fsdp"), None),
        P(("ctx", "fsdp"), None),
        P(("ctx", "fsdp"), None),
        P(("ctx", "fsdp")),
        P("fsdp", "ctx"),
        P("fsdp", "ctx"),
        P("fsdp", "ctx"),
    )
    return jax.shard_map(shards, mesh=mesh, in_specs=in_specs, out_specs=out_specs, check_vma=False)
```

time: 1860 us -> 1490 us (0.80); the launches traced: 1830 us -> 1480 us
  waiting for transfers between devices: 905 us -> 490 us
  Pallas kernels: 49.2 us -> 171 us
  other arithmetic: 114 us -> 231 us
  starting transfers between devices: 151 us -> 83.2 us
  matrix products: 489 us -> 424 us
  local copies, waits for them, and re-layouts: 107 us -> 67.3 us
    ppermute x38 -> x20, waiting for transfers between devices: 664 us -> 263 us  [fsdp_shift(): return lax.ppermute(a, 'fsdp', [(i, move(i)) for i in range(fsdp_count)])]
    ppermute x38 -> x20, starting transfers between devices: 150 us -> 23.1 us  [fsdp_shift(): return lax.ppermute(a, 'fsdp', [(i, move(i)) for i in range(fsdp_count)])]
    pallas_call x0 -> x4, Pallas kernels: none -> 123 us  [expert_hidden(): pl.pallas_call(functools.partial(expert_kernel, len(kept)), grid=(units /...]
    all_gather x1, waiting for transfers between devices: 241 us -> 141 us  [shards(): gathered = lax.all_gather(packed, 'fsdp', axis=0, tiled=True)]
    concatenate x1 -> x6, other arithmetic: 1.04 us -> 95.1 us  [the longest x3 89.4 us: pair_weights(): return jnp.concatenate(rows_of, axis=0)]
    convert_element_type x5 -> x19, other arithmetic: 17.4 us -> 91.7 us  [the longest x3 29.8 us: core_sum(): return total.astype(bf16)]
    dot_general x28 -> x43, matrix products: 489 us -> 424 us  [dot(): lax.dot_general(a, b, (((ca,), (cb,)), ((), ())), preferred_element_type=...]
    all_to_all x0 -> x12, starting transfers between devices: none -> 57.3 us  [swap_experts(): lax.all_to_all(blocks, 'fsdp', 0, 0, axis_index_groups=lines, tiled=True)]
  transfers between devices with their start and end apart: 54 -> 52, of which waited for: 21 -> 22; matrix products, arithmetic and copies ran while one was open for 27% -> 42% of each run, Pallas kernels for 3% -> 7%
where the time goes in v2:
time: 1490 us; the launch traced here: 1480 us
  waiting for transfers between devices  490 us (33%)
  matrix products  424 us (28%)
  other arithmetic  231 us (16%)
  Pallas kernels  171 us (11%)
  starting transfers between devices  83.2 us (6%)
  local copies, waits for them, and re-layouts  67.3 us (5%)
  between operations  15.7 us (1%)
    dot_general x43, matrix products, dot(): lax.dot_general(a, b, (((ca,), (cb,)), ((), ())), preferred_element_type=...  424 us
    ppermute x20, waiting for transfers between devices, fsdp_shift(): return lax.ppermute(a, 'fsdp', [(i, move(i)) for i in range(fsdp_count)])  263 us
    all_gather x1, waiting for transfers between devices, shards(): gathered = lax.all_gather(packed, 'fsdp', axis=0, tiled=True)  141 us
    pallas_call x4, Pallas kernels, expert_hidden(): pl.pallas_call(functools.partial(expert_kernel, len(kept)), grid=(units /...  123 us
    concatenate x3, other arithmetic, pair_weights(): return jnp.concatenate(rows_of, axis=0)  89.4 us
    all_to_all x12, starting transfers between devices, swap_experts(): lax.all_to_all(blocks, 'fsdp', 0, 0, axis_index_groups=lines, tiled=True)  57.3 us
    all_gather x3, waiting for transfers between devices, shards(): lax.all_gather(part, 'fsdp', axis=0, tiled=True, axis_index_groups=sides)  49.8 us
  transfers between devices with their start and end apart: 52, of which 22 were waited for; matrix products, arithmetic and copies ran while one was open for 42% of the time, Pallas kernels for 7%

profile of v2, /device:TPU:0, one launch (start us, length us, event | category | flops | bytes accessed | tf_op | source)
XLA Modules:
  0.0 1482.5 jit_solution(5817609039466501030)
XLA Ops:
  38.0 13.3 fusion.25
  51.4 13.6 fusion.26
  65.0 140.7 %all-gather.5.cloned.1.call-done = bf16[2048,4096]{1,0:T(8,128)(2,1)} async-done(((bf16[128,4096]{1,0:T(8,128)(2,1)}), bf16[2048,4096]{1,0:T(8,128)(2,1)}) %all-gather.5.cloned.1.call-update) | async-done | bytes 16777232 | tf_op jit(solution)/shard_map/all_gather | solution.py:313
  223.9 9.9 fusion.55.pre_v
  233.7 10.0 fusion.61.pre_k
  243.7 10.0 fusion.67.pre_q
  253.6 21.7 %attention_forward.1 = (bf16[1024,1024]{1,0:T(8,128)(2,1)}, bf16[1024,1024]{1,0:T(8,128)(2,1)}, bf16[1024,1024]{1,0:T(8,128)(2,1)}, bf16[1024,1024]{1,0:T(8,128)(2,1)}, f32[1024,1024]{1,0:T(8,128)}) custom-call(s32[4]{0:T(128)} %fusion.189.perm, f32[1024,1024]{1,0:T(8,128)} %fusion.67.pre_q, f32[1024,1024]{1,0:T(8,128)} %fusion.61.pre_k, ...), custom_call_target="tpu_custom_call" | custom-call | tf_op jit(solution)/shard_map/attention_forward/pallas_call | solution.py:156
  306.2 49.8 %all-gather.9.cloned.1.call-done = bf16[1408,2048]{1,0:T(8,128)(2,1)} async-done(((bf16[704,2048]{1,0:T(8,128)(2,1)}), bf16[1408,2048]{1,0:T(8,128)(2,1)}) %all-gather.9.cloned.1.call-update) | async-done | bytes 5767184 | tf_op jit(solution)/shard_map/all_gather | solution.py:387
  378.7 29.8 %pad_maximum_fusion.1.wu_ref = bf16[2816,2048]{1,0:T(8,128)(2,1)} fusion(bf16[704,2048]{1,0:T(8,128)(2,1)S(1)} %get-tuple-element.256, bf16[704,2048]{1,0:T(8,128)(2,1)S(1)} %get-tuple-element.255, bf16[704,2048]{1,0:T(8,128)(2,1)S(1)} %get-tuple-element.254, bf16[704,2048]{1,0:T(8,128)(2,1)S(1)} %get-tuple-element.253), kind=kLoop, calls=%fused_computation.5 | loop fusion | flops 46137344 | bytes 23068672 | tf_op jit(solution)/shard_map/concatenate | solution.py:399
  408.6 29.8 %pad_maximum_fusion.wg_ref = bf16[2816,2048]{1,0:T(8,128)(2,1)} fusion(bf16[704,2048]{1,0:T(8,128)(2,1)S(1)} %get-tuple-element.260, bf16[704,2048]{1,0:T(8,128)(2,1)S(1)} %get-tuple-element.259, bf16[704,2048]{1,0:T(8,128)(2,1)S(1)} %get-tuple-element.258, bf16[704,2048]{1,0:T(8,128)(2,1)S(1)} %get-tuple-element.257), kind=kLoop, calls=%fused_computation.4 | loop fusion | flops 46137344 | bytes 23068672 | tf_op jit(solution)/shard_map/concatenate | solution.py:399
  452.9 29.8 %pad_maximum_fusion.2.wd_ref = bf16[2816,2048]{1,0:T(8,128)(2,1)} fusion(bf16[704,2048]{1,0:T(8,128)(2,1)S(1)} %get-tuple-element.252, bf16[704,2048]{1,0:T(8,128)(2,1)S(1)} %get-tuple-element.251, bf16[704,2048]{1,0:T(8,128)(2,1)S(1)} %get-tuple-element.250, bf16[704,2048]{1,0:T(8,128)(2,1)S(1)} %get-tuple-element.249), kind=kLoop, calls=%fused_computation.6 | loop fusion | flops 46137344 | bytes 23068672 | tf_op jit(solution)/shard_map/concatenate | solution.py:399
  482.7 30.6 %expert_hidden.4 = (bf16[2560,2816]{1,0:T(8,128)(2,1)}, bf16[2560,2816]{1,0:T(8,128)(2,1)}, bf16[2560,2816]{1,0:T(8,128)(2,1)}) custom-call(bf16[640,2048]{1,0:T(8,128)(2,1)} %bitcast.135, bf16[640,2048]{1,0:T(8,128)(2,1)} %bitcast.11.g_ref, bf16[2816,2048]{1,0:T(8,128)(2,1)} %pad_maximum_fusion.wg_ref, bf16[2816,2048]{1,0:T(8,128)(2,1)} %pad_maximum_fusion.1.wu_ref, ...), custom_call_target="tpu_custom_call" | custom-call | tf_op jit(solution)/shard_map/expert_hidden/pallas_call | solution.py:208
  513.3 30.6 %expert_hidden.5 = (bf16[2560,2816]{1,0:T(8,128)(2,1)}, bf16[2560,2816]{1,0:T(8,128)(2,1)}, bf16[2560,2816]{1,0:T(8,128)(2,1)}) custom-call(bf16[640,2048]{1,0:T(8,128)(2,1)} %collective-permute-done.8.x_ref, bf16[640,2048]{1,0:T(8,128)(2,1)} %collective-permute-done.3.g_ref, ...), custom_call_target="tpu_custom_call", output_to_operand_aliasing={{0}: (5, {}), {1}: (6, {}), {2}: (7, {})} | custom-call | tf_op jit(solution)/shard_map/expert_hidden/pallas_call | solution.py:208
  544.0 11.7 fusion.47
  555.6 12.9 add_convert_fusion.10
  570.0 11.5 fusion.43
  581.7 11.1 add_convert_fusion.9
  592.8 30.6 %expert_hidden.6 = (bf16[2560,2816]{1,0:T(8,128)(2,1)}, bf16[2560,2816]{1,0:T(8,128)(2,1)}, bf16[2560,2816]{1,0:T(8,128)(2,1)}) custom-call(bf16[640,2048]{1,0:T(8,128)(2,1)} %bitcast.17.x_ref, bf16[640,2048]{1,0:T(8,128)(2,1)} %bitcast.13.g_ref, ...), custom_call_target="tpu_custom_call", output_to_operand_aliasing={{0}: (5, {}), {1}: (6, {}), {2}: (7, {})} | custom-call | tf_op jit(solution)/shard_map/expert_hidden/pallas_call | solution.py:208
  635.0 48.9 %collective-permute-done.9.x_ref = bf16[640,2048]{1,0:T(8,128)(2,1)S(1)} collective-permute-done((bf16[640,2048]{1,0:T(8,128)(2,1)}, bf16[640,2048]{1,0:T(8,128)(2,1)S(1)}, u32[]{:S(2)}, u32[]{:S(2)}) %collective-permute-start.9) | collective-permute-done | bytes 2621472 | tf_op jit(solution)/shard_map/ppermute | solution.py:283
  685.3 30.8 %expert_hidden.7 = (bf16[2560,2816]{1,0:T(8,128)(2,1)}, bf16[2560,2816]{1,0:T(8,128)(2,1)}, bf16[2560,2816]{1,0:T(8,128)(2,1)}) custom-call(bf16[640,2048]{1,0:T(8,128)(2,1)} %copy-done.9, bf16[640,2048]{1,0:T(8,128)(2,1)} %collective-permute-done.6.g_ref, ...), custom_call_target="tpu_custom_call", output_to_operand_aliasing={{0}: (5, {}), {1}: (6, {}), {2}: (7, {})} | custom-call | tf_op jit(solution)/shard_map/expert_hidden/pallas_call | solution.py:208
  716.2 11.7 fusion.39
  727.9 12.7 add_convert_fusion.7
  740.6 10.9 fusion.35
  751.5 11.6 add_convert_fusion.6
  769.2 38.7 %convolution_convert_fusion.2 = bf16[2816,2048]{1,0:T(8,128)(2,1)} fusion(bf16[2560,2816]{1,0:T(8,128)(2,1)} %get-tuple-element.201, bf16[640,2048]{1,0:T(8,128)(2,1)} %collective-permute-done.6.g_ref, bf16[640,2048]{1,0:T(8,128)(2,1)} %bitcast.13.g_ref, bf16[640,2048]{1,0:T(8,128)(2,1)} %collective-permute-done.3.g_ref, bf16[640,2048]{1,0:T(8,128)(2,1)} %bitcast.11.g_ref), kind=kOutput, calls=%fused_computation.12 | convolution fusion | flops 29575610368 | bytes 36438016 | tf_op jit(solution)/shard_map/dot_general | solution.py:27
  809.6 11.9 collective-permute-done.11
  842.6 38.7 %convolution_convert_fusion.1 = bf16[2816,2048]{1,0:T(8,128)(2,1)} fusion(bf16[2560,2816]{1,0:T(8,128)(2,1)} %get-tuple-element.196, bf16[2560,2048]{1,0:T(8,128)(2,1)} %constant_dynamic-update-slice_fusion), kind=kOutput, calls=%fused_computation.11 | convolution fusion | flops 29533667328 | bytes 36438016 | tf_op jit(solution)/shard_map/dot_general | solution.py:27
  881.3 9.8 add_convert_fusion.2
  897.6 13.0 fusion.72
  910.6 12.8 fusion.69
  923.4 8.9 fusion.78
  932.3 9.3 fusion.75
  941.6 10.0 add_convert_fusion.1
  983.8 26.4 %attention_backward.1 = (bf16[1024,1024]{1,0:T(8,128)(2,1)}, bf16[1024,1024]{1,0:T(8,128)(2,1)}, bf16[1024,1024]{1,0:T(8,128)(2,1)}) custom-call(s32[4]{0:T(128)} %fusion.189.perm, bf16[1024,1024]{1,0:T(8,128)(2,1)} %get-tuple-element.185.q_ref, bf16[1024,1024]{1,0:T(8,128)(2,1)} %get-tuple-element.186.k_ref, bf16[1024,1024]{1,0:T(8,128)(2,1)} %get-tuple-element.187.v_ref, ...), custom_call_target="tpu_custom_call" | custom-call | tf_op jit(solution)/shard_map/attention_backward/pallas_call | solution.py:173
  1010.1 10.3 collective-permute-done.15
  1045.9 36.1 %convolution_convert_fusion = bf16[2816,2048]{1,0:T(8,128)(2,1)} fusion(bf16[2560,2816]{1,0:T(8,128)(2,1)S(1)} %bitcast.132, bf16[2560,2048]{1,0:T(8,128)(2,1)} %constant_dynamic-update-slice_fusion), kind=kOutput, calls=%fused_computation.10 | convolution fusion | flops 29533667328 | bytes 36438016 | tf_op jit(solution)/shard_map/dot_general | solution.py:27
  1122.0 7.9 add_add_fusion
  1134.3 13.8 collective-permute-done.16
  1150.9 41.9 %collective-permute-done.17 = bf16[512,2048]{1,0:T(8,128)(2,1)S(1)} collective-permute-done((bf16[512,2048]{1,0:T(8,128)(2,1)}, bf16[512,2048]{1,0:T(8,128)(2,1)S(1)}, u32[]{:S(2)}, u32[]{:S(2)}) %collective-permute-start.17) | collective-permute-done | bytes 2097184 | tf_op jit(solution)/shard_map/ppermute | solution.py:283
  1194.9 10.0 add_convert_fusion
  1208.5 8.4 add_convert_fusion.11
  1216.9 15.3 %collective-permute-done.32 = bf16[256,2048]{1,0:T(8,128)(2,1)S(1)} collective-permute-done((bf16[256,2048]{1,0:T(8,128)(2,1)S(1)}, bf16[256,2048]{1,0:T(8,128)(2,1)S(1)}, u32[]{:S(2)}, u32[]{:S(2)}) %collective-permute-start.32) | collective-permute-done | bytes 1048608 | tf_op jit(solution)/shard_map/ppermute | solution.py:283
  1254.3 13.5 collective-permute-done.28
  1275.4 8.4 fusion.20
  1284.6 46.6 %collective-permute-done.29 = bf16[512,1024]{1,0:T(8,128)(2,1)S(1)} collective-permute-done((bf16[512,1024]{1,0:T(8,128)(2,1)S(1)}, bf16[512,1024]{1,0:T(8,128)(2,1)S(1)}, u32[]{:S(2)}, u32[]{:S(2)}) %collective-permute-start.29) | collective-permute-done | bytes 1048608 | tf_op jit(solution)/shard_map/ppermute | solution.py:283
  1338.1 20.6 %collective-permute-done.30 = bf16[512,1024]{1,0:T(8,128)(2,1)S(1)} collective-permute-done((bf16[512,1024]{1,0:T(8,128)(2,1)S(1)}, bf16[512,1024]{1,0:T(8,128)(2,1)S(1)}, u32[]{:S(2)}, u32[]{:S(2)}) %collective-permute-start.30) | collective-permute-done | bytes 1048608 | tf_op jit(solution)/shard_map/ppermute | solution.py:283
  1370.2 17.1 %all-to-all-done.10 = bf16[4,128,1024]{2,1,0:T(8,128)(2,1)S(1)} async-done(((bf16[4,128,1024]{2,1,0:T(8,128)(2,1)}), bf16[4,128,1024]{2,1,0:T(8,128)(2,1)S(1)}, u32[]{:S(2)}, u32[]{:S(2)}) %all-to-all-start.10) | async-done | bytes 1048608 | tf_op jit(solution)/shard_map/all_to_all | solution.py:377
  1404.0 29.0 %collective-permute-done.26 = f32[2,2048]{1,0:T(2,128)S(1)} collective-permute-done((f32[2,2048]{1,0:T(2,128)S(1)}, f32[2,2048]{1,0:T(2,128)S(1)}, u32[]{:S(2)}, u32[]{:S(2)}) %collective-permute-start.26) | collective-permute-done | bytes 16416 | tf_op jit(solution)/shard_map/ppermute | solution.py:283
  (392 shorter events, 384.4 us)
Async XLA Ops:
  7.2 198.5 %all-gather.5.cloned.1.call-start = ((), (), s32[]{:S(2)}) async-start(), calls=%async_computation.15 | async-start | bytes 17825792 | tf_op jit(solution)/shard_map/all_gather | solution.py:313
  10.6 295.6 %all-gather.7.cloned.1.call-start = ((), (), s32[]{:S(2)}) async-start(), calls=%async_computation.16 | async-start | bytes 8650752 | tf_op jit(solution)/shard_map/all_gather | solution.py:387
  13.1 25.0 %collective-permute-start = (bf16[512,2048]{1,0:T(8,128)(2,1)}, bf16[512,2048]{1,0:T(8,128)(2,1)}, u32[]{:S(2)}, u32[]{:S(2)}) collective-permute-start(bf16[512,2048]{1,0:T(8,128)(2,1)} %fusion.15), channel_id=1, source_target_pairs={{0,16},{16,0},{1,17},{17,1},{2,18},{18,2},{3,19},{19,3},{4,20},{20... | collective-permute-start | bytes 6291464 | tf_op jit(solution)/shard_map/ppermute | solution.py:280
  215.7 69.0 %all-to-all-start = ((bf16[4,160,2048]{2,1,0:T(8,128)(2,1)}), bf16[4,160,2048]{2,1,0:T(8,128)(2,1)}, u32[]{:S(2)}, u32[]{:S(2)}) async-start(bf16[4,160,2048]{2,1,0:T(8,128)(2,1)} %bitcast.146), calls=%async_computation | async-start | bytes 5242880 | tf_op jit(solution)/shard_map/all_to_all | solution.py:377
  220.3 135.7 %all-gather.9.cloned.1.call-start = ((), (), s32[]{:S(2)}) async-start(), calls=%async_computation.17 | async-start | bytes 8650752 | tf_op jit(solution)/shard_map/all_gather | solution.py:387
  223.8 51.6 %collective-permute-start.1 = (bf16[1024,1024]{1,0:T(8,128)(2,1)}, bf16[1024,1024]{1,0:T(8,128)(2,1)}, u32[]{:S(2)}, u32[]{:S(2)}) collective-permute-start(bf16[1024,1024]{1,0:T(8,128)(2,1)} %constant_dynamic-slice_fusion.9), channel_id=1, source_target_pairs={{0,16},{16,0},{1,17},{17,1},{2,18},{18,2},{3,19},{19,3},{4,20},{20... | collective-permute-start | bytes 6291464 | tf_op jit(solution)/shard_map/ppermute | solution.py:280
  284.6 71.4 %all-to-all-start.1 = ((bf16[4,160,2048]{2,1,0:T(8,128)(2,1)}), bf16[4,160,2048]{2,1,0:T(8,128)(2,1)}, u32[]{:S(2)}, u32[]{:S(2)}) async-start(bf16[4,160,2048]{2,1,0:T(8,128)(2,1)} %bitcast.145), calls=%async_computation.1 | async-start | bytes 5242880 | tf_op jit(solution)/shard_map/all_to_all | solution.py:377
  289.6 148.7 %all-gather.11.cloned.1.call-start = ((), (), s32[]{:S(2)}) async-start(), calls=%async_computation.18 | async-start | bytes 8650752 | tf_op jit(solution)/shard_map/all_gather | solution.py:387
  289.9 66.1 %collective-permute-start.3 = (bf16[640,2048]{1,0:T(8,128)(2,1)}, bf16[640,2048]{1,0:T(8,128)(2,1)}, u32[]{:S(2)}, u32[]{:S(2)}) collective-permute-start(bf16[640,2048]{1,0:T(8,128)(2,1)} %bitcast.11.g_ref), channel_id=1, source_target_pairs={{0,2},{1,3},{2,0},{3,1},{4,6},{5,7},{6,4},{7,5},{8,10},{9,11},{10,... | collective-permute-start | bytes 7864328 | tf_op jit(solution)/shard_map/ppermute | solution.py:283
  356.0 9.8 collective-permute-start.5
  356.0 18.0 %collective-permute-start.4 = (bf16[1408,2048]{1,0:T(8,128)(2,1)}, bf16[1408,2048]{1,0:T(8,128)(2,1)}, u32[]{:S(2)}, u32[]{:S(2)}) collective-permute-start(bf16[1408,2048]{1,0:T(8,128)(2,1)} %all-gather.7.cloned.1.call-done), channel_id=1, source_target_pairs={{0,16},{16,0},{1,17},{17,1},{2,18},{18,2},{3,19},{19,3},{4,20},{20... | collective-permute-start | bytes 17301512 | tf_op jit(solution)/shard_map/ppermute | solution.py:280
  356.5 81.8 %collective-permute-start.6 = (bf16[640,2048]{1,0:T(8,128)(2,1)}, bf16[640,2048]{1,0:T(8,128)(2,1)}, u32[]{:S(2)}, u32[]{:S(2)}) collective-permute-start(bf16[640,2048]{1,0:T(8,128)(2,1)} %bitcast.13.g_ref), channel_id=1, source_target_pairs={{0,2},{1,3},{2,0},{3,1},{4,6},{5,7},{6,4},{7,5},{8,10},{9,11},{10,... | collective-permute-start | bytes 7864328 | tf_op jit(solution)/shard_map/ppermute | solution.py:283
  358.1 80.3 %all-to-all-start.2 = ((bf16[4,160,2048]{2,1,0:T(8,128)(2,1)}), bf16[4,160,2048]{2,1,0:T(8,128)(2,1)S(1)}, u32[]{:S(2)}, u32[]{:S(2)}) async-start(bf16[4,160,2048]{2,1,0:T(8,128)(2,1)} %bitcast.148), calls=%async_computation.2 | async-start | bytes 5242880 | tf_op jit(solution)/shard_map/all_to_all | solution.py:377
  438.4 9.8 collective-permute-start.7
  438.6 74.8 %all-to-all-start.3 = ((bf16[4,160,2048]{2,1,0:T(8,128)(2,1)}), bf16[4,160,2048]{2,1,0:T(8,128)(2,1)}, u32[]{:S(2)}, u32[]{:S(2)}) async-start(bf16[4,160,2048]{2,1,0:T(8,128)(2,1)} %bitcast.147), calls=%async_computation.3 | async-start | bytes 5242880 | tf_op jit(solution)/shard_map/all_to_all | solution.py:377
  443.6 69.7 %collective-permute-start.8 = (bf16[640,2048]{1,0:T(8,128)(2,1)S(1)}, bf16[640,2048]{1,0:T(8,128)(2,1)}, u32[]{:S(2)}, u32[]{:S(2)}) collective-permute-start(bf16[640,2048]{1,0:T(8,128)(2,1)S(1)} %bitcast.133), channel_id=1, source_target_pairs={{0,2},{1,3},{2,0},{3,1},{4,6},{5,7},{6,4},{7,5},{8,10},{9,11},{10,... | collective-permute-start | bytes 7864328 | tf_op jit(solution)/shard_map/ppermute | solution.py:283
  568.5 62.2 %collective-permute-start.10 = (bf16[640,2048]{1,0:T(8,128)(2,1)}, bf16[640,2048]{1,0:T(8,128)(2,1)}, u32[]{:S(2)}, u32[]{:S(2)}) collective-permute-start(bf16[640,2048]{1,0:T(8,128)(2,1)} %add_convert_fusion.10), channel_id=1, source_target_pairs={{0,2},{1,3},{2,0},{3,1},{4,6},{5,7},{6,4},{7,5},{8,10},{9,11},{10,... | collective-permute-start | bytes 7864328 | tf_op jit(solution)/shard_map/ppermute | solution.py:283
  581.5 102.4 %collective-permute-start.9 = (bf16[640,2048]{1,0:T(8,128)(2,1)}, bf16[640,2048]{1,0:T(8,128)(2,1)S(1)}, u32[]{:S(2)}, u32[]{:S(2)}) collective-permute-start(bf16[640,2048]{1,0:T(8,128)(2,1)} %bitcast.17.x_ref), channel_id=1, source_target_pairs={{0,2},{1,3},{2,0},{3,1},{4,6},{5,7},{6,4},{7,5},{8,10},{9,11},{10,... | collective-permute-start | bytes 7864328 | tf_op jit(solution)/shard_map/ppermute | solution.py:283
  763.1 58.4 %collective-permute-start.11 = (bf16[640,2048]{1,0:T(8,128)(2,1)}, bf16[640,2048]{1,0:T(8,128)(2,1)}, u32[]{:S(2)}, u32[]{:S(2)}) collective-permute-start(bf16[640,2048]{1,0:T(8,128)(2,1)} %add_convert_fusion.7), channel_id=1, source_target_pairs={{0,2},{1,3},{2,0},{3,1},{4,6},{5,7},{6,4},{7,5},{8,10},{9,11},{10,... | collective-permute-start | bytes 7864328 | tf_op jit(solution)/shard_map/ppermute | solution.py:283
  764.6 63.2 %all-to-all-start.4 = ((bf16[4,160,2048]{2,1,0:T(8,128)(2,1)}), bf16[4,160,2048]{2,1,0:T(8,128)(2,1)S(1)}, u32[]{:S(2)}, u32[]{:S(2)}) async-start(bf16[4,160,2048]{2,1,0:T(8,128)(2,1)} %bitcast.138), calls=%async_computation.4 | async-start | bytes 5242880 | tf_op jit(solution)/shard_map/all_to_all | solution.py:377
  833.7 47.6 %collective-permute-start.12 = (bf16[2816,1024]{1,0:T(8,128)(2,1)}, bf16[2816,1024]{1,0:T(8,128)(2,1)}, u32[]{:S(2)}, u32[]{:S(2)}) collective-permute-start(bf16[2816,1024]{1,0:T(8,128)(2,1)} %constant_dynamic-slice_fusion.8), channel_id=1, source_target_pairs={{0,16},{16,0},{1,17},{17,1},{2,18},{18,2},{3,19},{19,3},{4,20},{20... | collective-permute-start | bytes 17301512 | tf_op jit(solution)/shard_map/ppermute | solution.py:280
  838.0 113.6 %all-to-all-start.5 = ((bf16[4,160,2048]{2,1,0:T(8,128)(2,1)}), bf16[4,160,2048]{2,1,0:T(8,128)(2,1)}, u32[]{:S(2)}, u32[]{:S(2)}) async-start(bf16[4,160,2048]{2,1,0:T(8,128)(2,1)} %bitcast.137), calls=%async_computation.5 | async-start | bytes 5242880 | tf_op jit(solution)/shard_map/all_to_all | solution.py:377
  842.6 595.4 %reduce-scatter.8.cloned.1.call-start = ((), (), s32[]{:S(2)}) async-start(), calls=%async_computation.21 | async-start | bytes 8650752 | tf_op jit(solution)/shard_map/reduce_scatter | solution.py:500
  896.9 44.7 %collective-permute-start.13 = (bf16[2816,1024]{1,0:T(8,128)(2,1)}, bf16[2816,1024]{1,0:T(8,128)(2,1)}, u32[]{:S(2)}, u32[]{:S(2)}) collective-permute-start(bf16[2816,1024]{1,0:T(8,128)(2,1)} %constant_dynamic-slice_fusion.7), channel_id=1, source_target_pairs={{0,16},{16,0},{1,17},{17,1},{2,18},{18,2},{3,19},{19,3},{4,20},{20... | collective-permute-start | bytes 17301512 | tf_op jit(solution)/shard_map/ppermute | solution.py:280
  897.5 557.1 %reduce-scatter.4.cloned.1.call-start = ((), (), s32[]{:S(2)}) async-start(), calls=%async_computation.19 | async-start | bytes 8650752 | tf_op jit(solution)/shard_map/reduce_scatter | solution.py:500
  961.0 59.4 %collective-permute-start.15 = (bf16[640,2048]{1,0:T(8,128)(2,1)}, bf16[640,2048]{1,0:T(8,128)(2,1)}, u32[]{:S(2)}, u32[]{:S(2)}) collective-permute-start(bf16[640,2048]{1,0:T(8,128)(2,1)} %fusion.69), channel_id=1, source_target_pairs={{0,2},{1,3},{2,0},{3,1},{4,6},{5,7},{6,4},{7,5},{8,10},{9,11},{10,... | collective-permute-start | bytes 7864328 | tf_op jit(solution)/shard_map/ppermute | solution.py:283
  1088.0 106.9 %collective-permute-start.18 = (bf16[2816,1024]{1,0:T(8,128)(2,1)}, bf16[2816,1024]{1,0:T(8,128)(2,1)}, u32[]{:S(2)}, u32[]{:S(2)}) collective-permute-start(bf16[2816,1024]{1,0:T(8,128)(2,1)} %constant_dynamic-slice_fusion.4), channel_id=1, source_target_pairs={{0,16},{16,0},{1,17},{17,1},{2,18},{18,2},{3,19},{19,3},{4,20},{20... | collective-permute-start | bytes 17301512 | tf_op jit(solution)/shard_map/ppermute | solution.py:280
  1088.0 116.9 %collective-permute-start.19 = (bf16[640,2048]{1,0:T(8,128)(2,1)}, bf16[640,2048]{1,0:T(8,128)(2,1)}, u32[]{:S(2)}, u32[]{:S(2)}) collective-permute-start(bf16[640,2048]{1,0:T(8,128)(2,1)} %fusion.72), channel_id=1, source_target_pairs={{0,2},{1,3},{2,0},{3,1},{4,6},{5,7},{6,4},{7,5},{8,10},{9,11},{10,... | collective-permute-start | bytes 7864328 | tf_op jit(solution)/shard_map/ppermute | solution.py:283
  1092.8 112.2 %all-to-all-start.6 = ((bf16[4,160,2048]{2,1,0:T(8,128)(2,1)}), bf16[4,160,2048]{2,1,0:T(8,128)(2,1)S(1)}, u32[]{:S(2)}, u32[]{:S(2)}) async-start(bf16[4,160,2048]{2,1,0:T(8,128)(2,1)} %bitcast.136), calls=%async_computation.6 | async-start | bytes 5242880 | tf_op jit(solution)/shard_map/all_to_all | solution.py:377
  1097.6 95.2 %collective-permute-start.17 = (bf16[512,2048]{1,0:T(8,128)(2,1)}, bf16[512,2048]{1,0:T(8,128)(2,1)S(1)}, u32[]{:S(2)}, u32[]{:S(2)}) collective-permute-start(bf16[512,2048]{1,0:T(8,128)(2,1)} %bitcast.149), channel_id=1, source_target_pairs={{0,2},{1,3},{2,0},{3,1},{4,6},{5,7},{6,4},{7,5},{8,10},{9,11},{10,... | collective-permute-start | bytes 6291464 | tf_op jit(solution)/shard_map/ppermute | solution.py:283
  1099.4 48.8 %collective-permute-start.16 = (bf16[1024,1024]{1,0:T(8,128)(2,1)}, bf16[1024,1024]{1,0:T(8,128)(2,1)S(1)}, u32[]{:S(2)}, u32[]{:S(2)}) collective-permute-start(bf16[1024,1024]{1,0:T(8,128)(2,1)} %convolution_convert_fusion.11), channel_id=1, source_target_pairs={{0,1},{1,0},{2,3},{3,2},{4,5},{5,4},{6,7},{7,6},{8,9},{9,8},{10,11... | collective-permute-start | bytes 6291464 | tf_op jit(solution)/shard_map/ppermute | solution.py:283
  1120.5 117.9 %collective-permute-start.21 = (bf16[1024,1024]{1,0:T(8,128)(2,1)}, bf16[1024,1024]{1,0:T(8,128)(2,1)}, u32[]{:S(2)}, u32[]{:S(2)}) collective-permute-start(bf16[1024,1024]{1,0:T(8,128)(2,1)} %convolution_convert_fusion.9), channel_id=1, source_target_pairs={{0,1},{1,0},{2,3},{3,2},{4,5},{5,4},{6,7},{7,6},{8,9},{9,8},{10,11... | collective-permute-start | bytes 6291464 | tf_op jit(solution)/shard_map/ppermute | solution.py:283
  1148.1 96.5 %collective-permute-start.20 = (bf16[1024,1024]{1,0:T(8,128)(2,1)}, bf16[1024,1024]{1,0:T(8,128)(2,1)}, u32[]{:S(2)}, u32[]{:S(2)}) collective-permute-start(bf16[1024,1024]{1,0:T(8,128)(2,1)} %fusion.107), channel_id=1, source_target_pairs={{0,2},{1,3},{2,0},{3,1},{4,6},{5,7},{6,4},{7,5},{8,10},{9,11},{10,... | collective-permute-start | bytes 6291464 | tf_op jit(solution)/shard_map/ppermute | solution.py:283
  1207.7 24.5 %collective-permute-start.32 = (bf16[256,2048]{1,0:T(8,128)(2,1)S(1)}, bf16[256,2048]{1,0:T(8,128)(2,1)S(1)}, u32[]{:S(2)}, u32[]{:S(2)}) collective-permute-start(bf16[256,2048]{1,0:T(8,128)(2,1)S(1)} %bitcast.154), channel_id=1, source_target_pairs={{0,1},{1,0},{2,3},{3,2},{4,5},{5,4},{6,7},{7,6},{8,9},{9,8},{10,11... | collective-permute-start | bytes 3145736 | tf_op jit(solution)/shard_map/ppermute | solution.py:283
  1216.9 31.6 %collective-permute-start.22 = (bf16[512,2048]{1,0:T(8,128)(2,1)}, bf16[512,2048]{1,0:T(8,128)(2,1)}, u32[]{:S(2)}, u32[]{:S(2)}) collective-permute-start(bf16[512,2048]{1,0:T(8,128)(2,1)} %add_convert_fusion.11), channel_id=1, source_target_pairs={{0,16},{16,0},{1,17},{17,1},{2,18},{18,2},{3,19},{19,3},{4,20},{20... | collective-permute-start | bytes 6291464 | tf_op jit(solution)/shard_map/ppermute | solution.py:280
  1233.6 37.0 %all-to-all-start.11 = ((bf16[4,64,2048]{2,1,0:T(8,128)(2,1)}), bf16[4,64,2048]{2,1,0:T(8,128)(2,1)S(1)}, u32[]{:S(2)}, u32[]{:S(2)}) async-start(bf16[4,64,2048]{2,1,0:T(8,128)(2,1)} %bitcast.46), calls=%async_computation.11 | async-start | bytes 2097152 | tf_op jit(solution)/shard_map/all_to_all | solution.py:377
  1238.5 231.6 %reduce-scatter.6.cloned.1.call-start = ((), (), s32[]{:S(2)}) async-start(), calls=%async_computation.20 | async-start | bytes 8650752 | tf_op jit(solution)/shard_map/reduce_scatter | solution.py:500
  1244.3 23.6 %collective-permute-start.28 = (bf16[512,1024]{1,0:T(8,128)(2,1)}, bf16[512,1024]{1,0:T(8,128)(2,1)}, u32[]{:S(2)}, u32[]{:S(2)}) collective-permute-start(bf16[512,1024]{1,0:T(8,128)(2,1)} %slice.241), channel_id=1, source_target_pairs={{0,2},{1,3},{2,0},{3,1},{4,6},{5,7},{6,4},{7,5},{8,10},{9,11},{10,... | collective-permute-start | bytes 3145736 | tf_op jit(solution)/shard_map/ppermute | solution.py:283
  1270.6 62.0 %all-to-all-start.8 = ((bf16[4,128,1024]{2,1,0:T(8,128)(2,1)}), bf16[4,128,1024]{2,1,0:T(8,128)(2,1)}, u32[]{:S(2)}, u32[]{:S(2)}) async-start(bf16[4,128,1024]{2,1,0:T(8,128)(2,1)} %bitcast.32), calls=%async_computation.8 | async-start | bytes 2097152 | tf_op jit(solution)/shard_map/all_to_all | solution.py:377
  1283.9 47.3 %collective-permute-start.29 = (bf16[512,1024]{1,0:T(8,128)(2,1)S(1)}, bf16[512,1024]{1,0:T(8,128)(2,1)S(1)}, u32[]{:S(2)}, u32[]{:S(2)}) collective-permute-start(bf16[512,1024]{1,0:T(8,128)(2,1)S(1)} %slice.243), channel_id=1, source_target_pairs={{0,1},{1,0},{2,3},{3,2},{4,5},{5,4},{6,7},{7,6},{8,9},{9,8},{10,11... | collective-permute-start | bytes 3145736 | tf_op jit(solution)/shard_map/ppermute | solution.py:283
  1332.6 27.6 %all-to-all-start.9 = ((bf16[4,128,1024]{2,1,0:T(8,128)(2,1)}), bf16[4,128,1024]{2,1,0:T(8,128)(2,1)}, u32[]{:S(2)}, u32[]{:S(2)}) async-start(bf16[4,128,1024]{2,1,0:T(8,128)(2,1)} %bitcast.34), calls=%async_computation.9 | async-start | bytes 2097152 | tf_op jit(solution)/shard_map/all_to_all | solution.py:377
  1337.6 21.2 %collective-permute-start.30 = (bf16[512,1024]{1,0:T(8,128)(2,1)S(1)}, bf16[512,1024]{1,0:T(8,128)(2,1)S(1)}, u32[]{:S(2)}, u32[]{:S(2)}) collective-permute-start(bf16[512,1024]{1,0:T(8,128)(2,1)S(1)} %slice.245), channel_id=1, source_target_pairs={{0,2},{1,3},{2,0},{3,1},{4,6},{5,7},{6,4},{7,5},{8,10},{9,11},{10,... | collective-permute-start | bytes 3145736 | tf_op jit(solution)/shard_map/ppermute | solution.py:283
  1360.2 27.1 %all-to-all-start.10 = ((bf16[4,128,1024]{2,1,0:T(8,128)(2,1)}), bf16[4,128,1024]{2,1,0:T(8,128)(2,1)S(1)}, u32[]{:S(2)}, u32[]{:S(2)}) async-start(bf16[4,128,1024]{2,1,0:T(8,128)(2,1)} %bitcast.36), calls=%async_computation.10 | async-start | bytes 2097152 | tf_op jit(solution)/shard_map/all_to_all | solution.py:377
  1387.3 72.4 %all-to-all-start.7 = ((bf16[4,160,2048]{2,1,0:T(8,128)(2,1)}), bf16[4,160,2048]{2,1,0:T(8,128)(2,1)}, u32[]{:S(2)}, u32[]{:S(2)}) async-start(bf16[4,160,2048]{2,1,0:T(8,128)(2,1)} %bitcast.25), calls=%async_computation.7 | async-start | bytes 5242880 | tf_op jit(solution)/shard_map/all_to_all | solution.py:377
  1393.2 5.0 collective-permute-start.24
  1398.1 53.9 %collective-permute-start.31 = (f32[3,64,1024]{2,1,0:T(8,128)}, f32[3,64,1024]{2,1,0:T(8,128)}, u32[]{:S(2)}, u32[]{:S(2)}) collective-permute-start(f32[3,64,1024]{2,1,0:T(8,128)} %dynamic-slice_bitcast_fusion), channel_id=1, source_target_pairs={{0,16},{16,0},{1,17},{17,1},{2,18},{18,2},{3,19},{19,3},{4,20},{20... | collective-permute-start | bytes 2359304 | tf_op jit(solution)/shard_map/ppermute | solution.py:280
  1402.0 31.1 %collective-permute-start.26 = (f32[2,2048]{1,0:T(2,128)S(1)}, f32[2,2048]{1,0:T(2,128)S(1)}, u32[]{:S(2)}, u32[]{:S(2)}) collective-permute-start(f32[2,2048]{1,0:T(2,128)S(1)} %add.583), channel_id=1, source_target_pairs={{0,4},{1,5},{2,6},{3,7},{4,0},{5,1},{6,2},{7,3},{8,12},{9,13},{10,... | collective-permute-start | bytes 49160 | tf_op jit(solution)/shard_map/ppermute | solution.py:283
  1433.1 17.4 %collective-permute-start.27 = (f32[2,2048]{1,0:T(2,128)S(1)}, f32[2,2048]{1,0:T(2,128)S(1)}, u32[]{:S(2)}, u32[]{:S(2)}) collective-permute-start(f32[2,2048]{1,0:T(2,128)S(1)} %add.584), channel_id=1, source_target_pairs={{0,8},{1,9},{2,10},{3,11},{4,12},{5,13},{6,14},{7,15},{8,0},{9,1},... | collective-permute-start | bytes 49160 | tf_op jit(solution)/shard_map/ppermute | solution.py:283
  (90 other events, 1637.4 us)
Sparse Core Ops, SparseCore 0:
  11.4 194.3 all-gather.4
  207.3 72.6 all-gather.6
  281.5 74.4 all-gather.8
  357.4 74.4 all-gather.10
  897.6 70.5 reduce-scatter.7
  971.0 71.3 reduce-scatter.3
  1248.6 94.5 reduce-scatter.5

commit v3 on v2

--- a/solution.py
+++ b/solution.py
@@ -109,8 +109,7 @@
     do_ref,
     cos_ref,
     sin_ref,
-    out_q,
-    out_k,
+    out_qk,
     out_v,
     dk_ref,
     dv_ref,
@@ -138,18 +137,18 @@
         back = dot(grad_scores, keys, 1, 0) * scale
         cos, sin = cos_ref[rows, :], sin_ref[rows, :]
         back = back * cos - pltpu.roll(back, HD // 2, 1) * sin
-        store_tile(out_q, perm, t, block, slice(None), back.astype(bf16))
+        store_tile(out_qk, perm, t, block, slice(0, HD), back.astype(bf16))
     for t in range(tiles):
         rows = slice(t * TILE, (t + 1) * TILE)
         cos, sin = cos_ref[rows, :], sin_ref[rows, :]
         back = dk_ref[rows, :] * scale
         back = back * cos - pltpu.roll(back, HD // 2, 1) * sin
-        store_tile(out_k, perm, t, block, slice(None), back.astype(bf16))
+        store_tile(out_qk, perm, t, block, slice(HD, 2 * HD), back.astype(bf16))
         store_tile(out_v, perm, t, block, slice(None), dv_ref[rows, :].astype(bf16))
 
 
 def attention_forward(perm, block, pre, cos, sin):
-    rows, heads = pre[0].shape[0], pre[0].shape[1] // HD
+    rows, heads = pre.shape[0], pre.shape[1] // (3 * HD)
     per_head = pl.BlockSpec((rows, HD), lambda h, p: (0, h))
     table = pl.BlockSpec((rows, HD), lambda h, p: (0, 0))
     head_array = jax.ShapeDtypeStruct((rows, heads * HD), bf16)
@@ -158,12 +157,18 @@
         grid_spec=pltpu.PrefetchScalarGridSpec(
             num_scalar_prefetch=1,
             grid=(heads,),
-            in_specs=[per_head] * 3 + [table, table],
+            in_specs=[
+                pl.BlockSpec((rows, HD), lambda h, p: (0, 2 * h)),
+                pl.BlockSpec((rows, HD), lambda h, p: (0, 2 * h + 1)),
+                pl.BlockSpec((rows, HD), lambda h, p: (0, 2 * heads + h)),
+                table,
+                table,
+            ],
             out_specs=[per_head] * 5,
         ),
         out_shape=[head_array] * 4 + [jax.ShapeDtypeStruct((rows, heads * HD), f32)],
         name="attention_forward",
-    )(perm, *pre, cos, sin)
+    )(perm, pre, pre, pre, cos, sin)
 
 
 def attention_backward(perm, block, q, k, v, log_total, grad, cos, sin):
@@ -176,10 +181,13 @@
             num_scalar_prefetch=1,
             grid=(heads,),
             in_specs=[per_head] * 5 + [table, table],
-            out_specs=[per_head] * 3,
+            out_specs=[pl.BlockSpec((rows, 2 * HD), lambda h, p: (0, h)), per_head],
             scratch_shapes=[pltpu.VMEM((rows, HD), f32), pltpu.VMEM((rows, HD), f32)],
         ),
-        out_shape=[jax.ShapeDtypeStruct((rows, heads * HD), bf16)] * 3,
+        out_shape=[
+            jax.ShapeDtypeStruct((rows, 2 * heads * HD), bf16),
+            jax.ShapeDtypeStruct((rows, heads * HD), bf16),
+        ],
         name="attention_backward",
     )(perm, q, k, v, log_total, grad, cos, sin)
 
@@ -214,6 +222,63 @@
         input_output_aliases={5 + i: i for i in range(len(kept))},
         name="expert_hidden",
     )(slots, grads, *weights, *kept)
+
+
+def rows_kernel(count, *refs):
+    total = dot(refs[0][...], refs[count][...], 1, 0)
+    for i in range(1, count):
+        total = total + dot(refs[i][...], refs[count + i][...], 1, 0)
+    refs[-1][...] = total.astype(bf16)
+
+
+def expert_rows(part, rows, left, right):
+    units, tile = right[0].shape[0], 256
+    return pl.pallas_call(
+        functools.partial(rows_kernel, len(left)),
+        grid=(D // tile,),
+        in_specs=[pl.BlockSpec((rows, units), lambda n: (part, 0))] * len(left)
+        + [pl.BlockSpec((units, tile), lambda n: (0, n))] * len(right),
+        out_specs=pl.BlockSpec((rows, tile), lambda n: (0, n)),
+        out_shape=jax.ShapeDtypeStruct((rows, D), bf16),
+        name="expert_rows",
+    )(*left, *right)
+
+
+def join_kernel(where, own_ref, *refs):
+    parts, out_ref, sems = refs[:-2], refs[-2], refs[-1]
+    side, core = where[0], where[1]
+    size, count = own_ref.shape[0], parts[0].shape[0]
+    copies = [
+        pltpu.make_async_copy(
+            own_ref, out_ref.at[pl.ds(pl.multiple_of(side * size, 8), size)], sems.at[0]
+        )
+    ]
+    for s, part in enumerate(parts):
+        source = lax.rem(core - s + len(parts), len(parts))
+        start = pl.multiple_of((1 - side) * size + source * count, 8)
+        copies.append(
+            pltpu.make_async_copy(part, out_ref.at[pl.ds(start, count)], sems.at[1 + s])
+        )
+    for copy in copies:
+        copy.start()
+    for copy in copies:
+        copy.wait()
+
+
+def join_weights(where, own, parts):
+    anywhere = pl.BlockSpec(memory_space=pl.ANY)
+    return pl.pallas_call(
+        join_kernel,
+        grid_spec=pltpu.PrefetchScalarGridSpec(
+            num_scalar_prefetch=1,
+            grid=(1,),
+            in_specs=[anywhere] * (1 + len(parts)),
+            out_specs=anywhere,
+            scratch_shapes=[pltpu.SemaphoreType.DMA((1 + len(parts),))],
+        ),
+        out_shape=jax.ShapeDtypeStruct((2 * own.shape[0], own.shape[1]), own.dtype),
+        name="join_weights",
+    )(where, own, *parts)
 
 
 def rope_tables(group_len):
@@ -309,7 +374,11 @@
     def own_columns(w):
         return lax.dynamic_slice_in_dim(w, core * width, width, axis=1)
 
-    packed = jnp.concatenate([own_columns(w) for w in (w_query, w_key, w_value, w_out)], axis=1)
+    by_head = [own_columns(w).reshape(-1, heads, HD) for w in (w_query, w_key)]
+    packed = jnp.concatenate(
+        [jnp.stack(by_head, axis=2).reshape(-1, 2 * width), own_columns(w_value), own_columns(w_out)],
+        axis=1,
+    )
     gathered = lax.all_gather(packed, "fsdp", axis=0, tiled=True)
 
     halves = 2
@@ -342,33 +411,32 @@
     mine = lax.axis_index("fsdp")
     my_column, my_side = (mine % repeats) // pair, mine % pair
 
-    def feature_order(side_first):
+    def feature_order(relative):
         index = jnp.arange(D, dtype=jnp.int32)
         rest, j = index // per, index % per
         rest, c = rest // ctx_count, rest % ctx_count
-        rest, e = rest // EXPERTS, rest % EXPERTS
-        if side_first:
+        if relative:
+            rest, e = rest // EXPERTS, rest % EXPERTS
             w, t = rest // columns, rest % columns
-        else:
-            t, w = rest // pair, rest % pair
-        t, w = (my_column + t) % columns, (my_side + w) % pair
-        source = c * (D // ctx_count) + (e * repeats + t * pair + w) * per + j
+            t, w = (my_column + t) % columns, (my_side + w) % pair
+            rest = e * repeats + t * pair + w
+        source = c * (D // ctx_count) + rest * per + j
         shuffle = (jnp.arange(D, dtype=jnp.int32)[:, None] == source[None, :]).astype(bf16)
         return dot(normed, shuffle, 1, 0, bf16)
 
-    normed_side, normed_column = feature_order(True), feature_order(False)
+    normed_side, normed_mixed = feature_order(True), feature_order(False)
 
     def weight_part(w):
         count = w.shape[0] // ctx_count
         return lax.dynamic_slice_in_dim(w, core * count, count, axis=0)
 
     weight_parts = [weight_part(w) for w in (w_gate, w_up, w_down)]
-    gathered, *tied = after(gathered, normed_side, normed_column, *grad_blocks, *weight_parts)
-    normed_side, normed_column = tied[:2]
+    gathered, *tied = after(gathered, normed_side, normed_mixed, *grad_blocks, *weight_parts)
+    normed_side, normed_mixed = tied[:2]
     grad_blocks, weight_parts = tied[2 : 2 + halves], tied[2 + halves :]
-    full_q, full_k, full_v, out_columns = (
-        gathered[:, i * width : (i + 1) * width] for i in range(4)
-    )
+    full_qk, full_v = gathered[:, : 2 * width], gathered[:, 2 * width : 3 * width]
+    out_columns = gathered[:, 3 * width :]
+    full_qkv = gathered[:, : 3 * width]
 
     lines = [[r + e * repeats for e in range(EXPERTS)] for r in range(repeats)]
 
@@ -388,19 +456,16 @@
         for part in weight_parts
     ]
 
-    def pair_weights(part):
-        if ctx_count == 2:
-            again = core_shift(part, 1)
-            count = part.shape[0] // pair
-            rows_of = []
-            for i in range(pair):
-                a, b = part[i * count : (i + 1) * count], again[i * count : (i + 1) * count]
-                rows_of += [jnp.where(core == 0, a, b), jnp.where(core == 0, b, a)]
-            return jnp.concatenate(rows_of, axis=0)
-        every = lax.all_gather(part, "ctx", axis=0, tiled=False)
-        return every.reshape(ctx_count, pair, -1, D).transpose(1, 0, 2, 3).reshape(-1, D)
-
-    pre = [dot(normed, w, 1, 0) for w in (full_q, full_k, full_v)]
+    where = jnp.stack([my_side, core]).astype(jnp.int32)
+
+    def pair_weights(own, both):
+        count = both.shape[0] // pair
+        part = lax.dynamic_slice_in_dim(both, (1 - my_side) * count, count, axis=0)
+        return join_weights(
+            where, own, [part] + [core_shift(part, s) for s in range(1, ctx_count)]
+        )
+
+    pre = dot(normed, full_qkv, 1, 0)
     context, q, k, v, log_total = attention_forward(perm, block, pre, cos, sin)
 
     def out_rows(c):
@@ -434,24 +499,20 @@
     grad_parts[1:] = got[5:]
     grad_parts += to_columns(grads_second)
     first = swap_experts(slots_a).reshape(half, D)
-    wg, wu = (pair_weights(w) for w in swapped_two)
+    wg, wu = (pair_weights(*w) for w in zip((w_gate, w_up), swapped_two))
     got = after(first, slots_b, swapped[2], wg, wu, *grad_parts[columns + 1 :])
     first, slots_b, swapped_down, wg, wu = got[:5]
     grad_parts[columns + 1 :] = got[5:]
     second = swap_experts(slots_b).reshape(half, D)
-    wd = pair_weights(swapped_down)
+    wd = pair_weights(w_down, swapped_down)
     weights = (wg, wu, wd)
     parts = halves * columns
 
     def hidden_part(index, slots, state):
         return expert_hidden(index, parts, slots, grad_parts[index], weights, state)
 
-    def part_rows(index):
-        return slice(index * half, (index + 1) * half)
-
     def grad_rows(index, state):
-        part = part_rows(index)
-        return (dot(state[1][part], wg, 1, 0) + dot(state[2][part], wu, 1, 0)).astype(bf16)
+        return expert_rows(index, half, state[1:], (wg, wu))
 
     def columns_home(pieces):
         return [column_shift(part, -(j + 1)) for j, part in enumerate(pieces)]
@@ -481,7 +542,11 @@
         for j in [*range(1, columns), 0]:
             index = h * columns + j
             back[index] = grad_rows(index, state)
-            back[index], *state = after(back[index], *state)
+            tied = after(back[index], *state, *slot_parts[(1 + h) * columns + 1 :])
+            back[index], state = tied[0], tied[1:4]
+            slot_parts[(1 + h) * columns + 1 :] = tied[4:]
+            if h == 1 and j == columns - 1:
+                home_first, *state = after(home_first, *state)
         came.append(columns_home([back[h * columns + j] for j in range(1, columns)]))
     hidden, grad_gate, grad_up = state
     all_slots = jnp.concatenate(slot_parts, axis=0)
@@ -501,25 +566,32 @@
             total, "fsdp", scatter_dimension=0, tiled=True, axis_index_groups=sides
         ).astype(f32)
 
+    def out_rows_of(h, j, left):
+        return expert_rows(h * columns + j, half, (left,), (wd,))
+
     hidden_t = after(hidden, *(back[i] for i in range(parts)))[0]
     down_part = dot(hidden_t, all_grads, 0, 0, bf16)
-    down_part, gate_t, home_first, *came[1] = after(down_part, grad_gate, home_first, *came[1])
-    home_second = swap_experts(add_parts(back[columns], came[1]))
+    down_part, hidden_t, gate_t, *got = after(down_part, hidden_t, grad_gate, *came[1])
+    home_second = swap_experts(add_parts(back[columns], got))
     gate_part = dot(gate_t, all_slots, 0, 0, bf16)
     down_total = core_sum(down_part)
-    gate_part, down_total, hidden_t = after(gate_part, down_total, hidden)
+    gate_part, hidden_t = after(gate_part, hidden_t)
+    away_first = [out_rows_of(0, j, hidden_t) for j in range(1, columns)]
+    own_first = out_rows_of(0, 0, hidden_t)
+    home_second, down_total, hidden_t, own_first, *away_first = after(
+        home_second, down_total, hidden_t, own_first, *away_first
+    )
     down_grad = side_sum(down_total)
+    away_first = columns_home(away_first)
+
+    def side_swap_sum(total):
+        def side_rows(i):
+            size = total.shape[0] // pair
+            return lax.dynamic_slice_in_dim(total, (i % pair) * size, size, axis=0)
+
+        return side_rows(my_side), pair_swap(side_rows(my_side + 1))
 
     gate_total = core_sum(gate_part)
-    outs, away_out = [None] * parts, []
-    for j in [*range(1, columns), 0]:
-        for h in range(halves):
-            outs[h * columns + j] = dot(hidden_t[part_rows(h * columns + j)], wd, 1, 0, bf16)
-        if j:
-            *tied, hidden_t = after(*(o for o in outs if o is not None), hidden_t)
-    away_out = [columns_home(outs[h * columns + 1 : (h + 1) * columns]) for h in range(halves)]
-    gate_total, home_second, *outs = after(gate_total, home_second, *outs)
-    gate_grad = side_sum(gate_total)
     grad_slot_in = jnp.concatenate([home_first, home_second], axis=0).reshape(halves * half, D)
 
     grad_normed_two = dot(select[0] + select[1], grad_slot_in, 1, 0)
@@ -556,55 +628,78 @@
 
     out_part = dot(context, grad_attention, 0, 0, bf16)
     blocks_o = row_blocks(out_part, columns, my_column)
-    grad_attention, *blocks_o = after(grad_attention, *blocks_o)
-    sum_o = reduce_blocks(blocks_o, column_shift)
+    got = after(grad_attention, gate_total, *blocks_o)
+    grad_attention, gate_total, blocks_o = got[0], got[1], got[2:]
+    gate_own, gate_came = side_swap_sum(gate_total)
+    came_o = [column_shift(block, d) for d, block in enumerate(blocks_o) if d]
     grad_context = dot(grad_attention, w_o, 1, 1, bf16)
-    grad_q, grad_k, grad_v = attention_backward(
+    grad_qk, grad_v = attention_backward(
         perm, block, q, k, v, log_total, grad_context, cos, sin
     )
-    grad_q, grad_k, grad_v, *away_out[0] = after(grad_q, grad_k, grad_v, *away_out[0])
-    outs_first = swap_experts(add_parts(outs[0], away_out[0]))
-    blocks_q = first_blocks(normed_side, grad_q, pair)
-    blocks_k = first_blocks(normed_column, grad_k, columns)
+    qk_part = dot(normed_mixed, grad_qk, 0, 0, bf16)
+    qk_sum = lax.psum_scatter(qk_part, "fsdp", scatter_dimension=0, tiled=True)
+    got = after(qk_part, grad_qk, grad_v, hidden_t, grad_up, down_grad, *away_first)
+    grad_qk, grad_v, hidden_t, up_t, down_grad, *away_first = got[1:]
+    outs_first = swap_experts(add_parts(own_first, away_first))
     blocks_v = first_blocks(normed_side, grad_v, pair)
-    up_t, *tied = after(grad_up, grad_q, grad_k, grad_v, *blocks_q, *blocks_k, *blocks_v)
-    grad_q, grad_k, grad_v = tied[:3]
-    tied = tied[3:]
-    blocks_q, blocks_k, blocks_v = tied[:pair], tied[pair : pair + columns], tied[pair + columns :]
-    sum_q = reduce_blocks(blocks_q, side_shift)
-    sum_k = reduce_blocks(blocks_k, column_shift)
-    sum_v = reduce_blocks(blocks_v, side_shift)
-    up_part = dot(up_t, all_slots, 0, 0, bf16)
+    hidden_t, grad_qk, grad_v, *blocks_v = after(hidden_t, grad_qk, grad_v, *blocks_v)
+    away_second = [out_rows_of(1, j, hidden_t) for j in range(1, columns)]
+    hidden_t, grad_qk, grad_v, *away_second = after(hidden_t, grad_qk, grad_v, *away_second)
+    away_second = columns_home(away_second)
 
     def back_rows(s, out):
         part = slice(s * rows, (s + 1) * rows)
-        total = dot(grad_q[part], full_q, 1, 1) + dot(grad_k[part], full_k, 1, 1)
-        return (total + dot(grad_v[part], full_v, 1, 1)).astype(out)
-
-    up_part, grad_q, grad_k, grad_v = after(up_part, grad_q, grad_k, grad_v)
-    up_total = core_sum(up_part)
+        return (dot(grad_qk[part], full_qk, 1, 1) + dot(grad_v[part], full_v, 1, 1)).astype(out)
+
     back_away = [back_rows(s, bf16) for s in range(1, ctx_count)]
     grad_normed = back_rows(0, f32)
-
-    sum_q, sum_o, grad_normed, up_total, outs_first, own, *away_out[1] = after(
-        sum_q, sum_o, grad_normed, up_total, outs_first, outs[columns], *away_out[1]
-    )
-    up_grad = side_sum(up_total)
-    outs_second = swap_experts(add_parts(own, away_out[1]))
-    sum_q = reduce_blocks(cut(sum_q, columns), column_shift)
+    grad_normed, gate_own, gate_came, *came_o = after(grad_normed, gate_own, gate_came, *came_o)
+    gate_grad = gate_own.astype(f32) + gate_came.astype(f32)
+    sum_o = add_parts(blocks_o[0], came_o)
     sum_o = reduce_blocks(row_blocks(sum_o, pair, my_side), side_shift)
     for s in range(1, ctx_count):
         grad_normed = grad_normed + core_shift(back_away[s - 1], -s).astype(f32)
     _, unit_one, inverse_one = normalize_parts(inputs, norm1_gain)
     grad_norm_one, norm1_part = norm_backward(grad_normed, unit_one, inverse_one, norm1_gain)
     tokens_grad = (grad_hidden_in + grad_norm_one).astype(bf16)
-
-    sum_k, sum_v, tokens_grad = after(sum_k, sum_v, tokens_grad)
-    sum_k = reduce_blocks(cut(sum_k, pair), side_shift)
-    sum_v = reduce_blocks(cut(sum_v, columns), column_shift)
+    up_t, norm1_part, tokens_grad, *away_second = after(
+        up_t, norm1_part, tokens_grad, *away_second
+    )
+
+    up_part = dot(up_t, all_slots, 0, 0, bf16)
+    came_v = [side_shift(block, d) for d, block in enumerate(blocks_v) if d]
+    up_part, sum_o, outs_first, hidden_t, *came_v = after(
+        up_part, sum_o, outs_first, hidden_t, *came_v
+    )
+    sum_v = reduce_blocks(cut(add_parts(blocks_v[0], came_v), columns), column_shift)
     out_grad = expert_sum(sum_o)
-    sums = jnp.stack([expert_sum(a) for a in (sum_q, sum_k, sum_v)]).reshape(
-        3, ctx_count, per, width
+    up_total = core_sum(up_part)
+    own_second = out_rows_of(1, 0, hidden_t)
+    own_second, up_total, out_grad, sum_v, qk_sum = after(
+        own_second, up_total, out_grad, sum_v, qk_sum
+    )
+    up_own, up_came = side_swap_sum(up_total)
+
+    gains = jnp.stack([norm1_part, norm2_part]).reshape(2, ctx_count, fsdp_count, per)
+    gains = lax.all_to_all(gains.transpose(2, 1, 0, 3), "fsdp", 0, 0, tiled=True)
+    gains = jnp.sum(gains, axis=0)
+
+    def gains_of(c):
+        return lax.dynamic_index_in_dim(gains, c % ctx_count, 0, keepdims=False)
+
+    gains_own = gains_of(core)
+    for s in range(1, ctx_count):
+        gains_own = gains_own + core_shift(gains_of(core + s), s)
+    value_part = expert_sum(sum_v).reshape(ctx_count, per, width)
+    outs_second = swap_experts(add_parts(own_second, away_second))
+    up_grad = up_own.astype(f32) + up_came.astype(f32)
+    qk_parts = qk_sum.astype(f32).reshape(ctx_count, per, heads, 2, HD)
+    sums = jnp.stack(
+        [
+            qk_parts[:, :, :, 0].reshape(ctx_count, per, width),
+            qk_parts[:, :, :, 1].reshape(ctx_count, per, width),
+            value_part,
+        ]
     )
 
     def core_piece(c):
@@ -619,18 +714,6 @@
         qkv_own = lax.all_to_all(sums.astype(bf16), "ctx", 1, 1).astype(f32)
         qkv_own = qkv_own.transpose(0, 2, 1, 3).reshape(3, per, D)
     query_grad, key_grad, value_grad = qkv_own[0], qkv_own[1], qkv_own[2]
-
-    gains = jnp.stack([norm1_part, norm2_part])
-    step = 1
-    while step < ctx_count:
-        gains = gains + lax.ppermute(gains, "ctx", [(i, i ^ step) for i in range(ctx_count)])
-        step *= 2
-    step = 1
-    while step < fsdp_count:
-        gains = gains + fsdp_shift(gains, lambda i, step=step: i ^ step)
-        step *= 2
-    place_own = (core * fsdp_count + mine) * per
-    gains_own = lax.dynamic_slice_in_dim(gains, place_own, per, axis=1)
 
     slot_out = jnp.concatenate([outs_first, outs_second], axis=0).reshape(halves * half, D)
     mixed = hidden_in

time: 1490 us -> 2410 us (1.62)
  Pallas kernels: 171 us -> 1360 us
  matrix products: 424 us -> 273 us
  other arithmetic: 231 us -> 116 us
    pallas_call x0 -> x11, Pallas kernels: none -> 1190 us  [the longest x3 1050 us: join_weights(): pl.pallas_call(join_kernel, grid_spec=pltpu.PrefetchScalarGridSpec(num_sc...]
    dot_general x43 -> x24, matrix products: 424 us -> 273 us  [dot(): lax.dot_general(a, b, (((ca,), (cb,)), ((), ())), preferred_element_type=...]
    ppermute x20 -> x14, waiting for transfers between devices: 263 us -> 170 us  [fsdp_shift(): return lax.ppermute(a, 'fsdp', [(i, move(i)) for i in range(fsdp_count)])]
    concatenate x4 -> x1, other arithmetic: 90.5 us -> 1.04 us  [shards(): jnp.concatenate([jnp.stack(by_head, axis=2).reshape(-1, 2 * width), own_c...]
    all_gather x1, waiting for transfers between devices: 141 us -> 187 us  [shards(): gathered = lax.all_gather(packed, 'fsdp', axis=0, tiled=True)]
    all_to_all x12 -> x10, starting transfers between devices: 57.3 us -> 54.5 us  [swap_experts(): lax.all_to_all(blocks, 'fsdp', 0, 0, axis_index_groups=lines, tiled=True)]
  transfers between devices with their start and end apart: 52 -> 44, of which waited for: 22 -> 15; matrix products, arithmetic and copies ran while one was open for 42% -> 18% of each run, Pallas kernels for 7% -> 57%
where the time goes in v3:
time: 2410 us
  Pallas kernels  1360 us (56%)
  waiting for transfers between devices  469 us (19%)
  matrix products  273 us (11%)
  other arithmetic  116 us (5%)
  starting transfers between devices  88.3 us (4%)
  local copies, waits for them, and re-layouts  83.9 us (3%)
    pallas_call x3, Pallas kernels, join_weights(): pl.pallas_call(join_kernel, grid_spec=pltpu.PrefetchScalarGridSpec(num_sc...  1050 us
    dot_general x24, matrix products, dot(): lax.dot_general(a, b, (((ca,), (cb,)), ((), ())), preferred_element_type=...  273 us
    all_gather x1, waiting for transfers between devices, shards(): gathered = lax.all_gather(packed, 'fsdp', axis=0, tiled=True)  187 us
    ppermute x14, waiting for transfers between devices, fsdp_shift(): return lax.ppermute(a, 'fsdp', [(i, move(i)) for i in range(fsdp_count)])  170 us
    pallas_call x8, Pallas kernels, expert_rows(): pl.pallas_call(functools.partial(rows_kernel, len(left)), grid=(D // tile...  138 us
    pallas_call x4, Pallas kernels, expert_hidden(): pl.pallas_call(functools.partial(expert_kernel, len(kept)), grid=(units /...  123 us
    all_gather x3, waiting for transfers between devices, shards(): lax.all_gather(part, 'fsdp', axis=0, tiled=True, axis_index_groups=sides)  59.8 us
    all_to_all x10, starting transfers between devices, swap_experts(): lax.all_to_all(blocks, 'fsdp', 0, 0, axis_index_groups=lines, tiled=True)  54.5 us
  transfers between devices with their start and end apart: 44, of which 15 were waited for; matrix products, arithmetic and copies ran while one was open for 18% of the time, Pallas kernels for 57%

profile of v3, /device:TPU:0, one launch (start us, length us, event | category | flops | bytes accessed | tf_op | source)
XLA Modules:
  0.0 2408.3 jit_solution(425163045072909312)
XLA Ops:
  22.2 6.8 constant_dynamic-slice_fusion.16
  39.0 13.3 fusion.32
  52.4 24.1 fusion.31
  76.4 187.5 %all-gather.5.cloned.1.call-done = bf16[2048,4096]{0,1:T(8,128)(2,1)} async-done(((bf16[128,4096]{0,1:T(8,128)(2,1)}), bf16[2048,4096]{0,1:T(8,128)(2,1)}) %all-gather.5.cloned.1.call-update) | async-done | bytes 16777232 | tf_op jit(solution)/shard_map/all_gather | solution.py:382
  282.6 19.2 fusion.2.pre_q.pre_k.pre_v
  301.8 21.7 attention_forward.1
  342.5 6.0 multiply_reduce_fusion.2
  355.0 59.8 %all-gather.9.cloned.1.call-done = bf16[1408,2048]{1,0:T(8,128)(2,1)} async-done(((bf16[704,2048]{1,0:T(8,128)(2,1)}), bf16[1408,2048]{1,0:T(8,128)(2,1)}) %all-gather.9.cloned.1.call-update) | async-done | bytes 5767184 | tf_op jit(solution)/shard_map/all_gather | solution.py:455
  428.5 351.2 %join_weights.3.wg_ref.refs_2_ = bf16[2816,2048]{1,0:T(8,128)(2,1)} custom-call(s32[2]{0:T(128)} %pad_add_fusion.where, bf16[1408,2048]{1,0:T(8,128)(2,1)} %own_ref.3, bf16[704,2048]{1,0:T(8,128)(2,1)} %copy-done.14, bf16[704,2048]{1,0:T(8,128)(2,1)} %collective-permute-done.4.refs_1_), custom_call_target="tpu_custom_call" | custom-call | tf_op jit(solution)/shard_map/join_weights/pallas_call | solution.py:270
  779.7 351.2 %join_weights.4.wu_ref.refs_3_ = bf16[2816,2048]{1,0:T(8,128)(2,1)} custom-call(s32[2]{0:T(128)} %pad_add_fusion.where, bf16[1408,2048]{1,0:T(8,128)(2,1)} %own_ref.4, bf16[704,2048]{1,0:T(8,128)(2,1)} %constant_dynamic-slice_fusion.13.refs_0_, bf16[704,2048]{1,0:T(8,128)(2,1)} %collective-permute-done.5.refs_1_), custom_call_target="tpu_custom_call" | custom-call | tf_op jit(solution)/shard_map/join_weights/pallas_call | solution.py:270
  1144.0 351.2 %join_weights.5.wd_ref.refs_1_ = bf16[2816,2048]{1,0:T(8,128)(2,1)} custom-call(s32[2]{0:T(128)} %pad_add_fusion.where, bf16[1408,2048]{1,0:T(8,128)(2,1)} %own_ref.5, bf16[704,2048]{1,0:T(8,128)(2,1)} %copy-done.15, bf16[704,2048]{1,0:T(8,128)(2,1)} %collective-permute-done.7.refs_1_), custom_call_target="tpu_custom_call" | custom-call | tf_op jit(solution)/shard_map/join_weights/pallas_call | solution.py:270
  1495.2 30.6 %expert_hidden.4 = (bf16[2560,2816]{1,0:T(8,128)(2,1)}, bf16[2560,2816]{1,0:T(8,128)(2,1)}, bf16[2560,2816]{1,0:T(8,128)(2,1)}) custom-call(bf16[640,2048]{1,0:T(8,128)(2,1)} %bitcast.122, bf16[640,2048]{1,0:T(8,128)(2,1)} %bitcast.14.g_ref, bf16[2816,2048]{1,0:T(8,128)(2,1)} %join_weights.3.wg_ref.refs_2_, bf16[2816,2048]{1,0:T(8,128)(2,1)} %join_weights.4.wu_ref.refs_3_, ...), custom_call_target="tpu_custom_call" | custom-call | tf_op jit(solution)/shard_map/expert_hidden/pallas_call | solution.py:216
  1527.4 30.6 %expert_hidden.5 = (bf16[2560,2816]{1,0:T(8,128)(2,1)}, bf16[2560,2816]{1,0:T(8,128)(2,1)}, bf16[2560,2816]{1,0:T(8,128)(2,1)}) custom-call(bf16[640,2048]{1,0:T(8,128)(2,1)} %collective-permute-done.8.x_ref, bf16[640,2048]{1,0:T(8,128)(2,1)} %collective-permute-done.3.g_ref, ...), custom_call_target="tpu_custom_call", output_to_operand_aliasing={{0}: (5, {}), {1}: (6, {}), {2}: (7, {})} | custom-call | tf_op jit(solution)/shard_map/expert_hidden/pallas_call | solution.py:216
  1558.1 21.1 expert_rows.8
  1586.5 21.1 expert_rows.9
  1607.7 30.6 %expert_hidden.6 = (bf16[2560,2816]{1,0:T(8,128)(2,1)}, bf16[2560,2816]{1,0:T(8,128)(2,1)}, bf16[2560,2816]{1,0:T(8,128)(2,1)}) custom-call(bf16[640,2048]{1,0:T(8,128)(2,1)} %bitcast.22.x_ref, bf16[640,2048]{1,0:T(8,128)(2,1)} %bitcast.16.g_ref, ...), custom_call_target="tpu_custom_call", output_to_operand_aliasing={{0}: (5, {}), {1}: (6, {}), {2}: (7, {})} | custom-call | tf_op jit(solution)/shard_map/expert_hidden/pallas_call | solution.py:216
  1664.9 30.6 %expert_hidden.7 = (bf16[2560,2816]{1,0:T(8,128)(2,1)}, bf16[2560,2816]{1,0:T(8,128)(2,1)}, bf16[2560,2816]{1,0:T(8,128)(2,1)}) custom-call(bf16[640,2048]{1,0:T(8,128)(2,1)} %copy-done.17, bf16[640,2048]{1,0:T(8,128)(2,1)} %collective-permute-done.6.g_ref, ...), custom_call_target="tpu_custom_call", output_to_operand_aliasing={{0}: (5, {}), {1}: (6, {}), {2}: (7, {})} | custom-call | tf_op jit(solution)/shard_map/expert_hidden/pallas_call | solution.py:216
  1695.6 21.1 expert_rows.10
  1718.1 21.1 expert_rows.11
  1739.1 38.7 %convolution_convert_fusion.2 = bf16[2816,2048]{1,0:T(8,128)(2,1)} fusion(bf16[2560,2816]{1,0:T(8,128)(2,1)} %get-tuple-element.247.refs_0_, bf16[640,2048]{1,0:T(8,128)(2,1)} %collective-permute-done.6.g_ref, bf16[640,2048]{1,0:T(8,128)(2,1)} %bitcast.16.g_ref, bf16[640,2048]{1,0:T(8,128)(2,1)} %collective-permute-done.3.g_ref, ...), kind=kOutput, calls=%fused_computation.11 | convolution fusion | flops 29575610368 | bytes 36438016 | tf_op jit(solution)/shard_map/dot_general | solution.py:27
  1791.3 38.8 %convolution_convert_fusion.1 = bf16[2816,2048]{1,0:T(8,128)(2,1)} fusion(bf16[2560,2816]{1,0:T(8,128)(2,1)} %get-tuple-element.213.refs_0_, bf16[2560,2048]{1,0:T(8,128)(2,1)} %constant_dynamic-update-slice_fusion), kind=kOutput, calls=%fused_computation.10 | convolution fusion | flops 29533667328 | bytes 36438016 | tf_op jit(solution)/shard_map/dot_general | solution.py:27
  1830.1 13.5 expert_rows.12
  1843.6 13.5 expert_rows.13
  1863.4 9.8 add_convert_fusion.2
  1883.2 7.4 add_convert_fusion.1
  1890.7 7.3 convolution_convert_fusion.4
  1913.6 27.1 %attention_backward.1 = (bf16[1024,2048]{1,0:T(8,128)(2,1)}, bf16[1024,1024]{1,0:T(8,128)(2,1)}) custom-call(s32[4]{0:T(128)} %fusion.126.perm, bf16[1024,1024]{1,0:T(8,128)(2,1)} %get-tuple-element.141.q_ref, bf16[1024,1024]{1,0:T(8,128)(2,1)} %get-tuple-element.142.k_ref, bf16[1024,1024]{1,0:T(8,128)(2,1)} %get-tuple-element.143.v_ref, ...), custom_call_target="tpu_custom_call" | custom-call | tf_op jit(solution)/shard_map/attention_backward/pallas_call | solution.py:178
  1940.7 14.2 convolution_convert_fusion.3
  1954.9 23.5 reduce-scatter.3.cloned.1.call-done
  1991.1 13.5 expert_rows.14
  2004.5 7.0 fusion.35
  2011.6 6.7 fusion.33
  2018.3 10.2 fusion.37
  2028.5 10.0 collective-permute-done.16
  2038.5 7.3 add_convert_fusion.10
  2057.5 7.3 all-to-all-start.6
  2066.9 44.8 %collective-permute-done.20 = bf16[256,2048]{1,0:T(8,128)(2,1)} collective-permute-done((bf16[256,2048]{1,0:T(8,128)(2,1)}, bf16[256,2048]{1,0:T(8,128)(2,1)}, u32[]{:S(2)}, u32[]{:S(2)}) %collective-permute-start.20) | collective-permute-done | bytes 1048608 | tf_op jit(solution)/shard_map/ppermute | solution.py:348
  2119.1 6.6 fusion.27
  2125.7 10.7 collective-permute-done.19
  2136.5 36.2 %convolution_convert_fusion = bf16[2816,2048]{1,0:T(8,128)(2,1)} fusion(bf16[2560,2816]{1,0:T(8,128)(2,1)S(1)} %bitcast.120, bf16[2560,2048]{1,0:T(8,128)(2,1)} %constant_dynamic-update-slice_fusion), kind=kOutput, calls=%fused_computation.9 | convolution fusion | flops 29533667328 | bytes 36438016 | tf_op jit(solution)/shard_map/dot_general | solution.py:27
  2172.6 38.5 %collective-permute-done.21 = bf16[1024,1024]{1,0:T(8,128)(2,1)} collective-permute-done((bf16[1024,1024]{1,0:T(8,128)(2,1)}, bf16[1024,1024]{1,0:T(8,128)(2,1)}, u32[]{:S(2)}, u32[]{:S(2)}) %collective-permute-start.21) | collective-permute-done | bytes 2097184 | tf_op jit(solution)/shard_map/ppermute | solution.py:348
  2217.0 7.2 all-to-all-start.7
  2228.5 9.2 collective-permute-start.23
  2238.6 13.4 expert_rows.15
  2252.0 12.6 collective-permute-done.23
  2271.7 10.0 add_convert_fusion
  2290.9 21.3 all-to-all-done.10
  2342.6 41.9 %collective-permute-done.26 = bf16[1408,1024]{1,0:T(8,128)(2,1)} collective-permute-done((bf16[1408,1024]{1,0:T(8,128)(2,1)}, bf16[1408,1024]{1,0:T(8,128)(2,1)}, u32[]{:S(2)}, u32[]{:S(2)}) %collective-permute-start.26) | collective-permute-done | bytes 2883616 | tf_op jit(solution)/shard_map/ppermute | solution.py:348
  (330 shorter events, 286.1 us)
Async XLA Ops:
  7.2 256.7 %all-gather.5.cloned.1.call-start = ((), (), s32[]{:S(2)}) async-start(), calls=%async_computation.13 | async-start | bytes 17825792 | tf_op jit(solution)/shard_map/all_gather | solution.py:382
  11.4 343.6 %all-gather.7.cloned.1.call-start = ((), (), s32[]{:S(2)}) async-start(), calls=%async_computation.14 | async-start | bytes 8650752 | tf_op jit(solution)/shard_map/all_gather | solution.py:455
  13.8 25.2 %collective-permute-start = (bf16[512,2048]{1,0:T(8,128)(2,1)}, bf16[512,2048]{1,0:T(8,128)(2,1)}, u32[]{:S(2)}, u32[]{:S(2)}) collective-permute-start(bf16[512,2048]{1,0:T(8,128)(2,1)} %fusion.21), channel_id=1, source_target_pairs={{0,16},{16,0},{1,17},{17,1},{2,18},{18,2},{3,19},{19,3},{4,20},{20... | collective-permute-start | bytes 6291464 | tf_op jit(solution)/shard_map/ppermute | solution.py:345
  18.3 321.4 %copy-start.36 = (s32[512]{0:T(512)}, s32[512]{0:T(512)S(1)}, u32[]{:S(2)}) copy-start(s32[512]{0:T(512)S(1)} %get-tuple-element.269) | copy-start | bytes 6148
  18.3 321.4 %copy-start.39 = (s32[512]{0:T(512)}, s32[512]{0:T(512)S(1)}, u32[]{:S(2)}) copy-start(s32[512]{0:T(512)S(1)} %get-tuple-element.270) | copy-start | bytes 6148
  263.9 150.8 %all-gather.9.cloned.1.call-start = ((), (), s32[]{:S(2)}) async-start(), calls=%async_computation.15 | async-start | bytes 8650752 | tf_op jit(solution)/shard_map/all_gather | solution.py:455
  264.6 68.1 %all-to-all-start = ((bf16[4,160,2048]{2,1,0:T(8,128)(2,1)}), bf16[4,160,2048]{2,1,0:T(8,128)(2,1)}, u32[]{:S(2)}, u32[]{:S(2)}) async-start(bf16[4,160,2048]{2,1,0:T(8,128)(2,1)} %bitcast.138), calls=%async_computation | async-start | bytes 5242880 | tf_op jit(solution)/shard_map/all_to_all | solution.py:445
  282.6 40.9 %collective-permute-start.1 = (bf16[1024,1024]{0,1:T(8,128)(2,1)}, bf16[1024,1024]{0,1:T(8,128)(2,1)}, u32[]{:S(2)}, u32[]{:S(2)}) collective-permute-start(bf16[1024,1024]{0,1:T(8,128)(2,1)} %constant_dynamic-slice_fusion.15), channel_id=1, source_target_pairs={{0,16},{16,0},{1,17},{17,1},{2,18},{18,2},{3,19},{19,3},{4,20},{20... | collective-permute-start | bytes 6291464 | tf_op jit(solution)/shard_map/ppermute | solution.py:345
  332.8 82.0 %all-to-all-start.1 = ((bf16[4,160,2048]{2,1,0:T(8,128)(2,1)}), bf16[4,160,2048]{2,1,0:T(8,128)(2,1)}, u32[]{:S(2)}, u32[]{:S(2)}) async-start(bf16[4,160,2048]{2,1,0:T(8,128)(2,1)} %bitcast.137), calls=%async_computation.1 | async-start | bytes 5242880 | tf_op jit(solution)/shard_map/all_to_all | solution.py:445
  337.8 793.2 %all-gather.11.cloned.1.call-start = ((), (), s32[]{:S(2)}) async-start(), calls=%async_computation.16 | async-start | bytes 8650752 | tf_op jit(solution)/shard_map/all_gather | solution.py:455
  338.0 4.6 collective-permute-start.2
  338.3 76.5 %collective-permute-start.3 = (bf16[640,2048]{1,0:T(8,128)(2,1)}, bf16[640,2048]{1,0:T(8,128)(2,1)}, u32[]{:S(2)}, u32[]{:S(2)}) collective-permute-start(bf16[640,2048]{1,0:T(8,128)(2,1)} %bitcast.14.g_ref), channel_id=1, source_target_pairs={{0,2},{1,3},{2,0},{3,1},{4,6},{5,7},{6,4},{7,5},{8,10},{9,11},{10,... | collective-permute-start | bytes 7864328 | tf_op jit(solution)/shard_map/ppermute | solution.py:348
  414.7 716.2 %all-to-all-start.2 = ((bf16[4,160,2048]{2,1,0:T(8,128)(2,1)}), bf16[4,160,2048]{2,1,0:T(8,128)(2,1)S(1)}, u32[]{:S(2)}, u32[]{:S(2)}) async-start(bf16[4,160,2048]{2,1,0:T(8,128)(2,1)} %bitcast.140), calls=%async_computation.2 | async-start | bytes 5242880 | tf_op jit(solution)/shard_map/all_to_all | solution.py:445
  423.1 5.4 collective-permute-start.4
  426.0 353.7 %collective-permute-start.5 = (bf16[704,2048]{1,0:T(8,128)(2,1)}, bf16[704,2048]{1,0:T(8,128)(2,1)}, u32[]{:S(2)}, u32[]{:S(2)}) collective-permute-start(bf16[704,2048]{1,0:T(8,128)(2,1)} %constant_dynamic-slice_fusion.13.refs_0_), channel_id=1, source_target_pairs={{0,16},{16,0},{1,17},{17,1},{2,18},{18,2},{3,19},{19,3},{4,20},{20... | collective-permute-start | bytes 8650760 | tf_op jit(solution)/shard_map/ppermute | solution.py:345
  426.0 705.0 %collective-permute-start.6 = (bf16[640,2048]{1,0:T(8,128)(2,1)}, bf16[640,2048]{1,0:T(8,128)(2,1)}, u32[]{:S(2)}, u32[]{:S(2)}) collective-permute-start(bf16[640,2048]{1,0:T(8,128)(2,1)} %bitcast.16.g_ref), channel_id=1, source_target_pairs={{0,2},{1,3},{2,0},{3,1},{4,6},{5,7},{6,4},{7,5},{8,10},{9,11},{10,... | collective-permute-start | bytes 7864328 | tf_op jit(solution)/shard_map/ppermute | solution.py:348
  1131.0 394.9 %all-to-all-start.3 = ((bf16[4,160,2048]{2,1,0:T(8,128)(2,1)}), bf16[4,160,2048]{2,1,0:T(8,128)(2,1)}, u32[]{:S(2)}, u32[]{:S(2)}) async-start(bf16[4,160,2048]{2,1,0:T(8,128)(2,1)} %bitcast.139), calls=%async_computation.3 | async-start | bytes 5242880 | tf_op jit(solution)/shard_map/all_to_all | solution.py:445
  1138.6 5.5 collective-permute-start.7
  1138.6 387.2 %collective-permute-start.8 = (bf16[640,2048]{1,0:T(8,128)(2,1)S(1)}, bf16[640,2048]{1,0:T(8,128)(2,1)}, u32[]{:S(2)}, u32[]{:S(2)}) collective-permute-start(bf16[640,2048]{1,0:T(8,128)(2,1)S(1)} %bitcast.121), channel_id=1, source_target_pairs={{0,2},{1,3},{2,0},{3,1},{4,6},{5,7},{6,4},{7,5},{8,10},{9,11},{10,... | collective-permute-start | bytes 7864328 | tf_op jit(solution)/shard_map/ppermute | solution.py:348
  1525.9 59.2 %collective-permute-start.9 = (bf16[640,2048]{1,0:T(8,128)(2,1)}, bf16[640,2048]{1,0:T(8,128)(2,1)S(1)}, u32[]{:S(2)}, u32[]{:S(2)}) collective-permute-start(bf16[640,2048]{1,0:T(8,128)(2,1)} %bitcast.22.x_ref), channel_id=1, source_target_pairs={{0,2},{1,3},{2,0},{3,1},{4,6},{5,7},{6,4},{7,5},{8,10},{9,11},{10,... | collective-permute-start | bytes 7864328 | tf_op jit(solution)/shard_map/ppermute | solution.py:348
  1585.1 58.4 %collective-permute-start.10 = (bf16[640,2048]{1,0:T(8,128)(2,1)}, bf16[640,2048]{1,0:T(8,128)(2,1)}, u32[]{:S(2)}, u32[]{:S(2)}) collective-permute-start(bf16[640,2048]{1,0:T(8,128)(2,1)} %expert_rows.8), channel_id=1, source_target_pairs={{0,2},{1,3},{2,0},{3,1},{4,6},{5,7},{6,4},{7,5},{8,10},{9,11},{10,... | collective-permute-start | bytes 7864328 | tf_op jit(solution)/shard_map/ppermute | solution.py:348
  1648.7 69.4 %all-to-all-start.4 = ((bf16[4,160,2048]{2,1,0:T(8,128)(2,1)}), bf16[4,160,2048]{2,1,0:T(8,128)(2,1)}, u32[]{:S(2)}, u32[]{:S(2)}) async-start(bf16[4,160,2048]{2,1,0:T(8,128)(2,1)} %bitcast.129), calls=%async_computation.4 | async-start | bytes 5242880 | tf_op jit(solution)/shard_map/all_to_all | solution.py:445
  1716.6 61.2 %collective-permute-start.11 = (bf16[640,2048]{1,0:T(8,128)(2,1)}, bf16[640,2048]{1,0:T(8,128)(2,1)S(1)}, u32[]{:S(2)}, u32[]{:S(2)}) collective-permute-start(bf16[640,2048]{1,0:T(8,128)(2,1)} %expert_rows.10), channel_id=1, source_target_pairs={{0,2},{1,3},{2,0},{3,1},{4,6},{5,7},{6,4},{7,5},{8,10},{9,11},{10,... | collective-permute-start | bytes 7864328 | tf_op jit(solution)/shard_map/ppermute | solution.py:348
  1780.4 92.8 %all-to-all-start.5 = ((bf16[4,160,2048]{2,1,0:T(8,128)(2,1)}), bf16[4,160,2048]{2,1,0:T(8,128)(2,1)S(1)}, u32[]{:S(2)}, u32[]{:S(2)}) async-start(bf16[4,160,2048]{2,1,0:T(8,128)(2,1)} %bitcast.128), calls=%async_computation.5 | async-start | bytes 5242880 | tf_op jit(solution)/shard_map/all_to_all | solution.py:445
  1785.5 192.9 %reduce-scatter.3.cloned.1.call-start = ((), (), s32[]{:S(2)}) async-start(), calls=%async_computation.17 | async-start | bytes 8650752 | tf_op jit(solution)/shard_map/reduce_scatter | solution.py:565
  1791.3 72.1 %collective-permute-start.12 = (bf16[2816,1024]{1,0:T(8,128)(2,1)}, bf16[2816,1024]{1,0:T(8,128)(2,1)}, u32[]{:S(2)}, u32[]{:S(2)}) collective-permute-start(bf16[2816,1024]{1,0:T(8,128)(2,1)} %constant_dynamic-slice_fusion.11), channel_id=1, source_target_pairs={{0,16},{16,0},{1,17},{17,1},{2,18},{18,2},{3,19},{19,3},{4,20},{20... | collective-permute-start | bytes 17301512 | tf_op jit(solution)/shard_map/ppermute | solution.py:345
  1862.8 20.4 collective-permute-start.14
  1873.3 408.4 %reduce-scatter.5.cloned.1.call-start = ((), (), s32[]{:S(2)}) async-start(), calls=%async_computation.18 | async-start | bytes 8912896 | tf_op jit(solution)/shard_map/reduce_scatter | solution.py:640
  1882.6 8.0 collective-permute-start.13
  1882.6 100.9 %collective-permute-start.15 = (bf16[640,2048]{1,0:T(8,128)(2,1)}, bf16[640,2048]{1,0:T(8,128)(2,1)}, u32[]{:S(2)}, u32[]{:S(2)}) collective-permute-start(bf16[640,2048]{1,0:T(8,128)(2,1)} %expert_rows.13), channel_id=1, source_target_pairs={{0,2},{1,3},{2,0},{3,1},{4,6},{5,7},{6,4},{7,5},{8,10},{9,11},{10,... | collective-permute-start | bytes 7864328 | tf_op jit(solution)/shard_map/ppermute | solution.py:348
  1905.9 132.6 %collective-permute-start.16 = (bf16[1408,1024]{1,0:T(8,128)(2,1)}, bf16[1408,1024]{1,0:T(8,128)(2,1)}, u32[]{:S(2)}, u32[]{:S(2)}) collective-permute-start(bf16[1408,1024]{1,0:T(8,128)(2,1)} %get-tuple-element.273), channel_id=1, source_target_pairs={{0,1},{1,0},{2,3},{3,2},{4,5},{5,4},{6,7},{7,6},{8,9},{9,8},{10,11... | collective-permute-start | bytes 8650760 | tf_op jit(solution)/shard_map/ppermute | solution.py:348
  1906.3 122.2 %collective-permute-start.17 = (bf16[512,2048]{1,0:T(8,128)(2,1)}, bf16[512,2048]{1,0:T(8,128)(2,1)}, u32[]{:S(2)}, u32[]{:S(2)}) collective-permute-start(bf16[512,2048]{1,0:T(8,128)(2,1)} %bitcast.28), channel_id=1, source_target_pairs={{0,2},{1,3},{2,0},{3,1},{4,6},{5,7},{6,4},{7,5},{8,10},{9,11},{10,... | collective-permute-start | bytes 6291464 | tf_op jit(solution)/shard_map/ppermute | solution.py:348
  2045.8 68.7 %collective-permute-start.18 = (bf16[512,2048]{1,0:T(8,128)(2,1)}, bf16[512,2048]{1,0:T(8,128)(2,1)}, u32[]{:S(2)}, u32[]{:S(2)}) collective-permute-start(bf16[512,2048]{1,0:T(8,128)(2,1)} %add_convert_fusion.10), channel_id=1, source_target_pairs={{0,16},{16,0},{1,17},{17,1},{2,18},{18,2},{3,19},{19,3},{4,20},{20... | collective-permute-start | bytes 6291464 | tf_op jit(solution)/shard_map/ppermute | solution.py:345
  2049.5 62.2 %collective-permute-start.20 = (bf16[256,2048]{1,0:T(8,128)(2,1)}, bf16[256,2048]{1,0:T(8,128)(2,1)}, u32[]{:S(2)}, u32[]{:S(2)}) collective-permute-start(bf16[256,2048]{1,0:T(8,128)(2,1)} %bitcast.31), channel_id=1, source_target_pairs={{0,1},{1,0},{2,3},{3,2},{4,5},{5,4},{6,7},{7,6},{8,9},{9,8},{10,11... | collective-permute-start | bytes 3145736 | tf_op jit(solution)/shard_map/ppermute | solution.py:348
  2052.0 84.4 %collective-permute-start.19 = (bf16[640,2048]{1,0:T(8,128)(2,1)}, bf16[640,2048]{1,0:T(8,128)(2,1)}, u32[]{:S(2)}, u32[]{:S(2)}) collective-permute-start(bf16[640,2048]{1,0:T(8,128)(2,1)} %expert_rows.14), channel_id=1, source_target_pairs={{0,2},{1,3},{2,0},{3,1},{4,6},{5,7},{6,4},{7,5},{8,10},{9,11},{10,... | collective-permute-start | bytes 7864328 | tf_op jit(solution)/shard_map/ppermute | solution.py:348
  2057.5 57.0 %copy-start.31 = (f32[2048]{0:T(1024)S(1)}, f32[2048]{0:T(1024)}, u32[]{:S(2)}) copy-start(f32[2048]{0:T(1024)} %param.18) | copy-start | bytes 24580
  2057.5 57.0 %copy-start.35 = (f32[512]{0:T(512)S(1)}, f32[512]{0:T(512)}, u32[]{:S(2)}) copy-start(f32[512]{0:T(512)} %copy-done.34) | copy-start | bytes 6148
  2057.5 153.7 %all-to-all-start.6 = ((bf16[4,160,2048]{2,1,0:T(8,128)(2,1)}), bf16[4,160,2048]{2,1,0:T(8,128)(2,1)}, u32[]{:S(2)}, u32[]{:S(2)}) async-start(bf16[4,160,2048]{2,1,0:T(8,128)(2,1)} %bitcast.127), calls=%async_computation.7 | async-start | bytes 5242880 | tf_op jit(solution)/shard_map/all_to_all | solution.py:445
  2064.8 146.4 %collective-permute-start.21 = (bf16[1024,1024]{1,0:T(8,128)(2,1)}, bf16[1024,1024]{1,0:T(8,128)(2,1)}, u32[]{:S(2)}, u32[]{:S(2)}) collective-permute-start(bf16[1024,1024]{1,0:T(8,128)(2,1)} %fusion.58), channel_id=1, source_target_pairs={{0,1},{1,0},{2,3},{3,2},{4,5},{5,4},{6,7},{7,6},{8,9},{9,8},{10,11... | collective-permute-start | bytes 6291464 | tf_op jit(solution)/shard_map/ppermute | solution.py:348
  2217.0 54.7 %collective-permute-start.22 = (bf16[2816,1024]{1,0:T(8,128)(2,1)}, bf16[2816,1024]{1,0:T(8,128)(2,1)}, u32[]{:S(2)}, u32[]{:S(2)}) collective-permute-start(bf16[2816,1024]{1,0:T(8,128)(2,1)} %constant_dynamic-slice_fusion.3), channel_id=1, source_target_pairs={{0,16},{16,0},{1,17},{17,1},{2,18},{18,2},{3,19},{19,3},{4,20},{20... | collective-permute-start | bytes 17301512 | tf_op jit(solution)/shard_map/ppermute | solution.py:345
  2217.0 50.2 %all-to-all-start.7 = ((bf16[4,64,2048]{2,1,0:T(8,128)(2,1)}), bf16[4,64,2048]{2,1,0:T(8,128)(2,1)S(1)}, u32[]{:S(2)}, u32[]{:S(2)}) async-start(bf16[4,64,2048]{2,1,0:T(8,128)(2,1)} %bitcast.33), calls=%async_computation.8 | async-start | bytes 2097152 | tf_op jit(solution)/shard_map/all_to_all | solution.py:445
  2228.5 36.1 %collective-permute-start.23 = (bf16[512,1024]{1,0:T(8,128)(2,1)}, bf16[512,1024]{1,0:T(8,128)(2,1)}, u32[]{:S(2)}, u32[]{:S(2)}) collective-permute-start(bf16[512,1024]{1,0:T(8,128)(2,1)} %slice.138), channel_id=1, source_target_pairs={{0,2},{1,3},{2,0},{3,1},{4,6},{5,7},{6,4},{7,5},{8,10},{9,11},{10,... | collective-permute-start | bytes 3145736 | tf_op jit(solution)/shard_map/ppermute | solution.py:348
  2267.2 14.4 all-to-all-start.9
  2281.6 30.5 %all-to-all-start.10 = ((bf16[4,128,1024]{2,1,0:T(8,128)(2,1)}), bf16[4,128,1024]{2,1,0:T(8,128)(2,1)}, u32[]{:S(2)}, u32[]{:S(2)}) async-start(bf16[4,128,1024]{2,1,0:T(8,128)(2,1)} %bitcast.135), calls=%async_computation.12 | async-start | bytes 2097152 | tf_op jit(solution)/shard_map/all_to_all | solution.py:445
  2312.2 78.0 %all-to-all-start.8 = ((bf16[4,160,2048]{2,1,0:T(8,128)(2,1)}), bf16[4,160,2048]{2,1,0:T(8,128)(2,1)}, u32[]{:S(2)}, u32[]{:S(2)}) async-start(bf16[4,160,2048]{2,1,0:T(8,128)(2,1)} %bitcast.126), calls=%async_computation.10 | async-start | bytes 5242880 | tf_op jit(solution)/shard_map/all_to_all | solution.py:445
  2320.8 63.8 %collective-permute-start.26 = (bf16[1408,1024]{1,0:T(8,128)(2,1)}, bf16[1408,1024]{1,0:T(8,128)(2,1)}, u32[]{:S(2)}, u32[]{:S(2)}) collective-permute-start(bf16[1408,1024]{1,0:T(8,128)(2,1)} %constant_dynamic-slice_fusion), channel_id=1, source_target_pairs={{0,1},{1,0},{2,3},{3,2},{4,5},{5,4},{6,7},{7,6},{8,9},{9,8},{10,11... | collective-permute-start | bytes 8650760 | tf_op jit(solution)/shard_map/ppermute | solution.py:348
  2323.6 17.2 collective-permute-start.24
  2334.2 7.1 collective-permute-start.25
  (63 other events, 643.1 us)
Sparse Core Ops, SparseCore 0:
  11.5 252.3 all-gather.4
  266.0 72.6 all-gather.6
  340.2 74.4 all-gather.8
  416.1 74.4 all-gather.10
  1873.3 104.9 reduce-scatter.2
  1980.6 265.7 reduce-scatter.4

commit v4 on v3

--- a/solution.py
+++ b/solution.py
@@ -5,6 +5,7 @@
 import jax.numpy as jnp
 from jax import lax
 from jax.experimental import pallas as pl
+from jax.experimental.layout import Layout, with_layout_constraint
 from jax.experimental.pallas import tpu as pltpu
 from jax.sharding import PartitionSpec as P
 
@@ -244,39 +245,49 @@
     )(*left, *right)
 
 
-def join_kernel(where, own_ref, *refs):
-    parts, out_ref, sems = refs[:-2], refs[-2], refs[-1]
-    side, core = where[0], where[1]
-    size, count = own_ref.shape[0], parts[0].shape[0]
-    copies = [
-        pltpu.make_async_copy(
-            own_ref, out_ref.at[pl.ds(pl.multiple_of(side * size, 8), size)], sems.at[0]
+def join_kernel(own_blocks, part_blocks, where, own_ref, *refs):
+    parts, out_ref = refs[:-1], refs[-1]
+    i = pl.program_id(0)
+    inside = i - where[0] * own_blocks
+
+    @pl.when((inside >= 0) & (inside < own_blocks))
+    def _():
+        out_ref[...] = own_ref[...]
+
+    for s, part in enumerate(parts):
+        place = i - where[1 + s]
+
+        @pl.when((place >= 0) & (place < part_blocks))
+        def _(part=part):
+            out_ref[...] = part[...]
+
+
+def join_weights(side, starts, own, parts):
+    size, count = own.shape[0], parts[0].shape[0]
+    tile = count // 2 if count % 32 == 0 else count
+    own_blocks, part_blocks = size // tile, count // tile
+    where = jnp.stack([side] + [start * part_blocks for start in starts]).astype(jnp.int32)
+
+    def part_spec(s):
+        return pl.BlockSpec(
+            (tile, D), lambda i, w: (jnp.clip(i - w[1 + s], 0, part_blocks - 1), 0)
         )
-    ]
-    for s, part in enumerate(parts):
-        source = lax.rem(core - s + len(parts), len(parts))
-        start = pl.multiple_of((1 - side) * size + source * count, 8)
-        copies.append(
-            pltpu.make_async_copy(part, out_ref.at[pl.ds(start, count)], sems.at[1 + s])
-        )
-    for copy in copies:
-        copy.start()
-    for copy in copies:
-        copy.wait()
-
-
-def join_weights(where, own, parts):
-    anywhere = pl.BlockSpec(memory_space=pl.ANY)
+
     return pl.pallas_call(
-        join_kernel,
+        functools.partial(join_kernel, own_blocks, part_blocks),
         grid_spec=pltpu.PrefetchScalarGridSpec(
             num_scalar_prefetch=1,
-            grid=(1,),
-            in_specs=[anywhere] * (1 + len(parts)),
-            out_specs=anywhere,
-            scratch_shapes=[pltpu.SemaphoreType.DMA((1 + len(parts),))],
+            grid=(2 * own_blocks,),
+            in_specs=[
+                pl.BlockSpec(
+                    (tile, D),
+                    lambda i, w: (jnp.clip(i - w[0] * own_blocks, 0, own_blocks - 1), 0),
+                )
+            ]
+            + [part_spec(s) for s in range(len(parts))],
+            out_specs=pl.BlockSpec((tile, D), lambda i, w: (i, 0)),
         ),
-        out_shape=jax.ShapeDtypeStruct((2 * own.shape[0], own.shape[1]), own.dtype),
+        out_shape=jax.ShapeDtypeStruct((2 * size, D), own.dtype),
         name="join_weights",
     )(where, own, *parts)
 
@@ -379,7 +390,9 @@
         [jnp.stack(by_head, axis=2).reshape(-1, 2 * width), own_columns(w_value), own_columns(w_out)],
         axis=1,
     )
+    packed = with_layout_constraint(packed, Layout(major_to_minor=(0, 1)))
     gathered = lax.all_gather(packed, "fsdp", axis=0, tiled=True)
+    gathered = with_layout_constraint(gathered, Layout(major_to_minor=(0, 1)))
 
     halves = 2
     part_slots = capacity // halves
@@ -456,13 +469,13 @@
         for part in weight_parts
     ]
 
-    where = jnp.stack([my_side, core]).astype(jnp.int32)
+    starts = [(1 - my_side) * ctx_count + (core - s) % ctx_count for s in range(ctx_count)]
 
     def pair_weights(own, both):
         count = both.shape[0] // pair
         part = lax.dynamic_slice_in_dim(both, (1 - my_side) * count, count, axis=0)
         return join_weights(
-            where, own, [part] + [core_shift(part, s) for s in range(1, ctx_count)]
+            my_side, starts, own, [part] + [core_shift(part, s) for s in range(1, ctx_count)]
         )
 
     pre = dot(normed, full_qkv, 1, 0)

time: 2410 us -> 1390 us (0.58)
  Pallas kernels: 1360 us -> 347 us
    pallas_call x3, Pallas kernels: 1050 us -> 37.5 us  [join_weights(): pl.pallas_call(functools.partial(join_kernel, own_blocks, part_blocks), g...]
    all_gather x1, waiting for transfers between devices: 187 us -> 140 us  [shards(): gathered = lax.all_gather(packed, 'fsdp', axis=0, tiled=True)]
    all_gather x3, waiting for transfers between devices: 59.8 us -> 88.3 us  [shards(): lax.all_gather(part, 'fsdp', axis=0, tiled=True, axis_index_groups=sides)]
  transfers between devices with their start and end apart: 44 -> 44, of which waited for: 15 -> 18; matrix products, arithmetic and copies ran while one was open for 18% -> 32% of each run, Pallas kernels for 57% -> 25%
where the time goes in v4:
time: 1390 us; the launch traced here: 1380 us
  waiting for transfers between devices  464 us (33%)
  Pallas kernels  347 us (25%)
  matrix products  263 us (19%)
  other arithmetic  116 us (8%)
  starting transfers between devices  90.7 us (7%)
  local copies, waits for them, and re-layouts  86.5 us (6%)
  between operations  15.4 us (1%)
    dot_general x24, matrix products, dot(): lax.dot_general(a, b, (((ca,), (cb,)), ((), ())), preferred_element_type=...  263 us
    ppermute x14, waiting for transfers between devices, fsdp_shift(): return lax.ppermute(a, 'fsdp', [(i, move(i)) for i in range(fsdp_count)])  179 us
    all_gather x1, waiting for transfers between devices, shards(): gathered = lax.all_gather(packed, 'fsdp', axis=0, tiled=True)  140 us
    pallas_call x8, Pallas kernels, expert_rows(): pl.pallas_call(functools.partial(rows_kernel, len(left)), grid=(D // tile...  138 us
    pallas_call x4, Pallas kernels, expert_hidden(): pl.pallas_call(functools.partial(expert_kernel, len(kept)), grid=(units /...  122 us
    all_gather x3, waiting for transfers between devices, shards(): lax.all_gather(part, 'fsdp', axis=0, tiled=True, axis_index_groups=sides)  88.3 us
    all_to_all x10, starting transfers between devices, swap_experts(): lax.all_to_all(blocks, 'fsdp', 0, 0, axis_index_groups=lines, tiled=True)  54 us
    pallas_call x3, Pallas kernels, join_weights(): pl.pallas_call(functools.partial(join_kernel, own_blocks, part_blocks), g...  37.5 us
  transfers between devices with their start and end apart: 44, of which 18 were waited for; matrix products, arithmetic and copies ran while one was open for 32% of the time, Pallas kernels for 25%

profile of v4, /device:TPU:0, one launch (start us, length us, event | category | flops | bytes accessed | tf_op | source)
XLA Modules:
  0.0 1382.6 jit_solution(3042322569459591857)
XLA Ops:
  22.4 7.0 constant_dynamic-slice_fusion.16
  39.4 13.4 fusion.32
  52.8 13.6 fusion.31
  66.4 139.9 %all-gather.5.cloned.1.call-done = bf16[2048,4096]{1,0:T(8,128)(2,1)} async-done(((bf16[128,4096]{1,0:T(8,128)(2,1)}), bf16[2048,4096]{1,0:T(8,128)(2,1)}) %all-gather.5.cloned.1.call-update) | async-done | bytes 16777232 | tf_op jit(solution)/shard_map/all_gather | solution.py:394
  226.6 19.2 %fusion.2.pre_q.pre_k.pre_v = f32[1024,3072]{1,0:T(8,128)} fusion(bf16[2048,4096]{1,0:T(8,128)(2,1)} %all-gather.5.cloned.1.call-done, bf16[512,2048]{1,0:T(8,128)(2,1)} %collective-permute-done, bf16[512,2048]{1,0:T(8,128)(2,1)} %fusion.21), kind=kOutput, calls=%fused_computation.4 | convolution fusion | flops 12893290496 | bytes 29360128 | tf_op jit(solution)/shard_map/dot_general | solution.py:28
  245.7 21.7 %attention_forward.1 = (bf16[1024,1024]{1,0:T(8,128)(2,1)}, bf16[1024,1024]{1,0:T(8,128)(2,1)}, bf16[1024,1024]{1,0:T(8,128)(2,1)}, bf16[1024,1024]{1,0:T(8,128)(2,1)}, f32[1024,1024]{1,0:T(8,128)}) custom-call(s32[4]{0:T(128)} %fusion.126.perm, f32[1024,3072]{1,0:T(8,128)} %fusion.2.pre_q.pre_k.pre_v, f32[1024,3072]{1,0:T(8,128)} %fusion.2.pre_q.pre_k.pre_v, ...), custom_call_target="tpu_custom_call" | custom-call | tf_op jit(solution)/shard_map/attention_forward/pallas_call | solution.py:156
  305.5 51.6 %all-gather.9.cloned.1.call-done = bf16[1408,2048]{1,0:T(8,128)(2,1)} async-done(((bf16[704,2048]{1,0:T(8,128)(2,1)}), bf16[1408,2048]{1,0:T(8,128)(2,1)}) %all-gather.9.cloned.1.call-update) | async-done | bytes 5767184 | tf_op jit(solution)/shard_map/all_gather | solution.py:468
  371.3 12.7 join_weights.3.wg_ref.refs_2_
  384.0 12.4 join_weights.4.wu_ref.refs_3_
  396.4 36.6 %all-gather.11.cloned.1.call-done = bf16[1408,2048]{1,0:T(8,128)(2,1)} async-done(((bf16[704,2048]{1,0:T(8,128)(2,1)}), bf16[1408,2048]{1,0:T(8,128)(2,1)}) %all-gather.11.cloned.1.call-update) | async-done | bytes 5767184 | tf_op jit(solution)/shard_map/all_gather | solution.py:468
  445.3 12.4 join_weights.5.wd_ref.refs_1_
  457.7 30.6 %expert_hidden.4 = (bf16[2560,2816]{1,0:T(8,128)(2,1)}, bf16[2560,2816]{1,0:T(8,128)(2,1)}, bf16[2560,2816]{1,0:T(8,128)(2,1)}) custom-call(bf16[640,2048]{1,0:T(8,128)(2,1)} %bitcast.122, bf16[640,2048]{1,0:T(8,128)(2,1)} %bitcast.13.g_ref, bf16[2816,2048]{1,0:T(8,128)(2,1)} %join_weights.3.wg_ref.refs_2_, bf16[2816,2048]{1,0:T(8,128)(2,1)} %join_weights.4.wu_ref.refs_3_, ...), custom_call_target="tpu_custom_call" | custom-call | tf_op jit(solution)/shard_map/expert_hidden/pallas_call | solution.py:217
  488.3 11.1 collective-permute-done.8.x_ref
  500.8 30.6 %expert_hidden.5 = (bf16[2560,2816]{1,0:T(8,128)(2,1)}, bf16[2560,2816]{1,0:T(8,128)(2,1)}, bf16[2560,2816]{1,0:T(8,128)(2,1)}) custom-call(bf16[640,2048]{1,0:T(8,128)(2,1)} %collective-permute-done.8.x_ref, bf16[640,2048]{1,0:T(8,128)(2,1)} %collective-permute-done.3.g_ref, ...), custom_call_target="tpu_custom_call", output_to_operand_aliasing={{0}: (5, {}), {1}: (6, {}), {2}: (7, {})} | custom-call | tf_op jit(solution)/shard_map/expert_hidden/pallas_call | solution.py:217
  531.4 21.1 %expert_rows.8 = bf16[640,2048]{1,0:T(8,128)(2,1)} custom-call(bf16[2560,2816]{1,0:T(8,128)(2,1)} %get-tuple-element.179.refs_0_.refs_1_, bf16[2560,2816]{1,0:T(8,128)(2,1)} %get-tuple-element.180.refs_1_.refs_2_, bf16[2816,2048]{1,0:T(8,128)(2,1)} %join_weights.3.wg_ref.refs_2_, bf16[2816,2048]{1,0:T(8,128)(2,1)} %join_weights.4.wu_ref.refs_3_), custom_call_target="tpu_custom_call" | custom-call | tf_op jit(solution)/shard_map/expert_rows/pallas_call | solution.py:237
  559.4 21.1 %expert_rows.9 = bf16[640,2048]{1,0:T(8,128)(2,1)} custom-call(bf16[2560,2816]{1,0:T(8,128)(2,1)} %get-tuple-element.179.refs_0_.refs_1_, bf16[2560,2816]{1,0:T(8,128)(2,1)} %get-tuple-element.180.refs_1_.refs_2_, bf16[2816,2048]{1,0:T(8,128)(2,1)} %join_weights.3.wg_ref.refs_2_, bf16[2816,2048]{1,0:T(8,128)(2,1)} %join_weights.4.wu_ref.refs_3_), custom_call_target="tpu_custom_call" | custom-call | tf_op jit(solution)/shard_map/expert_rows/pallas_call | solution.py:237
  580.5 30.6 %expert_hidden.6 = (bf16[2560,2816]{1,0:T(8,128)(2,1)}, bf16[2560,2816]{1,0:T(8,128)(2,1)}, bf16[2560,2816]{1,0:T(8,128)(2,1)}) custom-call(bf16[640,2048]{1,0:T(8,128)(2,1)} %bitcast.22.x_ref, bf16[640,2048]{1,0:T(8,128)(2,1)} %bitcast.15.g_ref, ...), custom_call_target="tpu_custom_call", output_to_operand_aliasing={{0}: (5, {}), {1}: (6, {}), {2}: (7, {})} | custom-call | tf_op jit(solution)/shard_map/expert_hidden/pallas_call | solution.py:217
  637.5 30.7 %expert_hidden.7 = (bf16[2560,2816]{1,0:T(8,128)(2,1)}, bf16[2560,2816]{1,0:T(8,128)(2,1)}, bf16[2560,2816]{1,0:T(8,128)(2,1)}) custom-call(bf16[640,2048]{1,0:T(8,128)(2,1)} %copy-done.15, bf16[640,2048]{1,0:T(8,128)(2,1)} %collective-permute-done.6.g_ref, ...), custom_call_target="tpu_custom_call", output_to_operand_aliasing={{0}: (5, {}), {1}: (6, {}), {2}: (7, {})} | custom-call | tf_op jit(solution)/shard_map/expert_hidden/pallas_call | solution.py:217
  668.2 21.1 %expert_rows.10 = bf16[640,2048]{1,0:T(8,128)(2,1)} custom-call(bf16[2560,2816]{1,0:T(8,128)(2,1)} %get-tuple-element.213.refs_0_, bf16[2560,2816]{1,0:T(8,128)(2,1)} %get-tuple-element.239.refs_1_, bf16[2816,2048]{1,0:T(8,128)(2,1)} %join_weights.3.wg_ref.refs_2_, bf16[2816,2048]{1,0:T(8,128)(2,1)} %join_weights.4.wu_ref.refs_3_), custom_call_target="tpu_custom_call" | custom-call | tf_op jit(solution)/shard_map/expert_rows/pallas_call | solution.py:237
  690.8 21.1 %expert_rows.11 = bf16[640,2048]{1,0:T(8,128)(2,1)} custom-call(bf16[2560,2816]{1,0:T(8,128)(2,1)} %get-tuple-element.213.refs_0_, bf16[2560,2816]{1,0:T(8,128)(2,1)} %get-tuple-element.239.refs_1_, bf16[2816,2048]{1,0:T(8,128)(2,1)} %join_weights.3.wg_ref.refs_2_, bf16[2816,2048]{1,0:T(8,128)(2,1)} %join_weights.4.wu_ref.refs_3_), custom_call_target="tpu_custom_call" | custom-call | tf_op jit(solution)/shard_map/expert_rows/pallas_call | solution.py:237
  711.8 38.7 %convolution_convert_fusion.2 = bf16[2816,2048]{1,0:T(8,128)(2,1)} fusion(bf16[2560,2816]{1,0:T(8,128)(2,1)} %get-tuple-element.247.refs_0_, bf16[640,2048]{1,0:T(8,128)(2,1)} %collective-permute-done.6.g_ref, bf16[640,2048]{1,0:T(8,128)(2,1)} %bitcast.15.g_ref, bf16[640,2048]{1,0:T(8,128)(2,1)} %collective-permute-done.3.g_ref, ...), kind=kOutput, calls=%fused_computation.11 | convolution fusion | flops 29575610368 | bytes 36438016 | tf_op jit(solution)/shard_map/dot_general | solution.py:28
  764.0 38.6 %convolution_convert_fusion.1 = bf16[2816,2048]{1,0:T(8,128)(2,1)} fusion(bf16[2560,2816]{1,0:T(8,128)(2,1)} %get-tuple-element.213.refs_0_, bf16[2560,2048]{1,0:T(8,128)(2,1)} %constant_dynamic-update-slice_fusion), kind=kOutput, calls=%fused_computation.10 | convolution fusion | flops 29533667328 | bytes 36438016 | tf_op jit(solution)/shard_map/dot_general | solution.py:28
  802.6 13.4 expert_rows.12
  816.0 13.5 expert_rows.13
  835.8 9.8 add_convert_fusion.2
  855.7 7.4 add_convert_fusion.1
  863.2 7.3 convolution_convert_fusion.4
  886.1 27.1 %attention_backward.1 = (bf16[1024,2048]{1,0:T(8,128)(2,1)}, bf16[1024,1024]{1,0:T(8,128)(2,1)}) custom-call(s32[4]{0:T(128)} %fusion.126.perm, bf16[1024,1024]{1,0:T(8,128)(2,1)} %get-tuple-element.141.q_ref, bf16[1024,1024]{1,0:T(8,128)(2,1)} %get-tuple-element.142.k_ref, bf16[1024,1024]{1,0:T(8,128)(2,1)} %get-tuple-element.143.v_ref, ...), custom_call_target="tpu_custom_call" | custom-call | tf_op jit(solution)/shard_map/attention_backward/pallas_call | solution.py:179
  913.2 14.2 %convolution_convert_fusion.3 = bf16[2048,2048]{1,0:T(8,128)(2,1)} fusion(bf16[1024,2048]{1,0:T(8,128)(2,1)} %fusion.31, bf16[1024,2048]{1,0:T(8,128)(2,1)} %get-tuple-element.233), kind=kOutput, calls=%fused_computation.21 | convolution fusion | flops 8594128896 | bytes 16777216 | tf_op jit(solution)/shard_map/dot_general | solution.py:28
  927.5 23.4 %reduce-scatter.3.cloned.1.call-done = bf16[1408,1024]{1,0:T(8,128)(2,1)} async-done(((bf16[2816,1024]{1,0:T(8,128)(2,1)}), bf16[1408,1024]{1,0:T(8,128)(2,1)}) %reduce-scatter.3.cloned.1.call-update) | async-done | bytes 2883600 | tf_op jit(solution)/shard_map/reduce_scatter | solution.py:578
  963.4 13.4 expert_rows.14
  976.9 7.1 fusion.35
  988.7 10.4 fusion.37
  999.2 11.8 collective-permute-done.16
  1011.0 9.7 add_convert_fusion.10
  1032.4 7.0 all-to-all-start.6
  1041.4 45.0 %collective-permute-done.20 = bf16[256,2048]{1,0:T(8,128)(2,1)} collective-permute-done((bf16[256,2048]{1,0:T(8,128)(2,1)}, bf16[256,2048]{1,0:T(8,128)(2,1)}, u32[]{:S(2)}, u32[]{:S(2)}) %collective-permute-start.20) | collective-permute-done | bytes 1048608 | tf_op jit(solution)/shard_map/ppermute | solution.py:359
  1093.8 6.6 fusion.27
  1100.5 9.4 collective-permute-done.19
  1109.9 36.2 %convolution_convert_fusion = bf16[2816,2048]{1,0:T(8,128)(2,1)} fusion(bf16[2560,2816]{1,0:T(8,128)(2,1)S(1)} %bitcast.120, bf16[2560,2048]{1,0:T(8,128)(2,1)} %constant_dynamic-update-slice_fusion), kind=kOutput, calls=%fused_computation.9 | convolution fusion | flops 29533667328 | bytes 36438016 | tf_op jit(solution)/shard_map/dot_general | solution.py:28
  1146.1 39.4 %collective-permute-done.21 = bf16[1024,1024]{1,0:T(8,128)(2,1)} collective-permute-done((bf16[1024,1024]{1,0:T(8,128)(2,1)}, bf16[1024,1024]{1,0:T(8,128)(2,1)}, u32[]{:S(2)}, u32[]{:S(2)}) %collective-permute-start.21) | collective-permute-done | bytes 2097184 | tf_op jit(solution)/shard_map/ppermute | solution.py:359
  1191.3 7.6 all-to-all-start.7
  1203.1 10.3 collective-permute-start.23
  1214.2 13.5 expert_rows.15
  1227.7 10.2 collective-permute-done.23
  1246.9 10.0 add_convert_fusion
  1266.2 20.2 %all-to-all-done.10 = bf16[4,128,1024]{2,1,0:T(8,128)(2,1)} async-done(((bf16[4,128,1024]{2,1,0:T(8,128)(2,1)}), bf16[4,128,1024]{2,1,0:T(8,128)(2,1)}, u32[]{:S(2)}, u32[]{:S(2)}) %all-to-all-start.10) | async-done | bytes 1048608 | tf_op jit(solution)/shard_map/all_to_all | solution.py:458
  1316.9 41.9 %collective-permute-done.26 = bf16[1408,1024]{1,0:T(8,128)(2,1)} collective-permute-done((bf16[1408,1024]{1,0:T(8,128)(2,1)}, bf16[1408,1024]{1,0:T(8,128)(2,1)}, u32[]{:S(2)}, u32[]{:S(2)}) %collective-permute-start.26) | collective-permute-done | bytes 2883616 | tf_op jit(solution)/shard_map/ppermute | solution.py:359
  (317 shorter events, 306.0 us)
Async XLA Ops:
  7.2 199.1 %all-gather.5.cloned.1.call-start = ((), (), s32[]{:S(2)}) async-start(), calls=%async_computation.13 | async-start | bytes 17825792 | tf_op jit(solution)/shard_map/all_gather | solution.py:394
  11.8 293.7 %all-gather.7.cloned.1.call-start = ((), (), s32[]{:S(2)}) async-start(), calls=%async_computation.14 | async-start | bytes 8650752 | tf_op jit(solution)/shard_map/all_gather | solution.py:468
  14.2 25.2 %collective-permute-start = (bf16[512,2048]{1,0:T(8,128)(2,1)}, bf16[512,2048]{1,0:T(8,128)(2,1)}, u32[]{:S(2)}, u32[]{:S(2)}) collective-permute-start(bf16[512,2048]{1,0:T(8,128)(2,1)} %fusion.21), channel_id=1, source_target_pairs={{0,16},{16,0},{1,17},{17,1},{2,18},{18,2},{3,19},{19,3},{4,20},{20... | collective-permute-start | bytes 6291464 | tf_op jit(solution)/shard_map/ppermute | solution.py:356
  18.6 271.0 %copy-start.34 = (s32[512]{0:T(512)}, s32[512]{0:T(512)S(1)}, u32[]{:S(2)}) copy-start(s32[512]{0:T(512)S(1)} %get-tuple-element.269) | copy-start | bytes 6148
  18.6 271.0 %copy-start.37 = (s32[512]{0:T(512)}, s32[512]{0:T(512)S(1)}, u32[]{:S(2)}) copy-start(s32[512]{0:T(512)S(1)} %get-tuple-element.270) | copy-start | bytes 6148
  52.8 153.6 %copy-start.53 = (s32[1,4]{1,0:T(1,128)S(1)}, s32[1,4]{1,0:T(1,128)}, u32[]{:S(2)}) copy-start(s32[1,4]{1,0:T(1,128)} %param.17) | copy-start | bytes 52
  206.3 150.8 %all-gather.9.cloned.1.call-start = ((), (), s32[]{:S(2)}) async-start(), calls=%async_computation.15 | async-start | bytes 8650752 | tf_op jit(solution)/shard_map/all_gather | solution.py:468
  218.6 64.2 %all-to-all-start = ((bf16[4,160,2048]{2,1,0:T(8,128)(2,1)}), bf16[4,160,2048]{2,1,0:T(8,128)(2,1)}, u32[]{:S(2)}, u32[]{:S(2)}) async-start(bf16[4,160,2048]{2,1,0:T(8,128)(2,1)} %bitcast.138), calls=%async_computation | async-start | bytes 5242880 | tf_op jit(solution)/shard_map/all_to_all | solution.py:458
  226.6 40.9 %collective-permute-start.1 = (bf16[1024,1024]{1,0:T(8,128)(2,1)}, bf16[1024,1024]{1,0:T(8,128)(2,1)}, u32[]{:S(2)}, u32[]{:S(2)}) collective-permute-start(bf16[1024,1024]{1,0:T(8,128)(2,1)} %constant_dynamic-slice_fusion.15), channel_id=1, source_target_pairs={{0,16},{16,0},{1,17},{17,1},{2,18},{18,2},{3,19},{19,3},{4,20},{20... | collective-permute-start | bytes 6291464 | tf_op jit(solution)/shard_map/ppermute | solution.py:356
  282.8 74.3 %all-to-all-start.1 = ((bf16[4,160,2048]{2,1,0:T(8,128)(2,1)}), bf16[4,160,2048]{2,1,0:T(8,128)(2,1)}, u32[]{:S(2)}, u32[]{:S(2)}) async-start(bf16[4,160,2048]{2,1,0:T(8,128)(2,1)} %bitcast.137), calls=%async_computation.1 | async-start | bytes 5242880 | tf_op jit(solution)/shard_map/all_to_all | solution.py:458
  287.4 145.6 %all-gather.11.cloned.1.call-start = ((), (), s32[]{:S(2)}) async-start(), calls=%async_computation.16 | async-start | bytes 8650752 | tf_op jit(solution)/shard_map/all_gather | solution.py:468
  288.0 4.6 collective-permute-start.2
  288.0 69.1 %collective-permute-start.3 = (bf16[640,2048]{1,0:T(8,128)(2,1)}, bf16[640,2048]{1,0:T(8,128)(2,1)}, u32[]{:S(2)}, u32[]{:S(2)}) collective-permute-start(bf16[640,2048]{1,0:T(8,128)(2,1)} %bitcast.13.g_ref), channel_id=1, source_target_pairs={{0,2},{1,3},{2,0},{3,1},{4,6},{5,7},{6,4},{7,5},{8,10},{9,11},{10,... | collective-permute-start | bytes 7864328 | tf_op jit(solution)/shard_map/ppermute | solution.py:359
  357.1 75.9 %all-to-all-start.2 = ((bf16[4,160,2048]{2,1,0:T(8,128)(2,1)}), bf16[4,160,2048]{2,1,0:T(8,128)(2,1)S(1)}, u32[]{:S(2)}, u32[]{:S(2)}) async-start(bf16[4,160,2048]{2,1,0:T(8,128)(2,1)} %bitcast.140), calls=%async_computation.2 | async-start | bytes 5242880 | tf_op jit(solution)/shard_map/all_to_all | solution.py:458
  365.6 5.6 collective-permute-start.4
  368.4 15.6 %collective-permute-start.5 = (bf16[704,2048]{1,0:T(8,128)(2,1)}, bf16[704,2048]{1,0:T(8,128)(2,1)}, u32[]{:S(2)}, u32[]{:S(2)}) collective-permute-start(bf16[704,2048]{1,0:T(8,128)(2,1)} %constant_dynamic-slice_fusion.13.refs_0_), channel_id=1, source_target_pairs={{0,16},{16,0},{1,17},{17,1},{2,18},{18,2},{3,19},{19,3},{4,20},{20... | collective-permute-start | bytes 8650760 | tf_op jit(solution)/shard_map/ppermute | solution.py:356
  368.4 64.7 %collective-permute-start.6 = (bf16[640,2048]{1,0:T(8,128)(2,1)}, bf16[640,2048]{1,0:T(8,128)(2,1)}, u32[]{:S(2)}, u32[]{:S(2)}) collective-permute-start(bf16[640,2048]{1,0:T(8,128)(2,1)} %bitcast.15.g_ref), channel_id=1, source_target_pairs={{0,2},{1,3},{2,0},{3,1},{4,6},{5,7},{6,4},{7,5},{8,10},{9,11},{10,... | collective-permute-start | bytes 7864328 | tf_op jit(solution)/shard_map/ppermute | solution.py:359
  433.0 66.3 %all-to-all-start.3 = ((bf16[4,160,2048]{2,1,0:T(8,128)(2,1)}), bf16[4,160,2048]{2,1,0:T(8,128)(2,1)}, u32[]{:S(2)}, u32[]{:S(2)}) async-start(bf16[4,160,2048]{2,1,0:T(8,128)(2,1)} %bitcast.139), calls=%async_computation.3 | async-start | bytes 5242880 | tf_op jit(solution)/shard_map/all_to_all | solution.py:458
  439.9 5.5 collective-permute-start.7
  440.0 59.4 %collective-permute-start.8 = (bf16[640,2048]{1,0:T(8,128)(2,1)S(1)}, bf16[640,2048]{1,0:T(8,128)(2,1)}, u32[]{:S(2)}, u32[]{:S(2)}) collective-permute-start(bf16[640,2048]{1,0:T(8,128)(2,1)S(1)} %bitcast.121), channel_id=1, source_target_pairs={{0,2},{1,3},{2,0},{3,1},{4,6},{5,7},{6,4},{7,5},{8,10},{9,11},{10,... | collective-permute-start | bytes 7864328 | tf_op jit(solution)/shard_map/ppermute | solution.py:359
  499.3 58.6 %collective-permute-start.9 = (bf16[640,2048]{1,0:T(8,128)(2,1)}, bf16[640,2048]{1,0:T(8,128)(2,1)S(1)}, u32[]{:S(2)}, u32[]{:S(2)}) collective-permute-start(bf16[640,2048]{1,0:T(8,128)(2,1)} %bitcast.22.x_ref), channel_id=1, source_target_pairs={{0,2},{1,3},{2,0},{3,1},{4,6},{5,7},{6,4},{7,5},{8,10},{9,11},{10,... | collective-permute-start | bytes 7864328 | tf_op jit(solution)/shard_map/ppermute | solution.py:359
  558.0 57.8 %collective-permute-start.10 = (bf16[640,2048]{1,0:T(8,128)(2,1)}, bf16[640,2048]{1,0:T(8,128)(2,1)}, u32[]{:S(2)}, u32[]{:S(2)}) collective-permute-start(bf16[640,2048]{1,0:T(8,128)(2,1)} %expert_rows.8), channel_id=1, source_target_pairs={{0,2},{1,3},{2,0},{3,1},{4,6},{5,7},{6,4},{7,5},{8,10},{9,11},{10,... | collective-permute-start | bytes 7864328 | tf_op jit(solution)/shard_map/ppermute | solution.py:359
  621.1 69.7 %all-to-all-start.4 = ((bf16[4,160,2048]{2,1,0:T(8,128)(2,1)}), bf16[4,160,2048]{2,1,0:T(8,128)(2,1)}, u32[]{:S(2)}, u32[]{:S(2)}) async-start(bf16[4,160,2048]{2,1,0:T(8,128)(2,1)} %bitcast.129), calls=%async_computation.4 | async-start | bytes 5242880 | tf_op jit(solution)/shard_map/all_to_all | solution.py:458
  689.3 61.2 %collective-permute-start.11 = (bf16[640,2048]{1,0:T(8,128)(2,1)}, bf16[640,2048]{1,0:T(8,128)(2,1)S(1)}, u32[]{:S(2)}, u32[]{:S(2)}) collective-permute-start(bf16[640,2048]{1,0:T(8,128)(2,1)} %expert_rows.10), channel_id=1, source_target_pairs={{0,2},{1,3},{2,0},{3,1},{4,6},{5,7},{6,4},{7,5},{8,10},{9,11},{10,... | collective-permute-start | bytes 7864328 | tf_op jit(solution)/shard_map/ppermute | solution.py:359
  753.1 92.6 %all-to-all-start.5 = ((bf16[4,160,2048]{2,1,0:T(8,128)(2,1)}), bf16[4,160,2048]{2,1,0:T(8,128)(2,1)S(1)}, u32[]{:S(2)}, u32[]{:S(2)}) async-start(bf16[4,160,2048]{2,1,0:T(8,128)(2,1)} %bitcast.128), calls=%async_computation.5 | async-start | bytes 5242880 | tf_op jit(solution)/shard_map/all_to_all | solution.py:458
  758.2 192.6 %reduce-scatter.3.cloned.1.call-start = ((), (), s32[]{:S(2)}) async-start(), calls=%async_computation.17 | async-start | bytes 8650752 | tf_op jit(solution)/shard_map/reduce_scatter | solution.py:578
  764.0 71.8 %collective-permute-start.12 = (bf16[2816,1024]{1,0:T(8,128)(2,1)}, bf16[2816,1024]{1,0:T(8,128)(2,1)}, u32[]{:S(2)}, u32[]{:S(2)}) collective-permute-start(bf16[2816,1024]{1,0:T(8,128)(2,1)} %constant_dynamic-slice_fusion.11), channel_id=1, source_target_pairs={{0,16},{16,0},{1,17},{17,1},{2,18},{18,2},{3,19},{19,3},{4,20},{20... | collective-permute-start | bytes 17301512 | tf_op jit(solution)/shard_map/ppermute | solution.py:356
  835.3 20.4 %collective-permute-start.14 = (bf16[2816,1024]{1,0:T(8,128)(2,1)}, bf16[2816,1024]{1,0:T(8,128)(2,1)}, u32[]{:S(2)}, u32[]{:S(2)}) collective-permute-start(bf16[2816,1024]{1,0:T(8,128)(2,1)} %constant_dynamic-slice_fusion.10), channel_id=1, source_target_pairs={{0,16},{16,0},{1,17},{17,1},{2,18},{18,2},{3,19},{19,3},{4,20},{20... | collective-permute-start | bytes 17301512 | tf_op jit(solution)/shard_map/ppermute | solution.py:356
  845.7 411.2 %reduce-scatter.5.cloned.1.call-start = ((), (), s32[]{:S(2)}) async-start(), calls=%async_computation.18 | async-start | bytes 8912896 | tf_op jit(solution)/shard_map/reduce_scatter | solution.py:653
  855.2 8.0 collective-permute-start.13
  855.2 100.8 %collective-permute-start.15 = (bf16[640,2048]{1,0:T(8,128)(2,1)}, bf16[640,2048]{1,0:T(8,128)(2,1)}, u32[]{:S(2)}, u32[]{:S(2)}) collective-permute-start(bf16[640,2048]{1,0:T(8,128)(2,1)} %expert_rows.13), channel_id=1, source_target_pairs={{0,2},{1,3},{2,0},{3,1},{4,6},{5,7},{6,4},{7,5},{8,10},{9,11},{10,... | collective-permute-start | bytes 7864328 | tf_op jit(solution)/shard_map/ppermute | solution.py:359
  878.4 132.6 %collective-permute-start.16 = (bf16[1408,1024]{1,0:T(8,128)(2,1)}, bf16[1408,1024]{1,0:T(8,128)(2,1)}, u32[]{:S(2)}, u32[]{:S(2)}) collective-permute-start(bf16[1408,1024]{1,0:T(8,128)(2,1)} %get-tuple-element.273), channel_id=1, source_target_pairs={{0,1},{1,0},{2,3},{3,2},{4,5},{5,4},{6,7},{7,6},{8,9},{9,8},{10,11... | collective-permute-start | bytes 8650760 | tf_op jit(solution)/shard_map/ppermute | solution.py:359
  878.8 120.4 %collective-permute-start.17 = (bf16[512,2048]{1,0:T(8,128)(2,1)}, bf16[512,2048]{1,0:T(8,128)(2,1)}, u32[]{:S(2)}, u32[]{:S(2)}) collective-permute-start(bf16[512,2048]{1,0:T(8,128)(2,1)} %bitcast.28), channel_id=1, source_target_pairs={{0,2},{1,3},{2,0},{3,1},{4,6},{5,7},{6,4},{7,5},{8,10},{9,11},{10,... | collective-permute-start | bytes 6291464 | tf_op jit(solution)/shard_map/ppermute | solution.py:359
  1020.6 68.5 %collective-permute-start.18 = (bf16[512,2048]{1,0:T(8,128)(2,1)}, bf16[512,2048]{1,0:T(8,128)(2,1)}, u32[]{:S(2)}, u32[]{:S(2)}) collective-permute-start(bf16[512,2048]{1,0:T(8,128)(2,1)} %add_convert_fusion.10), channel_id=1, source_target_pairs={{0,16},{16,0},{1,17},{17,1},{2,18},{18,2},{3,19},{19,3},{4,20},{20... | collective-permute-start | bytes 6291464 | tf_op jit(solution)/shard_map/ppermute | solution.py:356
  1024.4 62.0 %collective-permute-start.20 = (bf16[256,2048]{1,0:T(8,128)(2,1)}, bf16[256,2048]{1,0:T(8,128)(2,1)}, u32[]{:S(2)}, u32[]{:S(2)}) collective-permute-start(bf16[256,2048]{1,0:T(8,128)(2,1)} %bitcast.31), channel_id=1, source_target_pairs={{0,1},{1,0},{2,3},{3,2},{4,5},{5,4},{6,7},{7,6},{8,9},{9,8},{10,11... | collective-permute-start | bytes 3145736 | tf_op jit(solution)/shard_map/ppermute | solution.py:359
  1026.8 83.0 %collective-permute-start.19 = (bf16[640,2048]{1,0:T(8,128)(2,1)}, bf16[640,2048]{1,0:T(8,128)(2,1)}, u32[]{:S(2)}, u32[]{:S(2)}) collective-permute-start(bf16[640,2048]{1,0:T(8,128)(2,1)} %expert_rows.14), channel_id=1, source_target_pairs={{0,2},{1,3},{2,0},{3,1},{4,6},{5,7},{6,4},{7,5},{8,10},{9,11},{10,... | collective-permute-start | bytes 7864328 | tf_op jit(solution)/shard_map/ppermute | solution.py:359
  1032.4 56.7 %copy-start.33 = (f32[512]{0:T(512)S(1)}, f32[512]{0:T(512)}, u32[]{:S(2)}) copy-start(f32[512]{0:T(512)} %copy-done.32) | copy-start | bytes 6148
  1032.4 153.0 %all-to-all-start.6 = ((bf16[4,160,2048]{2,1,0:T(8,128)(2,1)}), bf16[4,160,2048]{2,1,0:T(8,128)(2,1)}, u32[]{:S(2)}, u32[]{:S(2)}) async-start(bf16[4,160,2048]{2,1,0:T(8,128)(2,1)} %bitcast.127), calls=%async_computation.7 | async-start | bytes 5242880 | tf_op jit(solution)/shard_map/all_to_all | solution.py:458
  1039.4 146.0 %collective-permute-start.21 = (bf16[1024,1024]{1,0:T(8,128)(2,1)}, bf16[1024,1024]{1,0:T(8,128)(2,1)}, u32[]{:S(2)}, u32[]{:S(2)}) collective-permute-start(bf16[1024,1024]{1,0:T(8,128)(2,1)} %fusion.58), channel_id=1, source_target_pairs={{0,1},{1,0},{2,3},{3,2},{4,5},{5,4},{6,7},{7,6},{8,9},{9,8},{10,11... | collective-permute-start | bytes 6291464 | tf_op jit(solution)/shard_map/ppermute | solution.py:359
  1191.3 55.7 %collective-permute-start.22 = (bf16[2816,1024]{1,0:T(8,128)(2,1)}, bf16[2816,1024]{1,0:T(8,128)(2,1)}, u32[]{:S(2)}, u32[]{:S(2)}) collective-permute-start(bf16[2816,1024]{1,0:T(8,128)(2,1)} %constant_dynamic-slice_fusion.3), channel_id=1, source_target_pairs={{0,16},{16,0},{1,17},{17,1},{2,18},{18,2},{3,19},{19,3},{4,20},{20... | collective-permute-start | bytes 17301512 | tf_op jit(solution)/shard_map/ppermute | solution.py:356
  1191.3 49.2 %all-to-all-start.7 = ((bf16[4,64,2048]{2,1,0:T(8,128)(2,1)}), bf16[4,64,2048]{2,1,0:T(8,128)(2,1)S(1)}, u32[]{:S(2)}, u32[]{:S(2)}) async-start(bf16[4,64,2048]{2,1,0:T(8,128)(2,1)} %bitcast.33), calls=%async_computation.8 | async-start | bytes 2097152 | tf_op jit(solution)/shard_map/all_to_all | solution.py:458
  1203.1 34.8 %collective-permute-start.23 = (bf16[512,1024]{1,0:T(8,128)(2,1)}, bf16[512,1024]{1,0:T(8,128)(2,1)}, u32[]{:S(2)}, u32[]{:S(2)}) collective-permute-start(bf16[512,1024]{1,0:T(8,128)(2,1)} %slice.138), channel_id=1, source_target_pairs={{0,2},{1,3},{2,0},{3,1},{4,6},{5,7},{6,4},{7,5},{8,10},{9,11},{10,... | collective-permute-start | bytes 3145736 | tf_op jit(solution)/shard_map/ppermute | solution.py:359
  1240.5 16.4 %all-to-all-start.9 = ((f32[16,1,256]{2,1,0:T(1,128)}), f32[16,1,256]{2,1,0:T(1,128)S(1)}, u32[]{:S(2)}, u32[]{:S(2)}) async-start(f32[16,1,256]{2,1,0:T(1,128)} %reshape.371), calls=%async_computation.11 | async-start | bytes 32768 | tf_op jit(solution)/shard_map/all_to_all | solution.py:697
  1256.9 29.5 %all-to-all-start.10 = ((bf16[4,128,1024]{2,1,0:T(8,128)(2,1)}), bf16[4,128,1024]{2,1,0:T(8,128)(2,1)}, u32[]{:S(2)}, u32[]{:S(2)}) async-start(bf16[4,128,1024]{2,1,0:T(8,128)(2,1)} %bitcast.135), calls=%async_computation.12 | async-start | bytes 2097152 | tf_op jit(solution)/shard_map/all_to_all | solution.py:458
  1286.4 78.0 %all-to-all-start.8 = ((bf16[4,160,2048]{2,1,0:T(8,128)(2,1)}), bf16[4,160,2048]{2,1,0:T(8,128)(2,1)}, u32[]{:S(2)}, u32[]{:S(2)}) async-start(bf16[4,160,2048]{2,1,0:T(8,128)(2,1)} %bitcast.126), calls=%async_computation.10 | async-start | bytes 5242880 | tf_op jit(solution)/shard_map/all_to_all | solution.py:458
  1295.0 63.8 %collective-permute-start.26 = (bf16[1408,1024]{1,0:T(8,128)(2,1)}, bf16[1408,1024]{1,0:T(8,128)(2,1)}, u32[]{:S(2)}, u32[]{:S(2)}) collective-permute-start(bf16[1408,1024]{1,0:T(8,128)(2,1)} %constant_dynamic-slice_fusion), channel_id=1, source_target_pairs={{0,1},{1,0},{2,3},{3,2},{4,5},{5,4},{6,7},{7,6},{8,9},{9,8},{10,11... | collective-permute-start | bytes 8650760 | tf_op jit(solution)/shard_map/ppermute | solution.py:359
  1297.8 17.2 %collective-permute-start.24 = (f32[2,64]{1,0:T(2,128)S(1)}, f32[2,64]{1,0:T(2,128)S(1)}, u32[]{:S(2)}, u32[]{:S(2)}) collective-permute-start(f32[2,64]{1,0:T(2,128)S(1)} %bitcast.155), channel_id=1, source_target_pairs={{0,16},{16,0},{1,17},{17,1},{2,18},{18,2},{3,19},{19,3},{4,20},{20... | collective-permute-start | bytes 1544 | tf_op jit(solution)/shard_map/ppermute | solution.py:356
  1308.4 7.1 collective-permute-start.25
  (57 other events, 595.2 us)
Sparse Core Ops, SparseCore 0:
  11.9 194.3 all-gather.4
  208.4 72.6 all-gather.6
  282.6 74.4 all-gather.8
  358.5 74.4 all-gather.10
  845.8 104.9 reduce-scatter.2
  953.1 264.4 reduce-scatter.4

commit v5 on v4

--- a/solution.py
+++ b/solution.py
@@ -537,30 +537,32 @@
         return total.astype(bf16)
 
     slot_parts = to_columns(first)
-    state, back, came = (), {}, []
-    home_first = None
+    back, came = {}, [None] * halves
+    state = hidden_part(0, slot_parts[0], ())
+    second, *got = after(second, *state, *slot_parts[1:])
+    state, slot_parts[1:] = got[:3], got[3:]
+    slot_parts += to_columns(second)
     for h in range(halves):
-        for j in range(columns):
+        for j in range(1, columns):
             index = h * columns + j
             state = hidden_part(index, slot_parts[index], state)
-            if index == 0:
-                second, *got = after(second, *state, *slot_parts[1:])
-                state, slot_parts[1:] = got[:3], got[3:]
-                slot_parts += to_columns(second)
-            if h == 1 and j == 0:
-                tied = after(*state, *came[0])
-                home_first = add_parts(back[0], tied[3:])
-                *state, home_first = after(*tied[:3], home_first)
-                home_first = swap_experts(home_first)
-        for j in [*range(1, columns), 0]:
+        for j in range(1, columns):
             index = h * columns + j
             back[index] = grad_rows(index, state)
-            tied = after(back[index], *state, *slot_parts[(1 + h) * columns + 1 :])
-            back[index], state = tied[0], tied[1:4]
-            slot_parts[(1 + h) * columns + 1 :] = tied[4:]
-            if h == 1 and j == columns - 1:
-                home_first, *state = after(home_first, *state)
-        came.append(columns_home([back[h * columns + j] for j in range(1, columns)]))
+            back[index], *state = after(back[index], *state)
+        if h == 0:
+            got = after(*state, *slot_parts[columns + 1 :])
+            state, slot_parts[columns + 1 :] = got[:3], got[3:]
+        came[h] = columns_home([back[h * columns + j] for j in range(1, columns)])
+    back[0] = grad_rows(0, state)
+    home_first, *got = after(back[0], *state, *came[0])
+    state = got[:3]
+    home_first = add_parts(home_first, got[3:])
+    home_first, *state = after(home_first, *state)
+    home_first = swap_experts(home_first)
+    state = hidden_part(columns, slot_parts[columns], state)
+    back[columns] = grad_rows(columns, state)
+    back[columns], *state = after(back[columns], *state)
     hidden, grad_gate, grad_up = state
     all_slots = jnp.concatenate(slot_parts, axis=0)
     all_grads = jnp.concatenate(grad_parts, axis=0)
@@ -582,20 +584,16 @@
     def out_rows_of(h, j, left):
         return expert_rows(h * columns + j, half, (left,), (wd,))
 
-    hidden_t = after(hidden, *(back[i] for i in range(parts)))[0]
+    home_second, hidden_t, *got = after(back[columns], hidden, *came[1])
+    home_second = add_parts(home_second, got)
+    home_second, hidden_t = after(home_second, hidden_t)
+    home_second = swap_experts(home_second)
     down_part = dot(hidden_t, all_grads, 0, 0, bf16)
-    down_part, hidden_t, gate_t, *got = after(down_part, hidden_t, grad_gate, *came[1])
-    home_second = swap_experts(add_parts(back[columns], got))
-    gate_part = dot(gate_t, all_slots, 0, 0, bf16)
+    down_part, hidden_t = after(down_part, hidden_t)
+    away_first = [out_rows_of(0, j, hidden_t) for j in range(1, columns)]
+    home_second, hidden_t, *away_first = after(home_second, hidden_t, *away_first)
+    away_first = columns_home(away_first)
     down_total = core_sum(down_part)
-    gate_part, hidden_t = after(gate_part, hidden_t)
-    away_first = [out_rows_of(0, j, hidden_t) for j in range(1, columns)]
-    own_first = out_rows_of(0, 0, hidden_t)
-    home_second, down_total, hidden_t, own_first, *away_first = after(
-        home_second, down_total, hidden_t, own_first, *away_first
-    )
-    down_grad = side_sum(down_total)
-    away_first = columns_home(away_first)
 
     def side_swap_sum(total):
         def side_rows(i):
@@ -604,7 +602,6 @@
 
         return side_rows(my_side), pair_swap(side_rows(my_side + 1))
 
-    gate_total = core_sum(gate_part)
     grad_slot_in = jnp.concatenate([home_first, home_second], axis=0).reshape(halves * half, D)
 
     grad_normed_two = dot(select[0] + select[1], grad_slot_in, 1, 0)
@@ -641,9 +638,9 @@
 
     out_part = dot(context, grad_attention, 0, 0, bf16)
     blocks_o = row_blocks(out_part, columns, my_column)
-    got = after(grad_attention, gate_total, *blocks_o)
-    grad_attention, gate_total, blocks_o = got[0], got[1], got[2:]
-    gate_own, gate_came = side_swap_sum(gate_total)
+    got = after(grad_attention, down_total, *blocks_o)
+    grad_attention, down_total, blocks_o = got[0], got[1], got[2:]
+    down_grad = side_sum(down_total)
     came_o = [column_shift(block, d) for d, block in enumerate(blocks_o) if d]
     grad_context = dot(grad_attention, w_o, 1, 1, bf16)
     grad_qk, grad_v = attention_backward(
@@ -651,14 +648,40 @@
     )
     qk_part = dot(normed_mixed, grad_qk, 0, 0, bf16)
     qk_sum = lax.psum_scatter(qk_part, "fsdp", scatter_dimension=0, tiled=True)
-    got = after(qk_part, grad_qk, grad_v, hidden_t, grad_up, down_grad, *away_first)
-    grad_qk, grad_v, hidden_t, up_t, down_grad, *away_first = got[1:]
-    outs_first = swap_experts(add_parts(own_first, away_first))
+    got = after(qk_part, grad_qk, grad_v, hidden_t, grad_gate, grad_up, *away_first)
+    grad_qk, grad_v, hidden_t, gate_t, up_t, *away_first = got[1:]
+    gate_part = dot(gate_t, all_slots, 0, 0, bf16)
+    gate_part, grad_v, hidden_t = after(gate_part, grad_v, hidden_t)
+    gate_total = core_sum(gate_part)
+    outs_first = add_parts(out_rows_of(0, 0, hidden_t), away_first)
+    away_second = [out_rows_of(1, j, hidden_t) for j in range(1, columns)]
     blocks_v = first_blocks(normed_side, grad_v, pair)
-    hidden_t, grad_qk, grad_v, *blocks_v = after(hidden_t, grad_qk, grad_v, *blocks_v)
-    away_second = [out_rows_of(1, j, hidden_t) for j in range(1, columns)]
-    hidden_t, grad_qk, grad_v, *away_second = after(hidden_t, grad_qk, grad_v, *away_second)
-    away_second = columns_home(away_second)
+    got = after(outs_first, up_t, hidden_t, gate_total, *blocks_v, *away_second, *came_o)
+    outs_first, up_t, hidden_t, gate_total = got[:4]
+    blocks_v, came_o = got[4 : 4 + pair], got[3 + pair + columns :]
+    away_second = columns_home(got[4 + pair : 3 + pair + columns])
+    blocks_o = row_blocks(add_parts(blocks_o[0], came_o), pair, my_side)
+    outs_first = swap_experts(outs_first)
+    came_v = pair_swap(blocks_v[1])
+
+    up_part = dot(up_t, all_slots, 0, 0, bf16)
+    came_o = pair_swap(blocks_o[1])
+    got = after(
+        up_part, hidden_t, gate_total, outs_first, came_v, came_o, grad_qk, *away_second
+    )
+    up_part, hidden_t, gate_total, outs_first, came_v, came_o, grad_qk, *away_second = got
+    gate_own, gate_came = side_swap_sum(gate_total)
+    out_grad = expert_sum(add_parts(blocks_o[0], [came_o]))
+    blocks_v = cut(add_parts(blocks_v[0], [came_v]), columns)
+    came_v = [column_shift(block, d) for d, block in enumerate(blocks_v) if d]
+    own_second = out_rows_of(1, 0, hidden_t)
+    up_total = core_sum(up_part)
+    outs_second, out_grad = after(add_parts(own_second, away_second), out_grad)
+    outs_second = swap_experts(outs_second)
+    got = after(up_total, grad_qk, gate_own, gate_came, outs_second, *came_v)
+    up_total, grad_qk, gate_own, gate_came, outs_second, *came_v = got
+    value_part = expert_sum(add_parts(blocks_v[0], came_v)).reshape(ctx_count, per, width)
+    up_own, up_came = side_swap_sum(up_total)
 
     def back_rows(s, out):
         part = slice(s * rows, (s + 1) * rows)
@@ -666,32 +689,16 @@
 
     back_away = [back_rows(s, bf16) for s in range(1, ctx_count)]
     grad_normed = back_rows(0, f32)
-    grad_normed, gate_own, gate_came, *came_o = after(grad_normed, gate_own, gate_came, *came_o)
+    grad_normed, qk_sum = after(grad_normed, qk_sum)
     gate_grad = gate_own.astype(f32) + gate_came.astype(f32)
-    sum_o = add_parts(blocks_o[0], came_o)
-    sum_o = reduce_blocks(row_blocks(sum_o, pair, my_side), side_shift)
     for s in range(1, ctx_count):
         grad_normed = grad_normed + core_shift(back_away[s - 1], -s).astype(f32)
     _, unit_one, inverse_one = normalize_parts(inputs, norm1_gain)
     grad_norm_one, norm1_part = norm_backward(grad_normed, unit_one, inverse_one, norm1_gain)
     tokens_grad = (grad_hidden_in + grad_norm_one).astype(bf16)
-    up_t, norm1_part, tokens_grad, *away_second = after(
-        up_t, norm1_part, tokens_grad, *away_second
-    )
-
-    up_part = dot(up_t, all_slots, 0, 0, bf16)
-    came_v = [side_shift(block, d) for d, block in enumerate(blocks_v) if d]
-    up_part, sum_o, outs_first, hidden_t, *came_v = after(
-        up_part, sum_o, outs_first, hidden_t, *came_v
-    )
-    sum_v = reduce_blocks(cut(add_parts(blocks_v[0], came_v), columns), column_shift)
-    out_grad = expert_sum(sum_o)
-    up_total = core_sum(up_part)
-    own_second = out_rows_of(1, 0, hidden_t)
-    own_second, up_total, out_grad, sum_v, qk_sum = after(
-        own_second, up_total, out_grad, sum_v, qk_sum
-    )
-    up_own, up_came = side_swap_sum(up_total)
+    up_own, up_came, value_part, norm1_part, tokens_grad = after(
+        up_own, up_came, value_part, norm1_part, tokens_grad
+    )
 
     gains = jnp.stack([norm1_part, norm2_part]).reshape(2, ctx_count, fsdp_count, per)
     gains = lax.all_to_all(gains.transpose(2, 1, 0, 3), "fsdp", 0, 0, tiled=True)
@@ -703,8 +710,6 @@
     gains_own = gains_of(core)
     for s in range(1, ctx_count):
         gains_own = gains_own + core_shift(gains_of(core + s), s)
-    value_part = expert_sum(sum_v).reshape(ctx_count, per, width)
-    outs_second = swap_experts(add_parts(own_second, away_second))
     up_grad = up_own.astype(f32) + up_came.astype(f32)
     qk_parts = qk_sum.astype(f32).reshape(ctx_count, per, heads, 2, HD)
     sums = jnp.stack(

time: 1390 us -> 1430 us (1.029)
  blocking collectives: 0 us -> 61.7 us
  waiting for transfers between devices: 464 us -> 431 us
  local copies, waits for them, and re-layouts: 86.5 us -> 101 us
    all_to_all x0 -> x1, blocking collectives: none -> 61.7 us  [swap_experts(): lax.all_to_all(blocks, 'fsdp', 0, 0, axis_index_groups=lines, tiled=True)]
    reduce_scatter x1, waiting for transfers between devices: 23.4 us -> 0.01 us  [side_sum(): lax.psum_scatter(total, 'fsdp', scatter_dimension=0, tiled=True, axis_ind...]
    all_to_all x10 -> x9, starting transfers between devices: 54 us -> 51.2 us  [swap_experts(): lax.all_to_all(blocks, 'fsdp', 0, 0, axis_index_groups=lines, tiled=True)]
  transfers between devices with their start and end apart: 44 -> 43, of which waited for: 18 -> 15; matrix products, arithmetic and copies ran while one was open for 32% -> 32% of each run, Pallas kernels for 25% -> 24%
where the time goes in v5:
time: 1430 us; the launch traced here: 1420 us
  waiting for transfers between devices  431 us (30%)
  Pallas kernels  348 us (24%)
  matrix products  271 us (19%)
  other arithmetic  118 us (8%)
  local copies, waits for them, and re-layouts  101 us (7%)
  starting transfers between devices  77.8 us (5%)
  blocking collectives  61.7 us (4%)
  between operations  15.6 us (1%)
    dot_general x24, matrix products, dot(): lax.dot_general(a, b, (((ca,), (cb,)), ((), ())), preferred_element_type=...  271 us
    ppermute x14, waiting for transfers between devices, fsdp_shift(): return lax.ppermute(a, 'fsdp', [(i, move(i)) for i in range(fsdp_count)])  178 us
    all_gather x1, waiting for transfers between devices, shards(): gathered = lax.all_gather(packed, 'fsdp', axis=0, tiled=True)  139 us
    pallas_call x8, Pallas kernels, expert_rows(): pl.pallas_call(functools.partial(rows_kernel, len(left)), grid=(D // tile...  139 us
    pallas_call x4, Pallas kernels, expert_hidden(): pl.pallas_call(functools.partial(expert_kernel, len(kept)), grid=(units /...  123 us
    all_gather x3, waiting for transfers between devices, shards(): lax.all_gather(part, 'fsdp', axis=0, tiled=True, axis_index_groups=sides)  88.8 us
    all_to_all x1, blocking collectives, swap_experts(): lax.all_to_all(blocks, 'fsdp', 0, 0, axis_index_groups=lines, tiled=True)  61.7 us
    all_to_all x9, starting transfers between devices, swap_experts(): lax.all_to_all(blocks, 'fsdp', 0, 0, axis_index_groups=lines, tiled=True)  51.2 us
  transfers between devices with their start and end apart: 43, of which 15 were waited for; matrix products, arithmetic and copies ran while one was open for 32% of the time, Pallas kernels for 24%

profile of v5, /device:TPU:0, one launch (start us, length us, event | category | flops | bytes accessed | tf_op | source)
XLA Modules:
  0.0 1424.5 jit_solution(87452592494590251)
XLA Ops:
  22.5 6.9 constant_dynamic-slice_fusion.17
  39.6 13.4 fusion.32
  53.0 13.9 fusion.31
  66.9 139.4 %all-gather.5.cloned.1.call-done = bf16[2048,4096]{1,0:T(8,128)(2,1)} async-done(((bf16[128,4096]{1,0:T(8,128)(2,1)}), bf16[2048,4096]{1,0:T(8,128)(2,1)}) %all-gather.5.cloned.1.call-update) | async-done | bytes 16777232 | tf_op jit(solution)/shard_map/all_gather | solution.py:394
  226.4 19.0 %fusion.2.pre_q.pre_k.pre_v = f32[1024,3072]{1,0:T(8,128)} fusion(bf16[2048,4096]{1,0:T(8,128)(2,1)} %all-gather.5.cloned.1.call-done, bf16[512,2048]{1,0:T(8,128)(2,1)} %collective-permute-done, bf16[512,2048]{1,0:T(8,128)(2,1)} %fusion.21), kind=kOutput, calls=%fused_computation.4 | convolution fusion | flops 12893290496 | bytes 29360128 | tf_op jit(solution)/shard_map/dot_general | solution.py:28
  245.4 21.7 %attention_forward.1 = (bf16[1024,1024]{1,0:T(8,128)(2,1)}, bf16[1024,1024]{1,0:T(8,128)(2,1)}, bf16[1024,1024]{1,0:T(8,128)(2,1)}, bf16[1024,1024]{1,0:T(8,128)(2,1)}, f32[1024,1024]{1,0:T(8,128)}) custom-call(s32[4]{0:T(128)} %fusion.126.perm, f32[1024,3072]{1,0:T(8,128)} %fusion.2.pre_q.pre_k.pre_v, f32[1024,3072]{1,0:T(8,128)} %fusion.2.pre_q.pre_k.pre_v, ...), custom_call_target="tpu_custom_call" | custom-call | tf_op jit(solution)/shard_map/attention_forward/pallas_call | solution.py:156
  292.0 6.6 multiply_reduce_fusion.2
  305.0 52.2 %all-gather.9.cloned.1.call-done = bf16[1408,2048]{1,0:T(8,128)(2,1)} async-done(((bf16[704,2048]{1,0:T(8,128)(2,1)}), bf16[1408,2048]{1,0:T(8,128)(2,1)}) %all-gather.9.cloned.1.call-update) | async-done | bytes 5767184 | tf_op jit(solution)/shard_map/all_gather | solution.py:468
  371.3 12.7 join_weights.3.wg_ref.refs_2_
  384.0 12.4 join_weights.4.wu_ref.refs_3_
  396.4 36.7 %all-gather.11.cloned.1.call-done = bf16[1408,2048]{1,0:T(8,128)(2,1)} async-done(((bf16[704,2048]{1,0:T(8,128)(2,1)}), bf16[1408,2048]{1,0:T(8,128)(2,1)}) %all-gather.11.cloned.1.call-update) | async-done | bytes 5767184 | tf_op jit(solution)/shard_map/all_gather | solution.py:468
  445.6 12.4 join_weights.5.wd_ref.refs_1_
  458.0 30.7 %expert_hidden.4 = (bf16[2560,2816]{1,0:T(8,128)(2,1)}, bf16[2560,2816]{1,0:T(8,128)(2,1)}, bf16[2560,2816]{1,0:T(8,128)(2,1)}) custom-call(bf16[640,2048]{1,0:T(8,128)(2,1)} %bitcast.121, bf16[640,2048]{1,0:T(8,128)(2,1)} %bitcast.13.g_ref, bf16[2816,2048]{1,0:T(8,128)(2,1)} %join_weights.3.wg_ref.refs_2_, bf16[2816,2048]{1,0:T(8,128)(2,1)} %join_weights.4.wu_ref.refs_3_, ...), custom_call_target="tpu_custom_call" | custom-call | tf_op jit(solution)/shard_map/expert_hidden/pallas_call | solution.py:217
  488.7 10.9 collective-permute-done.8.x_ref
  501.1 30.6 %expert_hidden.5 = (bf16[2560,2816]{1,0:T(8,128)(2,1)}, bf16[2560,2816]{1,0:T(8,128)(2,1)}, bf16[2560,2816]{1,0:T(8,128)(2,1)}) custom-call(bf16[640,2048]{1,0:T(8,128)(2,1)} %collective-permute-done.8.x_ref, bf16[640,2048]{1,0:T(8,128)(2,1)} %collective-permute-done.3.g_ref, ...), custom_call_target="tpu_custom_call", output_to_operand_aliasing={{0}: (5, {}), {1}: (6, {}), {2}: (7, {})} | custom-call | tf_op jit(solution)/shard_map/expert_hidden/pallas_call | solution.py:217
  531.6 21.1 %expert_rows.8 = bf16[640,2048]{1,0:T(8,128)(2,1)} custom-call(bf16[2560,2816]{1,0:T(8,128)(2,1)} %get-tuple-element.180.refs_0_.refs_1_, bf16[2560,2816]{1,0:T(8,128)(2,1)} %get-tuple-element.181.refs_1_.refs_2_, bf16[2816,2048]{1,0:T(8,128)(2,1)} %join_weights.3.wg_ref.refs_2_, bf16[2816,2048]{1,0:T(8,128)(2,1)} %join_weights.4.wu_ref.refs_3_), custom_call_target="tpu_custom_call" | custom-call | tf_op jit(solution)/shard_map/expert_rows/pallas_call | solution.py:237
  561.1 30.6 %expert_hidden.6 = (bf16[2560,2816]{1,0:T(8,128)(2,1)}, bf16[2560,2816]{1,0:T(8,128)(2,1)}, bf16[2560,2816]{1,0:T(8,128)(2,1)}) custom-call(bf16[640,2048]{1,0:T(8,128)(2,1)} %copy-done.15, bf16[640,2048]{1,0:T(8,128)(2,1)} %collective-permute-done.6.g_ref, ...), custom_call_target="tpu_custom_call", output_to_operand_aliasing={{0}: (5, {}), {1}: (6, {}), {2}: (7, {})} | custom-call | tf_op jit(solution)/shard_map/expert_hidden/pallas_call | solution.py:217
  591.6 21.1 %expert_rows.9 = bf16[640,2048]{1,0:T(8,128)(2,1)} custom-call(bf16[2560,2816]{1,0:T(8,128)(2,1)} %get-tuple-element.196.refs_0_.refs_1_, bf16[2560,2816]{1,0:T(8,128)(2,1)} %get-tuple-element.197.refs_1_.refs_2_, bf16[2816,2048]{1,0:T(8,128)(2,1)} %join_weights.3.wg_ref.refs_2_, bf16[2816,2048]{1,0:T(8,128)(2,1)} %join_weights.4.wu_ref.refs_3_), custom_call_target="tpu_custom_call" | custom-call | tf_op jit(solution)/shard_map/expert_rows/pallas_call | solution.py:237
  614.2 21.1 %expert_rows.10 = bf16[640,2048]{1,0:T(8,128)(2,1)} custom-call(bf16[2560,2816]{1,0:T(8,128)(2,1)} %get-tuple-element.196.refs_0_.refs_1_, bf16[2560,2816]{1,0:T(8,128)(2,1)} %get-tuple-element.197.refs_1_.refs_2_, bf16[2816,2048]{1,0:T(8,128)(2,1)} %join_weights.3.wg_ref.refs_2_, bf16[2816,2048]{1,0:T(8,128)(2,1)} %join_weights.4.wu_ref.refs_3_), custom_call_target="tpu_custom_call" | custom-call | tf_op jit(solution)/shard_map/expert_rows/pallas_call | solution.py:237
  640.6 30.8 %expert_hidden.7 = (bf16[2560,2816]{1,0:T(8,128)(2,1)}, bf16[2560,2816]{1,0:T(8,128)(2,1)}, bf16[2560,2816]{1,0:T(8,128)(2,1)}) custom-call(bf16[640,2048]{1,0:T(8,128)(2,1)} %bitcast.22.x_ref, bf16[640,2048]{1,0:T(8,128)(2,1)} %bitcast.15.g_ref, ...), custom_call_target="tpu_custom_call", output_to_operand_aliasing={{0}: (5, {}), {1}: (6, {}), {2}: (7, {})} | custom-call | tf_op jit(solution)/shard_map/expert_hidden/pallas_call | solution.py:217
  671.3 21.1 %expert_rows.11 = bf16[640,2048]{1,0:T(8,128)(2,1)} custom-call(bf16[2560,2816]{1,0:T(8,128)(2,1)} %get-tuple-element.219.refs_0_, bf16[2560,2816]{1,0:T(8,128)(2,1)} %get-tuple-element.229.refs_1_, bf16[2816,2048]{1,0:T(8,128)(2,1)} %join_weights.3.wg_ref.refs_2_, bf16[2816,2048]{1,0:T(8,128)(2,1)} %join_weights.4.wu_ref.refs_3_), custom_call_target="tpu_custom_call" | custom-call | tf_op jit(solution)/shard_map/expert_rows/pallas_call | solution.py:237
  695.2 61.7 %all_to_all.55 = bf16[4,160,2048]{2,1,0:T(8,128)(2,1)S(1)} all-to-all(bf16[4,160,2048]{2,1,0:T(8,128)(2,1)S(1)} %bitcast.125), channel_id=1, replica_groups={{0,4,8,12},{1,5,9,13},{2,6,10,14},{3,7,11,15},{16,20,24,28},{17,21,25,2..., dimensions={0} | all-to-all | bytes 5242880 | tf_op jit(solution)/shard_map/all_to_all | solution.py:458
  761.5 38.6 %convolution_convert_fusion.2 = bf16[2816,2048]{1,0:T(8,128)(2,1)} fusion(bf16[2560,2816]{1,0:T(8,128)(2,1)} %get-tuple-element.242.refs_0_, bf16[640,2048]{1,0:T(8,128)(2,1)} %collective-permute-done.6.g_ref, bf16[640,2048]{1,0:T(8,128)(2,1)} %bitcast.15.g_ref, bf16[640,2048]{1,0:T(8,128)(2,1)} %collective-permute-done.3.g_ref, ...), kind=kOutput, calls=%fused_computation.11 | convolution fusion | flops 29575610368 | bytes 36438016 | tf_op jit(solution)/shard_map/dot_general | solution.py:28
  805.9 13.8 expert_rows.12
  839.6 9.8 add_convert_fusion.2
  849.5 7.0 convolution_convert_fusion.4
  864.7 8.7 convolution_convert_fusion.10.do_ref
  873.4 27.1 %attention_backward.1 = (bf16[1024,2048]{1,0:T(8,128)(2,1)}, bf16[1024,1024]{1,0:T(8,128)(2,1)}) custom-call(s32[4]{0:T(128)} %fusion.126.perm, bf16[1024,1024]{1,0:T(8,128)(2,1)} %get-tuple-element.141.q_ref, bf16[1024,1024]{1,0:T(8,128)(2,1)} %get-tuple-element.142.k_ref, bf16[1024,1024]{1,0:T(8,128)(2,1)} %get-tuple-element.143.v_ref, ...), custom_call_target="tpu_custom_call" | custom-call | tf_op jit(solution)/shard_map/attention_backward/pallas_call | solution.py:179
  900.5 14.0 convolution_convert_fusion.3
  914.6 35.6 %convolution_convert_fusion.1 = bf16[2816,2048]{1,0:T(8,128)(2,1)S(1)} fusion(bf16[2560,2816]{1,0:T(8,128)(2,1)} %get-tuple-element.219.refs_0_, bf16[2560,2048]{1,0:T(8,128)(2,1)} %copy-done.36), kind=kOutput, calls=%fused_computation.10 | convolution fusion | flops 29533667328 | bytes 36438016 | tf_op jit(solution)/shard_map/dot_general | solution.py:28
  958.3 13.7 expert_rows.13
  972.0 13.9 expert_rows.14
  1000.1 9.9 add_convert_fusion.1
  1010.0 31.9 %collective-permute-done.16 = bf16[512,2048]{1,0:T(8,128)(2,1)} collective-permute-done((bf16[512,2048]{1,0:T(8,128)(2,1)S(1)}, bf16[512,2048]{1,0:T(8,128)(2,1)}, u32[]{:S(2)}, u32[]{:S(2)}) %collective-permute-start.16) | collective-permute-done | bytes 2097184 | tf_op jit(solution)/shard_map/ppermute | solution.py:359
  1041.9 13.2 all-to-all-start.6
  1061.4 38.5 %convolution_convert_fusion = bf16[2816,2048]{1,0:T(8,128)(2,1)} fusion(bf16[2560,2816]{1,0:T(8,128)(2,1)} %get-tuple-element.229.refs_1_, bf16[2560,2048]{1,0:T(8,128)(2,1)} %copy-done.36), kind=kOutput, calls=%fused_computation.9 | convolution fusion | flops 29533667328 | bytes 36438016 | tf_op jit(solution)/shard_map/dot_general | solution.py:28
  1099.9 99.8 %collective-permute-done.18 = bf16[256,2048]{1,0:T(8,128)(2,1)S(1)} collective-permute-done((bf16[256,2048]{1,0:T(8,128)(2,1)S(1)}, bf16[256,2048]{1,0:T(8,128)(2,1)S(1)}, u32[]{:S(2)}, u32[]{:S(2)}) %collective-permute-start.18) | collective-permute-done | bytes 1048608 | tf_op jit(solution)/shard_map/ppermute | solution.py:359
  1202.1 6.8 constant_dynamic-slice_fusion.7
  1214.9 13.5 expert_rows.15
  1233.7 7.7 all-to-all-done.7
  1254.6 7.1 fusion.35
  1266.2 6.5 fusion.33
  1277.8 9.8 add_convert_fusion
  1289.6 27.3 %collective-permute-done.21 = bf16[1408,1024]{1,0:T(8,128)(2,1)} collective-permute-done((bf16[1408,1024]{1,0:T(8,128)(2,1)}, bf16[1408,1024]{1,0:T(8,128)(2,1)}, u32[]{:S(2)}, u32[]{:S(2)}) %collective-permute-start.21) | collective-permute-done | bytes 2883616 | tf_op jit(solution)/shard_map/ppermute | solution.py:359
  1332.4 11.2 add_convert_fusion.7
  1353.9 9.9 fusion.37
  1385.2 6.5 fusion.27
  1392.6 7.4 all-to-all-start.10
  (330 shorter events, 292.8 us)
Async XLA Ops:
  7.2 199.1 %all-gather.5.cloned.1.call-start = ((), (), s32[]{:S(2)}) async-start(), calls=%async_computation.13 | async-start | bytes 17825792 | tf_op jit(solution)/shard_map/all_gather | solution.py:394
  11.8 293.2 %all-gather.7.cloned.1.call-start = ((), (), s32[]{:S(2)}) async-start(), calls=%async_computation.14 | async-start | bytes 8650752 | tf_op jit(solution)/shard_map/all_gather | solution.py:468
  14.2 25.3 %collective-permute-start = (bf16[512,2048]{1,0:T(8,128)(2,1)}, bf16[512,2048]{1,0:T(8,128)(2,1)}, u32[]{:S(2)}, u32[]{:S(2)}) collective-permute-start(bf16[512,2048]{1,0:T(8,128)(2,1)} %fusion.21), channel_id=1, source_target_pairs={{0,16},{16,0},{1,17},{17,1},{2,18},{18,2},{3,19},{19,3},{4,20},{20... | collective-permute-start | bytes 6291464 | tf_op jit(solution)/shard_map/ppermute | solution.py:356
  18.6 270.4 %copy-start.44 = (s32[512]{0:T(512)}, s32[512]{0:T(512)S(1)}, u32[]{:S(2)}) copy-start(s32[512]{0:T(512)S(1)} %get-tuple-element.269) | copy-start | bytes 6148
  18.7 270.4 %copy-start.47 = (s32[512]{0:T(512)}, s32[512]{0:T(512)S(1)}, u32[]{:S(2)}) copy-start(s32[512]{0:T(512)S(1)} %get-tuple-element.270) | copy-start | bytes 6148
  18.7 11.8 copy-start.55
  53.0 153.4 %copy-start.66 = (s32[1,4]{1,0:T(1,128)S(1)}, s32[1,4]{1,0:T(1,128)}, u32[]{:S(2)}) copy-start(s32[1,4]{1,0:T(1,128)} %param.17) | copy-start | bytes 52
  206.3 150.8 %all-gather.9.cloned.1.call-start = ((), (), s32[]{:S(2)}) async-start(), calls=%async_computation.15 | async-start | bytes 8650752 | tf_op jit(solution)/shard_map/all_gather | solution.py:468
  218.5 64.1 %all-to-all-start = ((bf16[4,160,2048]{2,1,0:T(8,128)(2,1)}), bf16[4,160,2048]{2,1,0:T(8,128)(2,1)}, u32[]{:S(2)}, u32[]{:S(2)}) async-start(bf16[4,160,2048]{2,1,0:T(8,128)(2,1)} %bitcast.134), calls=%async_computation | async-start | bytes 5242880 | tf_op jit(solution)/shard_map/all_to_all | solution.py:458
  226.4 40.8 %collective-permute-start.1 = (bf16[1024,1024]{1,0:T(8,128)(2,1)}, bf16[1024,1024]{1,0:T(8,128)(2,1)}, u32[]{:S(2)}, u32[]{:S(2)}) collective-permute-start(bf16[1024,1024]{1,0:T(8,128)(2,1)} %constant_dynamic-slice_fusion.16), channel_id=1, source_target_pairs={{0,16},{16,0},{1,17},{17,1},{2,18},{18,2},{3,19},{19,3},{4,20},{20... | collective-permute-start | bytes 6291464 | tf_op jit(solution)/shard_map/ppermute | solution.py:356
  282.6 74.5 %all-to-all-start.1 = ((bf16[4,160,2048]{2,1,0:T(8,128)(2,1)}), bf16[4,160,2048]{2,1,0:T(8,128)(2,1)}, u32[]{:S(2)}, u32[]{:S(2)}) async-start(bf16[4,160,2048]{2,1,0:T(8,128)(2,1)} %bitcast.133), calls=%async_computation.1 | async-start | bytes 5242880 | tf_op jit(solution)/shard_map/all_to_all | solution.py:458
  287.2 145.9 %all-gather.11.cloned.1.call-start = ((), (), s32[]{:S(2)}) async-start(), calls=%async_computation.16 | async-start | bytes 8650752 | tf_op jit(solution)/shard_map/all_gather | solution.py:468
  287.4 4.6 collective-permute-start.2
  287.5 69.6 %collective-permute-start.3 = (bf16[640,2048]{1,0:T(8,128)(2,1)}, bf16[640,2048]{1,0:T(8,128)(2,1)}, u32[]{:S(2)}, u32[]{:S(2)}) collective-permute-start(bf16[640,2048]{1,0:T(8,128)(2,1)} %bitcast.13.g_ref), channel_id=1, source_target_pairs={{0,2},{1,3},{2,0},{3,1},{4,6},{5,7},{6,4},{7,5},{8,10},{9,11},{10,... | collective-permute-start | bytes 7864328 | tf_op jit(solution)/shard_map/ppermute | solution.py:359
  357.1 75.9 %all-to-all-start.2 = ((bf16[4,160,2048]{2,1,0:T(8,128)(2,1)}), bf16[4,160,2048]{2,1,0:T(8,128)(2,1)S(1)}, u32[]{:S(2)}, u32[]{:S(2)}) async-start(bf16[4,160,2048]{2,1,0:T(8,128)(2,1)} %bitcast.136), calls=%async_computation.2 | async-start | bytes 5242880 | tf_op jit(solution)/shard_map/all_to_all | solution.py:458
  365.7 5.6 collective-permute-start.4
  368.4 15.6 %collective-permute-start.5 = (bf16[704,2048]{1,0:T(8,128)(2,1)}, bf16[704,2048]{1,0:T(8,128)(2,1)}, u32[]{:S(2)}, u32[]{:S(2)}) collective-permute-start(bf16[704,2048]{1,0:T(8,128)(2,1)} %constant_dynamic-slice_fusion.14.refs_0_), channel_id=1, source_target_pairs={{0,16},{16,0},{1,17},{17,1},{2,18},{18,2},{3,19},{19,3},{4,20},{20... | collective-permute-start | bytes 8650760 | tf_op jit(solution)/shard_map/ppermute | solution.py:356
  368.4 64.7 %collective-permute-start.6 = (bf16[640,2048]{1,0:T(8,128)(2,1)}, bf16[640,2048]{1,0:T(8,128)(2,1)}, u32[]{:S(2)}, u32[]{:S(2)}) collective-permute-start(bf16[640,2048]{1,0:T(8,128)(2,1)} %bitcast.15.g_ref), channel_id=1, source_target_pairs={{0,2},{1,3},{2,0},{3,1},{4,6},{5,7},{6,4},{7,5},{8,10},{9,11},{10,... | collective-permute-start | bytes 7864328 | tf_op jit(solution)/shard_map/ppermute | solution.py:359
  433.1 66.5 %all-to-all-start.3 = ((bf16[4,160,2048]{2,1,0:T(8,128)(2,1)}), bf16[4,160,2048]{2,1,0:T(8,128)(2,1)}, u32[]{:S(2)}, u32[]{:S(2)}) async-start(bf16[4,160,2048]{2,1,0:T(8,128)(2,1)} %bitcast.135), calls=%async_computation.3 | async-start | bytes 5242880 | tf_op jit(solution)/shard_map/all_to_all | solution.py:458
  440.1 5.5 collective-permute-start.7
  440.2 59.4 %collective-permute-start.8 = (bf16[640,2048]{1,0:T(8,128)(2,1)S(1)}, bf16[640,2048]{1,0:T(8,128)(2,1)}, u32[]{:S(2)}, u32[]{:S(2)}) collective-permute-start(bf16[640,2048]{1,0:T(8,128)(2,1)S(1)} %bitcast.120), channel_id=1, source_target_pairs={{0,2},{1,3},{2,0},{3,1},{4,6},{5,7},{6,4},{7,5},{8,10},{9,11},{10,... | collective-permute-start | bytes 7864328 | tf_op jit(solution)/shard_map/ppermute | solution.py:359
  499.6 60.0 %collective-permute-start.9 = (bf16[640,2048]{1,0:T(8,128)(2,1)}, bf16[640,2048]{1,0:T(8,128)(2,1)S(1)}, u32[]{:S(2)}, u32[]{:S(2)}) collective-permute-start(bf16[640,2048]{1,0:T(8,128)(2,1)} %bitcast.22.x_ref), channel_id=1, source_target_pairs={{0,2},{1,3},{2,0},{3,1},{4,6},{5,7},{6,4},{7,5},{8,10},{9,11},{10,... | collective-permute-start | bytes 7864328 | tf_op jit(solution)/shard_map/ppermute | solution.py:359
  552.7 82.6 %collective-permute-start.10 = (bf16[640,2048]{1,0:T(8,128)(2,1)}, bf16[640,2048]{1,0:T(8,128)(2,1)}, u32[]{:S(2)}, u32[]{:S(2)}) collective-permute-start(bf16[640,2048]{1,0:T(8,128)(2,1)} %expert_rows.8), channel_id=1, source_target_pairs={{0,2},{1,3},{2,0},{3,1},{4,6},{5,7},{6,4},{7,5},{8,10},{9,11},{10,... | collective-permute-start | bytes 7864328 | tf_op jit(solution)/shard_map/ppermute | solution.py:359
  612.7 79.7 %collective-permute-start.11 = (bf16[640,2048]{1,0:T(8,128)(2,1)}, bf16[640,2048]{1,0:T(8,128)(2,1)S(1)}, u32[]{:S(2)}, u32[]{:S(2)}) collective-permute-start(bf16[640,2048]{1,0:T(8,128)(2,1)} %expert_rows.9), channel_id=1, source_target_pairs={{0,2},{1,3},{2,0},{3,1},{4,6},{5,7},{6,4},{7,5},{8,10},{9,11},{10,... | collective-permute-start | bytes 7864328 | tf_op jit(solution)/shard_map/ppermute | solution.py:359
  756.9 62.9 %all-to-all-start.4 = ((bf16[4,160,2048]{2,1,0:T(8,128)(2,1)}), bf16[4,160,2048]{2,1,0:T(8,128)(2,1)}, u32[]{:S(2)}, u32[]{:S(2)}) async-start(bf16[4,160,2048]{2,1,0:T(8,128)(2,1)} %bitcast.123), calls=%async_computation.4 | async-start | bytes 5242880 | tf_op jit(solution)/shard_map/all_to_all | solution.py:458
  761.4 511.3 %reduce-scatter.5.cloned.1.call-start = ((), (), s32[]{:S(2)}) async-start(), calls=%async_computation.18 | async-start | bytes 8650752 | tf_op jit(solution)/shard_map/reduce_scatter | solution.py:580
  805.9 33.8 %collective-permute-start.13 = (bf16[2816,1024]{1,0:T(8,128)(2,1)}, bf16[2816,1024]{1,0:T(8,128)(2,1)}, u32[]{:S(2)}, u32[]{:S(2)}) collective-permute-start(bf16[2816,1024]{1,0:T(8,128)(2,1)} %constant_dynamic-slice_fusion.12), channel_id=1, source_target_pairs={{0,16},{16,0},{1,17},{17,1},{2,18},{18,2},{3,19},{19,3},{4,20},{20... | collective-permute-start | bytes 17301512 | tf_op jit(solution)/shard_map/ppermute | solution.py:356
  829.0 20.4 %collective-permute-start.12 = (bf16[512,2048]{1,0:T(8,128)(2,1)S(1)}, bf16[512,2048]{1,0:T(8,128)(2,1)}, u32[]{:S(2)}, u32[]{:S(2)}) collective-permute-start(bf16[512,2048]{1,0:T(8,128)(2,1)S(1)} %fusion.138), channel_id=1, source_target_pairs={{0,16},{16,0},{1,17},{17,1},{2,18},{18,2},{3,19},{19,3},{4,20},{20... | collective-permute-start | bytes 6291464 | tf_op jit(solution)/shard_map/ppermute | solution.py:356
  839.1 75.5 %collective-permute-start.14 = (bf16[640,2048]{1,0:T(8,128)(2,1)}, bf16[640,2048]{1,0:T(8,128)(2,1)}, u32[]{:S(2)}, u32[]{:S(2)}) collective-permute-start(bf16[640,2048]{1,0:T(8,128)(2,1)} %expert_rows.12), channel_id=1, source_target_pairs={{0,2},{1,3},{2,0},{3,1},{4,6},{5,7},{6,4},{7,5},{8,10},{9,11},{10,... | collective-permute-start | bytes 7864328 | tf_op jit(solution)/shard_map/ppermute | solution.py:359
  863.1 506.3 %reduce-scatter.3.cloned.1.call-start = ((), (), s32[]{:S(2)}) async-start(), calls=%async_computation.17 | async-start | bytes 8912896 | tf_op jit(solution)/shard_map/reduce_scatter | solution.py:650
  956.5 43.6 %collective-permute-start.15 = (bf16[2816,1024]{1,0:T(8,128)(2,1)}, bf16[2816,1024]{1,0:T(8,128)(2,1)}, u32[]{:S(2)}, u32[]{:S(2)}) collective-permute-start(bf16[2816,1024]{1,0:T(8,128)(2,1)} %constant_dynamic-slice_fusion.9), channel_id=1, source_target_pairs={{0,16},{16,0},{1,17},{17,1},{2,18},{18,2},{3,19},{19,3},{4,20},{20... | collective-permute-start | bytes 17301512 | tf_op jit(solution)/shard_map/ppermute | solution.py:356
  956.8 85.1 %collective-permute-start.16 = (bf16[512,2048]{1,0:T(8,128)(2,1)S(1)}, bf16[512,2048]{1,0:T(8,128)(2,1)}, u32[]{:S(2)}, u32[]{:S(2)}) collective-permute-start(bf16[512,2048]{1,0:T(8,128)(2,1)S(1)} %bitcast.137), channel_id=1, source_target_pairs={{0,2},{1,3},{2,0},{3,1},{4,6},{5,7},{6,4},{7,5},{8,10},{9,11},{10,... | collective-permute-start | bytes 6291464 | tf_op jit(solution)/shard_map/ppermute | solution.py:359
  1041.9 160.2 %all-to-all-start.6 = ((bf16[4,160,2048]{2,1,0:T(8,128)(2,1)}), bf16[4,160,2048]{2,1,0:T(8,128)(2,1)S(1)}, u32[]{:S(2)}, u32[]{:S(2)}) async-start(bf16[4,160,2048]{2,1,0:T(8,128)(2,1)} %bitcast.124), calls=%async_computation.6 | async-start | bytes 5242880 | tf_op jit(solution)/shard_map/all_to_all | solution.py:458
  1055.1 144.7 %collective-permute-start.17 = (bf16[1024,1024]{1,0:T(8,128)(2,1)}, bf16[1024,1024]{1,0:T(8,128)(2,1)S(1)}, u32[]{:S(2)}, u32[]{:S(2)}) collective-permute-start(bf16[1024,1024]{1,0:T(8,128)(2,1)} %fusion.58), channel_id=1, source_target_pairs={{0,1},{1,0},{2,3},{3,2},{4,5},{5,4},{6,7},{7,6},{8,9},{9,8},{10,11... | collective-permute-start | bytes 6291464 | tf_op jit(solution)/shard_map/ppermute | solution.py:359
  1059.5 140.3 %collective-permute-start.18 = (bf16[256,2048]{1,0:T(8,128)(2,1)S(1)}, bf16[256,2048]{1,0:T(8,128)(2,1)S(1)}, u32[]{:S(2)}, u32[]{:S(2)}) collective-permute-start(bf16[256,2048]{1,0:T(8,128)(2,1)S(1)} %bitcast.142), channel_id=1, source_target_pairs={{0,1},{1,0},{2,3},{3,2},{4,5},{5,4},{6,7},{7,6},{8,9},{9,8},{10,11... | collective-permute-start | bytes 3145736 | tf_op jit(solution)/shard_map/ppermute | solution.py:359
  1061.4 140.7 %collective-permute-start.19 = (bf16[640,2048]{1,0:T(8,128)(2,1)S(1)}, bf16[640,2048]{1,0:T(8,128)(2,1)}, u32[]{:S(2)}, u32[]{:S(2)}) collective-permute-start(bf16[640,2048]{1,0:T(8,128)(2,1)S(1)} %copy-done.25), channel_id=1, source_target_pairs={{0,2},{1,3},{2,0},{3,1},{4,6},{5,7},{6,4},{7,5},{8,10},{9,11},{10,... | collective-permute-start | bytes 7864328 | tf_op jit(solution)/shard_map/ppermute | solution.py:359
  1209.0 68.9 %collective-permute-start.20 = (bf16[2816,1024]{1,0:T(8,128)(2,1)}, bf16[2816,1024]{1,0:T(8,128)(2,1)}, u32[]{:S(2)}, u32[]{:S(2)}) collective-permute-start(bf16[2816,1024]{1,0:T(8,128)(2,1)} %constant_dynamic-slice_fusion.7), channel_id=1, source_target_pairs={{0,16},{16,0},{1,17},{17,1},{2,18},{18,2},{3,19},{19,3},{4,20},{20... | collective-permute-start | bytes 17301512 | tf_op jit(solution)/shard_map/ppermute | solution.py:356
  1210.4 30.9 %all-to-all-start.7 = ((bf16[4,64,2048]{2,1,0:T(8,128)(2,1)}), bf16[4,64,2048]{2,1,0:T(8,128)(2,1)S(1)}, u32[]{:S(2)}, u32[]{:S(2)}) async-start(bf16[4,64,2048]{2,1,0:T(8,128)(2,1)} %bitcast.33), calls=%async_computation.7 | async-start | bytes 2097152 | tf_op jit(solution)/shard_map/all_to_all | solution.py:458
  1242.3 74.6 %all-to-all-start.8 = ((bf16[4,160,2048]{2,1,0:T(8,128)(2,1)}), bf16[4,160,2048]{2,1,0:T(8,128)(2,1)}, u32[]{:S(2)}, u32[]{:S(2)}) async-start(bf16[4,160,2048]{2,1,0:T(8,128)(2,1)} %bitcast.34), calls=%async_computation.8 | async-start | bytes 5242880 | tf_op jit(solution)/shard_map/all_to_all | solution.py:458
  1252.1 64.8 %collective-permute-start.21 = (bf16[1408,1024]{1,0:T(8,128)(2,1)}, bf16[1408,1024]{1,0:T(8,128)(2,1)}, u32[]{:S(2)}, u32[]{:S(2)}) collective-permute-start(bf16[1408,1024]{1,0:T(8,128)(2,1)} %get-tuple-element.275), channel_id=1, source_target_pairs={{0,1},{1,0},{2,3},{3,2},{4,5},{5,4},{6,7},{7,6},{8,9},{9,8},{10,11... | collective-permute-start | bytes 8650760 | tf_op jit(solution)/shard_map/ppermute | solution.py:359
  1265.1 24.5 %collective-permute-start.22 = (bf16[512,1024]{1,0:T(8,128)(2,1)}, bf16[512,1024]{1,0:T(8,128)(2,1)}, u32[]{:S(2)}, u32[]{:S(2)}) collective-permute-start(bf16[512,1024]{1,0:T(8,128)(2,1)} %slice.137), channel_id=1, source_target_pairs={{0,2},{1,3},{2,0},{3,1},{4,6},{5,7},{6,4},{7,5},{8,10},{9,11},{10,... | collective-permute-start | bytes 3145736 | tf_op jit(solution)/shard_map/ppermute | solution.py:359
  1322.8 69.0 %collective-permute-start.23 = (bf16[1408,1024]{1,0:T(8,128)(2,1)}, bf16[1408,1024]{1,0:T(8,128)(2,1)}, u32[]{:S(2)}, u32[]{:S(2)}) collective-permute-start(bf16[1408,1024]{1,0:T(8,128)(2,1)} %get-tuple-element.273), channel_id=1, source_target_pairs={{0,1},{1,0},{2,3},{3,2},{4,5},{5,4},{6,7},{7,6},{8,9},{9,8},{10,11... | collective-permute-start | bytes 8650760 | tf_op jit(solution)/shard_map/ppermute | solution.py:359
  1327.2 51.9 %all-to-all-start.9 = ((bf16[4,128,1024]{2,1,0:T(8,128)(2,1)}), bf16[4,128,1024]{2,1,0:T(8,128)(2,1)}, u32[]{:S(2)}, u32[]{:S(2)}) async-start(bf16[4,128,1024]{2,1,0:T(8,128)(2,1)} %bitcast.131), calls=%async_computation.9 | async-start | bytes 2097152 | tf_op jit(solution)/shard_map/all_to_all | solution.py:458
  1343.5 37.0 %collective-permute-start.24 = (bf16[512,2048]{1,0:T(8,128)(2,1)}, bf16[512,2048]{1,0:T(8,128)(2,1)}, u32[]{:S(2)}, u32[]{:S(2)}) collective-permute-start(bf16[512,2048]{1,0:T(8,128)(2,1)} %add_convert_fusion.7), channel_id=1, source_target_pairs={{0,16},{16,0},{1,17},{17,1},{2,18},{18,2},{3,19},{19,3},{4,20},{20... | collective-permute-start | bytes 6291464 | tf_op jit(solution)/shard_map/ppermute | solution.py:356
  1391.8 17.0 %copy-start.14 = (bf16[1408,1024]{1,0:T(8,128)(2,1)S(1)}, bf16[1408,1024]{1,0:T(8,128)(2,1)}, u32[]{:S(2)}) copy-start(bf16[1408,1024]{1,0:T(8,128)(2,1)} %get-tuple-element.260) | copy-start | bytes 8650756
  1392.6 14.7 %all-to-all-start.10 = ((f32[16,1,256]{2,1,0:T(1,128)}), f32[16,1,256]{2,1,0:T(1,128)S(1)}, u32[]{:S(2)}, u32[]{:S(2)}) async-start(f32[16,1,256]{2,1,0:T(1,128)} %reshape.375), calls=%async_computation.11 | async-start | bytes 32768 | tf_op jit(solution)/shard_map/all_to_all | solution.py:704
  1403.4 11.6 collective-permute-start.26
  1408.6 5.8 collective-permute-start.25
  (64 other events, 305.1 us)
Sparse Core Ops, SparseCore 0:
  11.9 194.3 all-gather.4
  208.4 72.6 all-gather.6
  282.6 74.4 all-gather.8
  358.5 74.4 all-gather.10
  863.3 71.7 reduce-scatter.4
  958.4 245.5 reduce-scatter.2

commit v6 on v5

--- a/solution.py
+++ b/solution.py
@@ -110,8 +110,7 @@
     do_ref,
     cos_ref,
     sin_ref,
-    out_qk,
-    out_v,
+    out_ref,
     dk_ref,
     dv_ref,
 ):
@@ -138,14 +137,14 @@
         back = dot(grad_scores, keys, 1, 0) * scale
         cos, sin = cos_ref[rows, :], sin_ref[rows, :]
         back = back * cos - pltpu.roll(back, HD // 2, 1) * sin
-        store_tile(out_qk, perm, t, block, slice(0, HD), back.astype(bf16))
+        store_tile(out_ref, perm, t, block, slice(0, HD), back.astype(bf16))
     for t in range(tiles):
         rows = slice(t * TILE, (t + 1) * TILE)
         cos, sin = cos_ref[rows, :], sin_ref[rows, :]
         back = dk_ref[rows, :] * scale
         back = back * cos - pltpu.roll(back, HD // 2, 1) * sin
-        store_tile(out_qk, perm, t, block, slice(HD, 2 * HD), back.astype(bf16))
-        store_tile(out_v, perm, t, block, slice(None), dv_ref[rows, :].astype(bf16))
+        store_tile(out_ref, perm, t, block, slice(HD, 2 * HD), back.astype(bf16))
+        store_tile(out_ref, perm, t, block, slice(2 * HD, 3 * HD), dv_ref[rows, :].astype(bf16))
 
 
 def attention_forward(perm, block, pre, cos, sin):
@@ -159,9 +158,9 @@
             num_scalar_prefetch=1,
             grid=(heads,),
             in_specs=[
-                pl.BlockSpec((rows, HD), lambda h, p: (0, 2 * h)),
-                pl.BlockSpec((rows, HD), lambda h, p: (0, 2 * h + 1)),
-                pl.BlockSpec((rows, HD), lambda h, p: (0, 2 * heads + h)),
+                pl.BlockSpec((rows, HD), lambda h, p: (0, 3 * h)),
+                pl.BlockSpec((rows, HD), lambda h, p: (0, 3 * h + 1)),
+                pl.BlockSpec((rows, HD), lambda h, p: (0, 3 * h + 2)),
                 table,
                 table,
             ],
@@ -182,13 +181,10 @@
             num_scalar_prefetch=1,
             grid=(heads,),
             in_specs=[per_head] * 5 + [table, table],
-            out_specs=[pl.BlockSpec((rows, 2 * HD), lambda h, p: (0, h)), per_head],
+            out_specs=pl.BlockSpec((rows, 3 * HD), lambda h, p: (0, h)),
             scratch_shapes=[pltpu.VMEM((rows, HD), f32), pltpu.VMEM((rows, HD), f32)],
         ),
-        out_shape=[
-            jax.ShapeDtypeStruct((rows, 2 * heads * HD), bf16),
-            jax.ShapeDtypeStruct((rows, heads * HD), bf16),
-        ],
+        out_shape=jax.ShapeDtypeStruct((rows, 3 * heads * HD), bf16),
         name="attention_backward",
     )(perm, q, k, v, log_total, grad, cos, sin)
 
@@ -385,10 +381,9 @@
     def own_columns(w):
         return lax.dynamic_slice_in_dim(w, core * width, width, axis=1)
 
-    by_head = [own_columns(w).reshape(-1, heads, HD) for w in (w_query, w_key)]
+    by_head = [own_columns(w).reshape(-1, heads, HD) for w in (w_query, w_key, w_value)]
     packed = jnp.concatenate(
-        [jnp.stack(by_head, axis=2).reshape(-1, 2 * width), own_columns(w_value), own_columns(w_out)],
-        axis=1,
+        [jnp.stack(by_head, axis=2).reshape(-1, 3 * width), own_columns(w_out)], axis=1
     )
     packed = with_layout_constraint(packed, Layout(major_to_minor=(0, 1)))
     gathered = lax.all_gather(packed, "fsdp", axis=0, tiled=True)
@@ -424,30 +419,19 @@
     mine = lax.axis_index("fsdp")
     my_column, my_side = (mine % repeats) // pair, mine % pair
 
-    def feature_order(relative):
-        index = jnp.arange(D, dtype=jnp.int32)
-        rest, j = index // per, index % per
-        rest, c = rest // ctx_count, rest % ctx_count
-        if relative:
-            rest, e = rest // EXPERTS, rest % EXPERTS
-            w, t = rest // columns, rest % columns
-            t, w = (my_column + t) % columns, (my_side + w) % pair
-            rest = e * repeats + t * pair + w
-        source = c * (D // ctx_count) + rest * per + j
-        shuffle = (jnp.arange(D, dtype=jnp.int32)[:, None] == source[None, :]).astype(bf16)
-        return dot(normed, shuffle, 1, 0, bf16)
-
-    normed_side, normed_mixed = feature_order(True), feature_order(False)
+    index = jnp.arange(D, dtype=jnp.int32)
+    source = (index // per % ctx_count) * (D // ctx_count)
+    source = source + index // (per * ctx_count) * per + index % per
+    shuffle = (index[:, None] == source[None, :]).astype(bf16)
+    normed_mixed = dot(normed, shuffle, 1, 0, bf16)
 
     def weight_part(w):
         count = w.shape[0] // ctx_count
         return lax.dynamic_slice_in_dim(w, core * count, count, axis=0)
 
     weight_parts = [weight_part(w) for w in (w_gate, w_up, w_down)]
-    gathered, *tied = after(gathered, normed_side, normed_mixed, *grad_blocks, *weight_parts)
-    normed_side, normed_mixed = tied[:2]
-    grad_blocks, weight_parts = tied[2 : 2 + halves], tied[2 + halves :]
-    full_qk, full_v = gathered[:, : 2 * width], gathered[:, 2 * width : 3 * width]
+    gathered, normed_mixed, *tied = after(gathered, normed_mixed, *grad_blocks, *weight_parts)
+    grad_blocks, weight_parts = tied[:halves], tied[halves:]
     out_columns = gathered[:, 3 * width :]
     full_qkv = gathered[:, : 3 * width]
 
@@ -562,7 +546,7 @@
     home_first = swap_experts(home_first)
     state = hidden_part(columns, slot_parts[columns], state)
     back[columns] = grad_rows(columns, state)
-    back[columns], *state = after(back[columns], *state)
+    back[columns], home_first, *state = after(back[columns], home_first, *state)
     hidden, grad_gate, grad_up = state
     all_slots = jnp.concatenate(slot_parts, axis=0)
     all_grads = jnp.concatenate(grad_parts, axis=0)
@@ -618,13 +602,6 @@
         size = a.shape[0] // n
         return [a[i * size : (i + 1) * size] for i in range(n)]
 
-    def side_shift(a, d):
-        return pair_swap(a)
-
-    def first_blocks(left, grad, n):
-        size = D // n
-        return [dot(left[:, i * size : (i + 1) * size], grad, 0, 0, bf16) for i in range(n)]
-
     def expert_sum(total):
         blocks = swap_experts(total, total.shape[1])
         return jnp.sum(blocks.reshape(EXPERTS, -1, total.shape[1]).astype(f32), axis=0)
@@ -643,62 +620,52 @@
     down_grad = side_sum(down_total)
     came_o = [column_shift(block, d) for d, block in enumerate(blocks_o) if d]
     grad_context = dot(grad_attention, w_o, 1, 1, bf16)
-    grad_qk, grad_v = attention_backward(
+    grad_qkv = attention_backward(
         perm, block, q, k, v, log_total, grad_context, cos, sin
     )
-    qk_part = dot(normed_mixed, grad_qk, 0, 0, bf16)
-    qk_sum = lax.psum_scatter(qk_part, "fsdp", scatter_dimension=0, tiled=True)
-    got = after(qk_part, grad_qk, grad_v, hidden_t, grad_gate, grad_up, *away_first)
-    grad_qk, grad_v, hidden_t, gate_t, up_t, *away_first = got[1:]
+    qkv_part = dot(normed_mixed, grad_qkv, 0, 0, bf16)
+    qkv_sum = lax.psum_scatter(qkv_part, "fsdp", scatter_dimension=0, tiled=True)
+
+    got = after(qkv_part, grad_qkv, hidden_t, grad_gate, grad_up, *away_first)
+    grad_qkv, hidden_t, gate_t, up_t, *away_first = got[1:]
     gate_part = dot(gate_t, all_slots, 0, 0, bf16)
-    gate_part, grad_v, hidden_t = after(gate_part, grad_v, hidden_t)
-    gate_total = core_sum(gate_part)
+    gate_part, hidden_t = after(gate_part, hidden_t)
     outs_first = add_parts(out_rows_of(0, 0, hidden_t), away_first)
     away_second = [out_rows_of(1, j, hidden_t) for j in range(1, columns)]
-    blocks_v = first_blocks(normed_side, grad_v, pair)
-    got = after(outs_first, up_t, hidden_t, gate_total, *blocks_v, *away_second, *came_o)
-    outs_first, up_t, hidden_t, gate_total = got[:4]
-    blocks_v, came_o = got[4 : 4 + pair], got[3 + pair + columns :]
-    away_second = columns_home(got[4 + pair : 3 + pair + columns])
+    gate_total = core_sum(gate_part)
+    got = after(outs_first, gate_total, up_t, *away_second, *came_o)
+    outs_first, gate_total, up_t = got[:3]
+    away_second, came_o = columns_home(got[3 : 2 + columns]), got[2 + columns :]
+    outs_first = swap_experts(outs_first)
+    gate_own, gate_came = side_swap_sum(gate_total)
     blocks_o = row_blocks(add_parts(blocks_o[0], came_o), pair, my_side)
-    outs_first = swap_experts(outs_first)
-    came_v = pair_swap(blocks_v[1])
+    up_t, *blocks_o = after(up_t, *blocks_o)
+    came_o = pair_swap(blocks_o[1])
 
     up_part = dot(up_t, all_slots, 0, 0, bf16)
-    came_o = pair_swap(blocks_o[1])
-    got = after(
-        up_part, hidden_t, gate_total, outs_first, came_v, came_o, grad_qk, *away_second
-    )
-    up_part, hidden_t, gate_total, outs_first, came_v, came_o, grad_qk, *away_second = got
-    gate_own, gate_came = side_swap_sum(gate_total)
-    out_grad = expert_sum(add_parts(blocks_o[0], [came_o]))
-    blocks_v = cut(add_parts(blocks_v[0], [came_v]), columns)
-    came_v = [column_shift(block, d) for d, block in enumerate(blocks_v) if d]
-    own_second = out_rows_of(1, 0, hidden_t)
+    got = after(up_part, hidden_t, grad_qkv, outs_first, came_o, gate_came, *away_second)
+    up_part, hidden_t, grad_qkv, outs_first, came_o, gate_came, *away_second = got
+    gate_grad = gate_own.astype(f32) + gate_came.astype(f32)
+    outs_second = add_parts(out_rows_of(1, 0, hidden_t), away_second)
     up_total = core_sum(up_part)
-    outs_second, out_grad = after(add_parts(own_second, away_second), out_grad)
+    outs_second, up_total, grad_qkv = after(outs_second, up_total, grad_qkv)
     outs_second = swap_experts(outs_second)
-    got = after(up_total, grad_qk, gate_own, gate_came, outs_second, *came_v)
-    up_total, grad_qk, gate_own, gate_came, outs_second, *came_v = got
-    value_part = expert_sum(add_parts(blocks_v[0], came_v)).reshape(ctx_count, per, width)
     up_own, up_came = side_swap_sum(up_total)
 
     def back_rows(s, out):
-        part = slice(s * rows, (s + 1) * rows)
-        return (dot(grad_qk[part], full_qk, 1, 1) + dot(grad_v[part], full_v, 1, 1)).astype(out)
+        return dot(grad_qkv[s * rows : (s + 1) * rows], full_qkv, 1, 1, out)
 
     back_away = [back_rows(s, bf16) for s in range(1, ctx_count)]
     grad_normed = back_rows(0, f32)
-    grad_normed, qk_sum = after(grad_normed, qk_sum)
-    gate_grad = gate_own.astype(f32) + gate_came.astype(f32)
     for s in range(1, ctx_count):
         grad_normed = grad_normed + core_shift(back_away[s - 1], -s).astype(f32)
     _, unit_one, inverse_one = normalize_parts(inputs, norm1_gain)
     grad_norm_one, norm1_part = norm_backward(grad_normed, unit_one, inverse_one, norm1_gain)
     tokens_grad = (grad_hidden_in + grad_norm_one).astype(bf16)
-    up_own, up_came, value_part, norm1_part, tokens_grad = after(
-        up_own, up_came, value_part, norm1_part, tokens_grad
+    tokens_grad, norm1_part, outs_second, up_own, up_came, qkv_sum = after(
+        tokens_grad, norm1_part, outs_second, up_own, up_came, qkv_sum
     )
+    out_grad = expert_sum(add_parts(blocks_o[0], [came_o]))
 
     gains = jnp.stack([norm1_part, norm2_part]).reshape(2, ctx_count, fsdp_count, per)
     gains = lax.all_to_all(gains.transpose(2, 1, 0, 3), "fsdp", 0, 0, tiled=True)
@@ -711,14 +678,8 @@
     for s in range(1, ctx_count):
         gains_own = gains_own + core_shift(gains_of(core + s), s)
     up_grad = up_own.astype(f32) + up_came.astype(f32)
-    qk_parts = qk_sum.astype(f32).reshape(ctx_count, per, heads, 2, HD)
-    sums = jnp.stack(
-        [
-            qk_parts[:, :, :, 0].reshape(ctx_count, per, width),
-            qk_parts[:, :, :, 1].reshape(ctx_count, per, width),
-            value_part,
-        ]
-    )
+    sums = qkv_sum.reshape(ctx_count, per, heads, 3, HD).astype(f32)
+    sums = sums.transpose(3, 0, 1, 2, 4).reshape(3, ctx_count, per, width)
 
     def core_piece(c):
         return lax.dynamic_index_in_dim(sums, c % ctx_count, 1, keepdims=False)

time: 1430 us -> 1300 us (0.909)
  blocking collectives: 61.7 us -> 0 us
  matrix products: 271 us -> 239 us
  starting transfers between devices: 77.8 us -> 63 us
    all_to_all x1 -> x0, blocking collectives: 61.7 us -> none  [swap_experts(): lax.all_to_all(blocks, 'fsdp', 0, 0, axis_index_groups=lines, tiled=True)]
    dot_general x24 -> x19, matrix products: 271 us -> 239 us  [dot(): lax.dot_general(a, b, (((ca,), (cb,)), ((), ())), preferred_element_type=...]
    ppermute x14 -> x12, waiting for transfers between devices: 178 us -> 158 us  [fsdp_shift(): return lax.ppermute(a, 'fsdp', [(i, move(i)) for i in range(fsdp_count)])]
  transfers between devices with their start and end apart: 43 -> 41, of which waited for: 15 -> 16; matrix products, arithmetic and copies ran while one was open for 32% -> 31% of each run, Pallas kernels for 24% -> 27%
where the time goes in v6:
time: 1300 us; the launch traced here: 1290 us
  waiting for transfers between devices  422 us (32%)
  Pallas kernels  348 us (27%)
  matrix products  239 us (18%)
  other arithmetic  113 us (9%)
  local copies, waits for them, and re-layouts  93.6 us (7%)
  starting transfers between devices  63 us (5%)
  between operations  15.4 us (1%)
    dot_general x19, matrix products, dot(): lax.dot_general(a, b, (((ca,), (cb,)), ((), ())), preferred_element_type=...  239 us
    ppermute x12, waiting for transfers between devices, fsdp_shift(): return lax.ppermute(a, 'fsdp', [(i, move(i)) for i in range(fsdp_count)])  158 us
    all_gather x1, waiting for transfers between devices, shards(): gathered = lax.all_gather(packed, 'fsdp', axis=0, tiled=True)  154 us
    pallas_call x8, Pallas kernels, expert_rows(): pl.pallas_call(functools.partial(rows_kernel, len(left)), grid=(D // tile...  139 us
    pallas_call x4, Pallas kernels, expert_hidden(): pl.pallas_call(functools.partial(expert_kernel, len(kept)), grid=(units /...  122 us
    all_gather x3, waiting for transfers between devices, shards(): lax.all_gather(part, 'fsdp', axis=0, tiled=True, axis_index_groups=sides)  87.8 us
    all_to_all x9, starting transfers between devices, swap_experts(): lax.all_to_all(blocks, 'fsdp', 0, 0, axis_index_groups=lines, tiled=True)  43.3 us
    pallas_call x3, Pallas kernels, join_weights(): pl.pallas_call(functools.partial(join_kernel, own_blocks, part_blocks), g...  37.5 us
  transfers between devices with their start and end apart: 41, of which 16 were waited for; matrix products, arithmetic and copies ran while one was open for 31% of the time, Pallas kernels for 27%

profile of v6, /device:TPU:0, one launch (start us, length us, event | category | flops | bytes accessed | tf_op | source)
XLA Modules:
  0.0 1292.7 jit_solution(17586855647012761054)
XLA Ops:
  24.0 6.9 constant_dynamic-slice_fusion.16
  41.0 13.4 %fusion.29 = bf16[1024,2048]{1,0:T(8,128)(2,1)} fusion(s32[2048]{0:T(1024)S(1)} %fusion.86, bf16[512,2048]{1,0:T(8,128)(2,1)} %collective-permute-done, bf16[512,2048]{1,0:T(8,128)(2,1)} %fusion.19), kind=kOutput, calls=%fused_computation.62 | convolution fusion | flops 8604614656 | bytes 8396800 | tf_op jit(solution)/shard_map/dot_general | solution.py:28
  54.3 153.6 %all-gather.5.cloned.1.call-done = bf16[2048,4096]{1,0:T(8,128)(2,1)} async-done(((bf16[128,4096]{1,0:T(8,128)(2,1)}), bf16[2048,4096]{1,0:T(8,128)(2,1)}) %all-gather.5.cloned.1.call-update) | async-done | bytes 16777232 | tf_op jit(solution)/shard_map/all_gather | solution.py:389
  228.3 19.0 %fusion.12.pre_q.pre_k.pre_v = f32[1024,3072]{1,0:T(8,128)} fusion(bf16[2048,4096]{1,0:T(8,128)(2,1)} %all-gather.5.cloned.1.call-done, bf16[512,2048]{1,0:T(8,128)(2,1)} %collective-permute-done, bf16[512,2048]{1,0:T(8,128)(2,1)} %fusion.19), kind=kOutput, calls=%fused_computation.20 | convolution fusion | flops 12893290496 | bytes 29360128 | tf_op jit(solution)/shard_map/dot_general | solution.py:28
  247.3 21.7 %attention_forward.1 = (bf16[1024,1024]{1,0:T(8,128)(2,1)}, bf16[1024,1024]{1,0:T(8,128)(2,1)}, bf16[1024,1024]{1,0:T(8,128)(2,1)}, bf16[1024,1024]{1,0:T(8,128)(2,1)}, f32[1024,1024]{1,0:T(8,128)}) custom-call(s32[4]{0:T(128)} %fusion.95.perm, f32[1024,3072]{1,0:T(8,128)} %fusion.12.pre_q.pre_k.pre_v, f32[1024,3072]{1,0:T(8,128)} %fusion.12.pre_q.pre_k.pre_v, ...), custom_call_target="tpu_custom_call" | custom-call | tf_op jit(solution)/shard_map/attention_forward/pallas_call | solution.py:155
  278.2 6.2 all-to-all-done
  294.0 6.6 multiply_reduce_fusion.2
  307.0 51.2 %all-gather.9.cloned.1.call-done = bf16[1408,2048]{1,0:T(8,128)(2,1)} async-done(((bf16[704,2048]{1,0:T(8,128)(2,1)}), bf16[1408,2048]{1,0:T(8,128)(2,1)}) %all-gather.9.cloned.1.call-update) | async-done | bytes 5767184 | tf_op jit(solution)/shard_map/all_gather | solution.py:452
  372.3 12.7 join_weights.3.wg_ref.refs_2_
  385.0 12.5 join_weights.4.wu_ref.refs_3_
  397.5 36.6 %all-gather.11.cloned.1.call-done = bf16[1408,2048]{1,0:T(8,128)(2,1)} async-done(((bf16[704,2048]{1,0:T(8,128)(2,1)}), bf16[1408,2048]{1,0:T(8,128)(2,1)}) %all-gather.11.cloned.1.call-update) | async-done | bytes 5767184 | tf_op jit(solution)/shard_map/all_gather | solution.py:452
  446.4 12.4 join_weights.5.wd_ref.refs_1_
  458.8 30.7 %expert_hidden.4 = (bf16[2560,2816]{1,0:T(8,128)(2,1)}, bf16[2560,2816]{1,0:T(8,128)(2,1)}, bf16[2560,2816]{1,0:T(8,128)(2,1)}) custom-call(bf16[640,2048]{1,0:T(8,128)(2,1)} %bitcast.113, bf16[640,2048]{1,0:T(8,128)(2,1)} %bitcast.15.g_ref, bf16[2816,2048]{1,0:T(8,128)(2,1)} %join_weights.3.wg_ref.refs_2_, bf16[2816,2048]{1,0:T(8,128)(2,1)} %join_weights.4.wu_ref.refs_3_, ...), custom_call_target="tpu_custom_call" | custom-call | tf_op jit(solution)/shard_map/expert_hidden/pallas_call | solution.py:213
  489.5 10.9 collective-permute-done.8.x_ref
  501.9 30.6 %expert_hidden.5 = (bf16[2560,2816]{1,0:T(8,128)(2,1)}, bf16[2560,2816]{1,0:T(8,128)(2,1)}, bf16[2560,2816]{1,0:T(8,128)(2,1)}) custom-call(bf16[640,2048]{1,0:T(8,128)(2,1)} %collective-permute-done.8.x_ref, bf16[640,2048]{1,0:T(8,128)(2,1)} %collective-permute-done.3.g_ref, ...), custom_call_target="tpu_custom_call", output_to_operand_aliasing={{0}: (5, {}), {1}: (6, {}), {2}: (7, {})} | custom-call | tf_op jit(solution)/shard_map/expert_hidden/pallas_call | solution.py:213
  532.5 21.1 %expert_rows.8 = bf16[640,2048]{1,0:T(8,128)(2,1)} custom-call(bf16[2560,2816]{1,0:T(8,128)(2,1)} %get-tuple-element.169.refs_0_.refs_1_, bf16[2560,2816]{1,0:T(8,128)(2,1)} %get-tuple-element.170.refs_1_.refs_2_, bf16[2816,2048]{1,0:T(8,128)(2,1)} %join_weights.3.wg_ref.refs_2_, bf16[2816,2048]{1,0:T(8,128)(2,1)} %join_weights.4.wu_ref.refs_3_), custom_call_target="tpu_custom_call" | custom-call | tf_op jit(solution)/shard_map/expert_rows/pallas_call | solution.py:233
  554.1 6.3 collective-permute-done.9.x_ref
  561.9 30.6 %expert_hidden.6 = (bf16[2560,2816]{1,0:T(8,128)(2,1)}, bf16[2560,2816]{1,0:T(8,128)(2,1)}, bf16[2560,2816]{1,0:T(8,128)(2,1)}) custom-call(bf16[640,2048]{1,0:T(8,128)(2,1)} %copy-done.15, bf16[640,2048]{1,0:T(8,128)(2,1)} %collective-permute-done.6.g_ref, ...), custom_call_target="tpu_custom_call", output_to_operand_aliasing={{0}: (5, {}), {1}: (6, {}), {2}: (7, {})} | custom-call | tf_op jit(solution)/shard_map/expert_hidden/pallas_call | solution.py:213
  592.5 21.1 %expert_rows.9 = bf16[640,2048]{1,0:T(8,128)(2,1)} custom-call(bf16[2560,2816]{1,0:T(8,128)(2,1)} %get-tuple-element.184.refs_0_.refs_1_, bf16[2560,2816]{1,0:T(8,128)(2,1)} %get-tuple-element.185.refs_1_.refs_2_, bf16[2816,2048]{1,0:T(8,128)(2,1)} %join_weights.3.wg_ref.refs_2_, bf16[2816,2048]{1,0:T(8,128)(2,1)} %join_weights.4.wu_ref.refs_3_), custom_call_target="tpu_custom_call" | custom-call | tf_op jit(solution)/shard_map/expert_rows/pallas_call | solution.py:233
  613.6 21.1 %expert_rows.10 = bf16[640,2048]{1,0:T(8,128)(2,1)} custom-call(bf16[2560,2816]{1,0:T(8,128)(2,1)} %get-tuple-element.184.refs_0_.refs_1_, bf16[2560,2816]{1,0:T(8,128)(2,1)} %get-tuple-element.185.refs_1_.refs_2_, bf16[2816,2048]{1,0:T(8,128)(2,1)} %join_weights.3.wg_ref.refs_2_, bf16[2816,2048]{1,0:T(8,128)(2,1)} %join_weights.4.wu_ref.refs_3_), custom_call_target="tpu_custom_call" | custom-call | tf_op jit(solution)/shard_map/expert_rows/pallas_call | solution.py:233
  639.9 5.5 all-to-all-start.4
  647.0 30.6 %expert_hidden.7 = (bf16[2560,2816]{1,0:T(8,128)(2,1)}, bf16[2560,2816]{1,0:T(8,128)(2,1)}, bf16[2560,2816]{1,0:T(8,128)(2,1)}) custom-call(bf16[640,2048]{1,0:T(8,128)(2,1)} %bitcast.24.x_ref, bf16[640,2048]{1,0:T(8,128)(2,1)} %bitcast.17.g_ref, ...), custom_call_target="tpu_custom_call", output_to_operand_aliasing={{0}: (5, {}), {1}: (6, {}), {2}: (7, {})} | custom-call | tf_op jit(solution)/shard_map/expert_hidden/pallas_call | solution.py:213
  677.5 21.1 %expert_rows.11 = bf16[640,2048]{1,0:T(8,128)(2,1)} custom-call(bf16[2560,2816]{1,0:T(8,128)(2,1)} %get-tuple-element.207.refs_0_, bf16[2560,2816]{1,0:T(8,128)(2,1)} %get-tuple-element.217.refs_1_, bf16[2816,2048]{1,0:T(8,128)(2,1)} %join_weights.3.wg_ref.refs_2_, bf16[2816,2048]{1,0:T(8,128)(2,1)} %join_weights.4.wu_ref.refs_3_), custom_call_target="tpu_custom_call" | custom-call | tf_op jit(solution)/shard_map/expert_rows/pallas_call | solution.py:233
  712.3 38.6 %convolution_convert_fusion.2 = bf16[2816,2048]{1,0:T(8,128)(2,1)} fusion(bf16[2560,2816]{1,0:T(8,128)(2,1)} %get-tuple-element.224.refs_0_, bf16[640,2048]{1,0:T(8,128)(2,1)} %collective-permute-done.6.g_ref, bf16[640,2048]{1,0:T(8,128)(2,1)} %bitcast.17.g_ref, bf16[640,2048]{1,0:T(8,128)(2,1)} %collective-permute-done.3.g_ref, ...), kind=kOutput, calls=%fused_computation.7 | convolution fusion | flops 29575610368 | bytes 36438016 | tf_op jit(solution)/shard_map/dot_general | solution.py:28
  750.9 5.8 constant_dynamic-slice_fusion.11
  756.7 13.6 %expert_rows.12 = bf16[640,2048]{1,0:T(8,128)(2,1)} custom-call(bf16[2560,2816]{1,0:T(8,128)(2,1)} %get-tuple-element.224.refs_0_, bf16[2816,2048]{1,0:T(8,128)(2,1)} %join_weights.5.wd_ref.refs_1_), custom_call_target="tpu_custom_call" | custom-call | tf_op jit(solution)/shard_map/expert_rows/pallas_call | solution.py:233
  792.0 9.7 add_convert_fusion.2
  801.7 7.2 convolution_convert_fusion.4
  814.3 5.7 convolution_convert_fusion.10.do_ref
  820.1 27.3 %attention_backward.1 = bf16[1024,3072]{1,0:T(8,128)(2,1)} custom-call(s32[4]{0:T(128)} %fusion.95.perm, bf16[1024,1024]{1,0:T(8,128)(2,1)} %get-tuple-element.130.q_ref, bf16[1024,1024]{1,0:T(8,128)(2,1)} %get-tuple-element.131.k_ref, bf16[1024,1024]{1,0:T(8,128)(2,1)} %get-tuple-element.132.v_ref, f32[1024,1024]{1,0:T(8,128)} %get-tuple-element.133.log_ref, ...), custom_call_target="tpu_custom_call" | custom-call | tf_op jit(solution)/shard_map/attention_backward/pallas_call | solution.py:178
  847.5 19.3 %convolution_convert_fusion.3 = bf16[2048,3072]{1,0:T(8,128)(2,1)} fusion(bf16[1024,2048]{1,0:T(8,128)(2,1)} %fusion.29, bf16[1024,3072]{1,0:T(8,128)(2,1)} %attention_backward.1), kind=kOutput, calls=%fused_computation.8 | convolution fusion | flops 12891193344 | bytes 23068672 | tf_op jit(solution)/shard_map/dot_general | solution.py:28
  866.8 35.6 %convolution_convert_fusion.1 = bf16[2816,2048]{1,0:T(8,128)(2,1)S(1)} fusion(bf16[2560,2816]{1,0:T(8,128)(2,1)} %get-tuple-element.207.refs_0_, bf16[2560,2048]{1,0:T(8,128)(2,1)} %copy-done.30), kind=kOutput, calls=%fused_computation.6 | convolution fusion | flops 29533667328 | bytes 36438016 | tf_op jit(solution)/shard_map/dot_general | solution.py:28
  909.2 13.5 %expert_rows.13 = bf16[640,2048]{1,0:T(8,128)(2,1)} custom-call(bf16[2560,2816]{1,0:T(8,128)(2,1)} %get-tuple-element.224.refs_0_, bf16[2816,2048]{1,0:T(8,128)(2,1)} %join_weights.5.wd_ref.refs_1_), custom_call_target="tpu_custom_call" | custom-call | tf_op jit(solution)/shard_map/expert_rows/pallas_call | solution.py:233
  922.6 13.6 %expert_rows.14 = bf16[640,2048]{1,0:T(8,128)(2,1)} custom-call(bf16[2560,2816]{1,0:T(8,128)(2,1)} %get-tuple-element.224.refs_0_, bf16[2816,2048]{1,0:T(8,128)(2,1)} %join_weights.5.wd_ref.refs_1_), custom_call_target="tpu_custom_call" | custom-call | tf_op jit(solution)/shard_map/expert_rows/pallas_call | solution.py:233
  940.6 10.2 add_convert_fusion.1
  950.8 23.3 %collective-permute-done.16 = bf16[512,2048]{1,0:T(8,128)(2,1)} collective-permute-done((bf16[512,2048]{1,0:T(8,128)(2,1)}, bf16[512,2048]{1,0:T(8,128)(2,1)}, u32[]{:S(2)}, u32[]{:S(2)}) %collective-permute-start.16) | collective-permute-done | bytes 2097184 | tf_op jit(solution)/shard_map/ppermute | solution.py:355
  987.5 38.5 %convolution_convert_fusion = bf16[2816,2048]{1,0:T(8,128)(2,1)} fusion(bf16[2560,2816]{1,0:T(8,128)(2,1)} %get-tuple-element.217.refs_1_, bf16[2560,2048]{1,0:T(8,128)(2,1)} %copy-done.30), kind=kOutput, calls=%fused_computation.5 | convolution fusion | flops 29533667328 | bytes 36438016 | tf_op jit(solution)/shard_map/dot_general | solution.py:28
  1026.1 37.8 %collective-permute-done.19 = bf16[640,2048]{1,0:T(8,128)(2,1)S(1)} collective-permute-done((bf16[640,2048]{1,0:T(8,128)(2,1)S(1)}, bf16[640,2048]{1,0:T(8,128)(2,1)S(1)}, u32[]{:S(2)}, u32[]{:S(2)}) %collective-permute-start.19) | collective-permute-done | bytes 2621472 | tf_op jit(solution)/shard_map/ppermute | solution.py:355
  1065.3 34.9 %collective-permute-done.18 = bf16[1408,1024]{1,0:T(8,128)(2,1)} collective-permute-done((bf16[1408,1024]{1,0:T(8,128)(2,1)S(1)}, bf16[1408,1024]{1,0:T(8,128)(2,1)}, u32[]{:S(2)}, u32[]{:S(2)}) %collective-permute-start.18) | collective-permute-done | bytes 2883616 | tf_op jit(solution)/shard_map/ppermute | solution.py:355
  1100.2 6.8 constant_dynamic-slice_fusion.4
  1107.0 13.7 %expert_rows.15 = bf16[640,2048]{1,0:T(8,128)(2,1)} custom-call(bf16[2560,2816]{1,0:T(8,128)(2,1)} %get-tuple-element.224.refs_0_, bf16[2816,2048]{1,0:T(8,128)(2,1)} %join_weights.5.wd_ref.refs_1_), custom_call_target="tpu_custom_call" | custom-call | tf_op jit(solution)/shard_map/expert_rows/pallas_call | solution.py:233
  1133.4 10.5 add_convert_fusion
  1143.9 10.7 fusion.36
  1154.9 6.6 convert_add_fusion.3
  1183.4 13.3 %fusion.25 = (f32[2048]{0:T(1024)S(1)}, f32[512]{0:T(512)S(1)}, f32[512,2048]{1,0:T(8,128)}) fusion(bf16[1,512,2048]{2,1,0:T(8,128)(2,1)S(1)} %copy-done.3, f32[512]{0:T(512)S(1)} %copy-done.43, f32[2048]{0:T(1024)S(1)} %copy-done.32, bf16[512,2048]{1,0:T(8,128)(2,1)} %collective-permute-done.21, bf16[2048,4096]{1,0:T(8,128)(2,1)} %all-gather.5.cloned.1.call-done, ...), kind=kOutput, calls=%fused_computation.47 | convolution fusion | flops 6451885568 | bytes 24137728 | tf_op jit(solution)/shard_map/dot_general | solution.py:28
  1196.8 5.4 fusion.24
  1202.2 44.5 %collective-permute-done.22 = bf16[1408,1024]{1,0:T(8,128)(2,1)} collective-permute-done((bf16[1408,1024]{1,0:T(8,128)(2,1)}, bf16[1408,1024]{1,0:T(8,128)(2,1)}, u32[]{:S(2)}, u32[]{:S(2)}) %collective-permute-start.22) | collective-permute-done | bytes 2883616 | tf_op jit(solution)/shard_map/ppermute | solution.py:355
  1277.0 5.6 convert_add_fusion.2
  (297 shorter events, 243.3 us)
Async XLA Ops:
  7.2 200.7 %all-gather.5.cloned.1.call-start = ((), (), s32[]{:S(2)}) async-start(), calls=%async_computation.12 | async-start | bytes 17825792 | tf_op jit(solution)/shard_map/all_gather | solution.py:389
  13.4 293.5 %all-gather.7.cloned.1.call-start = ((), (), s32[]{:S(2)}) async-start(), calls=%async_computation.13 | async-start | bytes 8650752 | tf_op jit(solution)/shard_map/all_gather | solution.py:452
  15.9 25.1 %collective-permute-start = (bf16[512,2048]{1,0:T(8,128)(2,1)}, bf16[512,2048]{1,0:T(8,128)(2,1)}, u32[]{:S(2)}, u32[]{:S(2)}) collective-permute-start(bf16[512,2048]{1,0:T(8,128)(2,1)} %fusion.19), channel_id=1, source_target_pairs={{0,16},{16,0},{1,17},{17,1},{2,18},{18,2},{3,19},{19,3},{4,20},{20... | collective-permute-start | bytes 6291464 | tf_op jit(solution)/shard_map/ppermute | solution.py:352
  20.1 271.0 %copy-start.36 = (s32[512]{0:T(512)}, s32[512]{0:T(512)S(1)}, u32[]{:S(2)}) copy-start(s32[512]{0:T(512)S(1)} %get-tuple-element.245) | copy-start | bytes 6148
  20.1 271.0 %copy-start.39 = (s32[512]{0:T(512)}, s32[512]{0:T(512)S(1)}, u32[]{:S(2)}) copy-start(s32[512]{0:T(512)S(1)} %get-tuple-element.246) | copy-start | bytes 6148
  41.0 167.1 %copy-start.57 = (s32[1,4]{1,0:T(1,128)S(1)}, s32[1,4]{1,0:T(1,128)}, u32[]{:S(2)}) copy-start(s32[1,4]{1,0:T(1,128)} %param.17) | copy-start | bytes 52
  207.9 150.3 %all-gather.9.cloned.1.call-start = ((), (), s32[]{:S(2)}) async-start(), calls=%async_computation.14 | async-start | bytes 8650752 | tf_op jit(solution)/shard_map/all_gather | solution.py:452
  220.6 63.9 %all-to-all-start = ((bf16[4,160,2048]{2,1,0:T(8,128)(2,1)}), bf16[4,160,2048]{2,1,0:T(8,128)(2,1)}, u32[]{:S(2)}, u32[]{:S(2)}) async-start(bf16[4,160,2048]{2,1,0:T(8,128)(2,1)} %bitcast.132), calls=%async_computation | async-start | bytes 5242880 | tf_op jit(solution)/shard_map/all_to_all | solution.py:442
  228.3 40.7 %collective-permute-start.1 = (bf16[1024,1024]{1,0:T(8,128)(2,1)}, bf16[1024,1024]{1,0:T(8,128)(2,1)}, u32[]{:S(2)}, u32[]{:S(2)}) collective-permute-start(bf16[1024,1024]{1,0:T(8,128)(2,1)} %constant_dynamic-slice_fusion.15), channel_id=1, source_target_pairs={{0,16},{16,0},{1,17},{17,1},{2,18},{18,2},{3,19},{19,3},{4,20},{20... | collective-permute-start | bytes 6291464 | tf_op jit(solution)/shard_map/ppermute | solution.py:352
  284.4 73.8 %all-to-all-start.1 = ((bf16[4,160,2048]{2,1,0:T(8,128)(2,1)}), bf16[4,160,2048]{2,1,0:T(8,128)(2,1)}, u32[]{:S(2)}, u32[]{:S(2)}) async-start(bf16[4,160,2048]{2,1,0:T(8,128)(2,1)} %bitcast.130), calls=%async_computation.1 | async-start | bytes 5242880 | tf_op jit(solution)/shard_map/all_to_all | solution.py:442
  289.0 145.1 %all-gather.11.cloned.1.call-start = ((), (), s32[]{:S(2)}) async-start(), calls=%async_computation.15 | async-start | bytes 8650752 | tf_op jit(solution)/shard_map/all_gather | solution.py:452
  289.5 4.6 collective-permute-start.2
  289.6 68.6 %collective-permute-start.3 = (bf16[640,2048]{1,0:T(8,128)(2,1)}, bf16[640,2048]{1,0:T(8,128)(2,1)}, u32[]{:S(2)}, u32[]{:S(2)}) collective-permute-start(bf16[640,2048]{1,0:T(8,128)(2,1)} %bitcast.15.g_ref), channel_id=1, source_target_pairs={{0,2},{1,3},{2,0},{3,1},{4,6},{5,7},{6,4},{7,5},{8,10},{9,11},{10,... | collective-permute-start | bytes 7864328 | tf_op jit(solution)/shard_map/ppermute | solution.py:355
  358.2 75.9 %all-to-all-start.2 = ((bf16[4,160,2048]{2,1,0:T(8,128)(2,1)}), bf16[4,160,2048]{2,1,0:T(8,128)(2,1)S(1)}, u32[]{:S(2)}, u32[]{:S(2)}) async-start(bf16[4,160,2048]{2,1,0:T(8,128)(2,1)} %bitcast.133), calls=%async_computation.2 | async-start | bytes 5242880 | tf_op jit(solution)/shard_map/all_to_all | solution.py:442
  366.7 5.6 collective-permute-start.4
  369.4 15.6 %collective-permute-start.5 = (bf16[704,2048]{1,0:T(8,128)(2,1)}, bf16[704,2048]{1,0:T(8,128)(2,1)}, u32[]{:S(2)}, u32[]{:S(2)}) collective-permute-start(bf16[704,2048]{1,0:T(8,128)(2,1)} %constant_dynamic-slice_fusion.13.refs_0_), channel_id=1, source_target_pairs={{0,16},{16,0},{1,17},{17,1},{2,18},{18,2},{3,19},{19,3},{4,20},{20... | collective-permute-start | bytes 8650760 | tf_op jit(solution)/shard_map/ppermute | solution.py:352
  369.4 64.7 %collective-permute-start.6 = (bf16[640,2048]{1,0:T(8,128)(2,1)}, bf16[640,2048]{1,0:T(8,128)(2,1)}, u32[]{:S(2)}, u32[]{:S(2)}) collective-permute-start(bf16[640,2048]{1,0:T(8,128)(2,1)} %bitcast.17.g_ref), channel_id=1, source_target_pairs={{0,2},{1,3},{2,0},{3,1},{4,6},{5,7},{6,4},{7,5},{8,10},{9,11},{10,... | collective-permute-start | bytes 7864328 | tf_op jit(solution)/shard_map/ppermute | solution.py:355
  434.1 66.3 %all-to-all-start.3 = ((bf16[4,160,2048]{2,1,0:T(8,128)(2,1)}), bf16[4,160,2048]{2,1,0:T(8,128)(2,1)}, u32[]{:S(2)}, u32[]{:S(2)}) async-start(bf16[4,160,2048]{2,1,0:T(8,128)(2,1)} %bitcast.131), calls=%async_computation.3 | async-start | bytes 5242880 | tf_op jit(solution)/shard_map/all_to_all | solution.py:442
  440.9 5.5 collective-permute-start.7
  441.0 59.4 %collective-permute-start.8 = (bf16[640,2048]{1,0:T(8,128)(2,1)S(1)}, bf16[640,2048]{1,0:T(8,128)(2,1)}, u32[]{:S(2)}, u32[]{:S(2)}) collective-permute-start(bf16[640,2048]{1,0:T(8,128)(2,1)S(1)} %bitcast.112), channel_id=1, source_target_pairs={{0,2},{1,3},{2,0},{3,1},{4,6},{5,7},{6,4},{7,5},{8,10},{9,11},{10,... | collective-permute-start | bytes 7864328 | tf_op jit(solution)/shard_map/ppermute | solution.py:355
  500.4 60.0 %collective-permute-start.9 = (bf16[640,2048]{1,0:T(8,128)(2,1)}, bf16[640,2048]{1,0:T(8,128)(2,1)S(1)}, u32[]{:S(2)}, u32[]{:S(2)}) collective-permute-start(bf16[640,2048]{1,0:T(8,128)(2,1)} %bitcast.24.x_ref), channel_id=1, source_target_pairs={{0,2},{1,3},{2,0},{3,1},{4,6},{5,7},{6,4},{7,5},{8,10},{9,11},{10,... | collective-permute-start | bytes 7864328 | tf_op jit(solution)/shard_map/ppermute | solution.py:355
  553.6 81.1 %collective-permute-start.10 = (bf16[640,2048]{1,0:T(8,128)(2,1)}, bf16[640,2048]{1,0:T(8,128)(2,1)}, u32[]{:S(2)}, u32[]{:S(2)}) collective-permute-start(bf16[640,2048]{1,0:T(8,128)(2,1)} %expert_rows.8), channel_id=1, source_target_pairs={{0,2},{1,3},{2,0},{3,1},{4,6},{5,7},{6,4},{7,5},{8,10},{9,11},{10,... | collective-permute-start | bytes 7864328 | tf_op jit(solution)/shard_map/ppermute | solution.py:355
  639.9 62.5 %all-to-all-start.4 = ((bf16[4,160,2048]{2,1,0:T(8,128)(2,1)}), bf16[4,160,2048]{2,1,0:T(8,128)(2,1)S(1)}, u32[]{:S(2)}, u32[]{:S(2)}) async-start(bf16[4,160,2048]{2,1,0:T(8,128)(2,1)} %bitcast.117), calls=%async_computation.4 | async-start | bytes 5242880 | tf_op jit(solution)/shard_map/all_to_all | solution.py:442
  645.4 57.0 %collective-permute-start.11 = (bf16[640,2048]{1,0:T(8,128)(2,1)}, bf16[640,2048]{1,0:T(8,128)(2,1)}, u32[]{:S(2)}, u32[]{:S(2)}) collective-permute-start(bf16[640,2048]{1,0:T(8,128)(2,1)} %expert_rows.9), channel_id=1, source_target_pairs={{0,2},{1,3},{2,0},{3,1},{4,6},{5,7},{6,4},{7,5},{8,10},{9,11},{10,... | collective-permute-start | bytes 7864328 | tf_op jit(solution)/shard_map/ppermute | solution.py:355
  707.7 63.6 %all-to-all-start.5 = ((bf16[4,160,2048]{2,1,0:T(8,128)(2,1)}), bf16[4,160,2048]{2,1,0:T(8,128)(2,1)}, u32[]{:S(2)}, u32[]{:S(2)}) async-start(bf16[4,160,2048]{2,1,0:T(8,128)(2,1)} %bitcast.115), calls=%async_computation.5 | async-start | bytes 5242880 | tf_op jit(solution)/shard_map/all_to_all | solution.py:442
  712.3 449.2 %reduce-scatter.5.cloned.1.call-start = ((), (), s32[]{:S(2)}) async-start(), calls=%async_computation.17 | async-start | bytes 8650752 | tf_op jit(solution)/shard_map/reduce_scatter | solution.py:564
  756.7 35.2 %collective-permute-start.13 = (bf16[2816,1024]{1,0:T(8,128)(2,1)}, bf16[2816,1024]{1,0:T(8,128)(2,1)}, u32[]{:S(2)}, u32[]{:S(2)}) collective-permute-start(bf16[2816,1024]{1,0:T(8,128)(2,1)} %constant_dynamic-slice_fusion.11), channel_id=1, source_target_pairs={{0,16},{16,0},{1,17},{17,1},{2,18},{18,2},{3,19},{19,3},{4,20},{20... | collective-permute-start | bytes 17301512 | tf_op jit(solution)/shard_map/ppermute | solution.py:352
  780.6 21.1 %collective-permute-start.12 = (bf16[512,2048]{1,0:T(8,128)(2,1)S(1)}, bf16[512,2048]{1,0:T(8,128)(2,1)}, u32[]{:S(2)}, u32[]{:S(2)}) collective-permute-start(bf16[512,2048]{1,0:T(8,128)(2,1)S(1)} %fusion.106), channel_id=1, source_target_pairs={{0,16},{16,0},{1,17},{17,1},{2,18},{18,2},{3,19},{19,3},{4,20},{20... | collective-permute-start | bytes 6291464 | tf_op jit(solution)/shard_map/ppermute | solution.py:352
  790.5 76.3 %collective-permute-start.14 = (bf16[640,2048]{1,0:T(8,128)(2,1)}, bf16[640,2048]{1,0:T(8,128)(2,1)}, u32[]{:S(2)}, u32[]{:S(2)}) collective-permute-start(bf16[640,2048]{1,0:T(8,128)(2,1)} %expert_rows.12), channel_id=1, source_target_pairs={{0,2},{1,3},{2,0},{3,1},{4,6},{5,7},{6,4},{7,5},{8,10},{9,11},{10,... | collective-permute-start | bytes 7864328 | tf_op jit(solution)/shard_map/ppermute | solution.py:355
  820.1 426.6 %reduce-scatter.3.cloned.1.call-start = ((), (), s32[]{:S(2)}) async-start(), calls=%async_computation.16 | async-start | bytes 13369344 | tf_op jit(solution)/shard_map/reduce_scatter | solution.py:627
  908.4 32.2 %collective-permute-start.15 = (bf16[2816,1024]{1,0:T(8,128)(2,1)}, bf16[2816,1024]{1,0:T(8,128)(2,1)}, u32[]{:S(2)}, u32[]{:S(2)}) collective-permute-start(bf16[2816,1024]{1,0:T(8,128)(2,1)} %constant_dynamic-slice_fusion.8), channel_id=1, source_target_pairs={{0,16},{16,0},{1,17},{17,1},{2,18},{18,2},{3,19},{19,3},{4,20},{20... | collective-permute-start | bytes 17301512 | tf_op jit(solution)/shard_map/ppermute | solution.py:352
  908.4 65.6 %collective-permute-start.16 = (bf16[512,2048]{1,0:T(8,128)(2,1)}, bf16[512,2048]{1,0:T(8,128)(2,1)}, u32[]{:S(2)}, u32[]{:S(2)}) collective-permute-start(bf16[512,2048]{1,0:T(8,128)(2,1)} %bitcast.30), channel_id=1, source_target_pairs={{0,2},{1,3},{2,0},{3,1},{4,6},{5,7},{6,4},{7,5},{8,10},{9,11},{10,... | collective-permute-start | bytes 6291464 | tf_op jit(solution)/shard_map/ppermute | solution.py:355
  922.6 13.6 %copy-start.19 = (bf16[640,2048]{1,0:T(8,128)(2,1)S(1)}, bf16[640,2048]{1,0:T(8,128)(2,1)}, u32[]{:S(2)}) copy-start(bf16[640,2048]{1,0:T(8,128)(2,1)} %expert_rows.13) | copy-start | bytes 7864324
  940.6 33.4 %copy-start.20 = (bf16[4,1,128,2048]{3,2,1,0:T(8,128)(2,1)S(1)}, bf16[4,1,128,2048]{3,2,1,0:T(8,128)(2,1)}, u32[]{:S(2)}) copy-start(bf16[4,1,128,2048]{3,2,1,0:T(8,128)(2,1)} %get-tuple-element.252) | copy-start | bytes 6291460
  977.9 122.3 %all-to-all-start.6 = ((bf16[4,160,2048]{2,1,0:T(8,128)(2,1)}), bf16[4,160,2048]{2,1,0:T(8,128)(2,1)S(1)}, u32[]{:S(2)}, u32[]{:S(2)}) async-start(bf16[4,160,2048]{2,1,0:T(8,128)(2,1)} %bitcast.116), calls=%async_computation.6 | async-start | bytes 5242880 | tf_op jit(solution)/shard_map/all_to_all | solution.py:442
  982.8 43.3 %collective-permute-start.17 = (bf16[256,2048]{1,0:T(8,128)(2,1)}, bf16[256,2048]{1,0:T(8,128)(2,1)S(1)}, u32[]{:S(2)}, u32[]{:S(2)}) collective-permute-start(bf16[256,2048]{1,0:T(8,128)(2,1)} %bitcast.135), channel_id=1, source_target_pairs={{0,1},{1,0},{2,3},{3,2},{4,5},{5,4},{6,7},{7,6},{8,9},{9,8},{10,11... | collective-permute-start | bytes 3145736 | tf_op jit(solution)/shard_map/ppermute | solution.py:355
  985.1 115.1 %collective-permute-start.18 = (bf16[1408,1024]{1,0:T(8,128)(2,1)S(1)}, bf16[1408,1024]{1,0:T(8,128)(2,1)}, u32[]{:S(2)}, u32[]{:S(2)}) collective-permute-start(bf16[1408,1024]{1,0:T(8,128)(2,1)S(1)} %constant_dynamic-slice_fusion.5), channel_id=1, source_target_pairs={{0,1},{1,0},{2,3},{3,2},{4,5},{5,4},{6,7},{7,6},{8,9},{9,8},{10,11... | collective-permute-start | bytes 8650760 | tf_op jit(solution)/shard_map/ppermute | solution.py:355
  987.0 76.8 %collective-permute-start.19 = (bf16[640,2048]{1,0:T(8,128)(2,1)S(1)}, bf16[640,2048]{1,0:T(8,128)(2,1)S(1)}, u32[]{:S(2)}, u32[]{:S(2)}) collective-permute-start(bf16[640,2048]{1,0:T(8,128)(2,1)S(1)} %copy-done.22), channel_id=1, source_target_pairs={{0,2},{1,3},{2,0},{3,1},{4,6},{5,7},{6,4},{7,5},{8,10},{9,11},{10,... | collective-permute-start | bytes 7864328 | tf_op jit(solution)/shard_map/ppermute | solution.py:355
  1026.1 37.8 %copy-start.29 = (bf16[256,2048]{1,0:T(8,128)(2,1)}, bf16[256,2048]{1,0:T(8,128)(2,1)S(1)}, u32[]{:S(2)}) copy-start(bf16[256,2048]{1,0:T(8,128)(2,1)S(1)} %collective-permute-done.17) | copy-start | bytes 3145732
  1107.0 26.4 %collective-permute-start.20 = (bf16[2816,1024]{1,0:T(8,128)(2,1)}, bf16[2816,1024]{1,0:T(8,128)(2,1)}, u32[]{:S(2)}, u32[]{:S(2)}) collective-permute-start(bf16[2816,1024]{1,0:T(8,128)(2,1)} %constant_dynamic-slice_fusion.4), channel_id=1, source_target_pairs={{0,16},{16,0},{1,17},{17,1},{2,18},{18,2},{3,19},{19,3},{4,20},{20... | collective-permute-start | bytes 17301512 | tf_op jit(solution)/shard_map/ppermute | solution.py:352
  1123.7 47.5 %all-to-all-start.9 = ((bf16[4,64,2048]{2,1,0:T(8,128)(2,1)}), bf16[4,64,2048]{2,1,0:T(8,128)(2,1)}, u32[]{:S(2)}, u32[]{:S(2)}) async-start(bf16[4,64,2048]{2,1,0:T(8,128)(2,1)} %bitcast.127), calls=%async_computation.10 | async-start | bytes 2097152 | tf_op jit(solution)/shard_map/all_to_all | solution.py:442
  1128.9 15.0 %slice-start = ((s8[6291456]{0:T(1024)(128)(4,1)}), s8[4194304]{0:T(1024)(128)(4,1)S(1)}, s32[]{:S(2)}) async-start(s8[6291456]{0:T(1024)(128)(4,1)} %bitcast.121), calls=%async_computation.18 | async-start | bytes 8388608
  1154.6 28.7 %collective-permute-start.21 = (bf16[512,2048]{1,0:T(8,128)(2,1)}, bf16[512,2048]{1,0:T(8,128)(2,1)}, u32[]{:S(2)}, u32[]{:S(2)}) collective-permute-start(bf16[512,2048]{1,0:T(8,128)(2,1)} %fusion.36), channel_id=1, source_target_pairs={{0,16},{16,0},{1,17},{17,1},{2,18},{18,2},{3,19},{19,3},{4,20},{20... | collective-permute-start | bytes 6291464 | tf_op jit(solution)/shard_map/ppermute | solution.py:352
  1173.5 73.3 %all-to-all-start.7 = ((bf16[4,160,2048]{2,1,0:T(8,128)(2,1)}), bf16[4,160,2048]{2,1,0:T(8,128)(2,1)}, u32[]{:S(2)}, u32[]{:S(2)}) async-start(bf16[4,160,2048]{2,1,0:T(8,128)(2,1)} %bitcast.35), calls=%async_computation.7 | async-start | bytes 5242880 | tf_op jit(solution)/shard_map/all_to_all | solution.py:442
  1183.3 63.4 %collective-permute-start.22 = (bf16[1408,1024]{1,0:T(8,128)(2,1)}, bf16[1408,1024]{1,0:T(8,128)(2,1)}, u32[]{:S(2)}, u32[]{:S(2)}) collective-permute-start(bf16[1408,1024]{1,0:T(8,128)(2,1)} %get-tuple-element.249), channel_id=1, source_target_pairs={{0,1},{1,0},{2,3},{3,2},{4,5},{5,4},{6,7},{7,6},{8,9},{9,8},{10,11... | collective-permute-start | bytes 8650760 | tf_op jit(solution)/shard_map/ppermute | solution.py:355
  1258.7 16.4 %all-to-all-start.8 = ((f32[16,1,256]{2,1,0:T(1,128)}), f32[16,1,256]{2,1,0:T(1,128)S(1)}, u32[]{:S(2)}, u32[]{:S(2)}) async-start(f32[16,1,256]{2,1,0:T(1,128)} %reshape.269), calls=%async_computation.9 | async-start | bytes 32768 | tf_op jit(solution)/shard_map/all_to_all | solution.py:671
  1275.0 8.1 collective-permute-start.24
  1276.4 6.2 collective-permute-start.23
  (53 other events, 296.9 us)
Sparse Core Ops, SparseCore 0:
  13.6 194.3 all-gather.4
  209.5 72.6 all-gather.6
  283.7 74.4 all-gather.8
  359.6 74.4 all-gather.10
  820.2 69.9 reduce-scatter.4
  908.6 264.0 reduce-scatter.2

commit v7 on v6

--- a/solution.py
+++ b/solution.py
@@ -629,26 +629,25 @@
     got = after(qkv_part, grad_qkv, hidden_t, grad_gate, grad_up, *away_first)
     grad_qkv, hidden_t, gate_t, up_t, *away_first = got[1:]
     gate_part = dot(gate_t, all_slots, 0, 0, bf16)
-    gate_part, hidden_t = after(gate_part, hidden_t)
+    gate_part, hidden_t, *came_o = after(gate_part, hidden_t, *came_o)
+    blocks_o = row_blocks(add_parts(blocks_o[0], came_o), pair, my_side)
+    hidden_t, *blocks_o = after(hidden_t, *blocks_o)
+    came_o = pair_swap(blocks_o[1])
     outs_first = add_parts(out_rows_of(0, 0, hidden_t), away_first)
     away_second = [out_rows_of(1, j, hidden_t) for j in range(1, columns)]
     gate_total = core_sum(gate_part)
-    got = after(outs_first, gate_total, up_t, *away_second, *came_o)
-    outs_first, gate_total, up_t = got[:3]
-    away_second, came_o = columns_home(got[3 : 2 + columns]), got[2 + columns :]
+    outs_first, gate_total, up_t, *away_second = after(outs_first, gate_total, up_t, *away_second)
+    away_second = columns_home(away_second)
     outs_first = swap_experts(outs_first)
     gate_own, gate_came = side_swap_sum(gate_total)
-    blocks_o = row_blocks(add_parts(blocks_o[0], came_o), pair, my_side)
-    up_t, *blocks_o = after(up_t, *blocks_o)
-    came_o = pair_swap(blocks_o[1])
 
     up_part = dot(up_t, all_slots, 0, 0, bf16)
     got = after(up_part, hidden_t, grad_qkv, outs_first, came_o, gate_came, *away_second)
     up_part, hidden_t, grad_qkv, outs_first, came_o, gate_came, *away_second = got
-    gate_grad = gate_own.astype(f32) + gate_came.astype(f32)
+    out_grad = expert_sum(add_parts(blocks_o[0], [came_o]))
     outs_second = add_parts(out_rows_of(1, 0, hidden_t), away_second)
     up_total = core_sum(up_part)
-    outs_second, up_total, grad_qkv = after(outs_second, up_total, grad_qkv)
+    outs_second, up_total, grad_qkv, out_grad = after(outs_second, up_total, grad_qkv, out_grad)
     outs_second = swap_experts(outs_second)
     up_own, up_came = side_swap_sum(up_total)
 
@@ -662,10 +661,9 @@
     _, unit_one, inverse_one = normalize_parts(inputs, norm1_gain)
     grad_norm_one, norm1_part = norm_backward(grad_normed, unit_one, inverse_one, norm1_gain)
     tokens_grad = (grad_hidden_in + grad_norm_one).astype(bf16)
-    tokens_grad, norm1_part, outs_second, up_own, up_came, qkv_sum = after(
-        tokens_grad, norm1_part, outs_second, up_own, up_came, qkv_sum
-    )
-    out_grad = expert_sum(add_parts(blocks_o[0], [came_o]))
+    got = after(tokens_grad, norm1_part, outs_second, up_own, up_came, qkv_sum, gate_own)
+    tokens_grad, norm1_part, outs_second, up_own, up_came, qkv_sum, gate_own = got
+    gate_grad = gate_own.astype(f32) + gate_came.astype(f32)
 
     gains = jnp.stack([norm1_part, norm2_part]).reshape(2, ctx_count, fsdp_count, per)
     gains = lax.all_to_all(gains.transpose(2, 1, 0, 3), "fsdp", 0, 0, tiled=True)

time: 1300 us -> 1270 us (0.977)
  waiting for transfers between devices: 422 us -> 385 us
    ppermute x12, waiting for transfers between devices: 158 us -> 115 us  [fsdp_shift(): return lax.ppermute(a, 'fsdp', [(i, move(i)) for i in range(fsdp_count)])]
  transfers between devices with their start and end apart: 41 -> 41, of which waited for: 16 -> 16; matrix products, arithmetic and copies ran while one was open for 31% -> 32% of each run, Pallas kernels for 27% -> 28%
where the time goes in v7:
time: 1270 us; the launch traced here: 1260 us
  waiting for transfers between devices  385 us (30%)
  Pallas kernels  348 us (27%)
  matrix products  239 us (19%)
  other arithmetic  112 us (9%)
  local copies, waits for them, and re-layouts  94.6 us (7%)
  starting transfers between devices  66.5 us (5%)
  between operations  15.4 us (1%)
    dot_general x19, matrix products, dot(): lax.dot_general(a, b, (((ca,), (cb,)), ((), ())), preferred_element_type=...  239 us
    all_gather x1, waiting for transfers between devices, shards(): gathered = lax.all_gather(packed, 'fsdp', axis=0, tiled=True)  153 us
    pallas_call x8, Pallas kernels, expert_rows(): pl.pallas_call(functools.partial(rows_kernel, len(left)), grid=(D // tile...  139 us
    pallas_call x4, Pallas kernels, expert_hidden(): pl.pallas_call(functools.partial(expert_kernel, len(kept)), grid=(units /...  122 us
    ppermute x12, waiting for transfers between devices, fsdp_shift(): return lax.ppermute(a, 'fsdp', [(i, move(i)) for i in range(fsdp_count)])  115 us
    all_gather x3, waiting for transfers between devices, shards(): lax.all_gather(part, 'fsdp', axis=0, tiled=True, axis_index_groups=sides)  88.1 us
    all_to_all x9, starting transfers between devices, swap_experts(): lax.all_to_all(blocks, 'fsdp', 0, 0, axis_index_groups=lines, tiled=True)  42.7 us
    pallas_call x3, Pallas kernels, join_weights(): pl.pallas_call(functools.partial(join_kernel, own_blocks, part_blocks), g...  37.5 us
  transfers between devices with their start and end apart: 41, of which 16 were waited for; matrix products, arithmetic and copies ran while one was open for 32% of the time, Pallas kernels for 28%

profile of v7, /device:TPU:0, one launch (start us, length us, event | category | flops | bytes accessed | tf_op | source)
XLA Modules:
  0.0 1261.0 jit_solution(898986573643876179)
XLA Ops:
  24.1 6.9 constant_dynamic-slice_fusion.17
  41.1 13.4 %fusion.29 = bf16[1024,2048]{1,0:T(8,128)(2,1)} fusion(s32[2048]{0:T(1024)S(1)} %fusion.86, bf16[512,2048]{1,0:T(8,128)(2,1)} %collective-permute-done, bf16[512,2048]{1,0:T(8,128)(2,1)} %fusion.19), kind=kOutput, calls=%fused_computation.62 | convolution fusion | flops 8604614656 | bytes 8396800 | tf_op jit(solution)/shard_map/dot_general | solution.py:28
  54.4 153.5 %all-gather.5.cloned.1.call-done = bf16[2048,4096]{1,0:T(8,128)(2,1)} async-done(((bf16[128,4096]{1,0:T(8,128)(2,1)}), bf16[2048,4096]{1,0:T(8,128)(2,1)}) %all-gather.5.cloned.1.call-update) | async-done | bytes 16777232 | tf_op jit(solution)/shard_map/all_gather | solution.py:389
  228.3 19.0 %fusion.12.pre_q.pre_k.pre_v = f32[1024,3072]{1,0:T(8,128)} fusion(bf16[2048,4096]{1,0:T(8,128)(2,1)} %all-gather.5.cloned.1.call-done, bf16[512,2048]{1,0:T(8,128)(2,1)} %collective-permute-done, bf16[512,2048]{1,0:T(8,128)(2,1)} %fusion.19), kind=kOutput, calls=%fused_computation.20 | convolution fusion | flops 12893290496 | bytes 29360128 | tf_op jit(solution)/shard_map/dot_general | solution.py:28
  247.3 21.7 %attention_forward.1 = (bf16[1024,1024]{1,0:T(8,128)(2,1)}, bf16[1024,1024]{1,0:T(8,128)(2,1)}, bf16[1024,1024]{1,0:T(8,128)(2,1)}, bf16[1024,1024]{1,0:T(8,128)(2,1)}, f32[1024,1024]{1,0:T(8,128)}) custom-call(s32[4]{0:T(128)} %fusion.95.perm, f32[1024,3072]{1,0:T(8,128)} %fusion.12.pre_q.pre_k.pre_v, f32[1024,3072]{1,0:T(8,128)} %fusion.12.pre_q.pre_k.pre_v, ...), custom_call_target="tpu_custom_call" | custom-call | tf_op jit(solution)/shard_map/attention_forward/pallas_call | solution.py:155
  278.3 6.3 all-to-all-done
  294.3 6.6 multiply_reduce_fusion.2
  307.3 51.5 %all-gather.9.cloned.1.call-done = bf16[1408,2048]{1,0:T(8,128)(2,1)} async-done(((bf16[704,2048]{1,0:T(8,128)(2,1)}), bf16[1408,2048]{1,0:T(8,128)(2,1)}) %all-gather.9.cloned.1.call-update) | async-done | bytes 5767184 | tf_op jit(solution)/shard_map/all_gather | solution.py:452
  372.9 12.7 %join_weights.3.wg_ref.refs_2_ = bf16[2816,2048]{1,0:T(8,128)(2,1)} custom-call(s32[3]{0:T(128)} %pad_add_fusion.where, bf16[1408,2048]{1,0:T(8,128)(2,1)} %own_ref.3, bf16[704,2048]{1,0:T(8,128)(2,1)} %constant_dynamic-slice_fusion.15.refs_0_, bf16[704,2048]{1,0:T(8,128)(2,1)} %collective-permute-done.4.refs_1_), custom_call_target="tpu_custom_call" | custom-call | tf_op jit(solution)/shard_map/join_weights/pallas_call | solution.py:272
  385.6 12.5 join_weights.4.wu_ref.refs_3_
  398.1 36.6 %all-gather.11.cloned.1.call-done = bf16[1408,2048]{1,0:T(8,128)(2,1)} async-done(((bf16[704,2048]{1,0:T(8,128)(2,1)}), bf16[1408,2048]{1,0:T(8,128)(2,1)}) %all-gather.11.cloned.1.call-update) | async-done | bytes 5767184 | tf_op jit(solution)/shard_map/all_gather | solution.py:452
  447.0 12.4 join_weights.5.wd_ref.refs_1_
  459.4 30.7 %expert_hidden.4 = (bf16[2560,2816]{1,0:T(8,128)(2,1)}, bf16[2560,2816]{1,0:T(8,128)(2,1)}, bf16[2560,2816]{1,0:T(8,128)(2,1)}) custom-call(bf16[640,2048]{1,0:T(8,128)(2,1)} %bitcast.113, bf16[640,2048]{1,0:T(8,128)(2,1)} %bitcast.15.g_ref, bf16[2816,2048]{1,0:T(8,128)(2,1)} %join_weights.3.wg_ref.refs_2_, bf16[2816,2048]{1,0:T(8,128)(2,1)} %join_weights.4.wu_ref.refs_3_, ...), custom_call_target="tpu_custom_call" | custom-call | tf_op jit(solution)/shard_map/expert_hidden/pallas_call | solution.py:213
  490.1 10.9 collective-permute-done.8.x_ref
  502.5 30.6 %expert_hidden.5 = (bf16[2560,2816]{1,0:T(8,128)(2,1)}, bf16[2560,2816]{1,0:T(8,128)(2,1)}, bf16[2560,2816]{1,0:T(8,128)(2,1)}) custom-call(bf16[640,2048]{1,0:T(8,128)(2,1)} %collective-permute-done.8.x_ref, bf16[640,2048]{1,0:T(8,128)(2,1)} %collective-permute-done.3.g_ref, ...), custom_call_target="tpu_custom_call", output_to_operand_aliasing={{0}: (5, {}), {1}: (6, {}), {2}: (7, {})} | custom-call | tf_op jit(solution)/shard_map/expert_hidden/pallas_call | solution.py:213
  533.0 21.1 %expert_rows.8 = bf16[640,2048]{1,0:T(8,128)(2,1)} custom-call(bf16[2560,2816]{1,0:T(8,128)(2,1)} %get-tuple-element.171.refs_0_.refs_1_, bf16[2560,2816]{1,0:T(8,128)(2,1)} %get-tuple-element.172.refs_1_.refs_2_, bf16[2816,2048]{1,0:T(8,128)(2,1)} %join_weights.3.wg_ref.refs_2_, bf16[2816,2048]{1,0:T(8,128)(2,1)} %join_weights.4.wu_ref.refs_3_), custom_call_target="tpu_custom_call" | custom-call | tf_op jit(solution)/shard_map/expert_rows/pallas_call | solution.py:233
  554.7 6.3 collective-permute-done.9.x_ref
  562.5 30.6 %expert_hidden.6 = (bf16[2560,2816]{1,0:T(8,128)(2,1)}, bf16[2560,2816]{1,0:T(8,128)(2,1)}, bf16[2560,2816]{1,0:T(8,128)(2,1)}) custom-call(bf16[640,2048]{1,0:T(8,128)(2,1)} %copy-done.15, bf16[640,2048]{1,0:T(8,128)(2,1)} %collective-permute-done.6.g_ref, ...), custom_call_target="tpu_custom_call", output_to_operand_aliasing={{0}: (5, {}), {1}: (6, {}), {2}: (7, {})} | custom-call | tf_op jit(solution)/shard_map/expert_hidden/pallas_call | solution.py:213
  593.1 21.1 %expert_rows.9 = bf16[640,2048]{1,0:T(8,128)(2,1)} custom-call(bf16[2560,2816]{1,0:T(8,128)(2,1)} %get-tuple-element.186.refs_0_.refs_1_, bf16[2560,2816]{1,0:T(8,128)(2,1)} %get-tuple-element.187.refs_1_.refs_2_, bf16[2816,2048]{1,0:T(8,128)(2,1)} %join_weights.3.wg_ref.refs_2_, bf16[2816,2048]{1,0:T(8,128)(2,1)} %join_weights.4.wu_ref.refs_3_), custom_call_target="tpu_custom_call" | custom-call | tf_op jit(solution)/shard_map/expert_rows/pallas_call | solution.py:233
  614.1 21.1 %expert_rows.10 = bf16[640,2048]{1,0:T(8,128)(2,1)} custom-call(bf16[2560,2816]{1,0:T(8,128)(2,1)} %get-tuple-element.186.refs_0_.refs_1_, bf16[2560,2816]{1,0:T(8,128)(2,1)} %get-tuple-element.187.refs_1_.refs_2_, bf16[2816,2048]{1,0:T(8,128)(2,1)} %join_weights.3.wg_ref.refs_2_, bf16[2816,2048]{1,0:T(8,128)(2,1)} %join_weights.4.wu_ref.refs_3_), custom_call_target="tpu_custom_call" | custom-call | tf_op jit(solution)/shard_map/expert_rows/pallas_call | solution.py:233
  647.6 30.6 %expert_hidden.7 = (bf16[2560,2816]{1,0:T(8,128)(2,1)}, bf16[2560,2816]{1,0:T(8,128)(2,1)}, bf16[2560,2816]{1,0:T(8,128)(2,1)}) custom-call(bf16[640,2048]{1,0:T(8,128)(2,1)} %bitcast.24.x_ref, bf16[640,2048]{1,0:T(8,128)(2,1)} %bitcast.17.g_ref, ...), custom_call_target="tpu_custom_call", output_to_operand_aliasing={{0}: (5, {}), {1}: (6, {}), {2}: (7, {})} | custom-call | tf_op jit(solution)/shard_map/expert_hidden/pallas_call | solution.py:213
  678.1 21.1 %expert_rows.11 = bf16[640,2048]{1,0:T(8,128)(2,1)} custom-call(bf16[2560,2816]{1,0:T(8,128)(2,1)} %get-tuple-element.209.refs_0_, bf16[2560,2816]{1,0:T(8,128)(2,1)} %get-tuple-element.219.refs_1_, bf16[2816,2048]{1,0:T(8,128)(2,1)} %join_weights.3.wg_ref.refs_2_, bf16[2816,2048]{1,0:T(8,128)(2,1)} %join_weights.4.wu_ref.refs_3_), custom_call_target="tpu_custom_call" | custom-call | tf_op jit(solution)/shard_map/expert_rows/pallas_call | solution.py:233
  712.9 38.6 %convolution_convert_fusion.2 = bf16[2816,2048]{1,0:T(8,128)(2,1)} fusion(bf16[2560,2816]{1,0:T(8,128)(2,1)} %get-tuple-element.226.refs_0_, bf16[640,2048]{1,0:T(8,128)(2,1)} %collective-permute-done.6.g_ref, bf16[640,2048]{1,0:T(8,128)(2,1)} %bitcast.17.g_ref, bf16[640,2048]{1,0:T(8,128)(2,1)} %collective-permute-done.3.g_ref, ...), kind=kOutput, calls=%fused_computation.7 | convolution fusion | flops 29575610368 | bytes 36438016 | tf_op jit(solution)/shard_map/dot_general | solution.py:28
  751.5 5.8 constant_dynamic-slice_fusion.12
  757.3 13.6 %expert_rows.12 = bf16[640,2048]{1,0:T(8,128)(2,1)} custom-call(bf16[2560,2816]{1,0:T(8,128)(2,1)} %get-tuple-element.226.refs_0_, bf16[2816,2048]{1,0:T(8,128)(2,1)} %join_weights.5.wd_ref.refs_1_), custom_call_target="tpu_custom_call" | custom-call | tf_op jit(solution)/shard_map/expert_rows/pallas_call | solution.py:233
  792.9 9.8 add_convert_fusion.2
  802.7 7.0 convolution_convert_fusion.4
  814.6 5.7 convolution_convert_fusion.10.do_ref
  820.9 27.3 %attention_backward.1 = bf16[1024,3072]{1,0:T(8,128)(2,1)} custom-call(s32[4]{0:T(128)} %fusion.95.perm, bf16[1024,1024]{1,0:T(8,128)(2,1)} %get-tuple-element.132.q_ref, bf16[1024,1024]{1,0:T(8,128)(2,1)} %get-tuple-element.133.k_ref, bf16[1024,1024]{1,0:T(8,128)(2,1)} %get-tuple-element.134.v_ref, f32[1024,1024]{1,0:T(8,128)} %get-tuple-element.135.log_ref, ...), custom_call_target="tpu_custom_call" | custom-call | tf_op jit(solution)/shard_map/attention_backward/pallas_call | solution.py:178
  848.3 19.3 %convolution_convert_fusion.3 = bf16[2048,3072]{1,0:T(8,128)(2,1)} fusion(bf16[1024,2048]{1,0:T(8,128)(2,1)} %fusion.29, bf16[1024,3072]{1,0:T(8,128)(2,1)} %attention_backward.1), kind=kOutput, calls=%fused_computation.8 | convolution fusion | flops 12891193344 | bytes 23068672 | tf_op jit(solution)/shard_map/dot_general | solution.py:28
  867.6 35.9 %convolution_convert_fusion.1 = bf16[2816,2048]{1,0:T(8,128)(2,1)S(1)} fusion(bf16[2560,2816]{1,0:T(8,128)(2,1)} %get-tuple-element.209.refs_0_, bf16[2560,2048]{1,0:T(8,128)(2,1)} %copy-done.29), kind=kOutput, calls=%fused_computation.6 | convolution fusion | flops 29533667328 | bytes 36438016 | tf_op jit(solution)/shard_map/dot_general | solution.py:28
  913.5 13.5 %expert_rows.13 = bf16[640,2048]{1,0:T(8,128)(2,1)} custom-call(bf16[2560,2816]{1,0:T(8,128)(2,1)} %get-tuple-element.226.refs_0_, bf16[2816,2048]{1,0:T(8,128)(2,1)} %join_weights.5.wd_ref.refs_1_), custom_call_target="tpu_custom_call" | custom-call | tf_op jit(solution)/shard_map/expert_rows/pallas_call | solution.py:233
  927.0 14.1 %expert_rows.14 = bf16[640,2048]{1,0:T(8,128)(2,1)} custom-call(bf16[2560,2816]{1,0:T(8,128)(2,1)} %get-tuple-element.226.refs_0_, bf16[2816,2048]{1,0:T(8,128)(2,1)} %join_weights.5.wd_ref.refs_1_), custom_call_target="tpu_custom_call" | custom-call | tf_op jit(solution)/shard_map/expert_rows/pallas_call | solution.py:233
  945.9 10.0 add_convert_fusion.1
  967.2 38.4 %convolution_convert_fusion = bf16[2816,2048]{1,0:T(8,128)(2,1)} fusion(bf16[2560,2816]{1,0:T(8,128)(2,1)} %get-tuple-element.219.refs_1_, bf16[2560,2048]{1,0:T(8,128)(2,1)} %copy-done.29), kind=kOutput, calls=%fused_computation.5 | convolution fusion | flops 29533667328 | bytes 36438016 | tf_op jit(solution)/shard_map/dot_general | solution.py:28
  1005.7 32.0 %collective-permute-done.19 = bf16[640,2048]{1,0:T(8,128)(2,1)S(1)} collective-permute-done((bf16[640,2048]{1,0:T(8,128)(2,1)S(1)}, bf16[640,2048]{1,0:T(8,128)(2,1)S(1)}, u32[]{:S(2)}, u32[]{:S(2)}) %collective-permute-start.19) | collective-permute-done | bytes 2621472 | tf_op jit(solution)/shard_map/ppermute | solution.py:355
  1039.2 13.5 %collective-permute-done.18 = bf16[1408,1024]{1,0:T(8,128)(2,1)} collective-permute-done((bf16[1408,1024]{1,0:T(8,128)(2,1)S(1)}, bf16[1408,1024]{1,0:T(8,128)(2,1)}, u32[]{:S(2)}, u32[]{:S(2)}) %collective-permute-start.18) | collective-permute-done | bytes 2883616 | tf_op jit(solution)/shard_map/ppermute | solution.py:355
  1052.7 6.0 constant_dynamic-slice_fusion.5
  1065.7 13.6 %expert_rows.15 = bf16[640,2048]{1,0:T(8,128)(2,1)} custom-call(bf16[2560,2816]{1,0:T(8,128)(2,1)} %get-tuple-element.226.refs_0_, bf16[2816,2048]{1,0:T(8,128)(2,1)} %join_weights.5.wd_ref.refs_1_), custom_call_target="tpu_custom_call" | custom-call | tf_op jit(solution)/shard_map/expert_rows/pallas_call | solution.py:233
  1084.6 10.1 all-to-all-done.7
  1097.1 10.0 add_convert_fusion
  1107.2 10.8 fusion.36
  1128.2 6.0 constant_dynamic-slice_fusion.3
  1134.3 13.4 %fusion.25 = (f32[2048]{0:T(1024)S(1)}, f32[512]{0:T(512)S(1)}, f32[512,2048]{1,0:T(8,128)}) fusion(bf16[1,512,2048]{2,1,0:T(8,128)(2,1)S(1)} %copy-done.3, f32[512]{0:T(512)S(1)} %copy-done.42, f32[2048]{0:T(1024)S(1)} %copy-done.31, bf16[512,2048]{1,0:T(8,128)(2,1)} %collective-permute-done.21, bf16[2048,4096]{1,0:T(8,128)(2,1)} %all-gather.5.cloned.1.call-done, ...), kind=kOutput, calls=%fused_computation.47 | convolution fusion | flops 6451885568 | bytes 24137728 | tf_op jit(solution)/shard_map/dot_general | solution.py:28
  1153.2 52.0 %collective-permute-done.22 = bf16[1408,1024]{1,0:T(8,128)(2,1)} collective-permute-done((bf16[1408,1024]{1,0:T(8,128)(2,1)}, bf16[1408,1024]{1,0:T(8,128)(2,1)}, u32[]{:S(2)}, u32[]{:S(2)}) %collective-permute-start.22) | collective-permute-done | bytes 2883616 | tf_op jit(solution)/shard_map/ppermute | solution.py:355
  1217.5 8.2 all-to-all-start.9
  1236.9 5.6 convert_add_fusion.3
  1244.4 6.5 convert_add_fusion.2
  (295 shorter events, 241.8 us)
Async XLA Ops:
  7.2 200.7 %all-gather.5.cloned.1.call-start = ((), (), s32[]{:S(2)}) async-start(), calls=%async_computation.12 | async-start | bytes 17825792 | tf_op jit(solution)/shard_map/all_gather | solution.py:389
  13.4 293.9 %all-gather.7.cloned.1.call-start = ((), (), s32[]{:S(2)}) async-start(), calls=%async_computation.13 | async-start | bytes 8650752 | tf_op jit(solution)/shard_map/all_gather | solution.py:452
  15.9 25.2 %collective-permute-start = (bf16[512,2048]{1,0:T(8,128)(2,1)}, bf16[512,2048]{1,0:T(8,128)(2,1)}, u32[]{:S(2)}, u32[]{:S(2)}) collective-permute-start(bf16[512,2048]{1,0:T(8,128)(2,1)} %fusion.19), channel_id=1, source_target_pairs={{0,16},{16,0},{1,17},{17,1},{2,18},{18,2},{3,19},{19,3},{4,20},{20... | collective-permute-start | bytes 6291464 | tf_op jit(solution)/shard_map/ppermute | solution.py:352
  20.3 271.2 %copy-start.35 = (s32[512]{0:T(512)}, s32[512]{0:T(512)S(1)}, u32[]{:S(2)}) copy-start(s32[512]{0:T(512)S(1)} %get-tuple-element.249) | copy-start | bytes 6148
  20.3 271.2 %copy-start.38 = (s32[512]{0:T(512)}, s32[512]{0:T(512)S(1)}, u32[]{:S(2)}) copy-start(s32[512]{0:T(512)S(1)} %get-tuple-element.250) | copy-start | bytes 6148
  41.1 166.9 %copy-start.56 = (s32[1,4]{1,0:T(1,128)S(1)}, s32[1,4]{1,0:T(1,128)}, u32[]{:S(2)}) copy-start(s32[1,4]{1,0:T(1,128)} %param.17) | copy-start | bytes 52
  207.9 150.8 %all-gather.9.cloned.1.call-start = ((), (), s32[]{:S(2)}) async-start(), calls=%async_computation.14 | async-start | bytes 8650752 | tf_op jit(solution)/shard_map/all_gather | solution.py:452
  220.6 64.0 %all-to-all-start = ((bf16[4,160,2048]{2,1,0:T(8,128)(2,1)}), bf16[4,160,2048]{2,1,0:T(8,128)(2,1)}, u32[]{:S(2)}, u32[]{:S(2)}) async-start(bf16[4,160,2048]{2,1,0:T(8,128)(2,1)} %bitcast.132), calls=%async_computation | async-start | bytes 5242880 | tf_op jit(solution)/shard_map/all_to_all | solution.py:442
  228.3 40.7 %collective-permute-start.1 = (bf16[1024,1024]{1,0:T(8,128)(2,1)}, bf16[1024,1024]{1,0:T(8,128)(2,1)}, u32[]{:S(2)}, u32[]{:S(2)}) collective-permute-start(bf16[1024,1024]{1,0:T(8,128)(2,1)} %constant_dynamic-slice_fusion.16), channel_id=1, source_target_pairs={{0,16},{16,0},{1,17},{17,1},{2,18},{18,2},{3,19},{19,3},{4,20},{20... | collective-permute-start | bytes 6291464 | tf_op jit(solution)/shard_map/ppermute | solution.py:352
  284.6 74.2 %all-to-all-start.1 = ((bf16[4,160,2048]{2,1,0:T(8,128)(2,1)}), bf16[4,160,2048]{2,1,0:T(8,128)(2,1)}, u32[]{:S(2)}, u32[]{:S(2)}) async-start(bf16[4,160,2048]{2,1,0:T(8,128)(2,1)} %bitcast.130), calls=%async_computation.1 | async-start | bytes 5242880 | tf_op jit(solution)/shard_map/all_to_all | solution.py:442
  289.1 145.5 %all-gather.11.cloned.1.call-start = ((), (), s32[]{:S(2)}) async-start(), calls=%async_computation.15 | async-start | bytes 8650752 | tf_op jit(solution)/shard_map/all_gather | solution.py:452
  289.8 4.6 collective-permute-start.2
  289.9 68.9 %collective-permute-start.3 = (bf16[640,2048]{1,0:T(8,128)(2,1)}, bf16[640,2048]{1,0:T(8,128)(2,1)}, u32[]{:S(2)}, u32[]{:S(2)}) collective-permute-start(bf16[640,2048]{1,0:T(8,128)(2,1)} %bitcast.15.g_ref), channel_id=1, source_target_pairs={{0,2},{1,3},{2,0},{3,1},{4,6},{5,7},{6,4},{7,5},{8,10},{9,11},{10,... | collective-permute-start | bytes 7864328 | tf_op jit(solution)/shard_map/ppermute | solution.py:355
  358.8 75.9 %all-to-all-start.2 = ((bf16[4,160,2048]{2,1,0:T(8,128)(2,1)}), bf16[4,160,2048]{2,1,0:T(8,128)(2,1)S(1)}, u32[]{:S(2)}, u32[]{:S(2)}) async-start(bf16[4,160,2048]{2,1,0:T(8,128)(2,1)} %bitcast.133), calls=%async_computation.2 | async-start | bytes 5242880 | tf_op jit(solution)/shard_map/all_to_all | solution.py:442
  367.3 5.6 collective-permute-start.4
  370.0 15.6 %collective-permute-start.5 = (bf16[704,2048]{1,0:T(8,128)(2,1)}, bf16[704,2048]{1,0:T(8,128)(2,1)}, u32[]{:S(2)}, u32[]{:S(2)}) collective-permute-start(bf16[704,2048]{1,0:T(8,128)(2,1)} %constant_dynamic-slice_fusion.14.refs_0_), channel_id=1, source_target_pairs={{0,16},{16,0},{1,17},{17,1},{2,18},{18,2},{3,19},{19,3},{4,20},{20... | collective-permute-start | bytes 8650760 | tf_op jit(solution)/shard_map/ppermute | solution.py:352
  370.0 64.7 %collective-permute-start.6 = (bf16[640,2048]{1,0:T(8,128)(2,1)}, bf16[640,2048]{1,0:T(8,128)(2,1)}, u32[]{:S(2)}, u32[]{:S(2)}) collective-permute-start(bf16[640,2048]{1,0:T(8,128)(2,1)} %bitcast.17.g_ref), channel_id=1, source_target_pairs={{0,2},{1,3},{2,0},{3,1},{4,6},{5,7},{6,4},{7,5},{8,10},{9,11},{10,... | collective-permute-start | bytes 7864328 | tf_op jit(solution)/shard_map/ppermute | solution.py:355
  434.7 66.3 %all-to-all-start.3 = ((bf16[4,160,2048]{2,1,0:T(8,128)(2,1)}), bf16[4,160,2048]{2,1,0:T(8,128)(2,1)}, u32[]{:S(2)}, u32[]{:S(2)}) async-start(bf16[4,160,2048]{2,1,0:T(8,128)(2,1)} %bitcast.131), calls=%async_computation.3 | async-start | bytes 5242880 | tf_op jit(solution)/shard_map/all_to_all | solution.py:442
  441.5 5.5 collective-permute-start.7
  441.6 59.4 %collective-permute-start.8 = (bf16[640,2048]{1,0:T(8,128)(2,1)S(1)}, bf16[640,2048]{1,0:T(8,128)(2,1)}, u32[]{:S(2)}, u32[]{:S(2)}) collective-permute-start(bf16[640,2048]{1,0:T(8,128)(2,1)S(1)} %bitcast.112), channel_id=1, source_target_pairs={{0,2},{1,3},{2,0},{3,1},{4,6},{5,7},{6,4},{7,5},{8,10},{9,11},{10,... | collective-permute-start | bytes 7864328 | tf_op jit(solution)/shard_map/ppermute | solution.py:355
  501.0 60.0 %collective-permute-start.9 = (bf16[640,2048]{1,0:T(8,128)(2,1)}, bf16[640,2048]{1,0:T(8,128)(2,1)S(1)}, u32[]{:S(2)}, u32[]{:S(2)}) collective-permute-start(bf16[640,2048]{1,0:T(8,128)(2,1)} %bitcast.24.x_ref), channel_id=1, source_target_pairs={{0,2},{1,3},{2,0},{3,1},{4,6},{5,7},{6,4},{7,5},{8,10},{9,11},{10,... | collective-permute-start | bytes 7864328 | tf_op jit(solution)/shard_map/ppermute | solution.py:355
  554.2 81.1 %collective-permute-start.10 = (bf16[640,2048]{1,0:T(8,128)(2,1)}, bf16[640,2048]{1,0:T(8,128)(2,1)}, u32[]{:S(2)}, u32[]{:S(2)}) collective-permute-start(bf16[640,2048]{1,0:T(8,128)(2,1)} %expert_rows.8), channel_id=1, source_target_pairs={{0,2},{1,3},{2,0},{3,1},{4,6},{5,7},{6,4},{7,5},{8,10},{9,11},{10,... | collective-permute-start | bytes 7864328 | tf_op jit(solution)/shard_map/ppermute | solution.py:355
  640.5 62.5 %all-to-all-start.4 = ((bf16[4,160,2048]{2,1,0:T(8,128)(2,1)}), bf16[4,160,2048]{2,1,0:T(8,128)(2,1)S(1)}, u32[]{:S(2)}, u32[]{:S(2)}) async-start(bf16[4,160,2048]{2,1,0:T(8,128)(2,1)} %bitcast.117), calls=%async_computation.4 | async-start | bytes 5242880 | tf_op jit(solution)/shard_map/all_to_all | solution.py:442
  646.0 57.0 %collective-permute-start.11 = (bf16[640,2048]{1,0:T(8,128)(2,1)}, bf16[640,2048]{1,0:T(8,128)(2,1)}, u32[]{:S(2)}, u32[]{:S(2)}) collective-permute-start(bf16[640,2048]{1,0:T(8,128)(2,1)} %expert_rows.9), channel_id=1, source_target_pairs={{0,2},{1,3},{2,0},{3,1},{4,6},{5,7},{6,4},{7,5},{8,10},{9,11},{10,... | collective-permute-start | bytes 7864328 | tf_op jit(solution)/shard_map/ppermute | solution.py:355
  708.2 63.6 %all-to-all-start.5 = ((bf16[4,160,2048]{2,1,0:T(8,128)(2,1)}), bf16[4,160,2048]{2,1,0:T(8,128)(2,1)}, u32[]{:S(2)}, u32[]{:S(2)}) async-start(bf16[4,160,2048]{2,1,0:T(8,128)(2,1)} %bitcast.115), calls=%async_computation.5 | async-start | bytes 5242880 | tf_op jit(solution)/shard_map/all_to_all | solution.py:442
  712.8 405.2 %reduce-scatter.5.cloned.1.call-start = ((), (), s32[]{:S(2)}) async-start(), calls=%async_computation.17 | async-start | bytes 8650752 | tf_op jit(solution)/shard_map/reduce_scatter | solution.py:564
  757.3 35.6 %collective-permute-start.13 = (bf16[2816,1024]{1,0:T(8,128)(2,1)}, bf16[2816,1024]{1,0:T(8,128)(2,1)}, u32[]{:S(2)}, u32[]{:S(2)}) collective-permute-start(bf16[2816,1024]{1,0:T(8,128)(2,1)} %constant_dynamic-slice_fusion.12), channel_id=1, source_target_pairs={{0,16},{16,0},{1,17},{17,1},{2,18},{18,2},{3,19},{19,3},{4,20},{20... | collective-permute-start | bytes 17301512 | tf_op jit(solution)/shard_map/ppermute | solution.py:352
  781.1 21.6 %copy-start.18 = (bf16[512,2048]{1,0:T(8,128)(2,1)}, bf16[512,2048]{1,0:T(8,128)(2,1)S(1)}, u32[]{:S(2)}) copy-start(bf16[512,2048]{1,0:T(8,128)(2,1)S(1)} %fusion.106) | copy-start | bytes 6291460
  781.1 21.6 %collective-permute-start.12 = (bf16[512,2048]{1,0:T(8,128)(2,1)S(1)}, bf16[512,2048]{1,0:T(8,128)(2,1)}, u32[]{:S(2)}, u32[]{:S(2)}) collective-permute-start(bf16[512,2048]{1,0:T(8,128)(2,1)S(1)} %fusion.106), channel_id=1, source_target_pairs={{0,16},{16,0},{1,17},{17,1},{2,18},{18,2},{3,19},{19,3},{4,20},{20... | collective-permute-start | bytes 6291464 | tf_op jit(solution)/shard_map/ppermute | solution.py:352
  791.4 76.2 %collective-permute-start.14 = (bf16[640,2048]{1,0:T(8,128)(2,1)}, bf16[640,2048]{1,0:T(8,128)(2,1)}, u32[]{:S(2)}, u32[]{:S(2)}) collective-permute-start(bf16[640,2048]{1,0:T(8,128)(2,1)} %expert_rows.12), channel_id=1, source_target_pairs={{0,2},{1,3},{2,0},{3,1},{4,6},{5,7},{6,4},{7,5},{8,10},{9,11},{10,... | collective-permute-start | bytes 7864328 | tf_op jit(solution)/shard_map/ppermute | solution.py:355
  820.3 83.3 %collective-permute-start.15 = (bf16[512,2048]{1,0:T(8,128)(2,1)}, bf16[512,2048]{1,0:T(8,128)(2,1)}, u32[]{:S(2)}, u32[]{:S(2)}) collective-permute-start(bf16[512,2048]{1,0:T(8,128)(2,1)} %bitcast.30), channel_id=1, source_target_pairs={{0,2},{1,3},{2,0},{3,1},{4,6},{5,7},{6,4},{7,5},{8,10},{9,11},{10,... | collective-permute-start | bytes 6291464 | tf_op jit(solution)/shard_map/ppermute | solution.py:355
  820.9 384.6 %reduce-scatter.3.cloned.1.call-start = ((), (), s32[]{:S(2)}) async-start(), calls=%async_computation.16 | async-start | bytes 13369344 | tf_op jit(solution)/shard_map/reduce_scatter | solution.py:627
  909.6 36.3 %collective-permute-start.16 = (bf16[2816,1024]{1,0:T(8,128)(2,1)}, bf16[2816,1024]{1,0:T(8,128)(2,1)}, u32[]{:S(2)}, u32[]{:S(2)}) collective-permute-start(bf16[2816,1024]{1,0:T(8,128)(2,1)} %constant_dynamic-slice_fusion.7), channel_id=1, source_target_pairs={{0,16},{16,0},{1,17},{17,1},{2,18},{18,2},{3,19},{19,3},{4,20},{20... | collective-permute-start | bytes 17301512 | tf_op jit(solution)/shard_map/ppermute | solution.py:352
  927.0 14.7 %copy-start.17 = (bf16[640,2048]{1,0:T(8,128)(2,1)S(1)}, bf16[640,2048]{1,0:T(8,128)(2,1)}, u32[]{:S(2)}) copy-start(bf16[640,2048]{1,0:T(8,128)(2,1)} %expert_rows.13) | copy-start | bytes 7864324
  941.1 64.6 %collective-permute-start.17 = (bf16[256,2048]{1,0:T(8,128)(2,1)}, bf16[256,2048]{1,0:T(8,128)(2,1)}, u32[]{:S(2)}, u32[]{:S(2)}) collective-permute-start(bf16[256,2048]{1,0:T(8,128)(2,1)} %bitcast.135), channel_id=1, source_target_pairs={{0,1},{1,0},{2,3},{3,2},{4,5},{5,4},{6,7},{7,6},{8,9},{9,8},{10,11... | collective-permute-start | bytes 3145736 | tf_op jit(solution)/shard_map/ppermute | solution.py:355
  955.9 96.8 %all-to-all-start.6 = ((bf16[4,160,2048]{2,1,0:T(8,128)(2,1)}), bf16[4,160,2048]{2,1,0:T(8,128)(2,1)}, u32[]{:S(2)}, u32[]{:S(2)}) async-start(bf16[4,160,2048]{2,1,0:T(8,128)(2,1)} %bitcast.34), calls=%async_computation.6 | async-start | bytes 5242880 | tf_op jit(solution)/shard_map/all_to_all | solution.py:442
  964.0 88.7 %collective-permute-start.18 = (bf16[1408,1024]{1,0:T(8,128)(2,1)S(1)}, bf16[1408,1024]{1,0:T(8,128)(2,1)}, u32[]{:S(2)}, u32[]{:S(2)}) collective-permute-start(bf16[1408,1024]{1,0:T(8,128)(2,1)S(1)} %get-tuple-element.254), channel_id=1, source_target_pairs={{0,1},{1,0},{2,3},{3,2},{4,5},{5,4},{6,7},{7,6},{8,9},{9,8},{10,11... | collective-permute-start | bytes 8650760 | tf_op jit(solution)/shard_map/ppermute | solution.py:355
  965.6 72.0 %collective-permute-start.19 = (bf16[640,2048]{1,0:T(8,128)(2,1)S(1)}, bf16[640,2048]{1,0:T(8,128)(2,1)S(1)}, u32[]{:S(2)}, u32[]{:S(2)}) collective-permute-start(bf16[640,2048]{1,0:T(8,128)(2,1)S(1)} %copy-done.22), channel_id=1, source_target_pairs={{0,2},{1,3},{2,0},{3,1},{4,6},{5,7},{6,4},{7,5},{8,10},{9,11},{10,... | collective-permute-start | bytes 7864328 | tf_op jit(solution)/shard_map/ppermute | solution.py:355
  1058.7 38.5 %collective-permute-start.20 = (bf16[2816,1024]{1,0:T(8,128)(2,1)}, bf16[2816,1024]{1,0:T(8,128)(2,1)}, u32[]{:S(2)}, u32[]{:S(2)}) collective-permute-start(bf16[2816,1024]{1,0:T(8,128)(2,1)} %constant_dynamic-slice_fusion.5), channel_id=1, source_target_pairs={{0,16},{16,0},{1,17},{17,1},{2,18},{18,2},{3,19},{19,3},{4,20},{20... | collective-permute-start | bytes 17301512 | tf_op jit(solution)/shard_map/ppermute | solution.py:352
  1061.3 33.5 %all-to-all-start.7 = ((bf16[4,64,2048]{2,1,0:T(8,128)(2,1)}), bf16[4,64,2048]{2,1,0:T(8,128)(2,1)}, u32[]{:S(2)}, u32[]{:S(2)}) async-start(bf16[4,64,2048]{2,1,0:T(8,128)(2,1)} %bitcast.127), calls=%async_computation.7 | async-start | bytes 2097152 | tf_op jit(solution)/shard_map/all_to_all | solution.py:442
  1118.0 16.3 %collective-permute-start.21 = (bf16[512,2048]{1,0:T(8,128)(2,1)}, bf16[512,2048]{1,0:T(8,128)(2,1)}, u32[]{:S(2)}, u32[]{:S(2)}) collective-permute-start(bf16[512,2048]{1,0:T(8,128)(2,1)} %fusion.36), channel_id=1, source_target_pairs={{0,16},{16,0},{1,17},{17,1},{2,18},{18,2},{3,19},{19,3},{4,20},{20... | collective-permute-start | bytes 6291464 | tf_op jit(solution)/shard_map/ppermute | solution.py:352
  1123.1 82.4 %all-to-all-start.8 = ((bf16[4,160,2048]{2,1,0:T(8,128)(2,1)}), bf16[4,160,2048]{2,1,0:T(8,128)(2,1)}, u32[]{:S(2)}, u32[]{:S(2)}) async-start(bf16[4,160,2048]{2,1,0:T(8,128)(2,1)} %bitcast.116), calls=%async_computation.8 | async-start | bytes 5242880 | tf_op jit(solution)/shard_map/all_to_all | solution.py:442
  1134.2 13.5 %copy-start.45 = (f32[512]{0:T(512)S(1)}, f32[512]{0:T(512)}, u32[]{:S(2)}) copy-start(f32[512]{0:T(512)} %copy-done.43) | copy-start | bytes 6148
  1134.2 13.5 %copy-start.47 = (f32[512]{0:T(512)S(1)}, f32[512]{0:T(512)}, u32[]{:S(2)}) copy-start(f32[512]{0:T(512)} %copy-done.46) | copy-start | bytes 6148
  1134.2 71.0 %collective-permute-start.22 = (bf16[1408,1024]{1,0:T(8,128)(2,1)}, bf16[1408,1024]{1,0:T(8,128)(2,1)}, u32[]{:S(2)}, u32[]{:S(2)}) collective-permute-start(bf16[1408,1024]{1,0:T(8,128)(2,1)} %get-tuple-element.255), channel_id=1, source_target_pairs={{0,1},{1,0},{2,3},{3,2},{4,5},{5,4},{6,7},{7,6},{8,9},{9,8},{10,11... | collective-permute-start | bytes 8650760 | tf_op jit(solution)/shard_map/ppermute | solution.py:355
  1217.5 25.0 %all-to-all-start.9 = ((f32[16,1,256]{2,1,0:T(1,128)}), f32[16,1,256]{2,1,0:T(1,128)S(1)}, u32[]{:S(2)}, u32[]{:S(2)}) async-start(f32[16,1,256]{2,1,0:T(1,128)} %reshape.269), calls=%async_computation.10 | async-start | bytes 32768 | tf_op jit(solution)/shard_map/all_to_all | solution.py:669
  1236.9 14.6 %collective-permute-start.24 = (f32[3,64,1024]{2,1,0:T(8,128)}, f32[3,64,1024]{2,1,0:T(8,128)}, u32[]{:S(2)}, u32[]{:S(2)}) collective-permute-start(f32[3,64,1024]{2,1,0:T(8,128)} %dynamic-slice_bitcast_fusion), channel_id=1, source_target_pairs={{0,16},{16,0},{1,17},{17,1},{2,18},{18,2},{3,19},{19,3},{4,20},{20... | collective-permute-start | bytes 2359304 | tf_op jit(solution)/shard_map/ppermute | solution.py:352
  1243.9 7.1 collective-permute-start.23
  (52 other events, 279.8 us)
Sparse Core Ops, SparseCore 0:
  13.6 194.3 all-gather.4
  210.0 72.6 all-gather.6
  284.3 74.4 all-gather.8
  360.2 74.4 all-gather.10
  821.0 70.8 reduce-scatter.4
  909.7 287.9 reduce-scatter.2

commit v8 on v7

--- a/solution.py
+++ b/solution.py
@@ -190,8 +190,14 @@
 
 
 def expert_kernel(kept, x_ref, g_ref, wg_ref, wu_ref, wd_ref, *refs):
-    hidden_ref, gate_ref, up_ref = refs[kept:]
+    hidden_ref, gate_ref, up_ref, back_ref, total_ref = refs[kept:]
     count = x_ref.shape[0] // 2
+
+    @pl.when(pl.program_id(0) == 0)
+    def _():
+        total_ref[...] = jnp.zeros_like(total_ref)
+
+    both = jnp.concatenate([wg_ref[...], wu_ref[...]], axis=0)
     for p in range(2):
         rows = slice(p * count, (p + 1) * count)
         gate = dot(x_ref[rows, :], wg_ref[...], 1, 1)
@@ -200,8 +206,15 @@
         sigmoid = jax.nn.sigmoid(gate)
         silu = gate * sigmoid
         hidden_ref[rows, :] = (silu * up).astype(bf16)
-        gate_ref[rows, :] = (grad * up * sigmoid * (1.0 + gate * (1.0 - sigmoid))).astype(bf16)
-        up_ref[rows, :] = (grad * silu).astype(bf16)
+        grad_gate = (grad * up * sigmoid * (1.0 + gate * (1.0 - sigmoid))).astype(bf16)
+        grad_up = (grad * silu).astype(bf16)
+        gate_ref[rows, :] = grad_gate
+        up_ref[rows, :] = grad_up
+        total_ref[rows, :] += dot(jnp.concatenate([grad_gate, grad_up], axis=1), both, 1, 0)
+
+    @pl.when(pl.program_id(0) == pl.num_programs(0) - 1)
+    def _():
+        back_ref[...] = total_ref[...].astype(bf16)
 
 
 def expert_hidden(part, parts, slots, grads, weights, kept):
@@ -214,8 +227,10 @@
         functools.partial(expert_kernel, len(kept)),
         grid=(units // tile,),
         in_specs=[whole] * 2 + [weight] * 3 + [pl.BlockSpec(memory_space=pl.ANY)] * len(kept),
-        out_specs=[result] * 3,
-        out_shape=[jax.ShapeDtypeStruct((parts * rows, units), bf16)] * 3,
+        out_specs=[result] * 3 + [whole],
+        out_shape=[jax.ShapeDtypeStruct((parts * rows, units), bf16)] * 3
+        + [jax.ShapeDtypeStruct((rows, D), bf16)],
+        scratch_shapes=[pltpu.VMEM((rows, D), f32)],
         input_output_aliases={5 + i: i for i in range(len(kept))},
         name="expert_hidden",
     )(slots, grads, *weights, *kept)
@@ -506,10 +521,8 @@
     parts = halves * columns
 
     def hidden_part(index, slots, state):
-        return expert_hidden(index, parts, slots, grad_parts[index], weights, state)
-
-    def grad_rows(index, state):
-        return expert_rows(index, half, state[1:], (wg, wu))
+        *state, back = expert_hidden(index, parts, slots, grad_parts[index], weights, state)
+        return state, back
 
     def columns_home(pieces):
         return [column_shift(part, -(j + 1)) for j, part in enumerate(pieces)]
@@ -522,30 +535,25 @@
 
     slot_parts = to_columns(first)
     back, came = {}, [None] * halves
-    state = hidden_part(0, slot_parts[0], ())
+    state, back[0] = hidden_part(0, slot_parts[0], ())
     second, *got = after(second, *state, *slot_parts[1:])
     state, slot_parts[1:] = got[:3], got[3:]
     slot_parts += to_columns(second)
     for h in range(halves):
         for j in range(1, columns):
             index = h * columns + j
-            state = hidden_part(index, slot_parts[index], state)
-        for j in range(1, columns):
-            index = h * columns + j
-            back[index] = grad_rows(index, state)
+            state, back[index] = hidden_part(index, slot_parts[index], state)
             back[index], *state = after(back[index], *state)
         if h == 0:
             got = after(*state, *slot_parts[columns + 1 :])
             state, slot_parts[columns + 1 :] = got[:3], got[3:]
         came[h] = columns_home([back[h * columns + j] for j in range(1, columns)])
-    back[0] = grad_rows(0, state)
     home_first, *got = after(back[0], *state, *came[0])
     state = got[:3]
     home_first = add_parts(home_first, got[3:])
     home_first, *state = after(home_first, *state)
     home_first = swap_experts(home_first)
-    state = hidden_part(columns, slot_parts[columns], state)
-    back[columns] = grad_rows(columns, state)
+    state, back[columns] = hidden_part(columns, slot_parts[columns], state)
     back[columns], home_first, *state = after(back[columns], home_first, *state)
     hidden, grad_gate, grad_up = state
     all_slots = jnp.concatenate(slot_parts, axis=0)
@@ -661,8 +669,9 @@
     _, unit_one, inverse_one = normalize_parts(inputs, norm1_gain)
     grad_norm_one, norm1_part = norm_backward(grad_normed, unit_one, inverse_one, norm1_gain)
     tokens_grad = (grad_hidden_in + grad_norm_one).astype(bf16)
-    got = after(tokens_grad, norm1_part, outs_second, up_own, up_came, qkv_sum, gate_own)
-    tokens_grad, norm1_part, outs_second, up_own, up_came, qkv_sum, gate_own = got
+    tokens_grad, norm1_part, outs_second, qkv_sum = after(
+        tokens_grad, norm1_part, outs_second, qkv_sum
+    )
     gate_grad = gate_own.astype(f32) + gate_came.astype(f32)
 
     gains = jnp.stack([norm1_part, norm2_part]).reshape(2, ctx_count, fsdp_count, per)
@@ -675,6 +684,7 @@
     gains_own = gains_of(core)
     for s in range(1, ctx_count):
         gains_own = gains_own + core_shift(gains_of(core + s), s)
+    gains_own, up_own, up_came = after(gains_own, up_own, up_came)
     up_grad = up_own.astype(f32) + up_came.astype(f32)
     sums = qkv_sum.reshape(ctx_count, per, heads, 3, HD).astype(f32)
     sums = sums.transpose(3, 0, 1, 2, 4).reshape(3, ctx_count, per, width)

time: 1270 us -> 1260 us (level)
  Pallas kernels: 348 us -> 365 us
  waiting for transfers between devices: 385 us -> 368 us
    pallas_call x4, Pallas kernels: 122 us -> 224 us  [expert_hidden(): pl.pallas_call(functools.partial(expert_kernel, len(kept)), grid=(units /...]
    pallas_call x8 -> x4, Pallas kernels: 139 us -> 54.5 us  [expert_rows(): pl.pallas_call(functools.partial(rows_kernel, len(left)), grid=(D // tile...]
    ppermute x12, waiting for transfers between devices: 115 us -> 47 us  [fsdp_shift(): return lax.ppermute(a, 'fsdp', [(i, move(i)) for i in range(fsdp_count)])]
    all_to_all x9, waiting for transfers between devices: 21.4 us -> 72 us  [swap_experts(): lax.all_to_all(blocks, 'fsdp', 0, 0, axis_index_groups=lines, tiled=True)]
  transfers between devices with their start and end apart: 41 -> 41, of which waited for: 16 -> 14; matrix products, arithmetic and copies ran while one was open for 32% -> 33% of each run, Pallas kernels for 28% -> 29%
where the time goes in v8:
time: 1260 us
  waiting for transfers between devices  368 us (29%)
  Pallas kernels  365 us (29%)
  matrix products  240 us (19%)
  other arithmetic  111 us (9%)
  local copies, waits for them, and re-layouts  92.4 us (7%)
  starting transfers between devices  64.3 us (5%)
  between operations  15.5 us (1%)
    dot_general x19, matrix products, dot(): lax.dot_general(a, b, (((ca,), (cb,)), ((), ())), preferred_element_type=...  240 us
    pallas_call x4, Pallas kernels, expert_hidden(): pl.pallas_call(functools.partial(expert_kernel, len(kept)), grid=(units /...  224 us
    all_gather x1, waiting for transfers between devices, shards(): gathered = lax.all_gather(packed, 'fsdp', axis=0, tiled=True)  153 us
    all_gather x3, waiting for transfers between devices, shards(): lax.all_gather(part, 'fsdp', axis=0, tiled=True, axis_index_groups=sides)  88.3 us
    all_to_all x9, waiting for transfers between devices, swap_experts(): lax.all_to_all(blocks, 'fsdp', 0, 0, axis_index_groups=lines, tiled=True)  72 us
    pallas_call x4, Pallas kernels, expert_rows(): pl.pallas_call(functools.partial(rows_kernel, len(left)), grid=(D // tile...  54.5 us
    ppermute x12, waiting for transfers between devices, fsdp_shift(): return lax.ppermute(a, 'fsdp', [(i, move(i)) for i in range(fsdp_count)])  47 us
    all_to_all x9, starting transfers between devices, swap_experts(): lax.all_to_all(blocks, 'fsdp', 0, 0, axis_index_groups=lines, tiled=True)  42.5 us
  transfers between devices with their start and end apart: 41, of which 14 were waited for; matrix products, arithmetic and copies ran while one was open for 33% of the time, Pallas kernels for 29%

profile of v8, /device:TPU:0, one launch (start us, length us, event | category | flops | bytes accessed | tf_op | source)
XLA Modules:
  0.0 1255.6 jit_solution(13700774092177869021)
XLA Ops:
  24.1 6.9 constant_dynamic-slice_fusion.16
  41.0 13.5 %fusion.29 = bf16[1024,2048]{1,0:T(8,128)(2,1)} fusion(s32[2048]{0:T(1024)S(1)} %fusion.86, bf16[512,2048]{1,0:T(8,128)(2,1)} %collective-permute-done, bf16[512,2048]{1,0:T(8,128)(2,1)} %fusion.19), kind=kOutput, calls=%fused_computation.62 | convolution fusion | flops 8604614656 | bytes 8396800 | tf_op jit(solution)/shard_map/dot_general | solution.py:28
  54.5 153.4 %all-gather.5.cloned.1.call-done = bf16[2048,4096]{1,0:T(8,128)(2,1)} async-done(((bf16[128,4096]{1,0:T(8,128)(2,1)}), bf16[2048,4096]{1,0:T(8,128)(2,1)}) %all-gather.5.cloned.1.call-update) | async-done | bytes 16777232 | tf_op jit(solution)/shard_map/all_gather | solution.py:404
  215.4 5.4 slice.77
  228.5 19.1 %fusion.12.pre_q.pre_k.pre_v = f32[1024,3072]{1,0:T(8,128)} fusion(bf16[2048,4096]{1,0:T(8,128)(2,1)} %all-gather.5.cloned.1.call-done, bf16[512,2048]{1,0:T(8,128)(2,1)} %collective-permute-done, bf16[512,2048]{1,0:T(8,128)(2,1)} %fusion.19), kind=kOutput, calls=%fused_computation.20 | convolution fusion | flops 12893290496 | bytes 29360128 | tf_op jit(solution)/shard_map/dot_general | solution.py:28
  247.6 21.7 %attention_forward.1 = (bf16[1024,1024]{1,0:T(8,128)(2,1)}, bf16[1024,1024]{1,0:T(8,128)(2,1)}, bf16[1024,1024]{1,0:T(8,128)(2,1)}, bf16[1024,1024]{1,0:T(8,128)(2,1)}, f32[1024,1024]{1,0:T(8,128)}) custom-call(s32[4]{0:T(128)} %fusion.95.perm, f32[1024,3072]{1,0:T(8,128)} %fusion.12.pre_q.pre_k.pre_v, f32[1024,3072]{1,0:T(8,128)} %fusion.12.pre_q.pre_k.pre_v, ...), custom_call_target="tpu_custom_call" | custom-call | tf_op jit(solution)/shard_map/attention_forward/pallas_call | solution.py:155
  278.6 6.2 all-to-all-done
  294.1 6.6 multiply_reduce_fusion.2
  307.1 51.7 %all-gather.9.cloned.1.call-done = bf16[1408,2048]{1,0:T(8,128)(2,1)} async-done(((bf16[704,2048]{1,0:T(8,128)(2,1)}), bf16[1408,2048]{1,0:T(8,128)(2,1)}) %all-gather.9.cloned.1.call-update) | async-done | bytes 5767184 | tf_op jit(solution)/shard_map/all_gather | solution.py:467
  372.9 12.7 %join_weights.3.wg_ref = bf16[2816,2048]{1,0:T(8,128)(2,1)} custom-call(s32[3]{0:T(128)} %pad_add_fusion.where, bf16[1408,2048]{1,0:T(8,128)(2,1)} %own_ref.3, bf16[704,2048]{1,0:T(8,128)(2,1)} %constant_dynamic-slice_fusion.14.refs_0_, bf16[704,2048]{1,0:T(8,128)(2,1)} %collective-permute-done.4.refs_1_), custom_call_target="tpu_custom_call" | custom-call | tf_op jit(solution)/shard_map/join_weights/pallas_call | solution.py:287
  385.7 12.3 join_weights.4.wu_ref
  398.0 36.7 %all-gather.11.cloned.1.call-done = bf16[1408,2048]{1,0:T(8,128)(2,1)} async-done(((bf16[704,2048]{1,0:T(8,128)(2,1)}), bf16[1408,2048]{1,0:T(8,128)(2,1)}) %all-gather.11.cloned.1.call-update) | async-done | bytes 5767184 | tf_op jit(solution)/shard_map/all_gather | solution.py:467
  447.0 12.4 join_weights.5.wd_ref.refs_1_
  459.4 55.9 %expert_hidden.4 = (bf16[2560,2816]{1,0:T(8,128)(2,1)}, bf16[2560,2816]{1,0:T(8,128)(2,1)}, bf16[2560,2816]{1,0:T(8,128)(2,1)}, bf16[640,2048]{1,0:T(8,128)(2,1)}) custom-call(bf16[640,2048]{1,0:T(8,128)(2,1)} %bitcast.113, bf16[640,2048]{1,0:T(8,128)(2,1)} %bitcast.15.g_ref, bf16[2816,2048]{1,0:T(8,128)(2,1)} %join_weights.3.wg_ref, ...), custom_call_target="tpu_custom_call" | custom-call | tf_op jit(solution)/shard_map/expert_hidden/pallas_call | solution.py:226
  516.9 56.0 %expert_hidden.5 = (bf16[2560,2816]{1,0:T(8,128)(2,1)}, bf16[2560,2816]{1,0:T(8,128)(2,1)}, bf16[2560,2816]{1,0:T(8,128)(2,1)}, bf16[640,2048]{1,0:T(8,128)(2,1)}) custom-call(bf16[640,2048]{1,0:T(8,128)(2,1)} %collective-permute-done.8.x_ref, ...), custom_call_target="tpu_custom_call", output_to_operand_aliasing={{0}: (5, {}), {1}: (6, {}), {2}: (7, {})} | custom-call | tf_op jit(solution)/shard_map/expert_hidden/pallas_call | solution.py:226
  576.0 56.2 %expert_hidden.6 = (bf16[2560,2816]{1,0:T(8,128)(2,1)}, bf16[2560,2816]{1,0:T(8,128)(2,1)}, bf16[2560,2816]{1,0:T(8,128)(2,1)}, bf16[640,2048]{1,0:T(8,128)(2,1)}) custom-call(bf16[640,2048]{1,0:T(8,128)(2,1)} %copy-done.15, bf16[640,2048]{1,0:T(8,128)(2,1)} %collective-permute-done.6.g_ref, ...), custom_call_target="tpu_custom_call", output_to_operand_aliasing={{0}: (5, {}), {1}: (6, {}), {2}: (7, {})} | custom-call | tf_op jit(solution)/shard_map/expert_hidden/pallas_call | solution.py:226
  632.2 5.3 add_convert_fusion.6
  637.5 5.1 all-to-all-start.4
  644.1 55.8 %expert_hidden.7 = (bf16[2560,2816]{1,0:T(8,128)(2,1)}, bf16[2560,2816]{1,0:T(8,128)(2,1)}, bf16[2560,2816]{1,0:T(8,128)(2,1)}, bf16[640,2048]{1,0:T(8,128)(2,1)}) custom-call(bf16[640,2048]{1,0:T(8,128)(2,1)} %bitcast.24.x_ref, bf16[640,2048]{1,0:T(8,128)(2,1)} %bitcast.17.g_ref, ...), custom_call_target="tpu_custom_call", output_to_operand_aliasing={{0}: (5, {}), {1}: (6, {}), {2}: (7, {})} | custom-call | tf_op jit(solution)/shard_map/expert_hidden/pallas_call | solution.py:226
  701.5 5.3 add_convert_fusion.5
  711.4 39.1 %convolution_convert_fusion.2 = bf16[2816,2048]{1,0:T(8,128)(2,1)} fusion(bf16[2560,2816]{1,0:T(8,128)(2,1)} %get-tuple-element.234.refs_0_, bf16[640,2048]{1,0:T(8,128)(2,1)} %collective-permute-done.6.g_ref, bf16[640,2048]{1,0:T(8,128)(2,1)} %bitcast.17.g_ref, bf16[640,2048]{1,0:T(8,128)(2,1)} %collective-permute-done.3.g_ref, ...), kind=kOutput, calls=%fused_computation.7 | convolution fusion | flops 29575610368 | bytes 36438016 | tf_op jit(solution)/shard_map/dot_general | solution.py:28
  750.5 5.8 constant_dynamic-slice_fusion.11
  756.3 13.6 %expert_rows.4 = bf16[640,2048]{1,0:T(8,128)(2,1)} custom-call(bf16[2560,2816]{1,0:T(8,128)(2,1)} %get-tuple-element.234.refs_0_, bf16[2816,2048]{1,0:T(8,128)(2,1)} %join_weights.5.wd_ref.refs_1_), custom_call_target="tpu_custom_call" | custom-call | tf_op jit(solution)/shard_map/expert_rows/pallas_call | solution.py:248
  791.5 9.8 add_convert_fusion.2
  801.3 7.0 convolution_convert_fusion.4
  813.1 5.7 convolution_convert_fusion.10.do_ref
  819.5 27.3 %attention_backward.1 = bf16[1024,3072]{1,0:T(8,128)(2,1)} custom-call(s32[4]{0:T(128)} %fusion.95.perm, bf16[1024,1024]{1,0:T(8,128)(2,1)} %get-tuple-element.136.q_ref, bf16[1024,1024]{1,0:T(8,128)(2,1)} %get-tuple-element.137.k_ref, bf16[1024,1024]{1,0:T(8,128)(2,1)} %get-tuple-element.138.v_ref, f32[1024,1024]{1,0:T(8,128)} %get-tuple-element.139.log_ref, ...), custom_call_target="tpu_custom_call" | custom-call | tf_op jit(solution)/shard_map/attention_backward/pallas_call | solution.py:178
  846.9 19.4 %convolution_convert_fusion.3 = bf16[2048,3072]{1,0:T(8,128)(2,1)} fusion(bf16[1024,2048]{1,0:T(8,128)(2,1)} %fusion.29, bf16[1024,3072]{1,0:T(8,128)(2,1)} %attention_backward.1), kind=kOutput, calls=%fused_computation.8 | convolution fusion | flops 12891193344 | bytes 23068672 | tf_op jit(solution)/shard_map/dot_general | solution.py:28
  866.3 36.0 %convolution_convert_fusion.1 = bf16[2816,2048]{1,0:T(8,128)(2,1)S(1)} fusion(bf16[2560,2816]{1,0:T(8,128)(2,1)} %get-tuple-element.217, bf16[2560,2048]{1,0:T(8,128)(2,1)} %copy-done.30), kind=kOutput, calls=%fused_computation.6 | convolution fusion | flops 29533667328 | bytes 36438016 | tf_op jit(solution)/shard_map/dot_general | solution.py:28
  912.2 13.5 %expert_rows.5 = bf16[640,2048]{1,0:T(8,128)(2,1)} custom-call(bf16[2560,2816]{1,0:T(8,128)(2,1)} %get-tuple-element.234.refs_0_, bf16[2816,2048]{1,0:T(8,128)(2,1)} %join_weights.5.wd_ref.refs_1_), custom_call_target="tpu_custom_call" | custom-call | tf_op jit(solution)/shard_map/expert_rows/pallas_call | solution.py:248
  925.7 13.9 %expert_rows.6 = bf16[640,2048]{1,0:T(8,128)(2,1)} custom-call(bf16[2560,2816]{1,0:T(8,128)(2,1)} %get-tuple-element.234.refs_0_, bf16[2816,2048]{1,0:T(8,128)(2,1)} %join_weights.5.wd_ref.refs_1_), custom_call_target="tpu_custom_call" | custom-call | tf_op jit(solution)/shard_map/expert_rows/pallas_call | solution.py:248
  944.7 10.0 add_convert_fusion.1
  964.8 38.7 %convolution_convert_fusion = bf16[2816,2048]{1,0:T(8,128)(2,1)} fusion(bf16[2560,2816]{1,0:T(8,128)(2,1)} %get-tuple-element.227, bf16[2560,2048]{1,0:T(8,128)(2,1)} %copy-done.30), kind=kOutput, calls=%fused_computation.5 | convolution fusion | flops 29533667328 | bytes 36438016 | tf_op jit(solution)/shard_map/dot_general | solution.py:28
  1003.4 30.9 %collective-permute-done.19 = bf16[640,2048]{1,0:T(8,128)(2,1)S(1)} collective-permute-done((bf16[640,2048]{1,0:T(8,128)(2,1)S(1)}, bf16[640,2048]{1,0:T(8,128)(2,1)S(1)}, u32[]{:S(2)}, u32[]{:S(2)}) %collective-permute-start.19) | collective-permute-done | bytes 2621472 | tf_op jit(solution)/shard_map/ppermute | solution.py:370
  1035.9 14.9 %collective-permute-done.18 = bf16[1408,1024]{1,0:T(8,128)(2,1)} collective-permute-done((bf16[1408,1024]{1,0:T(8,128)(2,1)S(1)}, bf16[1408,1024]{1,0:T(8,128)(2,1)}, u32[]{:S(2)}, u32[]{:S(2)}) %collective-permute-start.18) | collective-permute-done | bytes 2883616 | tf_op jit(solution)/shard_map/ppermute | solution.py:370
  1050.8 6.8 constant_dynamic-slice_fusion.4
  1064.9 13.5 %expert_rows.7 = bf16[640,2048]{1,0:T(8,128)(2,1)} custom-call(bf16[2560,2816]{1,0:T(8,128)(2,1)} %get-tuple-element.234.refs_0_, bf16[2816,2048]{1,0:T(8,128)(2,1)} %join_weights.5.wd_ref.refs_1_), custom_call_target="tpu_custom_call" | custom-call | tf_op jit(solution)/shard_map/expert_rows/pallas_call | solution.py:248
  1078.4 5.3 add_convert_fusion.3
  1083.7 10.4 all-to-all-done.7
  1095.1 10.4 add_convert_fusion
  1105.6 10.8 fusion.36
  1116.5 5.1 convert_element_type.280
  1121.5 6.6 convert_add_fusion.3
  1138.4 13.2 %fusion.25 = (f32[2048]{0:T(1024)S(1)}, f32[512]{0:T(512)S(1)}, f32[512,2048]{1,0:T(8,128)}) fusion(bf16[1,512,2048]{2,1,0:T(8,128)(2,1)S(1)} %copy-done.3, f32[512]{0:T(512)S(1)} %copy-done.43, f32[2048]{0:T(1024)S(1)} %copy-done.32, bf16[512,2048]{1,0:T(8,128)(2,1)} %collective-permute-done.21, bf16[2048,4096]{1,0:T(8,128)(2,1)} %all-gather.5.cloned.1.call-done, ...), kind=kOutput, calls=%fused_computation.47 | convolution fusion | flops 6451885568 | bytes 24137728 | tf_op jit(solution)/shard_map/dot_general | solution.py:28
  1151.7 5.4 fusion.24
  1157.1 53.3 %all-to-all-done.8 = bf16[4,160,2048]{2,1,0:T(8,128)(2,1)} async-done(((bf16[4,160,2048]{2,1,0:T(8,128)(2,1)}), bf16[4,160,2048]{2,1,0:T(8,128)(2,1)}, u32[]{:S(2)}, u32[]{:S(2)}) %all-to-all-start.8) | async-done | bytes 2621472 | tf_op jit(solution)/shard_map/all_to_all | solution.py:457
  1211.2 6.2 all-to-all-start.9
  1241.4 5.8 convert_add_fusion.2
  (293 shorter events, 203.4 us)
Async XLA Ops:
  7.2 200.7 %all-gather.5.cloned.1.call-start = ((), (), s32[]{:S(2)}) async-start(), calls=%async_computation.12 | async-start | bytes 17825792 | tf_op jit(solution)/shard_map/all_gather | solution.py:404
  13.4 293.7 %all-gather.7.cloned.1.call-start = ((), (), s32[]{:S(2)}) async-start(), calls=%async_computation.13 | async-start | bytes 8650752 | tf_op jit(solution)/shard_map/all_gather | solution.py:467
  15.9 25.1 %collective-permute-start = (bf16[512,2048]{1,0:T(8,128)(2,1)}, bf16[512,2048]{1,0:T(8,128)(2,1)}, u32[]{:S(2)}, u32[]{:S(2)}) collective-permute-start(bf16[512,2048]{1,0:T(8,128)(2,1)} %fusion.19), channel_id=1, source_target_pairs={{0,16},{16,0},{1,17},{17,1},{2,18},{18,2},{3,19},{19,3},{4,20},{20... | collective-permute-start | bytes 6291464 | tf_op jit(solution)/shard_map/ppermute | solution.py:367
  20.3 270.9 %copy-start.36 = (s32[512]{0:T(512)}, s32[512]{0:T(512)S(1)}, u32[]{:S(2)}) copy-start(s32[512]{0:T(512)S(1)} %get-tuple-element.257) | copy-start | bytes 6148
  20.3 270.9 %copy-start.39 = (s32[512]{0:T(512)}, s32[512]{0:T(512)S(1)}, u32[]{:S(2)}) copy-start(s32[512]{0:T(512)S(1)} %get-tuple-element.258) | copy-start | bytes 6148
  41.0 167.0 %copy-start.57 = (s32[1,4]{1,0:T(1,128)S(1)}, s32[1,4]{1,0:T(1,128)}, u32[]{:S(2)}) copy-start(s32[1,4]{1,0:T(1,128)} %param.17) | copy-start | bytes 52
  207.9 150.8 %all-gather.9.cloned.1.call-start = ((), (), s32[]{:S(2)}) async-start(), calls=%async_computation.14 | async-start | bytes 8650752 | tf_op jit(solution)/shard_map/all_gather | solution.py:467
  220.8 63.9 %all-to-all-start = ((bf16[4,160,2048]{2,1,0:T(8,128)(2,1)}), bf16[4,160,2048]{2,1,0:T(8,128)(2,1)}, u32[]{:S(2)}, u32[]{:S(2)}) async-start(bf16[4,160,2048]{2,1,0:T(8,128)(2,1)} %bitcast.131), calls=%async_computation | async-start | bytes 5242880 | tf_op jit(solution)/shard_map/all_to_all | solution.py:457
  228.5 40.8 %collective-permute-start.1 = (bf16[1024,1024]{1,0:T(8,128)(2,1)}, bf16[1024,1024]{1,0:T(8,128)(2,1)}, u32[]{:S(2)}, u32[]{:S(2)}) collective-permute-start(bf16[1024,1024]{1,0:T(8,128)(2,1)} %constant_dynamic-slice_fusion.15), channel_id=1, source_target_pairs={{0,16},{16,0},{1,17},{17,1},{2,18},{18,2},{3,19},{19,3},{4,20},{20... | collective-permute-start | bytes 6291464 | tf_op jit(solution)/shard_map/ppermute | solution.py:367
  284.7 74.1 %all-to-all-start.1 = ((bf16[4,160,2048]{2,1,0:T(8,128)(2,1)}), bf16[4,160,2048]{2,1,0:T(8,128)(2,1)}, u32[]{:S(2)}, u32[]{:S(2)}) async-start(bf16[4,160,2048]{2,1,0:T(8,128)(2,1)} %bitcast.129), calls=%async_computation.1 | async-start | bytes 5242880 | tf_op jit(solution)/shard_map/all_to_all | solution.py:457
  289.3 145.3 %all-gather.11.cloned.1.call-start = ((), (), s32[]{:S(2)}) async-start(), calls=%async_computation.15 | async-start | bytes 8650752 | tf_op jit(solution)/shard_map/all_gather | solution.py:467
  289.6 4.6 collective-permute-start.2
  289.6 69.1 %collective-permute-start.3 = (bf16[640,2048]{1,0:T(8,128)(2,1)}, bf16[640,2048]{1,0:T(8,128)(2,1)}, u32[]{:S(2)}, u32[]{:S(2)}) collective-permute-start(bf16[640,2048]{1,0:T(8,128)(2,1)} %bitcast.15.g_ref), channel_id=1, source_target_pairs={{0,2},{1,3},{2,0},{3,1},{4,6},{5,7},{6,4},{7,5},{8,10},{9,11},{10,... | collective-permute-start | bytes 7864328 | tf_op jit(solution)/shard_map/ppermute | solution.py:370
  358.8 75.9 %all-to-all-start.2 = ((bf16[4,160,2048]{2,1,0:T(8,128)(2,1)}), bf16[4,160,2048]{2,1,0:T(8,128)(2,1)S(1)}, u32[]{:S(2)}, u32[]{:S(2)}) async-start(bf16[4,160,2048]{2,1,0:T(8,128)(2,1)} %bitcast.132), calls=%async_computation.2 | async-start | bytes 5242880 | tf_op jit(solution)/shard_map/all_to_all | solution.py:457
  367.3 5.6 collective-permute-start.4
  370.0 15.6 %collective-permute-start.5 = (bf16[704,2048]{1,0:T(8,128)(2,1)}, bf16[704,2048]{1,0:T(8,128)(2,1)}, u32[]{:S(2)}, u32[]{:S(2)}) collective-permute-start(bf16[704,2048]{1,0:T(8,128)(2,1)} %constant_dynamic-slice_fusion.13.refs_0_), channel_id=1, source_target_pairs={{0,16},{16,0},{1,17},{17,1},{2,18},{18,2},{3,19},{19,3},{4,20},{20... | collective-permute-start | bytes 8650760 | tf_op jit(solution)/shard_map/ppermute | solution.py:367
  370.0 64.7 %collective-permute-start.6 = (bf16[640,2048]{1,0:T(8,128)(2,1)}, bf16[640,2048]{1,0:T(8,128)(2,1)}, u32[]{:S(2)}, u32[]{:S(2)}) collective-permute-start(bf16[640,2048]{1,0:T(8,128)(2,1)} %bitcast.17.g_ref), channel_id=1, source_target_pairs={{0,2},{1,3},{2,0},{3,1},{4,6},{5,7},{6,4},{7,5},{8,10},{9,11},{10,... | collective-permute-start | bytes 7864328 | tf_op jit(solution)/shard_map/ppermute | solution.py:370
  434.7 80.7 %all-to-all-start.3 = ((bf16[4,160,2048]{2,1,0:T(8,128)(2,1)}), bf16[4,160,2048]{2,1,0:T(8,128)(2,1)}, u32[]{:S(2)}, u32[]{:S(2)}) async-start(bf16[4,160,2048]{2,1,0:T(8,128)(2,1)} %bitcast.130), calls=%async_computation.3 | async-start | bytes 5242880 | tf_op jit(solution)/shard_map/all_to_all | solution.py:457
  441.5 5.5 collective-permute-start.7
  441.6 73.7 %collective-permute-start.8 = (bf16[640,2048]{1,0:T(8,128)(2,1)S(1)}, bf16[640,2048]{1,0:T(8,128)(2,1)}, u32[]{:S(2)}, u32[]{:S(2)}) collective-permute-start(bf16[640,2048]{1,0:T(8,128)(2,1)S(1)} %bitcast.112), channel_id=1, source_target_pairs={{0,2},{1,3},{2,0},{3,1},{4,6},{5,7},{6,4},{7,5},{8,10},{9,11},{10,... | collective-permute-start | bytes 7864328 | tf_op jit(solution)/shard_map/ppermute | solution.py:370
  515.3 59.2 %collective-permute-start.9 = (bf16[640,2048]{1,0:T(8,128)(2,1)}, bf16[640,2048]{1,0:T(8,128)(2,1)S(1)}, u32[]{:S(2)}, u32[]{:S(2)}) collective-permute-start(bf16[640,2048]{1,0:T(8,128)(2,1)} %bitcast.24.x_ref), channel_id=1, source_target_pairs={{0,2},{1,3},{2,0},{3,1},{4,6},{5,7},{6,4},{7,5},{8,10},{9,11},{10,... | collective-permute-start | bytes 7864328 | tf_op jit(solution)/shard_map/ppermute | solution.py:370
  572.9 59.4 %collective-permute-start.10 = (bf16[640,2048]{1,0:T(8,128)(2,1)}, bf16[640,2048]{1,0:T(8,128)(2,1)}, u32[]{:S(2)}, u32[]{:S(2)}) collective-permute-start(bf16[640,2048]{1,0:T(8,128)(2,1)} %get-tuple-element.186), channel_id=1, source_target_pairs={{0,2},{1,3},{2,0},{3,1},{4,6},{5,7},{6,4},{7,5},{8,10},{9,11},{10,... | collective-permute-start | bytes 7864328 | tf_op jit(solution)/shard_map/ppermute | solution.py:370
  637.5 64.0 %all-to-all-start.4 = ((bf16[4,160,2048]{2,1,0:T(8,128)(2,1)}), bf16[4,160,2048]{2,1,0:T(8,128)(2,1)S(1)}, u32[]{:S(2)}, u32[]{:S(2)}) async-start(bf16[4,160,2048]{2,1,0:T(8,128)(2,1)} %bitcast.117), calls=%async_computation.4 | async-start | bytes 5242880 | tf_op jit(solution)/shard_map/all_to_all | solution.py:457
  642.6 58.9 %collective-permute-start.11 = (bf16[640,2048]{1,0:T(8,128)(2,1)}, bf16[640,2048]{1,0:T(8,128)(2,1)}, u32[]{:S(2)}, u32[]{:S(2)}) collective-permute-start(bf16[640,2048]{1,0:T(8,128)(2,1)} %get-tuple-element.203), channel_id=1, source_target_pairs={{0,2},{1,3},{2,0},{3,1},{4,6},{5,7},{6,4},{7,5},{8,10},{9,11},{10,... | collective-permute-start | bytes 7864328 | tf_op jit(solution)/shard_map/ppermute | solution.py:370
  706.8 63.5 %all-to-all-start.5 = ((bf16[4,160,2048]{2,1,0:T(8,128)(2,1)}), bf16[4,160,2048]{2,1,0:T(8,128)(2,1)}, u32[]{:S(2)}, u32[]{:S(2)}) async-start(bf16[4,160,2048]{2,1,0:T(8,128)(2,1)} %bitcast.115), calls=%async_computation.5 | async-start | bytes 5242880 | tf_op jit(solution)/shard_map/all_to_all | solution.py:457
  711.4 405.1 %reduce-scatter.5.cloned.1.call-start = ((), (), s32[]{:S(2)}) async-start(), calls=%async_computation.17 | async-start | bytes 8650752 | tf_op jit(solution)/shard_map/reduce_scatter | solution.py:572
  756.3 35.2 %collective-permute-start.13 = (bf16[2816,1024]{1,0:T(8,128)(2,1)}, bf16[2816,1024]{1,0:T(8,128)(2,1)}, u32[]{:S(2)}, u32[]{:S(2)}) collective-permute-start(bf16[2816,1024]{1,0:T(8,128)(2,1)} %constant_dynamic-slice_fusion.11), channel_id=1, source_target_pairs={{0,16},{16,0},{1,17},{17,1},{2,18},{18,2},{3,19},{19,3},{4,20},{20... | collective-permute-start | bytes 17301512 | tf_op jit(solution)/shard_map/ppermute | solution.py:367
  779.6 21.6 %copy-start.19 = (bf16[512,2048]{1,0:T(8,128)(2,1)}, bf16[512,2048]{1,0:T(8,128)(2,1)S(1)}, u32[]{:S(2)}) copy-start(bf16[512,2048]{1,0:T(8,128)(2,1)S(1)} %fusion.106) | copy-start | bytes 6291460
  779.6 21.6 %collective-permute-start.12 = (bf16[512,2048]{1,0:T(8,128)(2,1)S(1)}, bf16[512,2048]{1,0:T(8,128)(2,1)}, u32[]{:S(2)}, u32[]{:S(2)}) collective-permute-start(bf16[512,2048]{1,0:T(8,128)(2,1)S(1)} %fusion.106), channel_id=1, source_target_pairs={{0,16},{16,0},{1,17},{17,1},{2,18},{18,2},{3,19},{19,3},{4,20},{20... | collective-permute-start | bytes 6291464 | tf_op jit(solution)/shard_map/ppermute | solution.py:367
  790.0 76.3 %collective-permute-start.14 = (bf16[640,2048]{1,0:T(8,128)(2,1)}, bf16[640,2048]{1,0:T(8,128)(2,1)}, u32[]{:S(2)}, u32[]{:S(2)}) collective-permute-start(bf16[640,2048]{1,0:T(8,128)(2,1)} %expert_rows.4), channel_id=1, source_target_pairs={{0,2},{1,3},{2,0},{3,1},{4,6},{5,7},{6,4},{7,5},{8,10},{9,11},{10,... | collective-permute-start | bytes 7864328 | tf_op jit(solution)/shard_map/ppermute | solution.py:370
  818.8 83.5 %collective-permute-start.15 = (bf16[512,2048]{1,0:T(8,128)(2,1)}, bf16[512,2048]{1,0:T(8,128)(2,1)}, u32[]{:S(2)}, u32[]{:S(2)}) collective-permute-start(bf16[512,2048]{1,0:T(8,128)(2,1)} %bitcast.30), channel_id=1, source_target_pairs={{0,2},{1,3},{2,0},{3,1},{4,6},{5,7},{6,4},{7,5},{8,10},{9,11},{10,... | collective-permute-start | bytes 6291464 | tf_op jit(solution)/shard_map/ppermute | solution.py:370
  819.5 390.9 %reduce-scatter.3.cloned.1.call-start = ((), (), s32[]{:S(2)}) async-start(), calls=%async_computation.16 | async-start | bytes 13369344 | tf_op jit(solution)/shard_map/reduce_scatter | solution.py:635
  908.3 36.4 %collective-permute-start.16 = (bf16[2816,1024]{1,0:T(8,128)(2,1)}, bf16[2816,1024]{1,0:T(8,128)(2,1)}, u32[]{:S(2)}, u32[]{:S(2)}) collective-permute-start(bf16[2816,1024]{1,0:T(8,128)(2,1)} %constant_dynamic-slice_fusion.6), channel_id=1, source_target_pairs={{0,16},{16,0},{1,17},{17,1},{2,18},{18,2},{3,19},{19,3},{4,20},{20... | collective-permute-start | bytes 17301512 | tf_op jit(solution)/shard_map/ppermute | solution.py:367
  925.7 14.8 %copy-start.18 = (bf16[640,2048]{1,0:T(8,128)(2,1)S(1)}, bf16[640,2048]{1,0:T(8,128)(2,1)}, u32[]{:S(2)}) copy-start(bf16[640,2048]{1,0:T(8,128)(2,1)} %expert_rows.5) | copy-start | bytes 7864324
  939.6 63.8 %collective-permute-start.17 = (bf16[256,2048]{1,0:T(8,128)(2,1)}, bf16[256,2048]{1,0:T(8,128)(2,1)}, u32[]{:S(2)}, u32[]{:S(2)}) collective-permute-start(bf16[256,2048]{1,0:T(8,128)(2,1)} %bitcast.134), channel_id=1, source_target_pairs={{0,1},{1,0},{2,3},{3,2},{4,5},{5,4},{6,7},{7,6},{8,9},{9,8},{10,11... | collective-permute-start | bytes 3145736 | tf_op jit(solution)/shard_map/ppermute | solution.py:370
  954.8 96.0 %all-to-all-start.6 = ((bf16[4,160,2048]{2,1,0:T(8,128)(2,1)}), bf16[4,160,2048]{2,1,0:T(8,128)(2,1)S(1)}, u32[]{:S(2)}, u32[]{:S(2)}) async-start(bf16[4,160,2048]{2,1,0:T(8,128)(2,1)} %bitcast.116), calls=%async_computation.6 | async-start | bytes 5242880 | tf_op jit(solution)/shard_map/all_to_all | solution.py:457
  961.6 89.2 %collective-permute-start.18 = (bf16[1408,1024]{1,0:T(8,128)(2,1)S(1)}, bf16[1408,1024]{1,0:T(8,128)(2,1)}, u32[]{:S(2)}, u32[]{:S(2)}) collective-permute-start(bf16[1408,1024]{1,0:T(8,128)(2,1)S(1)} %constant_dynamic-slice_fusion.5), channel_id=1, source_target_pairs={{0,1},{1,0},{2,3},{3,2},{4,5},{5,4},{6,7},{7,6},{8,9},{9,8},{10,11... | collective-permute-start | bytes 8650760 | tf_op jit(solution)/shard_map/ppermute | solution.py:370
  963.2 71.2 %collective-permute-start.19 = (bf16[640,2048]{1,0:T(8,128)(2,1)S(1)}, bf16[640,2048]{1,0:T(8,128)(2,1)S(1)}, u32[]{:S(2)}, u32[]{:S(2)}) collective-permute-start(bf16[640,2048]{1,0:T(8,128)(2,1)S(1)} %copy-done.23), channel_id=1, source_target_pairs={{0,2},{1,3},{2,0},{3,1},{4,6},{5,7},{6,4},{7,5},{8,10},{9,11},{10,... | collective-permute-start | bytes 7864328 | tf_op jit(solution)/shard_map/ppermute | solution.py:370
  1057.6 37.5 %collective-permute-start.20 = (bf16[2816,1024]{1,0:T(8,128)(2,1)}, bf16[2816,1024]{1,0:T(8,128)(2,1)}, u32[]{:S(2)}, u32[]{:S(2)}) collective-permute-start(bf16[2816,1024]{1,0:T(8,128)(2,1)} %constant_dynamic-slice_fusion.4), channel_id=1, source_target_pairs={{0,16},{16,0},{1,17},{17,1},{2,18},{18,2},{3,19},{19,3},{4,20},{20... | collective-permute-start | bytes 17301512 | tf_op jit(solution)/shard_map/ppermute | solution.py:367
  1060.2 33.9 %all-to-all-start.7 = ((bf16[4,64,2048]{2,1,0:T(8,128)(2,1)}), bf16[4,64,2048]{2,1,0:T(8,128)(2,1)S(1)}, u32[]{:S(2)}, u32[]{:S(2)}) async-start(bf16[4,64,2048]{2,1,0:T(8,128)(2,1)} %bitcast.35), calls=%async_computation.7 | async-start | bytes 2097152 | tf_op jit(solution)/shard_map/all_to_all | solution.py:457
  1116.4 22.0 %collective-permute-start.21 = (bf16[512,2048]{1,0:T(8,128)(2,1)}, bf16[512,2048]{1,0:T(8,128)(2,1)}, u32[]{:S(2)}, u32[]{:S(2)}) collective-permute-start(bf16[512,2048]{1,0:T(8,128)(2,1)} %fusion.36), channel_id=1, source_target_pairs={{0,16},{16,0},{1,17},{17,1},{2,18},{18,2},{3,19},{19,3},{4,20},{20... | collective-permute-start | bytes 6291464 | tf_op jit(solution)/shard_map/ppermute | solution.py:367
  1128.2 82.2 %all-to-all-start.8 = ((bf16[4,160,2048]{2,1,0:T(8,128)(2,1)}), bf16[4,160,2048]{2,1,0:T(8,128)(2,1)}, u32[]{:S(2)}, u32[]{:S(2)}) async-start(bf16[4,160,2048]{2,1,0:T(8,128)(2,1)} %bitcast.36), calls=%async_computation.8 | async-start | bytes 5242880 | tf_op jit(solution)/shard_map/all_to_all | solution.py:457
  1138.3 13.4 %copy-start.46 = (f32[512]{0:T(512)S(1)}, f32[512]{0:T(512)}, u32[]{:S(2)}) copy-start(f32[512]{0:T(512)} %copy-done.44) | copy-start | bytes 6148
  1138.3 13.4 %copy-start.48 = (f32[512]{0:T(512)S(1)}, f32[512]{0:T(512)}, u32[]{:S(2)}) copy-start(f32[512]{0:T(512)} %copy-done.47) | copy-start | bytes 6148
  1138.3 102.6 %collective-permute-start.23 = (bf16[1408,1024]{1,0:T(8,128)(2,1)}, bf16[1408,1024]{1,0:T(8,128)(2,1)}, u32[]{:S(2)}, u32[]{:S(2)}) collective-permute-start(bf16[1408,1024]{1,0:T(8,128)(2,1)} %get-tuple-element.261), channel_id=1, source_target_pairs={{0,1},{1,0},{2,3},{3,2},{4,5},{5,4},{6,7},{7,6},{8,9},{9,8},{10,11... | collective-permute-start | bytes 8650760 | tf_op jit(solution)/shard_map/ppermute | solution.py:370
  1211.2 26.5 %all-to-all-start.9 = ((f32[16,1,256]{2,1,0:T(1,128)}), f32[16,1,256]{2,1,0:T(1,128)S(1)}, u32[]{:S(2)}, u32[]{:S(2)}) async-start(f32[16,1,256]{2,1,0:T(1,128)} %reshape.269), calls=%async_computation.10 | async-start | bytes 32768 | tf_op jit(solution)/shard_map/all_to_all | solution.py:678
  1239.1 1.8 collective-permute-start.22
  1240.4 6.9 collective-permute-start.24
  (53 other events, 278.7 us)
Sparse Core Ops, SparseCore 0:
  13.6 194.3 all-gather.4
  210.0 72.6 all-gather.6
  284.3 74.4 all-gather.8
  360.2 74.4 all-gather.10
  819.6 71.2 reduce-scatter.4
  908.4 271.9 reduce-scatter.2

commit v9 on v8

--- a/solution.py
+++ b/solution.py
@@ -654,10 +654,9 @@
     up_part, hidden_t, grad_qkv, outs_first, came_o, gate_came, *away_second = got
     out_grad = expert_sum(add_parts(blocks_o[0], [came_o]))
     outs_second = add_parts(out_rows_of(1, 0, hidden_t), away_second)
-    up_total = core_sum(up_part)
-    outs_second, up_total, grad_qkv, out_grad = after(outs_second, up_total, grad_qkv, out_grad)
+    outs_second, up_part, grad_qkv, out_grad = after(outs_second, up_part, grad_qkv, out_grad)
     outs_second = swap_experts(outs_second)
-    up_own, up_came = side_swap_sum(up_total)
+    up_own, up_came = side_swap_sum(core_sum(up_part))
 
     def back_rows(s, out):
         return dot(grad_qkv[s * rows : (s + 1) * rows], full_qkv, 1, 1, out)

time: 1260 us -> 1280 us (1.016)
  waiting for transfers between devices: 368 us -> 393 us
    ppermute x12, waiting for transfers between devices: 47 us -> 78.8 us  [fsdp_shift(): return lax.ppermute(a, 'fsdp', [(i, move(i)) for i in range(fsdp_count)])]
  transfers between devices with their start and end apart: 41 -> 41, of which waited for: 14 -> 17; matrix products, arithmetic and copies ran while one was open for 33% -> 31% of each run, Pallas kernels for 29% -> 29%
where the time goes in v9:
time: 1280 us
  waiting for transfers between devices  393 us (31%)
  Pallas kernels  365 us (29%)
  matrix products  240 us (19%)
  other arithmetic  112 us (9%)
  local copies, waits for them, and re-layouts  88 us (7%)
  starting transfers between devices  62.9 us (5%)
  between operations  15.4 us (1%)
    dot_general x19, matrix products, dot(): lax.dot_general(a, b, (((ca,), (cb,)), ((), ())), preferred_element_type=...  240 us
    pallas_call x4, Pallas kernels, expert_hidden(): pl.pallas_call(functools.partial(expert_kernel, len(kept)), grid=(units /...  224 us
    all_gather x1, waiting for transfers between devices, shards(): gathered = lax.all_gather(packed, 'fsdp', axis=0, tiled=True)  153 us
    all_gather x3, waiting for transfers between devices, shards(): lax.all_gather(part, 'fsdp', axis=0, tiled=True, axis_index_groups=sides)  88.3 us
    ppermute x12, waiting for transfers between devices, fsdp_shift(): return lax.ppermute(a, 'fsdp', [(i, move(i)) for i in range(fsdp_count)])  78.8 us
    all_to_all x9, waiting for transfers between devices, swap_experts(): lax.all_to_all(blocks, 'fsdp', 0, 0, axis_index_groups=lines, tiled=True)  59.4 us
    pallas_call x4, Pallas kernels, expert_rows(): pl.pallas_call(functools.partial(rows_kernel, len(left)), grid=(D // tile...  54.9 us
    all_to_all x9, starting transfers between devices, swap_experts(): lax.all_to_all(blocks, 'fsdp', 0, 0, axis_index_groups=lines, tiled=True)  42.3 us
  transfers between devices with their start and end apart: 41, of which 17 were waited for; matrix products, arithmetic and copies ran while one was open for 31% of the time, Pallas kernels for 29%

profile of v9, /device:TPU:0, one launch (start us, length us, event | category | flops | bytes accessed | tf_op | source)
XLA Modules:
  0.0 1276.3 jit_solution(7424934669133139504)
XLA Ops:
  24.1 6.9 constant_dynamic-slice_fusion.16
  41.1 13.5 %fusion.29 = bf16[1024,2048]{1,0:T(8,128)(2,1)} fusion(s32[2048]{0:T(1024)S(1)} %fusion.86, bf16[512,2048]{1,0:T(8,128)(2,1)} %collective-permute-done, bf16[512,2048]{1,0:T(8,128)(2,1)} %fusion.19), kind=kOutput, calls=%fused_computation.62 | convolution fusion | flops 8604614656 | bytes 8396800 | tf_op jit(solution)/shard_map/dot_general | solution.py:28
  54.6 153.3 %all-gather.5.cloned.1.call-done = bf16[2048,4096]{1,0:T(8,128)(2,1)} async-done(((bf16[128,4096]{1,0:T(8,128)(2,1)}), bf16[2048,4096]{1,0:T(8,128)(2,1)}) %all-gather.5.cloned.1.call-update) | async-done | bytes 16777232 | tf_op jit(solution)/shard_map/all_gather | solution.py:404
  215.4 5.4 slice.77
  228.5 18.9 %fusion.12.pre_q.pre_k.pre_v = f32[1024,3072]{1,0:T(8,128)} fusion(bf16[2048,4096]{1,0:T(8,128)(2,1)} %all-gather.5.cloned.1.call-done, bf16[512,2048]{1,0:T(8,128)(2,1)} %collective-permute-done, bf16[512,2048]{1,0:T(8,128)(2,1)} %fusion.19), kind=kOutput, calls=%fused_computation.20 | convolution fusion | flops 12893290496 | bytes 29360128 | tf_op jit(solution)/shard_map/dot_general | solution.py:28
  247.5 21.7 %attention_forward.1 = (bf16[1024,1024]{1,0:T(8,128)(2,1)}, bf16[1024,1024]{1,0:T(8,128)(2,1)}, bf16[1024,1024]{1,0:T(8,128)(2,1)}, bf16[1024,1024]{1,0:T(8,128)(2,1)}, f32[1024,1024]{1,0:T(8,128)}) custom-call(s32[4]{0:T(128)} %fusion.95.perm, f32[1024,3072]{1,0:T(8,128)} %fusion.12.pre_q.pre_k.pre_v, f32[1024,3072]{1,0:T(8,128)} %fusion.12.pre_q.pre_k.pre_v, ...), custom_call_target="tpu_custom_call" | custom-call | tf_op jit(solution)/shard_map/attention_forward/pallas_call | solution.py:155
  278.4 6.2 all-to-all-done
  294.0 6.6 multiply_reduce_fusion.2
  307.1 51.7 %all-gather.9.cloned.1.call-done = bf16[1408,2048]{1,0:T(8,128)(2,1)} async-done(((bf16[704,2048]{1,0:T(8,128)(2,1)}), bf16[1408,2048]{1,0:T(8,128)(2,1)}) %all-gather.9.cloned.1.call-update) | async-done | bytes 5767184 | tf_op jit(solution)/shard_map/all_gather | solution.py:467
  372.9 12.7 join_weights.3.wg_ref
  385.6 12.4 join_weights.4.wu_ref
  398.0 36.7 %all-gather.11.cloned.1.call-done = bf16[1408,2048]{1,0:T(8,128)(2,1)} async-done(((bf16[704,2048]{1,0:T(8,128)(2,1)}), bf16[1408,2048]{1,0:T(8,128)(2,1)}) %all-gather.11.cloned.1.call-update) | async-done | bytes 5767184 | tf_op jit(solution)/shard_map/all_gather | solution.py:467
  447.0 12.3 join_weights.5.wd_ref.refs_1_
  459.4 55.9 %expert_hidden.4 = (bf16[2560,2816]{1,0:T(8,128)(2,1)}, bf16[2560,2816]{1,0:T(8,128)(2,1)}, bf16[2560,2816]{1,0:T(8,128)(2,1)}, bf16[640,2048]{1,0:T(8,128)(2,1)}) custom-call(bf16[640,2048]{1,0:T(8,128)(2,1)} %bitcast.113, bf16[640,2048]{1,0:T(8,128)(2,1)} %bitcast.15.g_ref, bf16[2816,2048]{1,0:T(8,128)(2,1)} %join_weights.3.wg_ref, ...), custom_call_target="tpu_custom_call" | custom-call | tf_op jit(solution)/shard_map/expert_hidden/pallas_call | solution.py:226
  516.8 55.9 %expert_hidden.5 = (bf16[2560,2816]{1,0:T(8,128)(2,1)}, bf16[2560,2816]{1,0:T(8,128)(2,1)}, bf16[2560,2816]{1,0:T(8,128)(2,1)}, bf16[640,2048]{1,0:T(8,128)(2,1)}) custom-call(bf16[640,2048]{1,0:T(8,128)(2,1)} %collective-permute-done.8.x_ref, ...), custom_call_target="tpu_custom_call", output_to_operand_aliasing={{0}: (5, {}), {1}: (6, {}), {2}: (7, {})} | custom-call | tf_op jit(solution)/shard_map/expert_hidden/pallas_call | solution.py:226
  575.9 56.1 %expert_hidden.6 = (bf16[2560,2816]{1,0:T(8,128)(2,1)}, bf16[2560,2816]{1,0:T(8,128)(2,1)}, bf16[2560,2816]{1,0:T(8,128)(2,1)}, bf16[640,2048]{1,0:T(8,128)(2,1)}) custom-call(bf16[640,2048]{1,0:T(8,128)(2,1)} %copy-done.16, bf16[640,2048]{1,0:T(8,128)(2,1)} %collective-permute-done.6.g_ref, ...), custom_call_target="tpu_custom_call", output_to_operand_aliasing={{0}: (5, {}), {1}: (6, {}), {2}: (7, {})} | custom-call | tf_op jit(solution)/shard_map/expert_hidden/pallas_call | solution.py:226
  632.1 5.3 add_convert_fusion.6
  637.3 5.1 all-to-all-start.4
  643.9 55.9 %expert_hidden.7 = (bf16[2560,2816]{1,0:T(8,128)(2,1)}, bf16[2560,2816]{1,0:T(8,128)(2,1)}, bf16[2560,2816]{1,0:T(8,128)(2,1)}, bf16[640,2048]{1,0:T(8,128)(2,1)}) custom-call(bf16[640,2048]{1,0:T(8,128)(2,1)} %bitcast.24.x_ref, bf16[640,2048]{1,0:T(8,128)(2,1)} %bitcast.17.g_ref, ...), custom_call_target="tpu_custom_call", output_to_operand_aliasing={{0}: (5, {}), {1}: (6, {}), {2}: (7, {})} | custom-call | tf_op jit(solution)/shard_map/expert_hidden/pallas_call | solution.py:226
  701.3 5.3 add_convert_fusion.5
  711.2 39.0 %convolution_convert_fusion.2 = bf16[2816,2048]{1,0:T(8,128)(2,1)} fusion(bf16[2560,2816]{1,0:T(8,128)(2,1)} %get-tuple-element.234.refs_0_, bf16[640,2048]{1,0:T(8,128)(2,1)} %collective-permute-done.6.g_ref, bf16[640,2048]{1,0:T(8,128)(2,1)} %bitcast.17.g_ref, bf16[640,2048]{1,0:T(8,128)(2,1)} %collective-permute-done.3.g_ref, ...), kind=kOutput, calls=%fused_computation.7 | convolution fusion | flops 29575610368 | bytes 36438016 | tf_op jit(solution)/shard_map/dot_general | solution.py:28
  750.3 5.8 constant_dynamic-slice_fusion.11
  756.1 13.6 %expert_rows.4 = bf16[640,2048]{1,0:T(8,128)(2,1)} custom-call(bf16[2560,2816]{1,0:T(8,128)(2,1)} %get-tuple-element.234.refs_0_, bf16[2816,2048]{1,0:T(8,128)(2,1)} %join_weights.5.wd_ref.refs_1_), custom_call_target="tpu_custom_call" | custom-call | tf_op jit(solution)/shard_map/expert_rows/pallas_call | solution.py:248
  779.5 9.8 add_convert_fusion.2
  789.3 7.0 convolution_convert_fusion.4
  815.8 5.7 convolution_convert_fusion.10.do_ref
  821.5 27.4 %attention_backward.1 = bf16[1024,3072]{1,0:T(8,128)(2,1)} custom-call(s32[4]{0:T(128)} %fusion.95.perm, bf16[1024,1024]{1,0:T(8,128)(2,1)} %get-tuple-element.136.q_ref, bf16[1024,1024]{1,0:T(8,128)(2,1)} %get-tuple-element.137.k_ref, bf16[1024,1024]{1,0:T(8,128)(2,1)} %get-tuple-element.138.v_ref, f32[1024,1024]{1,0:T(8,128)} %get-tuple-element.139.log_ref, ...), custom_call_target="tpu_custom_call" | custom-call | tf_op jit(solution)/shard_map/attention_backward/pallas_call | solution.py:178
  848.8 19.4 %convolution_convert_fusion.3 = bf16[2048,3072]{1,0:T(8,128)(2,1)} fusion(bf16[1024,2048]{1,0:T(8,128)(2,1)} %fusion.29, bf16[1024,3072]{1,0:T(8,128)(2,1)} %attention_backward.1), kind=kOutput, calls=%fused_computation.8 | convolution fusion | flops 12891193344 | bytes 23068672 | tf_op jit(solution)/shard_map/dot_general | solution.py:28
  869.7 35.8 %convolution_convert_fusion.1 = bf16[2816,2048]{1,0:T(8,128)(2,1)S(1)} fusion(bf16[2560,2816]{1,0:T(8,128)(2,1)} %get-tuple-element.217, bf16[2560,2048]{1,0:T(8,128)(2,1)} %copy-done.32), kind=kOutput, calls=%fused_computation.6 | convolution fusion | flops 29533667328 | bytes 36438016 | tf_op jit(solution)/shard_map/dot_general | solution.py:28
  905.5 20.0 %collective-permute-done.15 = bf16[512,2048]{1,0:T(8,128)(2,1)} collective-permute-done((bf16[512,2048]{1,0:T(8,128)(2,1)}, bf16[512,2048]{1,0:T(8,128)(2,1)}, u32[]{:S(2)}, u32[]{:S(2)}) %collective-permute-start.15) | collective-permute-done | bytes 2097184 | tf_op jit(solution)/shard_map/ppermute | solution.py:370
  932.5 13.7 %expert_rows.5 = bf16[640,2048]{1,0:T(8,128)(2,1)} custom-call(bf16[2560,2816]{1,0:T(8,128)(2,1)} %get-tuple-element.234.refs_0_, bf16[2816,2048]{1,0:T(8,128)(2,1)} %join_weights.5.wd_ref.refs_1_), custom_call_target="tpu_custom_call" | custom-call | tf_op jit(solution)/shard_map/expert_rows/pallas_call | solution.py:248
  946.2 13.9 %expert_rows.6 = bf16[640,2048]{1,0:T(8,128)(2,1)} custom-call(bf16[2560,2816]{1,0:T(8,128)(2,1)} %get-tuple-element.234.refs_0_, bf16[2816,2048]{1,0:T(8,128)(2,1)} %join_weights.5.wd_ref.refs_1_), custom_call_target="tpu_custom_call" | custom-call | tf_op jit(solution)/shard_map/expert_rows/pallas_call | solution.py:248
  965.0 10.3 add_convert_fusion.1
  985.1 38.5 %convolution_convert_fusion = bf16[2816,2048]{1,0:T(8,128)(2,1)} fusion(bf16[2560,2816]{1,0:T(8,128)(2,1)} %get-tuple-element.227, bf16[2560,2048]{1,0:T(8,128)(2,1)} %copy-done.32), kind=kOutput, calls=%fused_computation.5 | convolution fusion | flops 29533667328 | bytes 36438016 | tf_op jit(solution)/shard_map/dot_general | solution.py:28
  1023.7 42.6 %collective-permute-done.19 = bf16[640,2048]{1,0:T(8,128)(2,1)S(1)} collective-permute-done((bf16[640,2048]{1,0:T(8,128)(2,1)S(1)}, bf16[640,2048]{1,0:T(8,128)(2,1)S(1)}, u32[]{:S(2)}, u32[]{:S(2)}) %collective-permute-start.19) | collective-permute-done | bytes 2621472 | tf_op jit(solution)/shard_map/ppermute | solution.py:370
  1067.8 13.6 %collective-permute-done.18 = bf16[1408,1024]{1,0:T(8,128)(2,1)} collective-permute-done((bf16[1408,1024]{1,0:T(8,128)(2,1)S(1)}, bf16[1408,1024]{1,0:T(8,128)(2,1)}, u32[]{:S(2)}, u32[]{:S(2)}) %collective-permute-start.18) | collective-permute-done | bytes 2883616 | tf_op jit(solution)/shard_map/ppermute | solution.py:370
  1089.8 13.8 %expert_rows.7 = bf16[640,2048]{1,0:T(8,128)(2,1)} custom-call(bf16[2560,2816]{1,0:T(8,128)(2,1)} %get-tuple-element.234.refs_0_, bf16[2816,2048]{1,0:T(8,128)(2,1)} %join_weights.5.wd_ref.refs_1_), custom_call_target="tpu_custom_call" | custom-call | tf_op jit(solution)/shard_map/expert_rows/pallas_call | solution.py:248
  1103.5 5.3 add_convert_fusion.3
  1108.9 22.9 %all-to-all-done.7 = bf16[4,64,2048]{2,1,0:T(8,128)(2,1)} async-done(((bf16[4,64,2048]{2,1,0:T(8,128)(2,1)}), bf16[4,64,2048]{2,1,0:T(8,128)(2,1)}, u32[]{:S(2)}, u32[]{:S(2)}) %all-to-all-start.7) | async-done | bytes 1048608 | tf_op jit(solution)/shard_map/all_to_all | solution.py:457
  1134.0 5.8 constant_dynamic-slice_fusion.2
  1139.8 11.6 fusion.36
  1157.0 6.5 convert_add_fusion.3
  1168.7 13.0 %fusion.25 = (f32[2048]{0:T(1024)S(1)}, f32[512]{0:T(512)S(1)}, f32[512,2048]{1,0:T(8,128)}) fusion(bf16[1,512,2048]{2,1,0:T(8,128)(2,1)S(1)} %copy-done.3, f32[512]{0:T(512)S(1)} %copy-done.45, f32[2048]{0:T(1024)S(1)} %copy-done.34, bf16[512,2048]{1,0:T(8,128)(2,1)} %collective-permute-done.20, bf16[2048,4096]{1,0:T(8,128)(2,1)} %all-gather.5.cloned.1.call-done, ...), kind=kOutput, calls=%fused_computation.47 | convolution fusion | flops 6451885568 | bytes 24137728 | tf_op jit(solution)/shard_map/dot_general | solution.py:28
  1181.7 7.3 add_convert_fusion
  1195.2 5.2 fusion.24
  1200.4 28.3 %all-to-all-done.8 = bf16[4,160,2048]{2,1,0:T(8,128)(2,1)} async-done(((bf16[4,160,2048]{2,1,0:T(8,128)(2,1)}), bf16[4,160,2048]{2,1,0:T(8,128)(2,1)}, u32[]{:S(2)}, u32[]{:S(2)}) %all-to-all-start.8) | async-done | bytes 2621472 | tf_op jit(solution)/shard_map/all_to_all | solution.py:457
  1252.5 6.0 all-to-all-done.9
  1262.2 5.8 convert_add_fusion.2
  (292 shorter events, 215.8 us)
Async XLA Ops:
  7.2 200.7 %all-gather.5.cloned.1.call-start = ((), (), s32[]{:S(2)}) async-start(), calls=%async_computation.12 | async-start | bytes 17825792 | tf_op jit(solution)/shard_map/all_gather | solution.py:404
  13.4 293.7 %all-gather.7.cloned.1.call-start = ((), (), s32[]{:S(2)}) async-start(), calls=%async_computation.13 | async-start | bytes 8650752 | tf_op jit(solution)/shard_map/all_gather | solution.py:467
  15.9 25.2 %collective-permute-start = (bf16[512,2048]{1,0:T(8,128)(2,1)}, bf16[512,2048]{1,0:T(8,128)(2,1)}, u32[]{:S(2)}, u32[]{:S(2)}) collective-permute-start(bf16[512,2048]{1,0:T(8,128)(2,1)} %fusion.19), channel_id=1, source_target_pairs={{0,16},{16,0},{1,17},{17,1},{2,18},{18,2},{3,19},{19,3},{4,20},{20... | collective-permute-start | bytes 6291464 | tf_op jit(solution)/shard_map/ppermute | solution.py:367
  20.3 270.9 %copy-start.38 = (s32[512]{0:T(512)}, s32[512]{0:T(512)S(1)}, u32[]{:S(2)}) copy-start(s32[512]{0:T(512)S(1)} %get-tuple-element.257) | copy-start | bytes 6148
  20.3 270.9 %copy-start.41 = (s32[512]{0:T(512)}, s32[512]{0:T(512)S(1)}, u32[]{:S(2)}) copy-start(s32[512]{0:T(512)S(1)} %get-tuple-element.258) | copy-start | bytes 6148
  41.1 166.9 %copy-start.59 = (s32[1,4]{1,0:T(1,128)S(1)}, s32[1,4]{1,0:T(1,128)}, u32[]{:S(2)}) copy-start(s32[1,4]{1,0:T(1,128)} %param.17) | copy-start | bytes 52
  207.9 150.8 %all-gather.9.cloned.1.call-start = ((), (), s32[]{:S(2)}) async-start(), calls=%async_computation.14 | async-start | bytes 8650752 | tf_op jit(solution)/shard_map/all_gather | solution.py:467
  220.8 63.9 %all-to-all-start = ((bf16[4,160,2048]{2,1,0:T(8,128)(2,1)}), bf16[4,160,2048]{2,1,0:T(8,128)(2,1)}, u32[]{:S(2)}, u32[]{:S(2)}) async-start(bf16[4,160,2048]{2,1,0:T(8,128)(2,1)} %bitcast.131), calls=%async_computation | async-start | bytes 5242880 | tf_op jit(solution)/shard_map/all_to_all | solution.py:457
  228.5 40.6 %collective-permute-start.1 = (bf16[1024,1024]{1,0:T(8,128)(2,1)}, bf16[1024,1024]{1,0:T(8,128)(2,1)}, u32[]{:S(2)}, u32[]{:S(2)}) collective-permute-start(bf16[1024,1024]{1,0:T(8,128)(2,1)} %constant_dynamic-slice_fusion.15), channel_id=1, source_target_pairs={{0,16},{16,0},{1,17},{17,1},{2,18},{18,2},{3,19},{19,3},{4,20},{20... | collective-permute-start | bytes 6291464 | tf_op jit(solution)/shard_map/ppermute | solution.py:367
  284.6 74.1 %all-to-all-start.1 = ((bf16[4,160,2048]{2,1,0:T(8,128)(2,1)}), bf16[4,160,2048]{2,1,0:T(8,128)(2,1)}, u32[]{:S(2)}, u32[]{:S(2)}) async-start(bf16[4,160,2048]{2,1,0:T(8,128)(2,1)} %bitcast.129), calls=%async_computation.1 | async-start | bytes 5242880 | tf_op jit(solution)/shard_map/all_to_all | solution.py:457
  289.3 145.4 %all-gather.11.cloned.1.call-start = ((), (), s32[]{:S(2)}) async-start(), calls=%async_computation.15 | async-start | bytes 8650752 | tf_op jit(solution)/shard_map/all_gather | solution.py:467
  289.5 4.6 collective-permute-start.2
  289.6 69.2 %collective-permute-start.3 = (bf16[640,2048]{1,0:T(8,128)(2,1)}, bf16[640,2048]{1,0:T(8,128)(2,1)}, u32[]{:S(2)}, u32[]{:S(2)}) collective-permute-start(bf16[640,2048]{1,0:T(8,128)(2,1)} %bitcast.15.g_ref), channel_id=1, source_target_pairs={{0,2},{1,3},{2,0},{3,1},{4,6},{5,7},{6,4},{7,5},{8,10},{9,11},{10,... | collective-permute-start | bytes 7864328 | tf_op jit(solution)/shard_map/ppermute | solution.py:370
  358.8 75.9 %all-to-all-start.2 = ((bf16[4,160,2048]{2,1,0:T(8,128)(2,1)}), bf16[4,160,2048]{2,1,0:T(8,128)(2,1)S(1)}, u32[]{:S(2)}, u32[]{:S(2)}) async-start(bf16[4,160,2048]{2,1,0:T(8,128)(2,1)} %bitcast.132), calls=%async_computation.2 | async-start | bytes 5242880 | tf_op jit(solution)/shard_map/all_to_all | solution.py:457
  367.3 5.6 collective-permute-start.4
  370.0 15.6 %collective-permute-start.5 = (bf16[704,2048]{1,0:T(8,128)(2,1)}, bf16[704,2048]{1,0:T(8,128)(2,1)}, u32[]{:S(2)}, u32[]{:S(2)}) collective-permute-start(bf16[704,2048]{1,0:T(8,128)(2,1)} %constant_dynamic-slice_fusion.13.refs_0_), channel_id=1, source_target_pairs={{0,16},{16,0},{1,17},{17,1},{2,18},{18,2},{3,19},{19,3},{4,20},{20... | collective-permute-start | bytes 8650760 | tf_op jit(solution)/shard_map/ppermute | solution.py:367
  370.0 64.7 %collective-permute-start.6 = (bf16[640,2048]{1,0:T(8,128)(2,1)}, bf16[640,2048]{1,0:T(8,128)(2,1)}, u32[]{:S(2)}, u32[]{:S(2)}) collective-permute-start(bf16[640,2048]{1,0:T(8,128)(2,1)} %bitcast.17.g_ref), channel_id=1, source_target_pairs={{0,2},{1,3},{2,0},{3,1},{4,6},{5,7},{6,4},{7,5},{8,10},{9,11},{10,... | collective-permute-start | bytes 7864328 | tf_op jit(solution)/shard_map/ppermute | solution.py:370
  434.7 80.6 %all-to-all-start.3 = ((bf16[4,160,2048]{2,1,0:T(8,128)(2,1)}), bf16[4,160,2048]{2,1,0:T(8,128)(2,1)}, u32[]{:S(2)}, u32[]{:S(2)}) async-start(bf16[4,160,2048]{2,1,0:T(8,128)(2,1)} %bitcast.130), calls=%async_computation.3 | async-start | bytes 5242880 | tf_op jit(solution)/shard_map/all_to_all | solution.py:457
  441.5 5.5 collective-permute-start.7
  441.6 73.6 %collective-permute-start.8 = (bf16[640,2048]{1,0:T(8,128)(2,1)S(1)}, bf16[640,2048]{1,0:T(8,128)(2,1)}, u32[]{:S(2)}, u32[]{:S(2)}) collective-permute-start(bf16[640,2048]{1,0:T(8,128)(2,1)S(1)} %bitcast.112), channel_id=1, source_target_pairs={{0,2},{1,3},{2,0},{3,1},{4,6},{5,7},{6,4},{7,5},{8,10},{9,11},{10,... | collective-permute-start | bytes 7864328 | tf_op jit(solution)/shard_map/ppermute | solution.py:370
  515.2 59.2 %collective-permute-start.9 = (bf16[640,2048]{1,0:T(8,128)(2,1)}, bf16[640,2048]{1,0:T(8,128)(2,1)S(1)}, u32[]{:S(2)}, u32[]{:S(2)}) collective-permute-start(bf16[640,2048]{1,0:T(8,128)(2,1)} %bitcast.24.x_ref), channel_id=1, source_target_pairs={{0,2},{1,3},{2,0},{3,1},{4,6},{5,7},{6,4},{7,5},{8,10},{9,11},{10,... | collective-permute-start | bytes 7864328 | tf_op jit(solution)/shard_map/ppermute | solution.py:370
  572.7 59.4 %collective-permute-start.10 = (bf16[640,2048]{1,0:T(8,128)(2,1)}, bf16[640,2048]{1,0:T(8,128)(2,1)}, u32[]{:S(2)}, u32[]{:S(2)}) collective-permute-start(bf16[640,2048]{1,0:T(8,128)(2,1)} %get-tuple-element.186), channel_id=1, source_target_pairs={{0,2},{1,3},{2,0},{3,1},{4,6},{5,7},{6,4},{7,5},{8,10},{9,11},{10,... | collective-permute-start | bytes 7864328 | tf_op jit(solution)/shard_map/ppermute | solution.py:370
  637.3 64.0 %all-to-all-start.4 = ((bf16[4,160,2048]{2,1,0:T(8,128)(2,1)}), bf16[4,160,2048]{2,1,0:T(8,128)(2,1)S(1)}, u32[]{:S(2)}, u32[]{:S(2)}) async-start(bf16[4,160,2048]{2,1,0:T(8,128)(2,1)} %bitcast.117), calls=%async_computation.4 | async-start | bytes 5242880 | tf_op jit(solution)/shard_map/all_to_all | solution.py:457
  642.4 58.9 %collective-permute-start.11 = (bf16[640,2048]{1,0:T(8,128)(2,1)}, bf16[640,2048]{1,0:T(8,128)(2,1)}, u32[]{:S(2)}, u32[]{:S(2)}) collective-permute-start(bf16[640,2048]{1,0:T(8,128)(2,1)} %get-tuple-element.203), channel_id=1, source_target_pairs={{0,2},{1,3},{2,0},{3,1},{4,6},{5,7},{6,4},{7,5},{8,10},{9,11},{10,... | collective-permute-start | bytes 7864328 | tf_op jit(solution)/shard_map/ppermute | solution.py:370
  706.6 63.6 %all-to-all-start.5 = ((bf16[4,160,2048]{2,1,0:T(8,128)(2,1)}), bf16[4,160,2048]{2,1,0:T(8,128)(2,1)}, u32[]{:S(2)}, u32[]{:S(2)}) async-start(bf16[4,160,2048]{2,1,0:T(8,128)(2,1)} %bitcast.118), calls=%async_computation.5 | async-start | bytes 5242880 | tf_op jit(solution)/shard_map/all_to_all | solution.py:457
  711.2 440.8 %reduce-scatter.5.cloned.1.call-start = ((), (), s32[]{:S(2)}) async-start(), calls=%async_computation.17 | async-start | bytes 8650752 | tf_op jit(solution)/shard_map/reduce_scatter | solution.py:572
  756.1 23.4 %collective-permute-start.13 = (bf16[2816,1024]{1,0:T(8,128)(2,1)}, bf16[2816,1024]{1,0:T(8,128)(2,1)}, u32[]{:S(2)}, u32[]{:S(2)}) collective-permute-start(bf16[2816,1024]{1,0:T(8,128)(2,1)} %constant_dynamic-slice_fusion.11), channel_id=1, source_target_pairs={{0,16},{16,0},{1,17},{17,1},{2,18},{18,2},{3,19},{19,3},{4,20},{20... | collective-permute-start | bytes 17301512 | tf_op jit(solution)/shard_map/ppermute | solution.py:367
  779.4 9.9 collective-permute-start.12
  803.1 425.5 %reduce-scatter.3.cloned.1.call-start = ((), (), s32[]{:S(2)}) async-start(), calls=%async_computation.16 | async-start | bytes 13369344 | tf_op jit(solution)/shard_map/reduce_scatter | solution.py:635
  809.9 59.8 %collective-permute-start.14 = (bf16[640,2048]{1,0:T(8,128)(2,1)S(1)}, bf16[640,2048]{1,0:T(8,128)(2,1)}, u32[]{:S(2)}, u32[]{:S(2)}) collective-permute-start(bf16[640,2048]{1,0:T(8,128)(2,1)S(1)} %copy-done.23), channel_id=1, source_target_pairs={{0,2},{1,3},{2,0},{3,1},{4,6},{5,7},{6,4},{7,5},{8,10},{9,11},{10,... | collective-permute-start | bytes 7864328 | tf_op jit(solution)/shard_map/ppermute | solution.py:370
  811.4 114.1 %collective-permute-start.15 = (bf16[512,2048]{1,0:T(8,128)(2,1)}, bf16[512,2048]{1,0:T(8,128)(2,1)}, u32[]{:S(2)}, u32[]{:S(2)}) collective-permute-start(bf16[512,2048]{1,0:T(8,128)(2,1)} %bitcast.30), channel_id=1, source_target_pairs={{0,2},{1,3},{2,0},{3,1},{4,6},{5,7},{6,4},{7,5},{8,10},{9,11},{10,... | collective-permute-start | bytes 6291464 | tf_op jit(solution)/shard_map/ppermute | solution.py:370
  905.5 23.2 %copy-start.14 = (bf16[2816,2048]{1,0:T(8,128)(2,1)}, bf16[2816,2048]{1,0:T(8,128)(2,1)S(1)}, u32[]{:S(2)}) copy-start(bf16[2816,2048]{1,0:T(8,128)(2,1)S(1)} %convolution_convert_fusion.1) | copy-start | bytes 34603012
  905.5 23.2 %copy-start.20 = (bf16[4,1,128,2048]{3,2,1,0:T(8,128)(2,1)S(1)}, bf16[4,1,128,2048]{3,2,1,0:T(8,128)(2,1)}, u32[]{:S(2)}) copy-start(bf16[4,1,128,2048]{3,2,1,0:T(8,128)(2,1)} %get-tuple-element.264) | copy-start | bytes 6291460
  928.7 36.3 %collective-permute-start.16 = (bf16[2816,1024]{1,0:T(8,128)(2,1)}, bf16[2816,1024]{1,0:T(8,128)(2,1)}, u32[]{:S(2)}, u32[]{:S(2)}) collective-permute-start(bf16[2816,1024]{1,0:T(8,128)(2,1)} %constant_dynamic-slice_fusion.6), channel_id=1, source_target_pairs={{0,16},{16,0},{1,17},{17,1},{2,18},{18,2},{3,19},{19,3},{4,20},{20... | collective-permute-start | bytes 17301512 | tf_op jit(solution)/shard_map/ppermute | solution.py:367
  960.1 63.6 %collective-permute-start.17 = (bf16[256,2048]{1,0:T(8,128)(2,1)}, bf16[256,2048]{1,0:T(8,128)(2,1)}, u32[]{:S(2)}, u32[]{:S(2)}) collective-permute-start(bf16[256,2048]{1,0:T(8,128)(2,1)} %bitcast.134), channel_id=1, source_target_pairs={{0,1},{1,0},{2,3},{3,2},{4,5},{5,4},{6,7},{7,6},{8,9},{9,8},{10,11... | collective-permute-start | bytes 3145736 | tf_op jit(solution)/shard_map/ppermute | solution.py:370
  975.3 106.1 %all-to-all-start.6 = ((bf16[4,160,2048]{2,1,0:T(8,128)(2,1)}), bf16[4,160,2048]{2,1,0:T(8,128)(2,1)S(1)}, u32[]{:S(2)}, u32[]{:S(2)}) async-start(bf16[4,160,2048]{2,1,0:T(8,128)(2,1)} %bitcast.116), calls=%async_computation.6 | async-start | bytes 5242880 | tf_op jit(solution)/shard_map/all_to_all | solution.py:457
  982.0 99.4 %collective-permute-start.18 = (bf16[1408,1024]{1,0:T(8,128)(2,1)S(1)}, bf16[1408,1024]{1,0:T(8,128)(2,1)}, u32[]{:S(2)}, u32[]{:S(2)}) collective-permute-start(bf16[1408,1024]{1,0:T(8,128)(2,1)S(1)} %constant_dynamic-slice_fusion.5), channel_id=1, source_target_pairs={{0,1},{1,0},{2,3},{3,2},{4,5},{5,4},{6,7},{7,6},{8,9},{9,8},{10,11... | collective-permute-start | bytes 8650760 | tf_op jit(solution)/shard_map/ppermute | solution.py:370
  983.6 82.7 %collective-permute-start.19 = (bf16[640,2048]{1,0:T(8,128)(2,1)S(1)}, bf16[640,2048]{1,0:T(8,128)(2,1)S(1)}, u32[]{:S(2)}, u32[]{:S(2)}) collective-permute-start(bf16[640,2048]{1,0:T(8,128)(2,1)S(1)} %copy-done.24), channel_id=1, source_target_pairs={{0,2},{1,3},{2,0},{3,1},{4,6},{5,7},{6,4},{7,5},{8,10},{9,11},{10,... | collective-permute-start | bytes 7864328 | tf_op jit(solution)/shard_map/ppermute | solution.py:370
  1081.4 22.1 %copy-start.18 = (bf16[4,160,2048]{2,1,0:T(8,128)(2,1)}, bf16[4,160,2048]{2,1,0:T(8,128)(2,1)S(1)}, u32[]{:S(2)}) copy-start(bf16[4,160,2048]{2,1,0:T(8,128)(2,1)S(1)} %all-to-all-done.6) | copy-start | bytes 7864324
  1085.3 46.5 %all-to-all-start.7 = ((bf16[4,64,2048]{2,1,0:T(8,128)(2,1)}), bf16[4,64,2048]{2,1,0:T(8,128)(2,1)}, u32[]{:S(2)}, u32[]{:S(2)}) async-start(bf16[4,64,2048]{2,1,0:T(8,128)(2,1)} %bitcast.126), calls=%async_computation.7 | async-start | bytes 2097152 | tf_op jit(solution)/shard_map/all_to_all | solution.py:457
  1139.8 41.9 %collective-permute-start.22 = (bf16[2816,1024]{1,0:T(8,128)(2,1)}, bf16[2816,1024]{1,0:T(8,128)(2,1)}, u32[]{:S(2)}, u32[]{:S(2)}) collective-permute-start(bf16[2816,1024]{1,0:T(8,128)(2,1)} %constant_dynamic-slice_fusion.2), channel_id=1, source_target_pairs={{0,16},{16,0},{1,17},{17,1},{2,18},{18,2},{3,19},{19,3},{4,20},{20... | collective-permute-start | bytes 17301512 | tf_op jit(solution)/shard_map/ppermute | solution.py:367
  1151.4 17.3 %collective-permute-start.20 = (bf16[512,2048]{1,0:T(8,128)(2,1)}, bf16[512,2048]{1,0:T(8,128)(2,1)}, u32[]{:S(2)}, u32[]{:S(2)}) collective-permute-start(bf16[512,2048]{1,0:T(8,128)(2,1)} %fusion.36), channel_id=1, source_target_pairs={{0,16},{16,0},{1,17},{17,1},{2,18},{18,2},{3,19},{19,3},{4,20},{20... | collective-permute-start | bytes 6291464 | tf_op jit(solution)/shard_map/ppermute | solution.py:367
  1163.6 65.0 %all-to-all-start.8 = ((bf16[4,160,2048]{2,1,0:T(8,128)(2,1)}), bf16[4,160,2048]{2,1,0:T(8,128)(2,1)}, u32[]{:S(2)}, u32[]{:S(2)}) async-start(bf16[4,160,2048]{2,1,0:T(8,128)(2,1)} %bitcast.115), calls=%async_computation.8 | async-start | bytes 5242880 | tf_op jit(solution)/shard_map/all_to_all | solution.py:457
  1192.7 68.9 %collective-permute-start.23 = (bf16[1408,1024]{1,0:T(8,128)(2,1)}, bf16[1408,1024]{1,0:T(8,128)(2,1)}, u32[]{:S(2)}, u32[]{:S(2)}) collective-permute-start(bf16[1408,1024]{1,0:T(8,128)(2,1)} %get-tuple-element.261), channel_id=1, source_target_pairs={{0,1},{1,0},{2,3},{3,2},{4,5},{5,4},{6,7},{7,6},{8,9},{9,8},{10,11... | collective-permute-start | bytes 8650760 | tf_op jit(solution)/shard_map/ppermute | solution.py:370
  1229.4 29.0 %all-to-all-start.9 = ((f32[16,1,256]{2,1,0:T(1,128)}), f32[16,1,256]{2,1,0:T(1,128)S(1)}, u32[]{:S(2)}, u32[]{:S(2)}) async-start(f32[16,1,256]{2,1,0:T(1,128)} %reshape.269), calls=%async_computation.10 | async-start | bytes 32768 | tf_op jit(solution)/shard_map/all_to_all | solution.py:677
  1247.0 15.2 %copy-start.15 = (bf16[1408,1024]{1,0:T(8,128)(2,1)S(1)}, bf16[1408,1024]{1,0:T(8,128)(2,1)}, u32[]{:S(2)}) copy-start(bf16[1408,1024]{1,0:T(8,128)(2,1)} %get-tuple-element.250) | copy-start | bytes 8650756
  1259.8 1.8 collective-permute-start.21
  1261.1 6.9 collective-permute-start.24
  (53 other events, 261.8 us)
Sparse Core Ops, SparseCore 0:
  13.6 194.3 all-gather.4
  210.0 72.6 all-gather.6
  284.3 74.4 all-gather.8
  360.2 74.4 all-gather.10
  803.2 71.8 reduce-scatter.4
  881.5 251.7 reduce-scatter.2

commit v10 on v7

--- a/solution.py
+++ b/solution.py
@@ -509,7 +509,7 @@
         return expert_hidden(index, parts, slots, grad_parts[index], weights, state)
 
     def grad_rows(index, state):
-        return expert_rows(index, half, state[1:], (wg, wu))
+        return expert_rows(index, half, state[1:], weights[:2])
 
     def columns_home(pieces):
         return [column_shift(part, -(j + 1)) for j, part in enumerate(pieces)]
@@ -523,22 +523,21 @@
     slot_parts = to_columns(first)
     back, came = {}, [None] * halves
     state = hidden_part(0, slot_parts[0], ())
-    second, *got = after(second, *state, *slot_parts[1:])
-    state, slot_parts[1:] = got[:3], got[3:]
+    second, *state = after(second, *state)
     slot_parts += to_columns(second)
+    back[0] = grad_rows(0, state)
+    back[0], *got = after(back[0], *state, *slot_parts[1:columns])
+    state, slot_parts[1:columns] = got[:3], got[3:]
     for h in range(halves):
         for j in range(1, columns):
             index = h * columns + j
             state = hidden_part(index, slot_parts[index], state)
-        for j in range(1, columns):
-            index = h * columns + j
             back[index] = grad_rows(index, state)
             back[index], *state = after(back[index], *state)
         if h == 0:
             got = after(*state, *slot_parts[columns + 1 :])
             state, slot_parts[columns + 1 :] = got[:3], got[3:]
         came[h] = columns_home([back[h * columns + j] for j in range(1, columns)])
-    back[0] = grad_rows(0, state)
     home_first, *got = after(back[0], *state, *came[0])
     state = got[:3]
     home_first = add_parts(home_first, got[3:])
@@ -661,8 +660,9 @@
     _, unit_one, inverse_one = normalize_parts(inputs, norm1_gain)
     grad_norm_one, norm1_part = norm_backward(grad_normed, unit_one, inverse_one, norm1_gain)
     tokens_grad = (grad_hidden_in + grad_norm_one).astype(bf16)
-    got = after(tokens_grad, norm1_part, outs_second, up_own, up_came, qkv_sum, gate_own)
-    tokens_grad, norm1_part, outs_second, up_own, up_came, qkv_sum, gate_own = got
+    tokens_grad, norm1_part, outs_second, qkv_sum = after(
+        tokens_grad, norm1_part, outs_second, qkv_sum
+    )
     gate_grad = gate_own.astype(f32) + gate_came.astype(f32)
 
     gains = jnp.stack([norm1_part, norm2_part]).reshape(2, ctx_count, fsdp_count, per)
@@ -675,6 +675,7 @@
     gains_own = gains_of(core)
     for s in range(1, ctx_count):
         gains_own = gains_own + core_shift(gains_of(core + s), s)
+    gains_own, up_own, up_came = after(gains_own, up_own, up_came)
     up_grad = up_own.astype(f32) + up_came.astype(f32)
     sums = qkv_sum.reshape(ctx_count, per, heads, 3, HD).astype(f32)
     sums = sums.transpose(3, 0, 1, 2, 4).reshape(3, ctx_count, per, width)

time: 1270 us -> 1260 us (level)
    all_to_all x9, waiting for transfers between devices: 21.4 us -> 87.2 us  [swap_experts(): lax.all_to_all(blocks, 'fsdp', 0, 0, axis_index_groups=lines, tiled=True)]
    ppermute x12, waiting for transfers between devices: 115 us -> 53.2 us  [fsdp_shift(): return lax.ppermute(a, 'fsdp', [(i, move(i)) for i in range(fsdp_count)])]
  transfers between devices with their start and end apart: 41 -> 41, of which waited for: 16 -> 15; matrix products, arithmetic and copies ran while one was open for 32% -> 33% of each run, Pallas kernels for 28% -> 28%
where the time goes in v10:
time: 1260 us; the launch traced here: 1250 us
  waiting for transfers between devices  389 us (31%)
  Pallas kernels  348 us (28%)
  matrix products  239 us (19%)
  other arithmetic  110 us (9%)
  local copies, waits for them, and re-layouts  94.9 us (8%)
  starting transfers between devices  57.9 us (5%)
  between operations  15.4 us (1%)
    dot_general x19, matrix products, dot(): lax.dot_general(a, b, (((ca,), (cb,)), ((), ())), preferred_element_type=...  239 us
    all_gather x1, waiting for transfers between devices, shards(): gathered = lax.all_gather(packed, 'fsdp', axis=0, tiled=True)  153 us
    pallas_call x8, Pallas kernels, expert_rows(): pl.pallas_call(functools.partial(rows_kernel, len(left)), grid=(D // tile...  139 us
    pallas_call x4, Pallas kernels, expert_hidden(): pl.pallas_call(functools.partial(expert_kernel, len(kept)), grid=(units /...  123 us
    all_gather x3, waiting for transfers between devices, shards(): lax.all_gather(part, 'fsdp', axis=0, tiled=True, axis_index_groups=sides)  88.3 us
    all_to_all x9, waiting for transfers between devices, swap_experts(): lax.all_to_all(blocks, 'fsdp', 0, 0, axis_index_groups=lines, tiled=True)  87.2 us
    ppermute x12, waiting for transfers between devices, fsdp_shift(): return lax.ppermute(a, 'fsdp', [(i, move(i)) for i in range(fsdp_count)])  53.2 us
    all_to_all x9, starting transfers between devices, swap_experts(): lax.all_to_all(blocks, 'fsdp', 0, 0, axis_index_groups=lines, tiled=True)  40.5 us
  transfers between devices with their start and end apart: 41, of which 15 were waited for; matrix products, arithmetic and copies ran while one was open for 33% of the time, Pallas kernels for 28%

profile of v10, /device:TPU:0, one launch (start us, length us, event | category | flops | bytes accessed | tf_op | source)
XLA Modules:
  0.0 1254.7 jit_solution(17067064648803923167)
XLA Ops:
  24.1 6.9 constant_dynamic-slice_fusion.16
  41.1 13.4 %fusion.29 = bf16[1024,2048]{1,0:T(8,128)(2,1)} fusion(s32[2048]{0:T(1024)S(1)} %fusion.86, bf16[512,2048]{1,0:T(8,128)(2,1)} %collective-permute-done, bf16[512,2048]{1,0:T(8,128)(2,1)} %fusion.19), kind=kOutput, calls=%fused_computation.62 | convolution fusion | flops 8604614656 | bytes 8396800 | tf_op jit(solution)/shard_map/dot_general | solution.py:28
  54.5 153.5 %all-gather.5.cloned.1.call-done = bf16[2048,4096]{1,0:T(8,128)(2,1)} async-done(((bf16[128,4096]{1,0:T(8,128)(2,1)}), bf16[2048,4096]{1,0:T(8,128)(2,1)}) %all-gather.5.cloned.1.call-update) | async-done | bytes 16777232 | tf_op jit(solution)/shard_map/all_gather | solution.py:389
  215.4 5.4 slice.77
  228.6 19.0 %fusion.12.pre_q.pre_k.pre_v = f32[1024,3072]{1,0:T(8,128)} fusion(bf16[2048,4096]{1,0:T(8,128)(2,1)} %all-gather.5.cloned.1.call-done, bf16[512,2048]{1,0:T(8,128)(2,1)} %collective-permute-done, bf16[512,2048]{1,0:T(8,128)(2,1)} %fusion.19), kind=kOutput, calls=%fused_computation.20 | convolution fusion | flops 12893290496 | bytes 29360128 | tf_op jit(solution)/shard_map/dot_general | solution.py:28
  247.6 21.7 %attention_forward.1 = (bf16[1024,1024]{1,0:T(8,128)(2,1)}, bf16[1024,1024]{1,0:T(8,128)(2,1)}, bf16[1024,1024]{1,0:T(8,128)(2,1)}, bf16[1024,1024]{1,0:T(8,128)(2,1)}, f32[1024,1024]{1,0:T(8,128)}) custom-call(s32[4]{0:T(128)} %fusion.95.perm, f32[1024,3072]{1,0:T(8,128)} %fusion.12.pre_q.pre_k.pre_v, f32[1024,3072]{1,0:T(8,128)} %fusion.12.pre_q.pre_k.pre_v, ...), custom_call_target="tpu_custom_call" | custom-call | tf_op jit(solution)/shard_map/attention_forward/pallas_call | solution.py:155
  278.5 6.1 all-to-all-done
  294.1 6.6 multiply_reduce_fusion.2
  307.0 51.7 %all-gather.9.cloned.1.call-done = bf16[1408,2048]{1,0:T(8,128)(2,1)} async-done(((bf16[704,2048]{1,0:T(8,128)(2,1)}), bf16[1408,2048]{1,0:T(8,128)(2,1)}) %all-gather.9.cloned.1.call-update) | async-done | bytes 5767184 | tf_op jit(solution)/shard_map/all_gather | solution.py:452
  372.9 12.7 %join_weights.3.wg_ref.refs_2_ = bf16[2816,2048]{1,0:T(8,128)(2,1)} custom-call(s32[3]{0:T(128)} %pad_add_fusion.where, bf16[1408,2048]{1,0:T(8,128)(2,1)} %own_ref.3, bf16[704,2048]{1,0:T(8,128)(2,1)} %constant_dynamic-slice_fusion.14.refs_0_, bf16[704,2048]{1,0:T(8,128)(2,1)} %collective-permute-done.4.refs_1_), custom_call_target="tpu_custom_call" | custom-call | tf_op jit(solution)/shard_map/join_weights/pallas_call | solution.py:272
  385.6 12.5 join_weights.4.wu_ref.refs_3_
  398.1 36.6 %all-gather.11.cloned.1.call-done = bf16[1408,2048]{1,0:T(8,128)(2,1)} async-done(((bf16[704,2048]{1,0:T(8,128)(2,1)}), bf16[1408,2048]{1,0:T(8,128)(2,1)}) %all-gather.11.cloned.1.call-update) | async-done | bytes 5767184 | tf_op jit(solution)/shard_map/all_gather | solution.py:452
  447.0 12.4 join_weights.5.wd_ref.refs_1_
  459.4 30.6 %expert_hidden.4 = (bf16[2560,2816]{1,0:T(8,128)(2,1)}, bf16[2560,2816]{1,0:T(8,128)(2,1)}, bf16[2560,2816]{1,0:T(8,128)(2,1)}) custom-call(bf16[640,2048]{1,0:T(8,128)(2,1)} %bitcast.113, bf16[640,2048]{1,0:T(8,128)(2,1)} %bitcast.15.g_ref, bf16[2816,2048]{1,0:T(8,128)(2,1)} %join_weights.3.wg_ref.refs_2_, bf16[2816,2048]{1,0:T(8,128)(2,1)} %join_weights.4.wu_ref.refs_3_, ...), custom_call_target="tpu_custom_call" | custom-call | tf_op jit(solution)/shard_map/expert_hidden/pallas_call | solution.py:213
  490.0 9.2 all-to-all-done.3
  500.7 21.1 %expert_rows.8 = bf16[640,2048]{1,0:T(8,128)(2,1)} custom-call(bf16[2560,2816]{1,0:T(8,128)(2,1)} %get-tuple-element.168.refs_0_.refs_1_, bf16[2560,2816]{1,0:T(8,128)(2,1)} %get-tuple-element.169.refs_1_.refs_2_, bf16[2816,2048]{1,0:T(8,128)(2,1)} %join_weights.3.wg_ref.refs_2_, bf16[2816,2048]{1,0:T(8,128)(2,1)} %join_weights.4.wu_ref.refs_3_), custom_call_target="tpu_custom_call" | custom-call | tf_op jit(solution)/shard_map/expert_rows/pallas_call | solution.py:233
  521.8 30.6 %expert_hidden.5 = (bf16[2560,2816]{1,0:T(8,128)(2,1)}, bf16[2560,2816]{1,0:T(8,128)(2,1)}, bf16[2560,2816]{1,0:T(8,128)(2,1)}) custom-call(bf16[640,2048]{1,0:T(8,128)(2,1)} %collective-permute-done.8.x_ref, bf16[640,2048]{1,0:T(8,128)(2,1)} %collective-permute-done.3.g_ref, ...), custom_call_target="tpu_custom_call", output_to_operand_aliasing={{0}: (5, {}), {1}: (6, {}), {2}: (7, {})} | custom-call | tf_op jit(solution)/shard_map/expert_hidden/pallas_call | solution.py:213
  552.4 21.1 %expert_rows.9 = bf16[640,2048]{1,0:T(8,128)(2,1)} custom-call(bf16[2560,2816]{1,0:T(8,128)(2,1)} %get-tuple-element.179.refs_0_.refs_1_, bf16[2560,2816]{1,0:T(8,128)(2,1)} %get-tuple-element.180.refs_1_.refs_2_, bf16[2816,2048]{1,0:T(8,128)(2,1)} %join_weights.3.wg_ref.refs_2_, bf16[2816,2048]{1,0:T(8,128)(2,1)} %join_weights.4.wu_ref.refs_3_), custom_call_target="tpu_custom_call" | custom-call | tf_op jit(solution)/shard_map/expert_rows/pallas_call | solution.py:233
  574.1 30.8 %expert_hidden.6 = (bf16[2560,2816]{1,0:T(8,128)(2,1)}, bf16[2560,2816]{1,0:T(8,128)(2,1)}, bf16[2560,2816]{1,0:T(8,128)(2,1)}) custom-call(bf16[640,2048]{1,0:T(8,128)(2,1)} %collective-permute-done.9.x_ref, bf16[640,2048]{1,0:T(8,128)(2,1)} %collective-permute-done.6.g_ref, ...), custom_call_target="tpu_custom_call", output_to_operand_aliasing={{0}: (5, {}), {1}: (6, {}), {2}: (7, {})} | custom-call | tf_op jit(solution)/shard_map/expert_hidden/pallas_call | solution.py:213
  604.9 21.2 %expert_rows.10 = bf16[640,2048]{1,0:T(8,128)(2,1)} custom-call(bf16[2560,2816]{1,0:T(8,128)(2,1)} %get-tuple-element.194.refs_0_.refs_1_, bf16[2560,2816]{1,0:T(8,128)(2,1)} %get-tuple-element.195.refs_1_.refs_2_, bf16[2816,2048]{1,0:T(8,128)(2,1)} %join_weights.3.wg_ref.refs_2_, bf16[2816,2048]{1,0:T(8,128)(2,1)} %join_weights.4.wu_ref.refs_3_), custom_call_target="tpu_custom_call" | custom-call | tf_op jit(solution)/shard_map/expert_rows/pallas_call | solution.py:233
  640.4 30.6 %expert_hidden.7 = (bf16[2560,2816]{1,0:T(8,128)(2,1)}, bf16[2560,2816]{1,0:T(8,128)(2,1)}, bf16[2560,2816]{1,0:T(8,128)(2,1)}) custom-call(bf16[640,2048]{1,0:T(8,128)(2,1)} %bitcast.24.x_ref, bf16[640,2048]{1,0:T(8,128)(2,1)} %bitcast.17.g_ref, ...), custom_call_target="tpu_custom_call", output_to_operand_aliasing={{0}: (5, {}), {1}: (6, {}), {2}: (7, {})} | custom-call | tf_op jit(solution)/shard_map/expert_hidden/pallas_call | solution.py:213
  671.0 21.1 %expert_rows.11 = bf16[640,2048]{1,0:T(8,128)(2,1)} custom-call(bf16[2560,2816]{1,0:T(8,128)(2,1)} %get-tuple-element.217.refs_0_, bf16[2560,2816]{1,0:T(8,128)(2,1)} %get-tuple-element.227.refs_1_, bf16[2816,2048]{1,0:T(8,128)(2,1)} %join_weights.3.wg_ref.refs_2_, bf16[2816,2048]{1,0:T(8,128)(2,1)} %join_weights.4.wu_ref.refs_3_), custom_call_target="tpu_custom_call" | custom-call | tf_op jit(solution)/shard_map/expert_rows/pallas_call | solution.py:233
  692.1 5.4 all-to-all-done.4
  707.4 38.6 %convolution_convert_fusion.2 = bf16[2816,2048]{1,0:T(8,128)(2,1)} fusion(bf16[2560,2816]{1,0:T(8,128)(2,1)} %get-tuple-element.234.refs_0_, bf16[640,2048]{1,0:T(8,128)(2,1)} %collective-permute-done.6.g_ref, bf16[640,2048]{1,0:T(8,128)(2,1)} %bitcast.17.g_ref, bf16[640,2048]{1,0:T(8,128)(2,1)} %collective-permute-done.3.g_ref, ...), kind=kOutput, calls=%fused_computation.7 | convolution fusion | flops 29575610368 | bytes 36438016 | tf_op jit(solution)/shard_map/dot_general | solution.py:28
  746.0 5.8 constant_dynamic-slice_fusion.11
  751.8 13.6 %expert_rows.12 = bf16[640,2048]{1,0:T(8,128)(2,1)} custom-call(bf16[2560,2816]{1,0:T(8,128)(2,1)} %get-tuple-element.234.refs_0_, bf16[2816,2048]{1,0:T(8,128)(2,1)} %join_weights.5.wd_ref.refs_1_), custom_call_target="tpu_custom_call" | custom-call | tf_op jit(solution)/shard_map/expert_rows/pallas_call | solution.py:233
  790.3 9.8 add_convert_fusion.2
  800.2 7.0 convolution_convert_fusion.4
  812.0 5.7 convolution_convert_fusion.10.do_ref
  819.3 27.4 %attention_backward.1 = bf16[1024,3072]{1,0:T(8,128)(2,1)} custom-call(s32[4]{0:T(128)} %fusion.95.perm, bf16[1024,1024]{1,0:T(8,128)(2,1)} %get-tuple-element.136.q_ref, bf16[1024,1024]{1,0:T(8,128)(2,1)} %get-tuple-element.137.k_ref, bf16[1024,1024]{1,0:T(8,128)(2,1)} %get-tuple-element.138.v_ref, f32[1024,1024]{1,0:T(8,128)} %get-tuple-element.139.log_ref, ...), custom_call_target="tpu_custom_call" | custom-call | tf_op jit(solution)/shard_map/attention_backward/pallas_call | solution.py:178
  846.6 19.4 %convolution_convert_fusion.3 = bf16[2048,3072]{1,0:T(8,128)(2,1)} fusion(bf16[1024,2048]{1,0:T(8,128)(2,1)} %fusion.29, bf16[1024,3072]{1,0:T(8,128)(2,1)} %attention_backward.1), kind=kOutput, calls=%fused_computation.8 | convolution fusion | flops 12891193344 | bytes 23068672 | tf_op jit(solution)/shard_map/dot_general | solution.py:28
  866.0 35.9 %convolution_convert_fusion.1 = bf16[2816,2048]{1,0:T(8,128)(2,1)S(1)} fusion(bf16[2560,2816]{1,0:T(8,128)(2,1)} %get-tuple-element.217.refs_0_, bf16[2560,2048]{1,0:T(8,128)(2,1)} %constant_dynamic-update-slice_fusion), kind=kOutput, calls=%fused_computation.6 | convolution fusion | flops 29533667328 | bytes 36438016 | tf_op jit(solution)/shard_map/dot_general | solution.py:28
  911.9 13.4 %expert_rows.13 = bf16[640,2048]{1,0:T(8,128)(2,1)} custom-call(bf16[2560,2816]{1,0:T(8,128)(2,1)} %get-tuple-element.234.refs_0_, bf16[2816,2048]{1,0:T(8,128)(2,1)} %join_weights.5.wd_ref.refs_1_), custom_call_target="tpu_custom_call" | custom-call | tf_op jit(solution)/shard_map/expert_rows/pallas_call | solution.py:233
  925.3 13.9 %expert_rows.14 = bf16[640,2048]{1,0:T(8,128)(2,1)} custom-call(bf16[2560,2816]{1,0:T(8,128)(2,1)} %get-tuple-element.234.refs_0_, bf16[2816,2048]{1,0:T(8,128)(2,1)} %join_weights.5.wd_ref.refs_1_), custom_call_target="tpu_custom_call" | custom-call | tf_op jit(solution)/shard_map/expert_rows/pallas_call | solution.py:233
  944.4 10.0 add_convert_fusion.1
  963.3 38.6 %convolution_convert_fusion = bf16[2816,2048]{1,0:T(8,128)(2,1)} fusion(bf16[2560,2816]{1,0:T(8,128)(2,1)} %get-tuple-element.227.refs_1_, bf16[2560,2048]{1,0:T(8,128)(2,1)} %constant_dynamic-update-slice_fusion), kind=kOutput, calls=%fused_computation.5 | convolution fusion | flops 29533667328 | bytes 36438016 | tf_op jit(solution)/shard_map/dot_general | solution.py:28
  1001.9 32.0 %collective-permute-done.19 = bf16[640,2048]{1,0:T(8,128)(2,1)S(1)} collective-permute-done((bf16[640,2048]{1,0:T(8,128)(2,1)S(1)}, bf16[640,2048]{1,0:T(8,128)(2,1)S(1)}, u32[]{:S(2)}, u32[]{:S(2)}) %collective-permute-start.19) | collective-permute-done | bytes 2621472 | tf_op jit(solution)/shard_map/ppermute | solution.py:355
  1035.3 15.8 %collective-permute-done.18 = bf16[1408,1024]{1,0:T(8,128)(2,1)} collective-permute-done((bf16[1408,1024]{1,0:T(8,128)(2,1)S(1)}, bf16[1408,1024]{1,0:T(8,128)(2,1)}, u32[]{:S(2)}, u32[]{:S(2)}) %collective-permute-start.18) | collective-permute-done | bytes 2883616 | tf_op jit(solution)/shard_map/ppermute | solution.py:355
  1051.2 6.8 constant_dynamic-slice_fusion.4
  1064.4 13.5 %expert_rows.15 = bf16[640,2048]{1,0:T(8,128)(2,1)} custom-call(bf16[2560,2816]{1,0:T(8,128)(2,1)} %get-tuple-element.234.refs_0_, bf16[2816,2048]{1,0:T(8,128)(2,1)} %join_weights.5.wd_ref.refs_1_), custom_call_target="tpu_custom_call" | custom-call | tf_op jit(solution)/shard_map/expert_rows/pallas_call | solution.py:233
  1083.1 12.6 %all-to-all-done.7 = bf16[4,64,2048]{2,1,0:T(8,128)(2,1)S(1)} async-done(((bf16[4,64,2048]{2,1,0:T(8,128)(2,1)}), bf16[4,64,2048]{2,1,0:T(8,128)(2,1)S(1)}, u32[]{:S(2)}, u32[]{:S(2)}) %all-to-all-start.7) | async-done | bytes 1048608 | tf_op jit(solution)/shard_map/all_to_all | solution.py:442
  1096.7 10.4 add_convert_fusion
  1107.1 10.8 fusion.36
  1123.0 6.6 convert_add_fusion.3
  1139.9 13.8 %fusion.25 = (f32[2048]{0:T(1024)S(1)}, f32[512]{0:T(512)S(1)}, f32[512,2048]{1,0:T(8,128)}) fusion(bf16[1,512,2048]{2,1,0:T(8,128)(2,1)S(1)} %copy-done.3, f32[512]{0:T(512)S(1)} %copy-done.41, f32[2048]{0:T(1024)S(1)} %copy-done.30, bf16[512,2048]{1,0:T(8,128)(2,1)} %collective-permute-done.21, bf16[2048,4096]{1,0:T(8,128)(2,1)} %all-gather.5.cloned.1.call-done, ...), kind=kOutput, calls=%fused_computation.47 | convolution fusion | flops 6451885568 | bytes 24137728 | tf_op jit(solution)/shard_map/dot_general | solution.py:28
  1153.7 5.4 fusion.24
  1159.1 53.0 %all-to-all-done.8 = bf16[4,160,2048]{2,1,0:T(8,128)(2,1)} async-done(((bf16[4,160,2048]{2,1,0:T(8,128)(2,1)}), bf16[4,160,2048]{2,1,0:T(8,128)(2,1)}, u32[]{:S(2)}, u32[]{:S(2)}) %all-to-all-start.8) | async-done | bytes 2621472 | tf_op jit(solution)/shard_map/all_to_all | solution.py:442
  1240.6 5.8 convert_add_fusion.2
  (293 shorter events, 233.6 us)
Async XLA Ops:
  7.2 200.7 %all-gather.5.cloned.1.call-start = ((), (), s32[]{:S(2)}) async-start(), calls=%async_computation.12 | async-start | bytes 17825792 | tf_op jit(solution)/shard_map/all_gather | solution.py:389
  13.4 293.6 %all-gather.7.cloned.1.call-start = ((), (), s32[]{:S(2)}) async-start(), calls=%async_computation.13 | async-start | bytes 8650752 | tf_op jit(solution)/shard_map/all_gather | solution.py:452
  15.9 25.2 %collective-permute-start = (bf16[512,2048]{1,0:T(8,128)(2,1)}, bf16[512,2048]{1,0:T(8,128)(2,1)}, u32[]{:S(2)}, u32[]{:S(2)}) collective-permute-start(bf16[512,2048]{1,0:T(8,128)(2,1)} %fusion.19), channel_id=1, source_target_pairs={{0,16},{16,0},{1,17},{17,1},{2,18},{18,2},{3,19},{19,3},{4,20},{20... | collective-permute-start | bytes 6291464 | tf_op jit(solution)/shard_map/ppermute | solution.py:352
  20.3 270.9 %copy-start.34 = (s32[512]{0:T(512)}, s32[512]{0:T(512)S(1)}, u32[]{:S(2)}) copy-start(s32[512]{0:T(512)S(1)} %get-tuple-element.257) | copy-start | bytes 6148
  20.3 270.9 %copy-start.37 = (s32[512]{0:T(512)}, s32[512]{0:T(512)S(1)}, u32[]{:S(2)}) copy-start(s32[512]{0:T(512)S(1)} %get-tuple-element.258) | copy-start | bytes 6148
  41.1 166.9 %copy-start.55 = (s32[1,4]{1,0:T(1,128)S(1)}, s32[1,4]{1,0:T(1,128)}, u32[]{:S(2)}) copy-start(s32[1,4]{1,0:T(1,128)} %param.17) | copy-start | bytes 52
  207.9 150.8 %all-gather.9.cloned.1.call-start = ((), (), s32[]{:S(2)}) async-start(), calls=%async_computation.14 | async-start | bytes 8650752 | tf_op jit(solution)/shard_map/all_gather | solution.py:452
  220.8 63.9 %all-to-all-start = ((bf16[4,160,2048]{2,1,0:T(8,128)(2,1)}), bf16[4,160,2048]{2,1,0:T(8,128)(2,1)}, u32[]{:S(2)}, u32[]{:S(2)}) async-start(bf16[4,160,2048]{2,1,0:T(8,128)(2,1)} %bitcast.131), calls=%async_computation | async-start | bytes 5242880 | tf_op jit(solution)/shard_map/all_to_all | solution.py:442
  228.6 40.7 %collective-permute-start.1 = (bf16[1024,1024]{1,0:T(8,128)(2,1)}, bf16[1024,1024]{1,0:T(8,128)(2,1)}, u32[]{:S(2)}, u32[]{:S(2)}) collective-permute-start(bf16[1024,1024]{1,0:T(8,128)(2,1)} %constant_dynamic-slice_fusion.15), channel_id=1, source_target_pairs={{0,16},{16,0},{1,17},{17,1},{2,18},{18,2},{3,19},{19,3},{4,20},{20... | collective-permute-start | bytes 6291464 | tf_op jit(solution)/shard_map/ppermute | solution.py:352
  284.7 74.1 %all-to-all-start.1 = ((bf16[4,160,2048]{2,1,0:T(8,128)(2,1)}), bf16[4,160,2048]{2,1,0:T(8,128)(2,1)}, u32[]{:S(2)}, u32[]{:S(2)}) async-start(bf16[4,160,2048]{2,1,0:T(8,128)(2,1)} %bitcast.129), calls=%async_computation.1 | async-start | bytes 5242880 | tf_op jit(solution)/shard_map/all_to_all | solution.py:442
  289.3 145.4 %all-gather.11.cloned.1.call-start = ((), (), s32[]{:S(2)}) async-start(), calls=%async_computation.15 | async-start | bytes 8650752 | tf_op jit(solution)/shard_map/all_gather | solution.py:452
  289.5 4.6 collective-permute-start.2
  289.6 69.2 %collective-permute-start.3 = (bf16[640,2048]{1,0:T(8,128)(2,1)}, bf16[640,2048]{1,0:T(8,128)(2,1)}, u32[]{:S(2)}, u32[]{:S(2)}) collective-permute-start(bf16[640,2048]{1,0:T(8,128)(2,1)} %bitcast.15.g_ref), channel_id=1, source_target_pairs={{0,2},{1,3},{2,0},{3,1},{4,6},{5,7},{6,4},{7,5},{8,10},{9,11},{10,... | collective-permute-start | bytes 7864328 | tf_op jit(solution)/shard_map/ppermute | solution.py:355
  358.8 75.9 %all-to-all-start.2 = ((bf16[4,160,2048]{2,1,0:T(8,128)(2,1)}), bf16[4,160,2048]{2,1,0:T(8,128)(2,1)S(1)}, u32[]{:S(2)}, u32[]{:S(2)}) async-start(bf16[4,160,2048]{2,1,0:T(8,128)(2,1)} %bitcast.132), calls=%async_computation.2 | async-start | bytes 5242880 | tf_op jit(solution)/shard_map/all_to_all | solution.py:442
  367.3 5.6 collective-permute-start.4
  370.0 15.6 %collective-permute-start.5 = (bf16[704,2048]{1,0:T(8,128)(2,1)}, bf16[704,2048]{1,0:T(8,128)(2,1)}, u32[]{:S(2)}, u32[]{:S(2)}) collective-permute-start(bf16[704,2048]{1,0:T(8,128)(2,1)} %constant_dynamic-slice_fusion.13.refs_0_), channel_id=1, source_target_pairs={{0,16},{16,0},{1,17},{17,1},{2,18},{18,2},{3,19},{19,3},{4,20},{20... | collective-permute-start | bytes 8650760 | tf_op jit(solution)/shard_map/ppermute | solution.py:352
  370.0 64.7 %collective-permute-start.6 = (bf16[640,2048]{1,0:T(8,128)(2,1)}, bf16[640,2048]{1,0:T(8,128)(2,1)}, u32[]{:S(2)}, u32[]{:S(2)}) collective-permute-start(bf16[640,2048]{1,0:T(8,128)(2,1)} %bitcast.17.g_ref), channel_id=1, source_target_pairs={{0,2},{1,3},{2,0},{3,1},{4,6},{5,7},{6,4},{7,5},{8,10},{9,11},{10,... | collective-permute-start | bytes 7864328 | tf_op jit(solution)/shard_map/ppermute | solution.py:355
  434.7 64.5 %all-to-all-start.3 = ((bf16[4,160,2048]{2,1,0:T(8,128)(2,1)}), bf16[4,160,2048]{2,1,0:T(8,128)(2,1)}, u32[]{:S(2)}, u32[]{:S(2)}) async-start(bf16[4,160,2048]{2,1,0:T(8,128)(2,1)} %bitcast.130), calls=%async_computation.3 | async-start | bytes 5242880 | tf_op jit(solution)/shard_map/all_to_all | solution.py:442
  441.6 5.5 collective-permute-start.7
  441.6 80.2 %collective-permute-start.8 = (bf16[640,2048]{1,0:T(8,128)(2,1)S(1)}, bf16[640,2048]{1,0:T(8,128)(2,1)}, u32[]{:S(2)}, u32[]{:S(2)}) collective-permute-start(bf16[640,2048]{1,0:T(8,128)(2,1)S(1)} %bitcast.112), channel_id=1, source_target_pairs={{0,2},{1,3},{2,0},{3,1},{4,6},{5,7},{6,4},{7,5},{8,10},{9,11},{10,... | collective-permute-start | bytes 7864328 | tf_op jit(solution)/shard_map/ppermute | solution.py:355
  499.2 74.9 %collective-permute-start.9 = (bf16[640,2048]{1,0:T(8,128)(2,1)}, bf16[640,2048]{1,0:T(8,128)(2,1)}, u32[]{:S(2)}, u32[]{:S(2)}) collective-permute-start(bf16[640,2048]{1,0:T(8,128)(2,1)} %bitcast.24.x_ref), channel_id=1, source_target_pairs={{0,2},{1,3},{2,0},{3,1},{4,6},{5,7},{6,4},{7,5},{8,10},{9,11},{10,... | collective-permute-start | bytes 7864328 | tf_op jit(solution)/shard_map/ppermute | solution.py:355
  573.5 57.9 %collective-permute-start.10 = (bf16[640,2048]{1,0:T(8,128)(2,1)}, bf16[640,2048]{1,0:T(8,128)(2,1)}, u32[]{:S(2)}, u32[]{:S(2)}) collective-permute-start(bf16[640,2048]{1,0:T(8,128)(2,1)} %expert_rows.9), channel_id=1, source_target_pairs={{0,2},{1,3},{2,0},{3,1},{4,6},{5,7},{6,4},{7,5},{8,10},{9,11},{10,... | collective-permute-start | bytes 7864328 | tf_op jit(solution)/shard_map/ppermute | solution.py:355
  604.9 26.6 %copy-start.17 = (bf16[640,2048]{1,0:T(8,128)(2,1)S(1)}, bf16[640,2048]{1,0:T(8,128)(2,1)}, u32[]{:S(2)}) copy-start(bf16[640,2048]{1,0:T(8,128)(2,1)} %expert_rows.8) | copy-start | bytes 7864324
  635.7 61.8 %all-to-all-start.4 = ((bf16[4,160,2048]{2,1,0:T(8,128)(2,1)}), bf16[4,160,2048]{2,1,0:T(8,128)(2,1)S(1)}, u32[]{:S(2)}, u32[]{:S(2)}) async-start(bf16[4,160,2048]{2,1,0:T(8,128)(2,1)} %bitcast.117), calls=%async_computation.4 | async-start | bytes 5242880 | tf_op jit(solution)/shard_map/all_to_all | solution.py:442
  639.8 57.7 %collective-permute-start.11 = (bf16[640,2048]{1,0:T(8,128)(2,1)}, bf16[640,2048]{1,0:T(8,128)(2,1)}, u32[]{:S(2)}, u32[]{:S(2)}) collective-permute-start(bf16[640,2048]{1,0:T(8,128)(2,1)} %expert_rows.10), channel_id=1, source_target_pairs={{0,2},{1,3},{2,0},{3,1},{4,6},{5,7},{6,4},{7,5},{8,10},{9,11},{10,... | collective-permute-start | bytes 7864328 | tf_op jit(solution)/shard_map/ppermute | solution.py:355
  702.8 63.6 %all-to-all-start.5 = ((bf16[4,160,2048]{2,1,0:T(8,128)(2,1)}), bf16[4,160,2048]{2,1,0:T(8,128)(2,1)}, u32[]{:S(2)}, u32[]{:S(2)}) async-start(bf16[4,160,2048]{2,1,0:T(8,128)(2,1)} %bitcast.115), calls=%async_computation.5 | async-start | bytes 5242880 | tf_op jit(solution)/shard_map/all_to_all | solution.py:442
  707.3 410.6 %reduce-scatter.5.cloned.1.call-start = ((), (), s32[]{:S(2)}) async-start(), calls=%async_computation.17 | async-start | bytes 8650752 | tf_op jit(solution)/shard_map/reduce_scatter | solution.py:563
  751.8 38.5 %collective-permute-start.13 = (bf16[2816,1024]{1,0:T(8,128)(2,1)}, bf16[2816,1024]{1,0:T(8,128)(2,1)}, u32[]{:S(2)}, u32[]{:S(2)}) collective-permute-start(bf16[2816,1024]{1,0:T(8,128)(2,1)} %constant_dynamic-slice_fusion.11), channel_id=1, source_target_pairs={{0,16},{16,0},{1,17},{17,1},{2,18},{18,2},{3,19},{19,3},{4,20},{20... | collective-permute-start | bytes 17301512 | tf_op jit(solution)/shard_map/ppermute | solution.py:352
  775.6 24.5 %copy-start.18 = (bf16[512,2048]{1,0:T(8,128)(2,1)}, bf16[512,2048]{1,0:T(8,128)(2,1)S(1)}, u32[]{:S(2)}) copy-start(bf16[512,2048]{1,0:T(8,128)(2,1)S(1)} %fusion.106) | copy-start | bytes 6291460
  775.6 24.5 %collective-permute-start.12 = (bf16[512,2048]{1,0:T(8,128)(2,1)S(1)}, bf16[512,2048]{1,0:T(8,128)(2,1)}, u32[]{:S(2)}, u32[]{:S(2)}) collective-permute-start(bf16[512,2048]{1,0:T(8,128)(2,1)S(1)} %fusion.106), channel_id=1, source_target_pairs={{0,16},{16,0},{1,17},{17,1},{2,18},{18,2},{3,19},{19,3},{4,20},{20... | collective-permute-start | bytes 6291464 | tf_op jit(solution)/shard_map/ppermute | solution.py:352
  789.8 76.2 %collective-permute-start.14 = (bf16[640,2048]{1,0:T(8,128)(2,1)}, bf16[640,2048]{1,0:T(8,128)(2,1)}, u32[]{:S(2)}, u32[]{:S(2)}) collective-permute-start(bf16[640,2048]{1,0:T(8,128)(2,1)} %expert_rows.12), channel_id=1, source_target_pairs={{0,2},{1,3},{2,0},{3,1},{4,6},{5,7},{6,4},{7,5},{8,10},{9,11},{10,... | collective-permute-start | bytes 7864328 | tf_op jit(solution)/shard_map/ppermute | solution.py:355
  817.7 84.2 %collective-permute-start.15 = (bf16[512,2048]{1,0:T(8,128)(2,1)}, bf16[512,2048]{1,0:T(8,128)(2,1)}, u32[]{:S(2)}, u32[]{:S(2)}) collective-permute-start(bf16[512,2048]{1,0:T(8,128)(2,1)} %bitcast.30), channel_id=1, source_target_pairs={{0,2},{1,3},{2,0},{3,1},{4,6},{5,7},{6,4},{7,5},{8,10},{9,11},{10,... | collective-permute-start | bytes 6291464 | tf_op jit(solution)/shard_map/ppermute | solution.py:355
  819.2 392.9 %reduce-scatter.3.cloned.1.call-start = ((), (), s32[]{:S(2)}) async-start(), calls=%async_computation.16 | async-start | bytes 13369344 | tf_op jit(solution)/shard_map/reduce_scatter | solution.py:626
  908.0 36.4 %collective-permute-start.16 = (bf16[2816,1024]{1,0:T(8,128)(2,1)}, bf16[2816,1024]{1,0:T(8,128)(2,1)}, u32[]{:S(2)}, u32[]{:S(2)}) collective-permute-start(bf16[2816,1024]{1,0:T(8,128)(2,1)} %constant_dynamic-slice_fusion.6), channel_id=1, source_target_pairs={{0,16},{16,0},{1,17},{17,1},{2,18},{18,2},{3,19},{19,3},{4,20},{20... | collective-permute-start | bytes 17301512 | tf_op jit(solution)/shard_map/ppermute | solution.py:352
  925.3 14.9 %copy-start.16 = (bf16[640,2048]{1,0:T(8,128)(2,1)S(1)}, bf16[640,2048]{1,0:T(8,128)(2,1)}, u32[]{:S(2)}) copy-start(bf16[640,2048]{1,0:T(8,128)(2,1)} %expert_rows.13) | copy-start | bytes 7864324
  939.3 62.6 %collective-permute-start.17 = (bf16[256,2048]{1,0:T(8,128)(2,1)}, bf16[256,2048]{1,0:T(8,128)(2,1)}, u32[]{:S(2)}, u32[]{:S(2)}) collective-permute-start(bf16[256,2048]{1,0:T(8,128)(2,1)} %bitcast.134), channel_id=1, source_target_pairs={{0,1},{1,0},{2,3},{3,2},{4,5},{5,4},{6,7},{7,6},{8,9},{9,8},{10,11... | collective-permute-start | bytes 3145736 | tf_op jit(solution)/shard_map/ppermute | solution.py:355
  954.4 96.8 %all-to-all-start.6 = ((bf16[4,160,2048]{2,1,0:T(8,128)(2,1)}), bf16[4,160,2048]{2,1,0:T(8,128)(2,1)S(1)}, u32[]{:S(2)}, u32[]{:S(2)}) async-start(bf16[4,160,2048]{2,1,0:T(8,128)(2,1)} %bitcast.116), calls=%async_computation.6 | async-start | bytes 5242880 | tf_op jit(solution)/shard_map/all_to_all | solution.py:442
  961.1 90.1 %collective-permute-start.18 = (bf16[1408,1024]{1,0:T(8,128)(2,1)S(1)}, bf16[1408,1024]{1,0:T(8,128)(2,1)}, u32[]{:S(2)}, u32[]{:S(2)}) collective-permute-start(bf16[1408,1024]{1,0:T(8,128)(2,1)S(1)} %constant_dynamic-slice_fusion.5), channel_id=1, source_target_pairs={{0,1},{1,0},{2,3},{3,2},{4,5},{5,4},{6,7},{7,6},{8,9},{9,8},{10,11... | collective-permute-start | bytes 8650760 | tf_op jit(solution)/shard_map/ppermute | solution.py:355
  962.3 71.5 %collective-permute-start.19 = (bf16[640,2048]{1,0:T(8,128)(2,1)S(1)}, bf16[640,2048]{1,0:T(8,128)(2,1)S(1)}, u32[]{:S(2)}, u32[]{:S(2)}) collective-permute-start(bf16[640,2048]{1,0:T(8,128)(2,1)S(1)} %copy-done.22), channel_id=1, source_target_pairs={{0,2},{1,3},{2,0},{3,1},{4,6},{5,7},{6,4},{7,5},{8,10},{9,11},{10,... | collective-permute-start | bytes 7864328 | tf_op jit(solution)/shard_map/ppermute | solution.py:355
  1058.0 38.7 %collective-permute-start.20 = (bf16[2816,1024]{1,0:T(8,128)(2,1)}, bf16[2816,1024]{1,0:T(8,128)(2,1)}, u32[]{:S(2)}, u32[]{:S(2)}) collective-permute-start(bf16[2816,1024]{1,0:T(8,128)(2,1)} %constant_dynamic-slice_fusion.4), channel_id=1, source_target_pairs={{0,16},{16,0},{1,17},{17,1},{2,18},{18,2},{3,19},{19,3},{4,20},{20... | collective-permute-start | bytes 17301512 | tf_op jit(solution)/shard_map/ppermute | solution.py:352
  1060.6 35.1 %all-to-all-start.7 = ((bf16[4,64,2048]{2,1,0:T(8,128)(2,1)}), bf16[4,64,2048]{2,1,0:T(8,128)(2,1)S(1)}, u32[]{:S(2)}, u32[]{:S(2)}) async-start(bf16[4,64,2048]{2,1,0:T(8,128)(2,1)} %bitcast.35), calls=%async_computation.7 | async-start | bytes 2097152 | tf_op jit(solution)/shard_map/all_to_all | solution.py:442
  1117.9 22.0 %collective-permute-start.21 = (bf16[512,2048]{1,0:T(8,128)(2,1)}, bf16[512,2048]{1,0:T(8,128)(2,1)}, u32[]{:S(2)}, u32[]{:S(2)}) collective-permute-start(bf16[512,2048]{1,0:T(8,128)(2,1)} %fusion.36), channel_id=1, source_target_pairs={{0,16},{16,0},{1,17},{17,1},{2,18},{18,2},{3,19},{19,3},{4,20},{20... | collective-permute-start | bytes 6291464 | tf_op jit(solution)/shard_map/ppermute | solution.py:352
  1129.6 82.4 %all-to-all-start.8 = ((bf16[4,160,2048]{2,1,0:T(8,128)(2,1)}), bf16[4,160,2048]{2,1,0:T(8,128)(2,1)}, u32[]{:S(2)}, u32[]{:S(2)}) async-start(bf16[4,160,2048]{2,1,0:T(8,128)(2,1)} %bitcast.36), calls=%async_computation.8 | async-start | bytes 5242880 | tf_op jit(solution)/shard_map/all_to_all | solution.py:442
  1139.7 13.9 %copy-start.44 = (f32[512]{0:T(512)S(1)}, f32[512]{0:T(512)}, u32[]{:S(2)}) copy-start(f32[512]{0:T(512)} %copy-done.42) | copy-start | bytes 6148
  1139.8 100.3 %collective-permute-start.23 = (bf16[1408,1024]{1,0:T(8,128)(2,1)}, bf16[1408,1024]{1,0:T(8,128)(2,1)}, u32[]{:S(2)}, u32[]{:S(2)}) collective-permute-start(bf16[1408,1024]{1,0:T(8,128)(2,1)} %get-tuple-element.261), channel_id=1, source_target_pairs={{0,1},{1,0},{2,3},{3,2},{4,5},{5,4},{6,7},{7,6},{8,9},{9,8},{10,11... | collective-permute-start | bytes 8650760 | tf_op jit(solution)/shard_map/ppermute | solution.py:355
  1212.9 24.0 %all-to-all-start.9 = ((f32[16,1,256]{2,1,0:T(1,128)}), f32[16,1,256]{2,1,0:T(1,128)S(1)}, u32[]{:S(2)}, u32[]{:S(2)}) async-start(f32[16,1,256]{2,1,0:T(1,128)} %reshape.269), calls=%async_computation.10 | async-start | bytes 32768 | tf_op jit(solution)/shard_map/all_to_all | solution.py:669
  1238.2 1.8 collective-permute-start.22
  1239.5 6.9 collective-permute-start.24
  (51 other events, 286.4 us)
Sparse Core Ops, SparseCore 0:
  13.6 194.3 all-gather.4
  210.0 72.6 all-gather.6
  284.3 74.4 all-gather.8
  360.2 74.4 all-gather.10
  819.3 69.9 reduce-scatter.4
  908.1 274.2 reduce-scatter.2

commit v11 on v10

--- a/solution.py
+++ b/solution.py
@@ -646,7 +646,9 @@
     out_grad = expert_sum(add_parts(blocks_o[0], [came_o]))
     outs_second = add_parts(out_rows_of(1, 0, hidden_t), away_second)
     up_total = core_sum(up_part)
-    outs_second, up_total, grad_qkv, out_grad = after(outs_second, up_total, grad_qkv, out_grad)
+    gate_grad = gate_own.astype(f32) + gate_came.astype(f32)
+    got = after(outs_second, up_total, grad_qkv, out_grad, gate_grad, down_grad)
+    outs_second, up_total, grad_qkv, out_grad, gate_grad, down_grad = got
     outs_second = swap_experts(outs_second)
     up_own, up_came = side_swap_sum(up_total)
 
@@ -663,7 +665,6 @@
     tokens_grad, norm1_part, outs_second, qkv_sum = after(
         tokens_grad, norm1_part, outs_second, qkv_sum
     )
-    gate_grad = gate_own.astype(f32) + gate_came.astype(f32)
 
     gains = jnp.stack([norm1_part, norm2_part]).reshape(2, ctx_count, fsdp_count, per)
     gains = lax.all_to_all(gains.transpose(2, 1, 0, 3), "fsdp", 0, 0, tiled=True)

time: 1260 us -> 1250 us (level)
  no operation moved by 1% of the time
where the time goes in v11:
time: 1250 us
  waiting for transfers between devices  380 us (30%)
  Pallas kernels  348 us (28%)
  matrix products  239 us (19%)
  other arithmetic  110 us (9%)
  local copies, waits for them, and re-layouts  94.9 us (8%)
  starting transfers between devices  58.2 us (5%)
  between operations  15.4 us (1%)
    dot_general x19, matrix products, dot(): lax.dot_general(a, b, (((ca,), (cb,)), ((), ())), preferred_element_type=...  239 us
    all_gather x1, waiting for transfers between devices, shards(): gathered = lax.all_gather(packed, 'fsdp', axis=0, tiled=True)  153 us
    pallas_call x8, Pallas kernels, expert_rows(): pl.pallas_call(functools.partial(rows_kernel, len(left)), grid=(D // tile...  139 us
    pallas_call x4, Pallas kernels, expert_hidden(): pl.pallas_call(functools.partial(expert_kernel, len(kept)), grid=(units /...  123 us
    all_gather x3, waiting for transfers between devices, shards(): lax.all_gather(part, 'fsdp', axis=0, tiled=True, axis_index_groups=sides)  88.3 us
    all_to_all x9, waiting for transfers between devices, swap_experts(): lax.all_to_all(blocks, 'fsdp', 0, 0, axis_index_groups=lines, tiled=True)  77.8 us
    ppermute x12, waiting for transfers between devices, fsdp_shift(): return lax.ppermute(a, 'fsdp', [(i, move(i)) for i in range(fsdp_count)])  53.2 us
    all_to_all x9, starting transfers between devices, swap_experts(): lax.all_to_all(blocks, 'fsdp', 0, 0, axis_index_groups=lines, tiled=True)  40.9 us
  transfers between devices with their start and end apart: 41, of which 15 were waited for; matrix products, arithmetic and copies ran while one was open for 33% of the time, Pallas kernels for 28%

profile of v11, /device:TPU:0, one launch (start us, length us, event | category | flops | bytes accessed | tf_op | source)
XLA Modules:
  0.0 1245.4 jit_solution(8941758241581268742)
XLA Ops:
  24.1 6.9 constant_dynamic-slice_fusion.16
  41.1 13.4 %fusion.29 = bf16[1024,2048]{1,0:T(8,128)(2,1)} fusion(s32[2048]{0:T(1024)S(1)} %fusion.86, bf16[512,2048]{1,0:T(8,128)(2,1)} %collective-permute-done, bf16[512,2048]{1,0:T(8,128)(2,1)} %fusion.19), kind=kOutput, calls=%fused_computation.62 | convolution fusion | flops 8604614656 | bytes 8396800 | tf_op jit(solution)/shard_map/dot_general | solution.py:28
  54.5 153.5 %all-gather.5.cloned.1.call-done = bf16[2048,4096]{1,0:T(8,128)(2,1)} async-done(((bf16[128,4096]{1,0:T(8,128)(2,1)}), bf16[2048,4096]{1,0:T(8,128)(2,1)}) %all-gather.5.cloned.1.call-update) | async-done | bytes 16777232 | tf_op jit(solution)/shard_map/all_gather | solution.py:389
  215.4 5.4 slice.77
  228.6 19.0 %fusion.12.pre_q.pre_k.pre_v = f32[1024,3072]{1,0:T(8,128)} fusion(bf16[2048,4096]{1,0:T(8,128)(2,1)} %all-gather.5.cloned.1.call-done, bf16[512,2048]{1,0:T(8,128)(2,1)} %collective-permute-done, bf16[512,2048]{1,0:T(8,128)(2,1)} %fusion.19), kind=kOutput, calls=%fused_computation.20 | convolution fusion | flops 12893290496 | bytes 29360128 | tf_op jit(solution)/shard_map/dot_general | solution.py:28
  247.6 21.7 %attention_forward.1 = (bf16[1024,1024]{1,0:T(8,128)(2,1)}, bf16[1024,1024]{1,0:T(8,128)(2,1)}, bf16[1024,1024]{1,0:T(8,128)(2,1)}, bf16[1024,1024]{1,0:T(8,128)(2,1)}, f32[1024,1024]{1,0:T(8,128)}) custom-call(s32[4]{0:T(128)} %fusion.95.perm, f32[1024,3072]{1,0:T(8,128)} %fusion.12.pre_q.pre_k.pre_v, f32[1024,3072]{1,0:T(8,128)} %fusion.12.pre_q.pre_k.pre_v, ...), custom_call_target="tpu_custom_call" | custom-call | tf_op jit(solution)/shard_map/attention_forward/pallas_call | solution.py:155
  278.5 6.1 all-to-all-done
  294.1 6.6 multiply_reduce_fusion.2
  307.0 51.7 %all-gather.9.cloned.1.call-done = bf16[1408,2048]{1,0:T(8,128)(2,1)} async-done(((bf16[704,2048]{1,0:T(8,128)(2,1)}), bf16[1408,2048]{1,0:T(8,128)(2,1)}) %all-gather.9.cloned.1.call-update) | async-done | bytes 5767184 | tf_op jit(solution)/shard_map/all_gather | solution.py:452
  372.9 12.7 %join_weights.3.wg_ref.refs_2_ = bf16[2816,2048]{1,0:T(8,128)(2,1)} custom-call(s32[3]{0:T(128)} %pad_add_fusion.where, bf16[1408,2048]{1,0:T(8,128)(2,1)} %own_ref.3, bf16[704,2048]{1,0:T(8,128)(2,1)} %constant_dynamic-slice_fusion.14.refs_0_, bf16[704,2048]{1,0:T(8,128)(2,1)} %collective-permute-done.4.refs_1_), custom_call_target="tpu_custom_call" | custom-call | tf_op jit(solution)/shard_map/join_weights/pallas_call | solution.py:272
  385.6 12.5 %join_weights.4.wu_ref.refs_3_ = bf16[2816,2048]{1,0:T(8,128)(2,1)} custom-call(s32[3]{0:T(128)} %pad_add_fusion.where, bf16[1408,2048]{1,0:T(8,128)(2,1)} %own_ref.4, bf16[704,2048]{1,0:T(8,128)(2,1)} %constant_dynamic-slice_fusion.13.refs_0_, bf16[704,2048]{1,0:T(8,128)(2,1)} %collective-permute-done.5.refs_1_), custom_call_target="tpu_custom_call" | custom-call | tf_op jit(solution)/shard_map/join_weights/pallas_call | solution.py:272
  398.1 36.6 %all-gather.11.cloned.1.call-done = bf16[1408,2048]{1,0:T(8,128)(2,1)} async-done(((bf16[704,2048]{1,0:T(8,128)(2,1)}), bf16[1408,2048]{1,0:T(8,128)(2,1)}) %all-gather.11.cloned.1.call-update) | async-done | bytes 5767184 | tf_op jit(solution)/shard_map/all_gather | solution.py:452
  447.0 12.4 join_weights.5.wd_ref.refs_1_
  459.4 30.6 %expert_hidden.4 = (bf16[2560,2816]{1,0:T(8,128)(2,1)}, bf16[2560,2816]{1,0:T(8,128)(2,1)}, bf16[2560,2816]{1,0:T(8,128)(2,1)}) custom-call(bf16[640,2048]{1,0:T(8,128)(2,1)} %bitcast.113, bf16[640,2048]{1,0:T(8,128)(2,1)} %bitcast.15.g_ref, bf16[2816,2048]{1,0:T(8,128)(2,1)} %join_weights.3.wg_ref.refs_2_, bf16[2816,2048]{1,0:T(8,128)(2,1)} %join_weights.4.wu_ref.refs_3_, ...), custom_call_target="tpu_custom_call" | custom-call | tf_op jit(solution)/shard_map/expert_hidden/pallas_call | solution.py:213
  490.0 9.2 all-to-all-done.3
  500.7 21.1 %expert_rows.8 = bf16[640,2048]{1,0:T(8,128)(2,1)} custom-call(bf16[2560,2816]{1,0:T(8,128)(2,1)} %get-tuple-element.170.refs_0_.refs_1_, bf16[2560,2816]{1,0:T(8,128)(2,1)} %get-tuple-element.171.refs_1_.refs_2_, bf16[2816,2048]{1,0:T(8,128)(2,1)} %join_weights.3.wg_ref.refs_2_, bf16[2816,2048]{1,0:T(8,128)(2,1)} %join_weights.4.wu_ref.refs_3_), custom_call_target="tpu_custom_call" | custom-call | tf_op jit(solution)/shard_map/expert_rows/pallas_call | solution.py:233
  521.8 30.6 %expert_hidden.5 = (bf16[2560,2816]{1,0:T(8,128)(2,1)}, bf16[2560,2816]{1,0:T(8,128)(2,1)}, bf16[2560,2816]{1,0:T(8,128)(2,1)}) custom-call(bf16[640,2048]{1,0:T(8,128)(2,1)} %collective-permute-done.8.x_ref, bf16[640,2048]{1,0:T(8,128)(2,1)} %collective-permute-done.3.g_ref, ...), custom_call_target="tpu_custom_call", output_to_operand_aliasing={{0}: (5, {}), {1}: (6, {}), {2}: (7, {})} | custom-call | tf_op jit(solution)/shard_map/expert_hidden/pallas_call | solution.py:213
  552.4 21.1 %expert_rows.9 = bf16[640,2048]{1,0:T(8,128)(2,1)} custom-call(bf16[2560,2816]{1,0:T(8,128)(2,1)} %get-tuple-element.181.refs_0_.refs_1_, bf16[2560,2816]{1,0:T(8,128)(2,1)} %get-tuple-element.182.refs_1_.refs_2_, bf16[2816,2048]{1,0:T(8,128)(2,1)} %join_weights.3.wg_ref.refs_2_, bf16[2816,2048]{1,0:T(8,128)(2,1)} %join_weights.4.wu_ref.refs_3_), custom_call_target="tpu_custom_call" | custom-call | tf_op jit(solution)/shard_map/expert_rows/pallas_call | solution.py:233
  574.1 30.8 %expert_hidden.6 = (bf16[2560,2816]{1,0:T(8,128)(2,1)}, bf16[2560,2816]{1,0:T(8,128)(2,1)}, bf16[2560,2816]{1,0:T(8,128)(2,1)}) custom-call(bf16[640,2048]{1,0:T(8,128)(2,1)} %collective-permute-done.9.x_ref, bf16[640,2048]{1,0:T(8,128)(2,1)} %collective-permute-done.6.g_ref, ...), custom_call_target="tpu_custom_call", output_to_operand_aliasing={{0}: (5, {}), {1}: (6, {}), {2}: (7, {})} | custom-call | tf_op jit(solution)/shard_map/expert_hidden/pallas_call | solution.py:213
  604.9 21.2 %expert_rows.10 = bf16[640,2048]{1,0:T(8,128)(2,1)} custom-call(bf16[2560,2816]{1,0:T(8,128)(2,1)} %get-tuple-element.196.refs_0_.refs_1_, bf16[2560,2816]{1,0:T(8,128)(2,1)} %get-tuple-element.197.refs_1_.refs_2_, bf16[2816,2048]{1,0:T(8,128)(2,1)} %join_weights.3.wg_ref.refs_2_, bf16[2816,2048]{1,0:T(8,128)(2,1)} %join_weights.4.wu_ref.refs_3_), custom_call_target="tpu_custom_call" | custom-call | tf_op jit(solution)/shard_map/expert_rows/pallas_call | solution.py:233
  626.1 5.4 collective-permute-done.10
  640.4 30.6 %expert_hidden.7 = (bf16[2560,2816]{1,0:T(8,128)(2,1)}, bf16[2560,2816]{1,0:T(8,128)(2,1)}, bf16[2560,2816]{1,0:T(8,128)(2,1)}) custom-call(bf16[640,2048]{1,0:T(8,128)(2,1)} %bitcast.24.x_ref, bf16[640,2048]{1,0:T(8,128)(2,1)} %bitcast.17.g_ref, ...), custom_call_target="tpu_custom_call", output_to_operand_aliasing={{0}: (5, {}), {1}: (6, {}), {2}: (7, {})} | custom-call | tf_op jit(solution)/shard_map/expert_hidden/pallas_call | solution.py:213
  671.0 21.1 %expert_rows.11 = bf16[640,2048]{1,0:T(8,128)(2,1)} custom-call(bf16[2560,2816]{1,0:T(8,128)(2,1)} %get-tuple-element.219.refs_0_, bf16[2560,2816]{1,0:T(8,128)(2,1)} %get-tuple-element.229.refs_1_, bf16[2816,2048]{1,0:T(8,128)(2,1)} %join_weights.3.wg_ref.refs_2_, bf16[2816,2048]{1,0:T(8,128)(2,1)} %join_weights.4.wu_ref.refs_3_), custom_call_target="tpu_custom_call" | custom-call | tf_op jit(solution)/shard_map/expert_rows/pallas_call | solution.py:233
  692.1 5.4 all-to-all-done.4
  707.4 38.6 %convolution_convert_fusion.2 = bf16[2816,2048]{1,0:T(8,128)(2,1)} fusion(bf16[2560,2816]{1,0:T(8,128)(2,1)} %get-tuple-element.236.refs_0_, bf16[640,2048]{1,0:T(8,128)(2,1)} %collective-permute-done.6.g_ref, bf16[640,2048]{1,0:T(8,128)(2,1)} %bitcast.17.g_ref, bf16[640,2048]{1,0:T(8,128)(2,1)} %collective-permute-done.3.g_ref, ...), kind=kOutput, calls=%fused_computation.7 | convolution fusion | flops 29575610368 | bytes 36438016 | tf_op jit(solution)/shard_map/dot_general | solution.py:28
  746.0 5.8 constant_dynamic-slice_fusion.11
  751.8 13.6 %expert_rows.12 = bf16[640,2048]{1,0:T(8,128)(2,1)} custom-call(bf16[2560,2816]{1,0:T(8,128)(2,1)} %get-tuple-element.236.refs_0_, bf16[2816,2048]{1,0:T(8,128)(2,1)} %join_weights.5.wd_ref.refs_1_), custom_call_target="tpu_custom_call" | custom-call | tf_op jit(solution)/shard_map/expert_rows/pallas_call | solution.py:233
  790.3 9.8 add_convert_fusion.2
  800.2 7.0 convolution_convert_fusion.4
  812.0 5.7 convolution_convert_fusion.10.do_ref
  819.3 27.4 %attention_backward.1 = bf16[1024,3072]{1,0:T(8,128)(2,1)} custom-call(s32[4]{0:T(128)} %fusion.95.perm, bf16[1024,1024]{1,0:T(8,128)(2,1)} %get-tuple-element.138.q_ref, bf16[1024,1024]{1,0:T(8,128)(2,1)} %get-tuple-element.139.k_ref, bf16[1024,1024]{1,0:T(8,128)(2,1)} %get-tuple-element.140.v_ref, f32[1024,1024]{1,0:T(8,128)} %get-tuple-element.141.log_ref, ...), custom_call_target="tpu_custom_call" | custom-call | tf_op jit(solution)/shard_map/attention_backward/pallas_call | solution.py:178
  846.6 19.4 %convolution_convert_fusion.3 = bf16[2048,3072]{1,0:T(8,128)(2,1)} fusion(bf16[1024,2048]{1,0:T(8,128)(2,1)} %fusion.29, bf16[1024,3072]{1,0:T(8,128)(2,1)} %attention_backward.1), kind=kOutput, calls=%fused_computation.8 | convolution fusion | flops 12891193344 | bytes 23068672 | tf_op jit(solution)/shard_map/dot_general | solution.py:28
  866.0 35.9 %convolution_convert_fusion.1 = bf16[2816,2048]{1,0:T(8,128)(2,1)S(1)} fusion(bf16[2560,2816]{1,0:T(8,128)(2,1)} %get-tuple-element.219.refs_0_, bf16[2560,2048]{1,0:T(8,128)(2,1)} %constant_dynamic-update-slice_fusion), kind=kOutput, calls=%fused_computation.6 | convolution fusion | flops 29533667328 | bytes 36438016 | tf_op jit(solution)/shard_map/dot_general | solution.py:28
  911.9 13.4 %expert_rows.13 = bf16[640,2048]{1,0:T(8,128)(2,1)} custom-call(bf16[2560,2816]{1,0:T(8,128)(2,1)} %get-tuple-element.236.refs_0_, bf16[2816,2048]{1,0:T(8,128)(2,1)} %join_weights.5.wd_ref.refs_1_), custom_call_target="tpu_custom_call" | custom-call | tf_op jit(solution)/shard_map/expert_rows/pallas_call | solution.py:233
  925.3 14.0 %expert_rows.14 = bf16[640,2048]{1,0:T(8,128)(2,1)} custom-call(bf16[2560,2816]{1,0:T(8,128)(2,1)} %get-tuple-element.236.refs_0_, bf16[2816,2048]{1,0:T(8,128)(2,1)} %join_weights.5.wd_ref.refs_1_), custom_call_target="tpu_custom_call" | custom-call | tf_op jit(solution)/shard_map/expert_rows/pallas_call | solution.py:233
  944.5 10.0 add_convert_fusion.1
  963.4 38.6 %convolution_convert_fusion = bf16[2816,2048]{1,0:T(8,128)(2,1)} fusion(bf16[2560,2816]{1,0:T(8,128)(2,1)} %get-tuple-element.229.refs_1_, bf16[2560,2048]{1,0:T(8,128)(2,1)} %constant_dynamic-update-slice_fusion), kind=kOutput, calls=%fused_computation.5 | convolution fusion | flops 29533667328 | bytes 36438016 | tf_op jit(solution)/shard_map/dot_general | solution.py:28
  1002.0 32.3 %collective-permute-done.19 = bf16[640,2048]{1,0:T(8,128)(2,1)S(1)} collective-permute-done((bf16[640,2048]{1,0:T(8,128)(2,1)S(1)}, bf16[640,2048]{1,0:T(8,128)(2,1)S(1)}, u32[]{:S(2)}, u32[]{:S(2)}) %collective-permute-start.19) | collective-permute-done | bytes 2621472 | tf_op jit(solution)/shard_map/ppermute | solution.py:355
  1035.8 15.5 %collective-permute-done.18 = bf16[1408,1024]{1,0:T(8,128)(2,1)} collective-permute-done((bf16[1408,1024]{1,0:T(8,128)(2,1)S(1)}, bf16[1408,1024]{1,0:T(8,128)(2,1)}, u32[]{:S(2)}, u32[]{:S(2)}) %collective-permute-start.18) | collective-permute-done | bytes 2883616 | tf_op jit(solution)/shard_map/ppermute | solution.py:355
  1051.3 6.7 constant_dynamic-slice_fusion.4
  1069.8 13.4 %expert_rows.15 = bf16[640,2048]{1,0:T(8,128)(2,1)} custom-call(bf16[2560,2816]{1,0:T(8,128)(2,1)} %get-tuple-element.236.refs_0_, bf16[2816,2048]{1,0:T(8,128)(2,1)} %join_weights.5.wd_ref.refs_1_), custom_call_target="tpu_custom_call" | custom-call | tf_op jit(solution)/shard_map/expert_rows/pallas_call | solution.py:233
  1088.5 6.5 convert_add_fusion.3
  1099.1 10.4 add_convert_fusion
  1109.6 10.8 fusion.36
  1130.8 13.3 %fusion.25 = (f32[2048]{0:T(1024)S(1)}, f32[512]{0:T(512)S(1)}, f32[512,2048]{1,0:T(8,128)}) fusion(bf16[1,512,2048]{2,1,0:T(8,128)(2,1)S(1)} %copy-done.3, f32[512]{0:T(512)S(1)} %copy-done.41, f32[2048]{0:T(1024)S(1)} %copy-done.30, bf16[512,2048]{1,0:T(8,128)(2,1)} %collective-permute-done.21, bf16[2048,4096]{1,0:T(8,128)(2,1)} %all-gather.5.cloned.1.call-done, ...), kind=kOutput, calls=%fused_computation.47 | convolution fusion | flops 6451885568 | bytes 24137728 | tf_op jit(solution)/shard_map/dot_general | solution.py:28
  1144.2 5.4 fusion.24
  1149.6 53.1 %all-to-all-done.8 = bf16[4,160,2048]{2,1,0:T(8,128)(2,1)} async-done(((bf16[4,160,2048]{2,1,0:T(8,128)(2,1)}), bf16[4,160,2048]{2,1,0:T(8,128)(2,1)}, u32[]{:S(2)}, u32[]{:S(2)}) %all-to-all-start.8) | async-done | bytes 2621472 | tf_op jit(solution)/shard_map/all_to_all | solution.py:442
  1231.2 5.8 convert_add_fusion.2
  (293 shorter events, 231.9 us)
Async XLA Ops:
  7.2 200.7 %all-gather.5.cloned.1.call-start = ((), (), s32[]{:S(2)}) async-start(), calls=%async_computation.12 | async-start | bytes 17825792 | tf_op jit(solution)/shard_map/all_gather | solution.py:389
  13.4 293.6 %all-gather.7.cloned.1.call-start = ((), (), s32[]{:S(2)}) async-start(), calls=%async_computation.13 | async-start | bytes 8650752 | tf_op jit(solution)/shard_map/all_gather | solution.py:452
  15.9 25.2 %collective-permute-start = (bf16[512,2048]{1,0:T(8,128)(2,1)}, bf16[512,2048]{1,0:T(8,128)(2,1)}, u32[]{:S(2)}, u32[]{:S(2)}) collective-permute-start(bf16[512,2048]{1,0:T(8,128)(2,1)} %fusion.19), channel_id=1, source_target_pairs={{0,16},{16,0},{1,17},{17,1},{2,18},{18,2},{3,19},{19,3},{4,20},{20... | collective-permute-start | bytes 6291464 | tf_op jit(solution)/shard_map/ppermute | solution.py:352
  20.3 270.9 %copy-start.34 = (s32[512]{0:T(512)}, s32[512]{0:T(512)S(1)}, u32[]{:S(2)}) copy-start(s32[512]{0:T(512)S(1)} %get-tuple-element.261) | copy-start | bytes 6148
  20.3 270.9 %copy-start.37 = (s32[512]{0:T(512)}, s32[512]{0:T(512)S(1)}, u32[]{:S(2)}) copy-start(s32[512]{0:T(512)S(1)} %get-tuple-element.262) | copy-start | bytes 6148
  41.1 166.9 %copy-start.55 = (s32[1,4]{1,0:T(1,128)S(1)}, s32[1,4]{1,0:T(1,128)}, u32[]{:S(2)}) copy-start(s32[1,4]{1,0:T(1,128)} %param.17) | copy-start | bytes 52
  207.9 150.8 %all-gather.9.cloned.1.call-start = ((), (), s32[]{:S(2)}) async-start(), calls=%async_computation.14 | async-start | bytes 8650752 | tf_op jit(solution)/shard_map/all_gather | solution.py:452
  220.8 63.9 %all-to-all-start = ((bf16[4,160,2048]{2,1,0:T(8,128)(2,1)}), bf16[4,160,2048]{2,1,0:T(8,128)(2,1)}, u32[]{:S(2)}, u32[]{:S(2)}) async-start(bf16[4,160,2048]{2,1,0:T(8,128)(2,1)} %bitcast.131), calls=%async_computation | async-start | bytes 5242880 | tf_op jit(solution)/shard_map/all_to_all | solution.py:442
  228.6 40.7 %collective-permute-start.1 = (bf16[1024,1024]{1,0:T(8,128)(2,1)}, bf16[1024,1024]{1,0:T(8,128)(2,1)}, u32[]{:S(2)}, u32[]{:S(2)}) collective-permute-start(bf16[1024,1024]{1,0:T(8,128)(2,1)} %constant_dynamic-slice_fusion.15), channel_id=1, source_target_pairs={{0,16},{16,0},{1,17},{17,1},{2,18},{18,2},{3,19},{19,3},{4,20},{20... | collective-permute-start | bytes 6291464 | tf_op jit(solution)/shard_map/ppermute | solution.py:352
  284.7 74.1 %all-to-all-start.1 = ((bf16[4,160,2048]{2,1,0:T(8,128)(2,1)}), bf16[4,160,2048]{2,1,0:T(8,128)(2,1)}, u32[]{:S(2)}, u32[]{:S(2)}) async-start(bf16[4,160,2048]{2,1,0:T(8,128)(2,1)} %bitcast.129), calls=%async_computation.1 | async-start | bytes 5242880 | tf_op jit(solution)/shard_map/all_to_all | solution.py:442
  289.3 145.4 %all-gather.11.cloned.1.call-start = ((), (), s32[]{:S(2)}) async-start(), calls=%async_computation.15 | async-start | bytes 8650752 | tf_op jit(solution)/shard_map/all_gather | solution.py:452
  289.5 4.6 collective-permute-start.2
  289.6 69.2 %collective-permute-start.3 = (bf16[640,2048]{1,0:T(8,128)(2,1)}, bf16[640,2048]{1,0:T(8,128)(2,1)}, u32[]{:S(2)}, u32[]{:S(2)}) collective-permute-start(bf16[640,2048]{1,0:T(8,128)(2,1)} %bitcast.15.g_ref), channel_id=1, source_target_pairs={{0,2},{1,3},{2,0},{3,1},{4,6},{5,7},{6,4},{7,5},{8,10},{9,11},{10,... | collective-permute-start | bytes 7864328 | tf_op jit(solution)/shard_map/ppermute | solution.py:355
  358.8 75.9 %all-to-all-start.2 = ((bf16[4,160,2048]{2,1,0:T(8,128)(2,1)}), bf16[4,160,2048]{2,1,0:T(8,128)(2,1)S(1)}, u32[]{:S(2)}, u32[]{:S(2)}) async-start(bf16[4,160,2048]{2,1,0:T(8,128)(2,1)} %bitcast.132), calls=%async_computation.2 | async-start | bytes 5242880 | tf_op jit(solution)/shard_map/all_to_all | solution.py:442
  367.3 5.6 collective-permute-start.4
  370.0 15.6 %collective-permute-start.5 = (bf16[704,2048]{1,0:T(8,128)(2,1)}, bf16[704,2048]{1,0:T(8,128)(2,1)}, u32[]{:S(2)}, u32[]{:S(2)}) collective-permute-start(bf16[704,2048]{1,0:T(8,128)(2,1)} %constant_dynamic-slice_fusion.13.refs_0_), channel_id=1, source_target_pairs={{0,16},{16,0},{1,17},{17,1},{2,18},{18,2},{3,19},{19,3},{4,20},{20... | collective-permute-start | bytes 8650760 | tf_op jit(solution)/shard_map/ppermute | solution.py:352
  370.0 64.7 %collective-permute-start.6 = (bf16[640,2048]{1,0:T(8,128)(2,1)}, bf16[640,2048]{1,0:T(8,128)(2,1)}, u32[]{:S(2)}, u32[]{:S(2)}) collective-permute-start(bf16[640,2048]{1,0:T(8,128)(2,1)} %bitcast.17.g_ref), channel_id=1, source_target_pairs={{0,2},{1,3},{2,0},{3,1},{4,6},{5,7},{6,4},{7,5},{8,10},{9,11},{10,... | collective-permute-start | bytes 7864328 | tf_op jit(solution)/shard_map/ppermute | solution.py:355
  434.7 64.5 %all-to-all-start.3 = ((bf16[4,160,2048]{2,1,0:T(8,128)(2,1)}), bf16[4,160,2048]{2,1,0:T(8,128)(2,1)}, u32[]{:S(2)}, u32[]{:S(2)}) async-start(bf16[4,160,2048]{2,1,0:T(8,128)(2,1)} %bitcast.130), calls=%async_computation.3 | async-start | bytes 5242880 | tf_op jit(solution)/shard_map/all_to_all | solution.py:442
  441.6 5.5 collective-permute-start.7
  441.6 80.2 %collective-permute-start.8 = (bf16[640,2048]{1,0:T(8,128)(2,1)S(1)}, bf16[640,2048]{1,0:T(8,128)(2,1)}, u32[]{:S(2)}, u32[]{:S(2)}) collective-permute-start(bf16[640,2048]{1,0:T(8,128)(2,1)S(1)} %bitcast.112), channel_id=1, source_target_pairs={{0,2},{1,3},{2,0},{3,1},{4,6},{5,7},{6,4},{7,5},{8,10},{9,11},{10,... | collective-permute-start | bytes 7864328 | tf_op jit(solution)/shard_map/ppermute | solution.py:355
  499.2 74.9 %collective-permute-start.9 = (bf16[640,2048]{1,0:T(8,128)(2,1)}, bf16[640,2048]{1,0:T(8,128)(2,1)}, u32[]{:S(2)}, u32[]{:S(2)}) collective-permute-start(bf16[640,2048]{1,0:T(8,128)(2,1)} %bitcast.24.x_ref), channel_id=1, source_target_pairs={{0,2},{1,3},{2,0},{3,1},{4,6},{5,7},{6,4},{7,5},{8,10},{9,11},{10,... | collective-permute-start | bytes 7864328 | tf_op jit(solution)/shard_map/ppermute | solution.py:355
  573.5 57.9 %collective-permute-start.10 = (bf16[640,2048]{1,0:T(8,128)(2,1)}, bf16[640,2048]{1,0:T(8,128)(2,1)}, u32[]{:S(2)}, u32[]{:S(2)}) collective-permute-start(bf16[640,2048]{1,0:T(8,128)(2,1)} %expert_rows.9), channel_id=1, source_target_pairs={{0,2},{1,3},{2,0},{3,1},{4,6},{5,7},{6,4},{7,5},{8,10},{9,11},{10,... | collective-permute-start | bytes 7864328 | tf_op jit(solution)/shard_map/ppermute | solution.py:355
  604.9 26.6 %copy-start.17 = (bf16[640,2048]{1,0:T(8,128)(2,1)S(1)}, bf16[640,2048]{1,0:T(8,128)(2,1)}, u32[]{:S(2)}) copy-start(bf16[640,2048]{1,0:T(8,128)(2,1)} %expert_rows.8) | copy-start | bytes 7864324
  635.7 61.8 %all-to-all-start.4 = ((bf16[4,160,2048]{2,1,0:T(8,128)(2,1)}), bf16[4,160,2048]{2,1,0:T(8,128)(2,1)S(1)}, u32[]{:S(2)}, u32[]{:S(2)}) async-start(bf16[4,160,2048]{2,1,0:T(8,128)(2,1)} %bitcast.117), calls=%async_computation.4 | async-start | bytes 5242880 | tf_op jit(solution)/shard_map/all_to_all | solution.py:442
  639.8 57.7 %collective-permute-start.11 = (bf16[640,2048]{1,0:T(8,128)(2,1)}, bf16[640,2048]{1,0:T(8,128)(2,1)}, u32[]{:S(2)}, u32[]{:S(2)}) collective-permute-start(bf16[640,2048]{1,0:T(8,128)(2,1)} %expert_rows.10), channel_id=1, source_target_pairs={{0,2},{1,3},{2,0},{3,1},{4,6},{5,7},{6,4},{7,5},{8,10},{9,11},{10,... | collective-permute-start | bytes 7864328 | tf_op jit(solution)/shard_map/ppermute | solution.py:355
  702.8 63.6 %all-to-all-start.5 = ((bf16[4,160,2048]{2,1,0:T(8,128)(2,1)}), bf16[4,160,2048]{2,1,0:T(8,128)(2,1)}, u32[]{:S(2)}, u32[]{:S(2)}) async-start(bf16[4,160,2048]{2,1,0:T(8,128)(2,1)} %bitcast.115), calls=%async_computation.5 | async-start | bytes 5242880 | tf_op jit(solution)/shard_map/all_to_all | solution.py:442
  707.3 357.4 %reduce-scatter.3.cloned.1.call-start = ((), (), s32[]{:S(2)}) async-start(), calls=%async_computation.16 | async-start | bytes 8650752 | tf_op jit(solution)/shard_map/reduce_scatter | solution.py:563
  751.8 38.5 %collective-permute-start.13 = (bf16[2816,1024]{1,0:T(8,128)(2,1)}, bf16[2816,1024]{1,0:T(8,128)(2,1)}, u32[]{:S(2)}, u32[]{:S(2)}) collective-permute-start(bf16[2816,1024]{1,0:T(8,128)(2,1)} %constant_dynamic-slice_fusion.11), channel_id=1, source_target_pairs={{0,16},{16,0},{1,17},{17,1},{2,18},{18,2},{3,19},{19,3},{4,20},{20... | collective-permute-start | bytes 17301512 | tf_op jit(solution)/shard_map/ppermute | solution.py:352
  775.6 24.5 %copy-start.18 = (bf16[512,2048]{1,0:T(8,128)(2,1)}, bf16[512,2048]{1,0:T(8,128)(2,1)S(1)}, u32[]{:S(2)}) copy-start(bf16[512,2048]{1,0:T(8,128)(2,1)S(1)} %fusion.106) | copy-start | bytes 6291460
  775.6 24.5 %collective-permute-start.12 = (bf16[512,2048]{1,0:T(8,128)(2,1)S(1)}, bf16[512,2048]{1,0:T(8,128)(2,1)}, u32[]{:S(2)}, u32[]{:S(2)}) collective-permute-start(bf16[512,2048]{1,0:T(8,128)(2,1)S(1)} %fusion.106), channel_id=1, source_target_pairs={{0,16},{16,0},{1,17},{17,1},{2,18},{18,2},{3,19},{19,3},{4,20},{20... | collective-permute-start | bytes 6291464 | tf_op jit(solution)/shard_map/ppermute | solution.py:352
  789.8 76.2 %collective-permute-start.14 = (bf16[640,2048]{1,0:T(8,128)(2,1)}, bf16[640,2048]{1,0:T(8,128)(2,1)}, u32[]{:S(2)}, u32[]{:S(2)}) collective-permute-start(bf16[640,2048]{1,0:T(8,128)(2,1)} %expert_rows.12), channel_id=1, source_target_pairs={{0,2},{1,3},{2,0},{3,1},{4,6},{5,7},{6,4},{7,5},{8,10},{9,11},{10,... | collective-permute-start | bytes 7864328 | tf_op jit(solution)/shard_map/ppermute | solution.py:355
  817.7 84.2 %collective-permute-start.15 = (bf16[512,2048]{1,0:T(8,128)(2,1)}, bf16[512,2048]{1,0:T(8,128)(2,1)}, u32[]{:S(2)}, u32[]{:S(2)}) collective-permute-start(bf16[512,2048]{1,0:T(8,128)(2,1)} %bitcast.30), channel_id=1, source_target_pairs={{0,2},{1,3},{2,0},{3,1},{4,6},{5,7},{6,4},{7,5},{8,10},{9,11},{10,... | collective-permute-start | bytes 6291464 | tf_op jit(solution)/shard_map/ppermute | solution.py:355
  819.2 383.5 %reduce-scatter.5.cloned.1.call-start = ((), (), s32[]{:S(2)}) async-start(), calls=%async_computation.17 | async-start | bytes 13369344 | tf_op jit(solution)/shard_map/reduce_scatter | solution.py:626
  908.0 36.5 %collective-permute-start.16 = (bf16[2816,1024]{1,0:T(8,128)(2,1)}, bf16[2816,1024]{1,0:T(8,128)(2,1)}, u32[]{:S(2)}, u32[]{:S(2)}) collective-permute-start(bf16[2816,1024]{1,0:T(8,128)(2,1)} %constant_dynamic-slice_fusion.6), channel_id=1, source_target_pairs={{0,16},{16,0},{1,17},{17,1},{2,18},{18,2},{3,19},{19,3},{4,20},{20... | collective-permute-start | bytes 17301512 | tf_op jit(solution)/shard_map/ppermute | solution.py:352
  925.3 14.9 %copy-start.16 = (bf16[640,2048]{1,0:T(8,128)(2,1)S(1)}, bf16[640,2048]{1,0:T(8,128)(2,1)}, u32[]{:S(2)}) copy-start(bf16[640,2048]{1,0:T(8,128)(2,1)} %expert_rows.13) | copy-start | bytes 7864324
  939.3 62.7 %collective-permute-start.17 = (bf16[256,2048]{1,0:T(8,128)(2,1)}, bf16[256,2048]{1,0:T(8,128)(2,1)}, u32[]{:S(2)}, u32[]{:S(2)}) collective-permute-start(bf16[256,2048]{1,0:T(8,128)(2,1)} %bitcast.134), channel_id=1, source_target_pairs={{0,1},{1,0},{2,3},{3,2},{4,5},{5,4},{6,7},{7,6},{8,9},{9,8},{10,11... | collective-permute-start | bytes 3145736 | tf_op jit(solution)/shard_map/ppermute | solution.py:355
  954.5 96.8 %all-to-all-start.6 = ((bf16[4,160,2048]{2,1,0:T(8,128)(2,1)}), bf16[4,160,2048]{2,1,0:T(8,128)(2,1)S(1)}, u32[]{:S(2)}, u32[]{:S(2)}) async-start(bf16[4,160,2048]{2,1,0:T(8,128)(2,1)} %bitcast.116), calls=%async_computation.6 | async-start | bytes 5242880 | tf_op jit(solution)/shard_map/all_to_all | solution.py:442
  961.2 90.2 %collective-permute-start.18 = (bf16[1408,1024]{1,0:T(8,128)(2,1)S(1)}, bf16[1408,1024]{1,0:T(8,128)(2,1)}, u32[]{:S(2)}, u32[]{:S(2)}) collective-permute-start(bf16[1408,1024]{1,0:T(8,128)(2,1)S(1)} %constant_dynamic-slice_fusion.5), channel_id=1, source_target_pairs={{0,1},{1,0},{2,3},{3,2},{4,5},{5,4},{6,7},{7,6},{8,9},{9,8},{10,11... | collective-permute-start | bytes 8650760 | tf_op jit(solution)/shard_map/ppermute | solution.py:355
  962.4 71.9 %collective-permute-start.19 = (bf16[640,2048]{1,0:T(8,128)(2,1)S(1)}, bf16[640,2048]{1,0:T(8,128)(2,1)S(1)}, u32[]{:S(2)}, u32[]{:S(2)}) collective-permute-start(bf16[640,2048]{1,0:T(8,128)(2,1)S(1)} %copy-done.22), channel_id=1, source_target_pairs={{0,2},{1,3},{2,0},{3,1},{4,6},{5,7},{6,4},{7,5},{8,10},{9,11},{10,... | collective-permute-start | bytes 7864328 | tf_op jit(solution)/shard_map/ppermute | solution.py:355
  1058.0 41.1 %collective-permute-start.20 = (bf16[2816,1024]{1,0:T(8,128)(2,1)}, bf16[2816,1024]{1,0:T(8,128)(2,1)}, u32[]{:S(2)}, u32[]{:S(2)}) collective-permute-start(bf16[2816,1024]{1,0:T(8,128)(2,1)} %constant_dynamic-slice_fusion.4), channel_id=1, source_target_pairs={{0,16},{16,0},{1,17},{17,1},{2,18},{18,2},{3,19},{19,3},{4,20},{20... | collective-permute-start | bytes 17301512 | tf_op jit(solution)/shard_map/ppermute | solution.py:352
  1060.6 37.5 %all-to-all-start.7 = ((bf16[4,64,2048]{2,1,0:T(8,128)(2,1)}), bf16[4,64,2048]{2,1,0:T(8,128)(2,1)S(1)}, u32[]{:S(2)}, u32[]{:S(2)}) async-start(bf16[4,64,2048]{2,1,0:T(8,128)(2,1)} %bitcast.35), calls=%async_computation.7 | async-start | bytes 2097152 | tf_op jit(solution)/shard_map/all_to_all | solution.py:442
  1120.4 10.4 collective-permute-start.21
  1120.5 82.3 %all-to-all-start.8 = ((bf16[4,160,2048]{2,1,0:T(8,128)(2,1)}), bf16[4,160,2048]{2,1,0:T(8,128)(2,1)}, u32[]{:S(2)}, u32[]{:S(2)}) async-start(bf16[4,160,2048]{2,1,0:T(8,128)(2,1)} %bitcast.36), calls=%async_computation.9 | async-start | bytes 5242880 | tf_op jit(solution)/shard_map/all_to_all | solution.py:442
  1130.7 13.5 %copy-start.44 = (f32[512]{0:T(512)S(1)}, f32[512]{0:T(512)}, u32[]{:S(2)}) copy-start(f32[512]{0:T(512)} %copy-done.42) | copy-start | bytes 6148
  1130.7 100.0 %collective-permute-start.23 = (bf16[1408,1024]{1,0:T(8,128)(2,1)}, bf16[1408,1024]{1,0:T(8,128)(2,1)}, u32[]{:S(2)}, u32[]{:S(2)}) collective-permute-start(bf16[1408,1024]{1,0:T(8,128)(2,1)} %get-tuple-element.265), channel_id=1, source_target_pairs={{0,1},{1,0},{2,3},{3,2},{4,5},{5,4},{6,7},{7,6},{8,9},{9,8},{10,11... | collective-permute-start | bytes 8650760 | tf_op jit(solution)/shard_map/ppermute | solution.py:355
  1203.5 24.0 %all-to-all-start.9 = ((f32[16,1,256]{2,1,0:T(1,128)}), f32[16,1,256]{2,1,0:T(1,128)S(1)}, u32[]{:S(2)}, u32[]{:S(2)}) async-start(f32[16,1,256]{2,1,0:T(1,128)} %reshape.269), calls=%async_computation.11 | async-start | bytes 32768 | tf_op jit(solution)/shard_map/all_to_all | solution.py:670
  1228.8 1.8 collective-permute-start.22
  1230.1 6.9 collective-permute-start.24
  (51 other events, 284.3 us)
Sparse Core Ops, SparseCore 0:
  13.6 194.3 all-gather.4
  210.0 72.6 all-gather.6
  284.3 74.4 all-gather.8
  360.2 74.4 all-gather.10
  819.3 69.9 reduce-scatter.2
  908.1 286.7 reduce-scatter.4
